TPU v7x, 32 devices: a whole 2x2x4 slice. The times are simulated.
32 devices in a mesh: ctx: 8 (over y, x, core), wt: 4 (over z).
Axes of the slice: x: 2, y: 2, z: 4, core: 2. Of those that a mesh axis runs over, the one named last changes fastest.
Arguments:
- words: bfloat16 [6144, 512], P(('ctx', 'wt')), may hold values from -6 to 6
- teacher: bfloat16 [6144, 512], P(('ctx', 'wt')), may hold values from -6 to 6
- valid: int32 [6144], P(('ctx', 'wt')), may hold values from 0 to 1, as said below
- lengths: int32 [4], replicated, may hold values from 384 to 3072, as said below
- deal: int32 [32], replicated, may hold values from 0 to 31, as said below
- gain_attn: bfloat16 [512], P('wt'), may hold values from 0.25 to 1.75
- shift_attn: bfloat16 [512], P('wt'), may hold values from -3 to 3
- w_qkv: bfloat16 [512, 1536], P('wt'), may hold values from -0.25 to 0.25
- w_out: bfloat16 [512, 512], P('wt'), may hold values from -2 to 2
- gain_mlp: bfloat16 [512], P('wt'), may hold values from 0.25 to 1.75
- shift_mlp: bfloat16 [512], P('wt'), may hold values from -3 to 3
- w_up: bfloat16 [512, 2048], P('wt'), may hold values from -0.25 to 0.25
- w_down: bfloat16 [2048, 512], P('wt'), may hold values from -0.125 to 0.125
Outputs:
- layer_out: bfloat16 [6144, 512], P(('ctx', 'wt'))
- loss: float32 [], replicated
- grad_words: float32 [6144, 512], P(('ctx', 'wt'))
- grad_gain_attn: float32 [512], P('wt')
- grad_shift_attn: float32 [512], P('wt')
- grad_w_qkv: float32 [512, 1536], P('wt')
- grad_w_out: float32 [512, 512], P('wt')
- grad_gain_mlp: float32 [512], P('wt')
- grad_shift_mlp: float32 [512], P('wt')
- grad_w_up: float32 [512, 2048], P('wt')
- grad_w_down: float32 [2048, 512], P('wt')
Inputs may be any that keep to these rules, and one draw needn't show every extreme that they name: lengths are multiples of 192 that sum to 6144; one sequence has exactly 3072 words. `deal`: each initial block appears once; initial blocks that differ by a multiple of the number of ctx indices lie on the same ctx index. The first word of every dealt block is valid.
All inputs are finite; a program needn't handle non-finite values.
Results may differ from a plain program's by a relative error of at most 0.02.
Values may be sent and summed in bfloat16 or wider, within the bound.
No kernel may reach another device: no remote copies, remote signals or barrier semaphores. Data moves between devices by JAX's collectives and lax.ppermute only.
A program may use at most 128 MiB of HBM per device.

v0:
```python
import jax
import jax.numpy as jnp
from jax import lax
from jax.sharding import PartitionSpec as P

H = 8
HEAD = 64


EPS = 1e-05
LOSS_SCALE = 262144.0


def norm_forward(values, gain_vec, shift_vec):
    center = values - jnp.mean(values, axis=-1, keepdims=True)
    inverse = lax.rsqrt(jnp.mean(center * center, axis=-1, keepdims=True) + EPS)
    unit_rows = center * inverse
    return (unit_rows * gain_vec + shift_vec, unit_rows, inverse)


def norm_backward(upstream, unit_rows, inverse, gain_vec):
    scaled = upstream * gain_vec
    inner_term = jnp.mean(scaled * unit_rows, axis=-1, keepdims=True)
    result = inverse * (scaled - jnp.mean(scaled, axis=-1, keepdims=True) - unit_rows * inner_term)
    return (result, jnp.sum(upstream * unit_rows, axis=0), jnp.sum(upstream, axis=0))


def per_device(
    words,
    teacher,
    valid,
    lengths,
    deal,
    gain_attn,
    shift_attn,
    w_qkv,
    w_out,
    gain_mlp,
    shift_mlp,
    w_up,
    w_down,
):
    ctx_count = lax.axis_size("ctx")
    wt_count = lax.axis_size("wt")
    blk_rows = words.shape[0]
    model_width = words.shape[1]
    head_count = H // wt_count
    col_span = 3 * head_count * HEAD
    group_rows = blk_rows * wt_count
    score_scale = HEAD ** (-0.5)
    qkv_full, out_full, gain_first_raw, shift_first_raw = (
        lax.all_gather(w_qkv, "wt", axis=0, tiled=True),
        lax.all_gather(w_out, "wt", axis=0, tiled=True),
        lax.all_gather(gain_attn, "wt", axis=0, tiled=True),
        lax.all_gather(shift_attn, "wt", axis=0, tiled=True),
    )
    qkv_grouped = qkv_full.reshape(model_width, wt_count, col_span)
    out_grouped = out_full.reshape(wt_count, head_count * HEAD, model_width)
    gain_first = gain_first_raw.astype(jnp.float32)
    shift_first = shift_first_raw.astype(jnp.float32)
    inputs = words.astype(jnp.float32)
    normed_one, unit_first, inverse_first = norm_forward(inputs, gain_first, shift_first)
    packed_first = normed_one.astype(jnp.bfloat16)
    projected = jnp.einsum(
        "rd,dwc->wrc", packed_first, qkv_grouped, preferred_element_type=jnp.float32
    ).astype(jnp.bfloat16)
    head_rows = lax.all_to_all(
        projected.reshape(wt_count, blk_rows * col_span),
        "wt",
        split_axis=0,
        concat_axis=0,
        tiled=True,
    )
    head_rows = head_rows.reshape(group_rows, head_count, 3, HEAD)
    queries = head_rows[:, :, 0]
    own_kv = head_rows[:, :, 1:]
    key_values = own_kv.reshape(group_rows, head_count * 2 * HEAD)
    gathered = lax.all_gather(key_values, "ctx", axis=0, tiled=True).reshape(
        ctx_count, group_rows, head_count, 2, HEAD
    )
    offsets = jnp.arange(blk_rows, dtype=jnp.int32)
    bounds = jnp.cumsum(lengths)
    key_place = (deal[:, None] * blk_rows + offsets[None, :]).reshape(ctx_count, group_rows)
    key_seq = jnp.sum((key_place[:, :, None] >= bounds[None, None, :]).astype(jnp.int32), axis=-1)
    ctx_here = lax.axis_index("ctx")
    query_place = lax.dynamic_index_in_dim(key_place, ctx_here, 0, keepdims=False)
    query_seq = lax.dynamic_index_in_dim(key_seq, ctx_here, 0, keepdims=False)
    live_pieces = jnp.ones((ctx_count,), dtype=bool)
    scan_items = (gathered, key_place, key_seq, live_pieces)

    def scores_of(kv_piece, piece_place, piece_seq):
        raw_scores = (
            jnp.einsum(
                "qhd,khd->hqk", queries, kv_piece[:, :, 0], preferred_element_type=jnp.float32
            )
            * score_scale
        )
        visible = (piece_seq[None, :] == query_seq[:, None]) & (
            piece_place[None, :] <= query_place[:, None]
        )
        return (raw_scores, visible[None])

    def forward_step(carry, item):
        kv_piece, piece_place, piece_seq, live_piece = item
        running_max, running_sum, running_acc = carry
        raw_scores, visible = scores_of(kv_piece, piece_place, piece_seq)
        piece_max = jnp.max(jnp.where(visible, raw_scores, -1e30), axis=-1)
        new_max = jnp.maximum(running_max, piece_max)
        weights = jnp.where(visible, jnp.exp(raw_scores - new_max[..., None]), 0.0)
        factor = jnp.exp(running_max - new_max)
        new_sum = running_sum * factor + jnp.sum(weights, axis=-1)
        new_acc = running_acc * factor.T[:, :, None] + jnp.einsum(
            "hqk,khd->qhd",
            weights.astype(jnp.bfloat16),
            kv_piece[:, :, 1],
            preferred_element_type=jnp.float32,
        )
        return ((new_max, new_sum, new_acc), None)

    start_max = jnp.full((head_count, group_rows), -1e30, jnp.float32)
    start_sum = jnp.zeros((head_count, group_rows), jnp.float32)
    start_acc = jnp.zeros((group_rows, head_count, HEAD), jnp.float32)
    (row_max, row_sum, row_acc), _ = lax.scan(
        forward_step, (start_max, start_sum, start_acc), scan_items
    )
    log_total = row_max + jnp.log(row_sum)
    attended_full = row_acc / row_sum.T[:, :, None]
    attended_heads = attended_full.astype(jnp.bfloat16)
    attended_rows = lax.all_to_all(
        attended_heads.reshape(wt_count, blk_rows * head_count * HEAD),
        "wt",
        split_axis=0,
        concat_axis=0,
        tiled=True,
    ).reshape(wt_count, blk_rows, head_count * HEAD)
    residual_one = inputs + jnp.einsum(
        "wrc,wcd->rd", attended_rows, out_grouped, preferred_element_type=jnp.float32
    )
    up_full, down_full, gain_second_raw, shift_second_raw = (
        lax.all_gather(w_up, "wt", axis=0, tiled=True),
        lax.all_gather(w_down, "wt", axis=0, tiled=True),
        lax.all_gather(gain_mlp, "wt", axis=0, tiled=True),
        lax.all_gather(shift_mlp, "wt", axis=0, tiled=True),
    )
    gain_second = gain_second_raw.astype(jnp.float32)
    shift_second = shift_second_raw.astype(jnp.float32)
    normed_two, unit_second, inverse_second = norm_forward(residual_one, gain_second, shift_second)
    packed_second = normed_two.astype(jnp.bfloat16)
    before_act = jnp.dot(packed_second, up_full, preferred_element_type=jnp.float32)
    activated = jax.nn.gelu(before_act, approximate=False).astype(jnp.bfloat16)
    residual_two = residual_one + jnp.dot(activated, down_full, preferred_element_type=jnp.float32)
    distance = residual_two - teacher.astype(jnp.float32)
    valid_float = valid.astype(jnp.float32)
    count_all, square_all = lax.psum(
        (jnp.sum(valid_float), jnp.sum(valid_float * jnp.sum(distance * distance, axis=-1))),
        ("ctx", "wt"),
    )
    loss_value = square_all / (count_all * model_width)
    grad_two = 2.0 * LOSS_SCALE / (count_all * model_width) * valid_float[:, None] * distance
    grad_branch = grad_two.astype(jnp.bfloat16)
    grad_down = jnp.einsum("rf,rd->fd", activated, grad_branch, preferred_element_type=jnp.float32)
    grad_act = jnp.einsum("rd,fd->rf", grad_branch, down_full, preferred_element_type=jnp.float32)
    _, gelu_back = jax.vjp(lambda hidden_in: jax.nn.gelu(hidden_in, approximate=False), before_act)
    grad_pre = gelu_back(grad_act)[0].astype(jnp.bfloat16)
    grad_up = jnp.einsum("rd,rf->df", packed_second, grad_pre, preferred_element_type=jnp.float32)
    grad_normed_two = jnp.einsum("rf,df->rd", grad_pre, up_full, preferred_element_type=jnp.float32)
    back_two, grad_gain_second, grad_shift_second = norm_backward(
        grad_normed_two, unit_second, inverse_second, gain_second
    )
    grad_one = grad_two + back_two
    grad_attn_out = grad_one.astype(jnp.bfloat16)
    grad_out = jnp.einsum(
        "wrc,rd->wcd", attended_rows, grad_attn_out, preferred_element_type=jnp.float32
    ).reshape(model_width, model_width)
    grad_att_rows = jnp.einsum(
        "rd,wcd->wrc", grad_attn_out, out_grouped, preferred_element_type=jnp.float32
    ).astype(jnp.bfloat16)
    grad_att_heads = lax.all_to_all(
        grad_att_rows.reshape(wt_count, blk_rows * head_count * HEAD),
        "wt",
        split_axis=0,
        concat_axis=0,
        tiled=True,
    ).reshape(group_rows, head_count, HEAD)
    row_delta = jnp.sum(grad_att_heads.astype(jnp.float32) * attended_full, axis=-1).T

    def score_grads(kv_piece, piece_place, piece_seq):
        raw_scores, visible = scores_of(kv_piece, piece_place, piece_seq)
        probs = jnp.where(visible, jnp.exp(raw_scores - log_total[..., None]), 0.0)
        grad_probs = jnp.einsum(
            "qhd,khd->hqk", grad_att_heads, kv_piece[:, :, 1], preferred_element_type=jnp.float32
        )
        return (probs, (probs * (grad_probs - row_delta[..., None])).astype(jnp.bfloat16))

    def grad_step(carry, item):
        kv_piece, piece_place, piece_seq, live_piece = item
        probs, grad_scores = score_grads(kv_piece, piece_place, piece_seq)
        grad_keys = (
            jnp.einsum("hqk,qhd->khd", grad_scores, queries, preferred_element_type=jnp.float32)
            * score_scale
        )
        grad_values = jnp.einsum(
            "hqk,qhd->khd",
            probs.astype(jnp.bfloat16),
            grad_att_heads,
            preferred_element_type=jnp.float32,
        )
        grad_next = carry + jnp.einsum(
            "hqk,khd->qhd", grad_scores, kv_piece[:, :, 0], preferred_element_type=jnp.float32
        )
        return (grad_next, jnp.stack([grad_keys, grad_values], axis=2))

    grad_query_sum, grad_pieces = lax.scan(
        grad_step, jnp.zeros((group_rows, head_count, HEAD), jnp.float32), scan_items
    )
    grad_kv = lax.psum_scatter(
        grad_pieces.reshape(ctx_count * group_rows, head_count * 2 * HEAD).astype(jnp.bfloat16),
        "ctx",
        scatter_dimension=0,
        tiled=True,
    ).astype(jnp.float32)
    grad_kv = grad_kv.astype(jnp.bfloat16).reshape(group_rows, head_count, 2, HEAD)
    grad_queries = (grad_query_sum * score_scale).astype(jnp.bfloat16)
    grad_heads = jnp.concatenate([grad_queries[:, :, None], grad_kv], axis=2)
    grad_rows = lax.all_to_all(
        grad_heads.reshape(wt_count, blk_rows * col_span),
        "wt",
        split_axis=0,
        concat_axis=0,
        tiled=True,
    ).reshape(wt_count, blk_rows, col_span)
    grad_qkv = jnp.einsum(
        "rd,wrc->dwc", packed_first, grad_rows, preferred_element_type=jnp.float32
    ).reshape(model_width, 3 * model_width)
    grad_normed_one = jnp.einsum(
        "wrc,dwc->rd", grad_rows, qkv_grouped, preferred_element_type=jnp.float32
    )
    back_one, grad_gain_first, grad_shift_first = norm_backward(
        grad_normed_one, unit_first, inverse_first, gain_first
    )
    grad_words = grad_one + back_one
    shard_ga, shard_sa, shard_qkv, shard_out, shard_gm, shard_sm, shard_up, shard_down = (
        lax.psum_scatter(
            grad_gain_first.astype(jnp.bfloat16), "wt", scatter_dimension=0, tiled=True
        ).astype(jnp.float32),
        lax.psum_scatter(
            grad_shift_first.astype(jnp.bfloat16), "wt", scatter_dimension=0, tiled=True
        ).astype(jnp.float32),
        lax.psum_scatter(
            grad_qkv.astype(jnp.bfloat16), "wt", scatter_dimension=0, tiled=True
        ).astype(jnp.float32),
        lax.psum_scatter(
            grad_out.astype(jnp.bfloat16), "wt", scatter_dimension=0, tiled=True
        ).astype(jnp.float32),
        lax.psum_scatter(
            grad_gain_second.astype(jnp.bfloat16), "wt", scatter_dimension=0, tiled=True
        ).astype(jnp.float32),
        lax.psum_scatter(
            grad_shift_second.astype(jnp.bfloat16), "wt", scatter_dimension=0, tiled=True
        ).astype(jnp.float32),
        lax.psum_scatter(
            grad_up.astype(jnp.bfloat16), "wt", scatter_dimension=0, tiled=True
        ).astype(jnp.float32),
        lax.psum_scatter(
            grad_down.astype(jnp.bfloat16), "wt", scatter_dimension=0, tiled=True
        ).astype(jnp.float32),
    )
    summed = (
        lax.psum(shard_ga.astype(jnp.bfloat16), "ctx").astype(jnp.float32),
        lax.psum(shard_sa.astype(jnp.bfloat16), "ctx").astype(jnp.float32),
        lax.psum(shard_qkv.astype(jnp.bfloat16), "ctx").astype(jnp.float32),
        lax.psum(shard_out.astype(jnp.bfloat16), "ctx").astype(jnp.float32),
        lax.psum(shard_gm.astype(jnp.bfloat16), "ctx").astype(jnp.float32),
        lax.psum(shard_sm.astype(jnp.bfloat16), "ctx").astype(jnp.float32),
        lax.psum(shard_up.astype(jnp.bfloat16), "ctx").astype(jnp.float32),
        lax.psum(shard_down.astype(jnp.bfloat16), "ctx").astype(jnp.float32),
    )
    return (
        residual_two.astype(jnp.bfloat16),
        loss_value,
        grad_words,
        summed[0],
        summed[1],
        summed[2],
        summed[3],
        summed[4],
        summed[5],
        summed[6],
        summed[7],
    )


def solution(mesh):
    placed = (
        P(("ctx", "wt"), None),
        P(("ctx", "wt"), None),
        P(("ctx", "wt")),
        P(),
        P(),
        P("wt"),
        P("wt"),
        P("wt", None),
        P("wt", None),
        P("wt"),
        P("wt"),
        P("wt", None),
        P("wt", None),
    )
    return jax.shard_map(
        per_device,
        mesh=mesh,
        in_specs=placed,
        out_specs=(
            P(("ctx", "wt"), None),
            P(),
            P(("ctx", "wt"), None),
            P("wt"),
            P("wt"),
            P("wt", None),
            P("wt", None),
            P("wt"),
            P("wt"),
            P("wt", None),
            P("wt", None),
        ),
        check_vma=False,
    )
```

profile of v0, /device:TPU:0, one launch (start us, length us, event | category | flops | bytes accessed | tf_op | source)
XLA Modules:
  0.0 679.7 jit_solution(10840386280325061220)
XLA Ops:
  9.3 12.7 %all-gather = bf16[4,1,128]{2,1,0:T(2,128)(2,1)S(1)} all-gather(bf16[1,1,128]{2,1,0:T(2,128)(2,1)} %bitcast.256), channel_id=1, replica_groups=mesh['ctx'=8,'wt'=4] {'wt'}, dimensions={0}, use_global_device_ids=true | all-gather | bytes 1280 | tf_op jit(solution)/shard_map/all_gather | solution.py:54
  22.0 7.8 %all-gather.1 = bf16[4,1,128]{2,1,0:T(2,128)(2,1)S(1)} all-gather(bf16[1,1,128]{2,1,0:T(2,128)(2,1)} %bitcast.257), channel_id=1, replica_groups=mesh['ctx'=8,'wt'=4] {'wt'}, dimensions={0}, use_global_device_ids=true | all-gather | bytes 1280 | tf_op jit(solution)/shard_map/all_gather | solution.py:55
  32.0 18.6 %all-gather.9.cloned.1.call-done = bf16[512,1536]{0,1:T(8,128)(2,1)} async-done(((bf16[128,1536]{0,1:T(8,128)(2,1)}), bf16[512,1536]{0,1:T(8,128)(2,1)}) %all-gather.9.cloned.1.call-update) | async-done | bytes 1572880 | tf_op jit(solution)/shard_map/all_gather | solution.py:52
  53.6 4.4 reduce.16
  58.6 18.8 %all_to_all.40 = bf16[4,2,36864]{2,1,0:T(2,128)(2,1)S(1)} all-to-all(bf16[4,2,36864]{2,1,0:T(2,128)(2,1)S(1)} %reshape.330), channel_id=1, replica_groups=mesh['ctx'=8,'wt'=4] {'wt'}, dimensions={0} | all-to-all | bytes 1179648 | tf_op jit(solution)/shard_map/all_to_all | solution.py:67
  90.4 26.7 %all-gather.11.cloned.1.call-done = bf16[6144,256]{0,1:T(8,128)(2,1)} async-done(((bf16[768,256]{0,1:T(8,128)(2,1)}), bf16[6144,256]{0,1:T(8,128)(2,1)}) %all-gather.11.cloned.1.call-update) | async-done | bytes 3145744 | tf_op jit(solution)/shard_map/all_gather | solution.py:78
  122.3 84.7 %while.28 = (s32[]{:T(128)}, f32[2,768]{1,0:T(2,128)S(1)}, f32[2,768]{1,0:T(2,128)S(1)}, f32[768,2,64]{0,2,1:T(8,128)S(1)}, s32[8,768]{1,0:T(8,128)}, /*index=5*...) while((s32[]{:T(128)}, f32[2,768]{1,0:T(2,128)S(1)}, ...), condition=%wide.region_7.8_spmd.clone, body=%wide.region_4.7_spmd.clone.sunk | while | flops 317039616 | bytes 37675172 | solution.py:123
  127.8 3.8 fusion.123
  138.4 3.8 fusion.123
  148.9 3.8 fusion.123
  159.5 3.8 fusion.123
  170.0 4.1 fusion.123
  181.0 3.8 fusion.123
  191.5 3.9 fusion.123
  202.1 3.8 fusion.123
  213.4 4.5 all-to-all-start.1
  217.9 11.3 %all-gather.2 = bf16[4,1,128]{2,1,0:T(2,128)(2,1)S(1)} all-gather(bf16[1,1,128]{2,1,0:T(2,128)(2,1)S(1)} %bitcast.258), channel_id=1, replica_groups=mesh['ctx'=8,'wt'=4] {'wt'}, dimensions={0}, use_global_device_ids=true | all-gather | bytes 1280 | tf_op jit(solution)/shard_map/all_gather | solution.py:142
  229.2 7.7 %all-gather.3 = bf16[4,1,128]{2,1,0:T(2,128)(2,1)S(1)} all-gather(bf16[1,1,128]{2,1,0:T(2,128)(2,1)S(1)} %bitcast.259), channel_id=1, replica_groups=mesh['ctx'=8,'wt'=4] {'wt'}, dimensions={0}, use_global_device_ids=true | all-gather | bytes 1280 | tf_op jit(solution)/shard_map/all_gather | solution.py:143
  236.9 15.2 %all_gather.31 = bf16[512,512]{1,0:T(8,128)(2,1)S(1)} all-gather(bf16[128,512]{1,0:T(8,128)(2,1)S(1)} %copy-done.20), channel_id=1, replica_groups=mesh['ctx'=8,'wt'=4] {'wt'}, dimensions={0}, use_global_device_ids=true | all-gather | bytes 655360 | tf_op jit(solution)/shard_map/all_gather | solution.py:53
  254.2 6.9 %multiply_convert_fusion = (bf16[192,2048]{1,0:T(8,128)(2,1)}, f32[192,2048]{1,0:T(8,128)}, f32[192,2048]{1,0:T(8,128)}) fusion(bf16[512,2048]{1,0:T(8,128)(2,1)} %all-gather.13.cloned.1.call-done, f32[192,512]{1,0:T(8,128)S(1)} %get-tuple-element.400, f32[512]{0:T(512)S(1)} %bitcast.253, f32[512]{0:T(512)S(1)} %bitcast.249, f32[192]{0:T(256)S(1)} %add_rsqrt_fusion, ...), kind=kOutput, calls=%fused_computation.55 | convolution fusion | flops 428703744 | bytes 6428160 | tf_op jit(solution)/shard_map/dot_general | solution.py:149
  264.3 38.9 %all-reduce.4 = (f32[]{:T(128)}, f32[]{:T(128)}) all-reduce(f32[]{:T(128)} %get-tuple-element.324, f32[]{:T(128)} %get-tuple-element.323), channel_id=1, replica_groups=mesh['ctx'=8,'wt'=4] {'ctx','wt'}, use_global_device_ids=true, to_apply=%region_12.13 | all-reduce | flops 2 | bytes 16 | tf_op jit(solution)/shard_map/psum | solution.py:154
  318.0 5.9 all-to-all-done.2
  328.3 66.9 %while.29 = (s32[]{:T(128)}, f32[768,2,64]{0,2,1:T(8,128)S(1)}, bf16[8,768,2,2,64]{1,4,2,3,0:T(8,128)(2,1)}, bf16[8,768,2,2,64]{1,4,2,3,0:T(8,128)(2,1)}, s32[8,...) while((s32[]{:T(128)}, f32[768,2,64]{0,2,1:T(8,128)S(1)}, ...), condition=%wide.region_19.20_spmd.clone, body=%wide.region_18.19_spmd.clone.sunk | while | flops 769720320 | bytes 28011244 | solution.py:213
  409.4 38.5 %reduce-scatter.6.cloned.1.call-done = bf16[768,256]{0,1:T(8,128)(2,1)} async-done(((bf16[6144,256]{0,1:T(8,128)(2,1)}), bf16[768,256]{0,1:T(8,128)(2,1)}) %reduce-scatter.6.cloned.1.call-update) | async-done | bytes 393232 | tf_op jit(solution)/shard_map/reduce_scatter | solution.py:216
  452.1 5.6 reduce.19
  458.3 23.0 %all_to_all.41 = bf16[4,2,36864]{2,1,0:T(2,128)(2,1)S(1)} all-to-all(bf16[4,2,36864]{2,1,0:T(2,128)(2,1)S(1)} %reshape.336), channel_id=1, replica_groups=mesh['ctx'=8,'wt'=4] {'wt'}, dimensions={0} | all-to-all | bytes 1179648 | tf_op jit(solution)/shard_map/all_to_all | solution.py:225
  490.3 31.3 %reduce-scatter.12.cloned.1.call-done = bf16[128,2048]{1,0:T(8,128)(2,1)} async-done(((bf16[512,2048]{1,0:T(8,128)(2,1)}), bf16[128,2048]{1,0:T(8,128)(2,1)}) %reduce-scatter.12.cloned.1.call-update) | async-done | bytes 524304 | tf_op jit(solution)/shard_map/reduce_scatter | solution.py:261
  521.7 45.5 %reduce-scatter.14.cloned.1.call-done = bf16[512,512]{1,0:T(8,128)(2,1)} async-done(((bf16[2048,512]{1,0:T(8,128)(2,1)}), bf16[512,512]{1,0:T(8,128)(2,1)}) %reduce-scatter.14.cloned.1.call-update) | async-done | bytes 524304 | tf_op jit(solution)/shard_map/reduce_scatter | solution.py:264
  567.2 37.1 %reduce-scatter.8.cloned.1.call-done = bf16[128,1536]{1,0:T(8,128)(2,1)} async-done(((bf16[512,1536]{1,0:T(8,128)(2,1)}), bf16[128,1536]{1,0:T(8,128)(2,1)}) %reduce-scatter.8.cloned.1.call-update) | async-done | bytes 393232 | tf_op jit(solution)/shard_map/reduce_scatter | solution.py:249
  606.4 9.8 %all-reduce.7 = (bf16[512]{0:T(512)(128)(2,1)S(1)}, bf16[512]{0:T(512)(128)(2,1)S(1)}, bf16[512]{0:T(512)(128)(2,1)S(1)}, bf16[512]{0:T(512)(128)(2,1)S(1)}) all-reduce(bf16[512]{0:T(512)(128)(2,1)S(1)} %get-tuple-element.317, bf16[512]{0:T(512)(128)(2,1)S(1)} %get-tuple-element.322, ...), channel_id=3, replica_groups=mesh['ctx'=8,'wt'=4] {'wt'}, use_global_device_ids=true, to_apply=%region_24.25.clone | all-reduce | flops 2048 | bytes 8192
  616.5 11.9 %all-reduce.5 = (bf16[128]{0:T(256)(128)(2,1)S(1)}, bf16[128]{0:T(256)(128)(2,1)S(1)}, bf16[128]{0:T(256)(128)(2,1)S(1)}, bf16[128]{0:T(256)(128)(2,1)S(1)}) all-reduce(bf16[128]{0:T(256)(128)(2,1)S(1)} %dynamic-slice.1, bf16[128]{0:T(256)(128)(2,1)S(1)} %dynamic-slice.3, ...), channel_id=1, replica_groups=mesh['ctx'=8,'wt'=4] {'ctx'}, use_global_device_ids=true, to_apply=%region_25.26 | all-reduce | flops 512 | bytes 2048 | tf_op jit(solution)/shard_map/psum | solution.py:269
  631.3 35.2 %all-reduce.10.cloned.1.call-done = (bf16[128,1536]{1,0:T(8,128)(2,1)}, bf16[128,512]{1,0:T(8,128)(2,1)}, bf16[128,2048]{1,0:T(8,128)(2,1)}, bf16[512,512]{1,0:T(8,128)(2,1)}) async-done(((bf16[128,1536]{1,0:T(8,128)(2,1)}, bf16[128,512]{1,0:T(8,128)(2,1)}, bf16[128,2048]{1,0:T(8,128)(2,1)}, bf16[512,512]{1,0:T(8,128)(2,1)}), (bf16[128,1536]{1,0:T(8,128)(2,1)}, bf16[128,512]{1,0:T(8,128)(2,1)}, ...) | async-done | bytes 1572880 | tf_op jit(solution)/shard_map/psum | solution.py:271
  (418 shorter events, 212.1 us)
Async XLA Ops:
  7.2 43.5 %copy-start.3 = (bf16[192,512]{1,0:T(8,128)(2,1)S(1)}, bf16[192,512]{1,0:T(8,128)(2,1)}, u32[]{:S(2)}) copy-start(bf16[192,512]{1,0:T(8,128)(2,1)} %param.17) | copy-start | bytes 589828
  7.2 43.4 %all-gather.9.cloned.1.call-start = ((), (), s32[]{:S(2)}) async-start(), calls=%async_computation.9 | async-start | bytes 1966080 | tf_op jit(solution)/shard_map/all_gather | solution.py:52
  9.2 107.9 %all-gather.11.cloned.1.call-start = ((), (), s32[]{:S(2)}) async-start(), calls=%async_computation.10 | async-start | bytes 3538944 | tf_op jit(solution)/shard_map/all_gather | solution.py:78
  22.0 28.6 %copy-start.22 = (f32[4,1,128]{2,1,0:T(1,128)}, f32[4,1,128]{2,1,0:T(1,128)S(1)}, u32[]{:S(2)}) copy-start(f32[4,1,128]{2,1,0:T(1,128)S(1)} %convert_element_type.187) | copy-start | bytes 6148
  29.8 20.8 %copy-start.26 = (f32[4,1,128]{2,1,0:T(1,128)}, f32[4,1,128]{2,1,0:T(1,128)S(1)}, u32[]{:S(2)}) copy-start(f32[4,1,128]{2,1,0:T(1,128)S(1)} %convert_element_type.188) | copy-start | bytes 6148
  30.8 19.8 %copy-start.24 = (f32[192]{0:T(256)}, f32[192]{0:T(256)S(1)}, u32[]{:S(2)}) copy-start(f32[192]{0:T(256)S(1)} %broadcast_multiply_fusion.5) | copy-start | bytes 2308
  32.0 18.6 %copy-start.32 = (f32[192]{0:T(256)}, f32[192]{0:T(256)S(1)}, u32[]{:S(2)}) copy-start(f32[192]{0:T(256)S(1)} %add_rsqrt_fusion.1) | copy-start | bytes 2308
  85.4 168.8 %all-gather.13.cloned.1.call-start = ((), (), s32[]{:S(2)}) async-start(), calls=%async_computation.11 | async-start | bytes 2621440 | tf_op jit(solution)/shard_map/all_gather | solution.py:140
  86.1 175.0 %all-gather.15.cloned.1.call-start = ((), (), s32[]{:S(2)}) async-start(), calls=%async_computation.12 | async-start | bytes 2621440 | tf_op jit(solution)/shard_map/all_gather | solution.py:141
  138.4 3.8 copy-start
  170.0 4.3 copy-start
  191.5 3.9 copy-start
  210.4 7.5 %copy-start.43 = (bf16[128]{0:T(256)(128)(2,1)S(1)}, bf16[128]{0:T(256)(128)(2,1)}, u32[]{:S(2)}) copy-start(bf16[128]{0:T(256)(128)(2,1)} %param.26) | copy-start | bytes 772
  210.4 18.9 %copy-start.44 = (bf16[128]{0:T(256)(128)(2,1)S(1)}, bf16[128]{0:T(256)(128)(2,1)}, u32[]{:S(2)}) copy-start(bf16[128]{0:T(256)(128)(2,1)} %param.27) | copy-start | bytes 772
  210.4 26.5 %copy-start.20 = (bf16[128,512]{1,0:T(8,128)(2,1)S(1)}, bf16[128,512]{1,0:T(8,128)(2,1)}, u32[]{:S(2)}) copy-start(bf16[128,512]{1,0:T(8,128)(2,1)} %param.25) | copy-start | bytes 393220
  213.4 38.7 %all-to-all-start.1 = ((bf16[4,2,12288]{2,1,0:T(2,128)(2,1)}), bf16[4,2,12288]{2,1,0:T(2,128)(2,1)S(1)}, u32[]{:S(2)}, u32[]{:S(2)}) async-start(bf16[4,2,12288]{2,1,0:T(2,128)(2,1)} %reshape.332), calls=%async_computation.1 | async-start | bytes 393216 | tf_op jit(solution)/shard_map/all_to_all | solution.py:129
  229.2 80.0 %copy-start.28 = (f32[4,1,128]{2,1,0:T(1,128)}, f32[4,1,128]{2,1,0:T(1,128)S(1)}, u32[]{:S(2)}) copy-start(f32[4,1,128]{2,1,0:T(1,128)S(1)} %convert_element_type.189) | copy-start | bytes 6148
  236.9 17.3 %copy-start.36 = (f32[4,1,128]{2,1,0:T(1,128)}, f32[4,1,128]{2,1,0:T(1,128)S(1)}, u32[]{:S(2)}) copy-start(f32[4,1,128]{2,1,0:T(1,128)S(1)} %convert_element_type.190) | copy-start | bytes 6148
  253.5 7.6 %copy-start.8 = (bf16[4,24576]{1,0:T(4,128)(2,1)}, bf16[4,24576]{1,0:T(4,128)(2,1)S(1)}, u32[]{:S(2)}) copy-start(bf16[4,24576]{1,0:T(4,128)(2,1)S(1)} %reduce.7) | copy-start | bytes 589828
  253.9 55.3 %copy-start.1 = (f32[192,512]{1,0:T(8,128)}, f32[192,512]{1,0:T(8,128)S(1)}, u32[]{:S(2)}) copy-start(f32[192,512]{1,0:T(8,128)S(1)} %get-tuple-element.400) | copy-start | bytes 1179652
  253.9 55.3 %copy-start.30 = (f32[192]{0:T(256)}, f32[192]{0:T(256)S(1)}, u32[]{:S(2)}) copy-start(f32[192]{0:T(256)S(1)} %broadcast_multiply_fusion.4) | copy-start | bytes 2308
  254.1 55.1 %copy-start.34 = (f32[192]{0:T(256)}, f32[192]{0:T(256)S(1)}, u32[]{:S(2)}) copy-start(f32[192]{0:T(256)S(1)} %add_rsqrt_fusion) | copy-start | bytes 2308
  254.2 6.9 %copy-start.7 = (bf16[192,512]{1,0:T(8,128)(2,1)S(1)}, bf16[192,512]{1,0:T(8,128)(2,1)}, u32[]{:S(2)}) copy-start(bf16[192,512]{1,0:T(8,128)(2,1)} %param.18) | copy-start | bytes 589828
  310.1 13.9 %copy-start.4 = (f32[192,512]{1,0:T(8,128)}, f32[192,512]{1,0:T(8,128)S(1)}, u32[]{:S(2)}) copy-start(f32[192,512]{1,0:T(8,128)S(1)} %get-tuple-element.395) | copy-start | bytes 1179652
  310.1 7.2 %copy-start.18 = (f32[2,768]{1,0:T(2,128)S(1)}, f32[2,768]{1,0:T(2,128)}, u32[]{:S(2)}) copy-start(f32[2,768]{1,0:T(2,128)} %copy-done.17) | copy-start | bytes 18436
  313.3 10.5 %all-to-all-start.2 = ((bf16[4,2,12288]{2,1,0:T(2,128)(2,1)}), bf16[4,2,12288]{2,1,0:T(2,128)(2,1)S(1)}, u32[]{:S(2)}, u32[]{:S(2)}) async-start(bf16[4,2,12288]{2,1,0:T(2,128)(2,1)} %reshape.334), calls=%async_computation.2 | async-start | bytes 393216 | tf_op jit(solution)/shard_map/all_to_all | solution.py:178
  317.1 130.7 %reduce-scatter.6.cloned.1.call-start = ((), (), s32[]{:S(2)}) async-start(), calls=%async_computation.13 | async-start | bytes 3538944 | tf_op jit(solution)/shard_map/reduce_scatter | solution.py:216
  401.5 88.9 %reduce-scatter.10.cloned.1.call-start = ((), (), s32[]{:S(2)}) async-start(), calls=%async_computation.15 | async-start | bytes 655360 | tf_op jit(solution)/shard_map/reduce_scatter | solution.py:252
  403.6 118.1 %reduce-scatter.12.cloned.1.call-start = ((), (), s32[]{:S(2)}) async-start(), calls=%async_computation.16 | async-start | bytes 2621440 | tf_op jit(solution)/shard_map/reduce_scatter | solution.py:261
  405.9 161.3 %reduce-scatter.14.cloned.1.call-start = ((), (), s32[]{:S(2)}) async-start(), calls=%async_computation.17 | async-start | bytes 2621440 | tf_op jit(solution)/shard_map/reduce_scatter | solution.py:264
  409.3 195.0 %reduce-scatter.8.cloned.1.call-start = ((), (), s32[]{:S(2)}) async-start(), calls=%async_computation.14 | async-start | bytes 1966080 | tf_op jit(solution)/shard_map/reduce_scatter | solution.py:249
  488.4 178.2 %all-reduce.10.cloned.1.call-start = ((), (), s32[]{:S(2)}) async-start(), calls=%async_computation.18 | async-start | bytes 3145728 | tf_op jit(solution)/shard_map/psum | solution.py:271
  (57 other events, 97.6 us)
Sparse Core Ops, SparseCore 0:
  10.2 40.4 all-gather.8
  85.5 31.5 all-gather.10
  118.7 45.9 all-gather.12
  166.1 44.6 all-gather.14
  401.5 46.3 reduce-scatter.5
  450.7 23.8 reduce-scatter.9
  477.0 44.6 reduce-scatter.11
  523.9 43.1 reduce-scatter.13
  569.6 34.5 reduce-scatter.7
  608.1 58.3 all-reduce.9
where the time goes:
time: 687 us; the launch traced here: 680 us
  waiting for transfers between devices  240 us (35%)
  blocking collectives  157 us (23%)
  matrix products  124 us (18%)
  local copies, waits for them, and re-layouts  65.7 us (10%)
  other arithmetic  64.5 us (9%)
  between operations  18.4 us (3%)
  starting transfers between devices  9.25 us (1%)
    reduce_scatter x1, waiting for transfers between devices, per_device(): lax.psum_scatter(grad_down.astype(jnp.bfloat16), 'wt', scatter_dimension=...  45.5 us
    psum x1, blocking collectives, per_device(): lax.psum((jnp.sum(valid_float), jnp.sum(valid_float * jnp.sum(distance *...  38.9 us
    reduce_scatter x1, waiting for transfers between devices, per_device(): lax.psum_scatter(grad_pieces.reshape(ctx_count * group_rows, head_count *...  38.5 us
    reduce_scatter x1, waiting for transfers between devices, per_device(): lax.psum_scatter(grad_qkv.astype(jnp.bfloat16), 'wt', scatter_dimension=0...  37.1 us
    psum x1, waiting for transfers between devices, per_device(): lax.psum(shard_qkv.astype(jnp.bfloat16), 'ctx').astype(jnp.float32)  35.2 us
    dot_general x16, matrix products, scores_of(): jnp.einsum('qhd,khd->hqk', queries, kv_piece[:, :, 0], preferred_element_...  32 us
    reduce_scatter x1, waiting for transfers between devices, per_device(): lax.psum_scatter(grad_up.astype(jnp.bfloat16), 'wt', scatter_dimension=0,...  31.3 us
    dot_general x8, matrix products, forward_step(): jnp.einsum('hqk,khd->qhd', weights.astype(jnp.bfloat16), kv_piece[:, :, 1...  30.9 us
  transfers between devices with their start and end apart: 12, of which 8 were waited for; matrix products, arithmetic and copies ran while one was open for 20% of the time, Pallas kernels for 0%

commit v1 on v0

v1 whole, which is shorter than its diff:
```python
import jax
import jax.numpy as jnp
from jax import lax
from jax.experimental import pallas as pl
from jax.experimental.pallas import tpu as pltpu
from jax.sharding import PartitionSpec as P

H = 8
HEAD = 64
EPS = 1e-05
LOSS_SCALE = 262144.0
CTX_HEADS = 4
WT_HEADS = 2
CHUNK = 512
TILE = 16
F32 = jnp.float32
BF16 = jnp.bfloat16
NEG = -1e30
NT = (((1,), (1,)), ((), ()))
TN = (((0,), (0,)), ((), ()))
NN = (((1,), (0,)), ((), ()))


def mm(a, b, dims=NN):
    return lax.dot_general(a, b, dims, preferred_element_type=F32)


def lane_iota(shape):
    return lax.broadcasted_iota(jnp.int32, shape, len(shape) - 1)


def norm_stats(values):
    center = values - jnp.mean(values, axis=-1, keepdims=True)
    inverse = lax.rsqrt(jnp.mean(center * center, axis=-1, keepdims=True) + EPS)
    return center * inverse, inverse


def norm_back(upstream, unit, inverse, gain):
    scaled = upstream * gain
    inner = jnp.mean(scaled * unit, axis=-1, keepdims=True)
    return inverse * (scaled - jnp.mean(scaled, axis=-1, keepdims=True) - unit * inner)


SMEM = pl.BlockSpec(memory_space=pltpu.SMEM)
VMEM = pl.BlockSpec(memory_space=pltpu.VMEM)
ANY = pl.BlockSpec(memory_space=pl.ANY)


def call(body, name, ins, in_specs, outs, scratch=(), flops=0, trans=0, out_specs=None):
    nbytes = sum(x.size * x.dtype.itemsize for x in list(ins) + list(outs))
    return pl.pallas_call(
        body,
        name=name,
        out_shape=list(outs),
        in_specs=in_specs,
        out_specs=out_specs or [VMEM] * len(outs),
        scratch_shapes=list(scratch),
        compiler_params=pltpu.CompilerParams(vmem_limit_bytes=58 * 1024 * 1024),
        cost_estimate=pl.CostEstimate(flops=flops, bytes_accessed=nbytes, transcendentals=trans),
    )(*ins)


def sds(shape, dtype):
    return jax.ShapeDtypeStruct(shape, dtype)


class Plan:
    def __init__(self, n_ctx, n_wt):
        self.n_ctx, self.n_wt = n_ctx, n_wt
        ac, aw = CTX_HEADS, WT_HEADS
        assert ac * aw == H and n_ctx % ac == 0 and n_wt % aw == 0
        self.peers = [(mc, mw) for mw in range(aw) for mc in range(0, ac, 2)]
        self.slots = [(mc | k, mw) for k in (0, 1) for mc, mw in self.peers]
        self.groups = [(mc, mw) for mc in range(0, n_ctx, ac) for mw in range(0, n_wt, aw)]
        self.all_slots = [(gc ^ sc, gw ^ sw) for gc, gw in self.groups for sc, sw in self.slots]

    def head(self, ctx, wt):
        return (wt % WT_HEADS) * CTX_HEADS + ctx % CTX_HEADS

    def swap(self, x, mask):
        mc, mw = mask
        n = self.n_wt
        perm = [
            (c * n + w, (c ^ mc) * n + (w ^ mw)) for c in range(self.n_ctx) for w in range(n)
        ]
        return lax.ppermute(x, ("ctx", "wt"), perm)


def project_body(plan, shard, blk):
    ns, nw = len(plan.slots), plan.n_wt

    def body(info, *refs):
        xs, wps = refs[:ns], refs[ns : ns + nw]
        q_ref, kv_ref, normed_ref, wh_ref, vec_ref = refs[ns + nw :]
        wt = info[1]
        for m in range(nw):
            row = pl.multiple_of((wt ^ m) * shard, shard)
            wh_ref[pl.ds(row, shard), :] = wps[m][...]
        weight = wh_ref[...]
        rows = lax.broadcasted_iota(jnp.int32, (8, 4 * HEAD), 0)
        pick = jnp.where(lane_iota((8, 4 * HEAD)) == rows + 3 * HEAD, 1.0, 0.0).astype(BF16)
        vecs = mm(pick, weight, NT)
        vec_ref[...] = vecs
        gain, shift = vecs[0:1], vecs[1:2]
        low = lane_iota((blk, 2 * HEAD)) < HEAD
        for s in range(ns):
            unit, _ = norm_stats(xs[s][...].astype(F32))
            normed = (unit * gain + shift).astype(BF16)
            normed_ref[s] = normed
            y = mm(normed, weight)
            q_ref[s] = (
                jnp.where(low, y[:, : 2 * HEAD], 0.0).astype(BF16).astype(F32) * HEAD**-0.5
            ).astype(BF16)
            kv_ref[s] = pltpu.roll(y, 3 * HEAD, 1)[:, : 2 * HEAD].astype(BF16)

    return body


def fill_slots(plan, info, deal, slot_of):
    for s, (mc, mw) in enumerate(plan.all_slots):
        slot_of[deal[(info[0] ^ mc) * plan.n_wt + (info[1] ^ mw)]] = s


def slot_range(plan, info, deal, lengths, codes, i, blk, nseq):
    code = codes[i]
    here = deal[(info[0] ^ (code // plan.n_wt)) * plan.n_wt + (info[1] ^ (code % plan.n_wt))]
    first = jnp.int32(0)
    total = jnp.int32(0)
    for n in range(nseq):
        total = total + lengths[n]
        bound = total // blk
        first = jnp.where(bound <= here, bound, first)
    return first, here


def load_kv(kv_refs, kvs, sem, ns):
    copies = [
        pltpu.make_async_copy(ref, kvs.at[pl.ds(b * ns, ns)], sem.at[b])
        for b, ref in enumerate(kv_refs)
    ]
    for c in copies:
        c.start()
    for c in copies:
        c.wait()


def attend_body(plan, blk, nseq):
    ns, nb = len(plan.slots), len(plan.groups)

    def body(info, deal, lengths, codes, q_ref, *refs):
        kv_refs = refs[:nb]
        o_ref, of_ref, lse_ref = refs[nb : nb + 3]
        kvs, slot_of, acc_ref, m_ref, l_ref, sem = refs[nb + 3 :]
        load_kv(kv_refs, kvs, sem, ns)
        fill_slots(plan, info, deal, slot_of)
        core = info[0] % 2
        tri = lax.broadcasted_iota(jnp.int32, (blk, blk), 0) <= lane_iota((blk, blk))

        def one_block(i, _):
            first, here = slot_range(plan, info, deal, lengths, codes, i, blk, nseq)
            q = q_ref[i]
            kv = kvs[slot_of[here]]
            s = jnp.where(tri, mm(kv, q, NT), NEG)
            m = jnp.max(s, axis=0, keepdims=True)
            p = jnp.exp(s - m)
            m_ref[...] = m
            l_ref[...] = jnp.sum(p, axis=0, keepdims=True)
            acc_ref[...] = mm(kv, p.astype(BF16), TN)

            def step(b, _):
                kv = kvs[slot_of[b]]
                s = mm(kv, q, NT)
                m_old = m_ref[...]
                m = jnp.maximum(m_old, jnp.max(s, axis=0, keepdims=True))
                p = jnp.exp(s - m)
                factor = jnp.exp(m_old - m)
                m_ref[...] = m
                l_ref[...] = l_ref[...] * factor + jnp.sum(p, axis=0, keepdims=True)
                acc_ref[...] = acc_ref[...] * factor + mm(kv, p.astype(BF16), TN)
                return 0

            lax.fori_loop(first, here, step, 0)
            total = l_ref[...]
            lse_ref[i] = m_ref[...] + jnp.log(total)
            out = acc_ref[HEAD:, :] / total
            zero = jnp.zeros_like(out)
            placed = jnp.concatenate(
                [jnp.where(core == 0, out, zero), jnp.where(core == 1, out, zero)], axis=0
            )
            wide = placed.T
            of_ref[i] = wide
            o_ref[i] = wide.astype(BF16)
            return 0

        lax.fori_loop(0, ns, one_block, 0)

    return body


def attend_back_body(plan, blk, nseq):
    ns, nb, nj = len(plan.slots), len(plan.groups), len(plan.peers)

    def body(info, deal, lengths, codes, q_ref, of_ref, lse_ref, *refs):
        g_refs, gs_ref = refs[:nj], refs[nj]
        kv_refs = refs[nj + 1 : nj + 1 + nb]
        outs = refs[nj + 1 + nb :]
        dq_ref, dkv_refs = outs[0], outs[1 : 1 + nb]
        kvs, slot_of, dkvs, dq_acc, g_ext, delta_ref, sem = outs[1 + nb :]
        load_kv(kv_refs, kvs, sem, ns)
        fill_slots(plan, info, deal, slot_of)
        core = info[0] % 2
        tri = lax.broadcasted_iota(jnp.int32, (blk, blk), 0) <= lane_iota((blk, blk))
        high = lane_iota((blk, 2 * HEAD)) >= HEAD
        own_half = (lane_iota((blk, 2 * HEAD)) // HEAD) == core
        for s in range(ns):
            g = (g_refs[s][...] if s < nj else gs_ref[s - nj]).astype(F32)
            g = jnp.where(own_half, g, 0.0)
            delta_ref[s] = jnp.sum((g * of_ref[s]).T, axis=0, keepdims=True)
            turned = pltpu.roll(g, HEAD, 1)
            g_ext[s] = jnp.where(high, jnp.where(core == 1, g, turned), 0.0).astype(BF16)
        dkvs[...] = jnp.zeros_like(dkvs)

        def one_block(i, _):
            first, here = slot_range(plan, info, deal, lengths, codes, i, blk, nseq)
            q = q_ref[i]
            g = g_ext[i]
            lse = lse_ref[i]
            delta = delta_ref[i]

            def pair(b, mask):
                slot = slot_of[b]
                kv = kvs[slot]
                p = jnp.exp(mm(kv, q, NT) - lse)
                if mask:
                    p = jnp.where(tri, p, 0.0)
                ds = (p * (mm(kv, g, NT) - delta)).astype(BF16)
                dkvs[slot] += mm(ds, q) + mm(p.astype(BF16), g)
                return mm(kv, ds, TN)

            dq_acc[...] = pair(here, True)

            def step(b, _):
                dq_acc[...] += pair(b, False)
                return 0

            lax.fori_loop(first, here, step, 0)
            wide = dq_acc[...].T * HEAD**-0.5
            dq_ref[i] = jnp.where(high, 0.0, wide).astype(BF16)
            return 0

        lax.fori_loop(0, ns, one_block, 0)
        for b in range(nb):
            dkv_refs[b][...] = dkvs[b * ns : (b + 1) * ns].astype(BF16)

    return body


def mlp_body(plan, width, ff, blk, packed, pieces):
    nj, nw, nc = len(plan.peers), plan.n_wt, plan.n_ctx
    nq = ff // CHUNK

    def body(info, *refs):
        refs = list(refs)
        x_ref, teacher_ref, valid_ref, vec_ref, count_ref = refs[:5]
        att = refs[5 : 5 + nj]
        rest = refs[5 + nj :]
        nwt_in = len(pieces) if packed else 3
        w_in, rest = rest[:nwt_in], rest[nwt_in:]
        (lo_ref, sq_ref, g1_ref, gatt_ref, act_ref, gpre_ref, n2_ref, gb_ref, ga_ref, gv_ref) = (
            rest[:10]
        )
        if packed:
            wup, wdown, wout, meta, slope_ref, acc_ref, sem = rest[10:]
            copies = []
            for n, (jc, src) in enumerate(zip(pieces, w_in)):
                c = info[0] ^ jc
                for m in range(nw):
                    w = info[1] ^ m
                    copies += [
                        pltpu.make_async_copy(
                            src.at[m, pl.ds(nq + 4, 1)], wout.at[w, pl.ds(c, 1)], sem.at[0]
                        ),
                        pltpu.make_async_copy(src.at[m, pl.ds(0, nq)], wup.at[:, w, c], sem.at[1]),
                        pltpu.make_async_copy(
                            src.at[m, pl.ds(nq, 4)], wdown.at[w, pl.ds(c * 4, 4)], sem.at[2]
                        ),
                        pltpu.make_async_copy(
                            src.at[m, pl.ds(nq + 5, 1)], meta.at[w, pl.ds(c, 1)], sem.at[3]
                        ),
                    ]
            for cp in copies:
                cp.start()
            for cp in copies:
                cp.wait()
            w_up = lambda q: wup[q].reshape(width, CHUNK)
            w_down = lambda q: wdown[q].reshape(CHUNK, width)
            out_rows = width // nw
            pair_rows = 2 * HEAD
            wout_flat = wout.reshape(width, width)
            w_out = lambda row: wout_flat[pl.ds(row, pair_rows), :]
            count = jnp.sum(meta[:, :, 0:1, 0:1].astype(F32))
        else:
            slope_ref, acc_ref = rest[10:]
            w_up = lambda q: w_in[0][q]
            w_down = lambda q: w_in[1][q]
            w_out = lambda row: w_in[2][pl.ds(row, 2 * HEAD), :]
            count = count_ref[0]
        vecs = vec_ref[...]
        gain, shift = vecs[2:3], vecs[3:4]
        rows = []
        for mc, mw in plan.peers:
            head = plan.head(info[0] ^ mc, info[1] ^ mw)
            rows.append(pl.multiple_of((head // 2) * (2 * HEAD), 2 * HEAD))
        mixed = mm(att[0][...], w_out(rows[0]))
        for j in range(1, nj):
            mixed = mixed + mm(att[j][...], w_out(rows[j]))
        res = mixed + x_ref[...].astype(F32)
        unit, inverse = norm_stats(res)
        n2 = (unit * gain + shift).astype(BF16)
        n2_ref[...] = n2
        for q in range(nq):
            pre = mm(n2, w_up(q))
            cdf = 0.5 * (1.0 + lax.erf(pre * 0.7071067811865476))
            pdf = jnp.exp(-0.5 * pre * pre) * 0.3989422804014327
            act = (pre * cdf).astype(BF16)
            slope_ref[q] = cdf + pre * pdf
            act_ref[q] = act
            if q == 0:
                acc_ref[...] = mm(act, w_down(q))
            else:
                acc_ref[...] += mm(act, w_down(q))
        two = acc_ref[...] + res
        lo_ref[...] = two.astype(BF16)
        distance = two - teacher_ref[...].astype(F32)
        valid = valid_ref[...].astype(F32)
        weighed = valid * distance
        square = jnp.sum(weighed * distance)
        first_row = lax.broadcasted_iota(jnp.int32, (8, 128), 0) == 0
        sq_ref[...] = jnp.where(first_row, square, count)
        g2 = (2.0 * LOSS_SCALE / (count * width)) * weighed
        gb = g2.astype(BF16)
        gb_ref[...] = gb
        for q in range(nq):
            gpre = (mm(gb, w_down(q), NT) * slope_ref[q]).astype(BF16)
            gpre_ref[q] = gpre
            if q == 0:
                acc_ref[...] = mm(gpre, w_up(q), NT)
            else:
                acc_ref[...] += mm(gpre, w_up(q), NT)
        gn2 = acc_ref[...]
        g1 = g2 + norm_back(gn2, unit, inverse, gain)
        g1_ref[...] = g1
        gv_ref[...] = jnp.concatenate(
            [
                jnp.sum(gn2 * unit, axis=0, keepdims=True),
                jnp.sum(gn2, axis=0, keepdims=True),
                jnp.zeros((6, width), F32),
            ],
            axis=0,
        )
        ga = g1.astype(BF16)
        ga_ref[...] = ga
        for j in range(nj):
            gatt_ref[j] = mm(ga, w_out(rows[j]), NT).astype(BF16)

    return body


def mlp_grads_body(plan, width, ff, blk, packed):
    nj, nw, nc = len(plan.peers), plan.n_wt, plan.n_ctx
    nq = ff // CHUNK

    def body(info, act_ref, gpre_ref, n2_ref, gb_ref, ga_ref, gv_ref, sq_ref, *refs):
        att, outs = refs[:nj], refs[nj:]
        n2, gb, ga = n2_ref[...], gb_ref[...], ga_ref[...]
        ctx, wt = info[0], info[1]
        if packed:
            out_ref = outs[0]
            rows_up = width // (nw * nc)

        for q in range(nq):
            up = mm(n2, gpre_ref[q], TN).astype(BF16)
            down = mm(act_ref[q], gb, TN).astype(BF16)
            if packed:
                up_t = up.reshape(nw, nc, rows_up, CHUNK)
                down_t = down.reshape(nc, 4, TILE, width)
                for w in range(nw):
                    for c in range(nc):
                        put_tile(out_ref, info, c, w, q, up_t[w, c])
                for c in range(nc):
                    for t in range(4):
                        put_tile(out_ref, info, c, q, nq + t, down_t[c, t])
            else:
                outs[0][q] = up
                outs[1][q] = down
        for j, (mc, mw) in enumerate(plan.peers):
            head = plan.head(ctx ^ mc, wt ^ mw)
            part = mm(att[j][...], ga, TN).astype(BF16)
            if packed:
                per = width // nw
                part_t = part.reshape(2 * HEAD // TILE, TILE, width)
                base = (head // 2) * (2 * HEAD // TILE)
                for t in range(2 * HEAD // TILE):
                    at = base + t
                    w, c = at // nc, at % nc
                    put_tile(out_ref, info, c, w, nq + 4, part_t[t])
            else:
                row = pl.multiple_of((head // 2) * (2 * HEAD), 2 * HEAD)
                outs[2][pl.ds(row, 2 * HEAD), :] = part
        if packed:
            dev = ctx * nw + wt
            square = sq_ref[0:1, 0:1]
            high = square.astype(BF16).astype(F32)
            lane = lane_iota((1, CHUNK))
            n_dev = nw * nc
            line = jnp.where(lane == dev, high, 0.0) + jnp.where(
                lane == dev + n_dev, square - high, 0.0
            )
            for w in range(nw):
                per = width // nw
                vec = gv_ref[0:2, per * w : per * (w + 1)]
                vec = jnp.concatenate([vec, jnp.zeros((2, CHUNK - per), F32)], axis=1)
                tile = jnp.concatenate([line, vec, jnp.zeros((TILE - 3, CHUNK), F32)], axis=0)
                tile = tile.astype(BF16)
                for c in range(nc):
                    put_tile(out_ref, info, c, w, nq + 5, tile)

    return body


def put_tile(out_ref, info, c, w, tile, value):
    jc = c ^ info[0]
    out_ref[jc, w ^ info[1], tile] = value


def head_grads_body(plan, blk, width, shard):
    ns, nb, nw, nj = len(plan.slots), len(plan.groups), plan.n_wt, len(plan.peers)

    def body(info, dq_ref, wh_ref, normed_ref, *refs):
        xs = refs[:ns]
        parts = refs[ns : ns + nb]
        outs = refs[ns + nb :]
        own_ref, sib_ref, dw_refs = outs[0], outs[1], outs[2 : 2 + nw]
        acc = outs[2 + nw]
        weight = wh_ref[...]
        gsum = jnp.zeros((1, width), F32)
        ssum = jnp.zeros((1, width), F32)
        for s in range(ns):
            dkv = parts[0][s].astype(F32)
            for b in range(1, nb):
                dkv = dkv + parts[b][s].astype(F32)
            zero = jnp.zeros((blk, 2 * HEAD), F32)
            wide = pltpu.roll(jnp.concatenate([dkv, zero], axis=1), HEAD, 1)
            wide = wide + jnp.concatenate([dq_ref[s].astype(F32), zero], axis=1)
            gh = wide.astype(BF16)
            back = mm(gh, weight, NT)
            if s < nj:
                own_ref[s] = back.astype(BF16)
            else:
                sib_ref[s - nj] = back.astype(BF16)
            unit, _ = norm_stats(xs[s][...].astype(F32))
            gsum = gsum + jnp.sum(back * unit, axis=0, keepdims=True)
            ssum = ssum + jnp.sum(back, axis=0, keepdims=True)
            dw = mm(normed_ref[s], gh, TN)
            if s == 0:
                acc[...] = dw
            else:
                acc[...] += dw
        vecs = jnp.concatenate([gsum, ssum, jnp.zeros((6, width), F32)], axis=0).astype(BF16)
        rows = lax.broadcasted_iota(jnp.int32, (8, 4 * HEAD), 0)
        pick = jnp.where(lane_iota((8, 4 * HEAD)) == rows + 3 * HEAD, 1.0, 0.0).astype(BF16)
        acc[...] += mm(vecs, pick, TN)
        for m in range(nw):
            row = pl.multiple_of((info[1] ^ m) * shard, shard)
            dw_refs[m][...] = acc[pl.ds(row, shard), :].astype(BF16)

    return body


def words_body(nj):
    def body(x_ref, vec_ref, g1_ref, *refs):
        parts, sibs, out_ref = refs[:nj], refs[nj : 2 * nj], refs[-1]
        up = parts[0][...].astype(F32)
        for p in parts[1:]:
            up = up + p[...].astype(F32)
        unit, inverse = norm_stats(x_ref[...].astype(F32))
        out_ref[...] = g1_ref[...] + norm_back(up, unit, inverse, vec_ref[0:1, :])

    return body


def unpack_body(plan, width, ff, pieces):
    nq, nw, nc = ff // CHUNK, plan.n_wt, plan.n_ctx

    def body(info, *refs):
        srcs, outs = refs[: len(pieces)], refs[len(pieces) :]
        up_ref, down_ref, out_ref, meta_ref = outs
        for jc, src in zip(pieces, srcs):
            c = info[0] ^ jc
            row = pl.multiple_of(c * TILE, TILE)
            for q in range(nq):
                up_ref[pl.ds(row, TILE), q * CHUNK : (q + 1) * CHUNK] = src[q].astype(F32)
            for t in range(4):
                down_ref[pl.ds(pl.multiple_of(c * 4 * TILE + t * TILE, TILE), TILE), :] = src[
                    nq + t
                ].astype(F32)
            out_ref[pl.ds(row, TILE), :] = src[nq + 4].astype(F32)
        meta = srcs[0][nq + 5].astype(F32)
        meta_ref[...] = meta

    return body


def head_out_body(plan, shard):
    def body(info, *refs):
        srcs, (out_ref, vec_ref) = refs[:H], refs[H:]
        core = info[0] % 2
        total = srcs[0][...].astype(F32)
        for s in srcs[1:]:
            total = total + s[...].astype(F32)
        rows = lax.broadcasted_iota(jnp.int32, (8, 4 * HEAD), 0)
        pick = jnp.where(lane_iota((8, 4 * HEAD)) == rows + 3 * HEAD, 1.0, 0.0)
        vec_ref[...] = lax.dot_general(
            pick, total, NT, precision=lax.Precision.HIGHEST, preferred_element_type=F32
        )
        nj = len(plan.peers)
        for j, (mc, mw) in enumerate(plan.peers):
            head = plan.head(info[0] ^ mc, info[1] ^ mw)
            own = srcs[j][...].astype(F32)
            sib = srcs[nj + j][...].astype(F32)
            even = jnp.where(core == 0, own, sib)
            odd = jnp.where(core == 0, sib, own)
            turned = pltpu.roll(odd, 3 * HEAD, 1)
            lane = lane_iota((shard, 2 * HEAD))
            mid = jnp.where(lane < HEAD, even[:, 2 * HEAD :], turned[:, 2 * HEAD :])
            last = turned[:, : 2 * HEAD]
            col = pl.multiple_of((head // 2) * (6 * HEAD), 2 * HEAD)
            out_ref[:, pl.ds(col, 2 * HEAD)] = even[:, : 2 * HEAD]
            out_ref[:, pl.ds(col + 2 * HEAD, 2 * HEAD)] = mid
            out_ref[:, pl.ds(col + 4 * HEAD, 2 * HEAD)] = last

    return body


def per_device(
    words,
    teacher,
    valid,
    lengths,
    deal,
    gain_attn,
    shift_attn,
    w_qkv,
    w_out,
    gain_mlp,
    shift_mlp,
    w_up,
    w_down,
):
    n_ctx, n_wt = lax.axis_size("ctx"), lax.axis_size("wt")
    plan = Plan(n_ctx, n_wt)
    ctx, wt = lax.axis_index("ctx"), lax.axis_index("wt")
    blk, width = words.shape
    shard = width // n_wt
    ff = w_up.shape[1]
    nq = ff // CHUNK
    nseq = lengths.shape[0]
    ns, nb, nj = len(plan.slots), len(plan.groups), len(plan.peers)
    packed = width == CHUNK and width % (n_wt * n_ctx * TILE) == 0 and n_wt * CHUNK == ff
    info = jnp.stack([ctx, wt]).astype(jnp.int32)
    codes = jnp.array([mc * n_wt + mw for mc, mw in plan.slots], jnp.int32)
    core = (1, 0)

    xs = [words] + [plan.swap(words, m) for m in plan.peers[1:]]
    vec_cols = jnp.stack([gain_attn, shift_attn, gain_mlp, shift_mlp], axis=1)
    vec_cols = jnp.pad(vec_cols, ((0, 0), (0, HEAD - 4)))

    def head_cols(m):
        head = plan.head(ctx, wt ^ m)
        cols = lax.dynamic_slice_in_dim(w_qkv, head * 3 * HEAD, 3 * HEAD, 1)
        return jnp.concatenate([cols, vec_cols], axis=1)

    w_parts = [plan.swap(head_cols(m), (0, m)) for m in range(1, n_wt)]
    w_parts = [head_cols(0)] + w_parts
    xs = xs + [plan.swap(x, core) for x in xs]

    q, kv, normed, w_head, vecs = call(
        project_body(plan, shard, blk),
        "project",
        [info] + xs + w_parts,
        [SMEM] + [VMEM] * (ns + n_wt),
        [
            sds((ns, blk, 2 * HEAD), BF16),
            sds((ns, blk, 2 * HEAD), BF16),
            sds((ns, blk, width), BF16),
            sds((width, 4 * HEAD), BF16),
            sds((8, width), F32),
        ],
        flops=2 * ns * blk * width * 4 * HEAD,
    )
    kvs = [kv] + [plan.swap(kv, m) for m in plan.groups[1:]]

    if packed:
        rows_up = width // (n_wt * n_ctx)
        up_piece = lax.dynamic_slice_in_dim(w_up, ctx * rows_up, rows_up, 0)
        up_piece = up_piece.reshape(rows_up, nq, CHUNK).transpose(1, 0, 2)
        down_piece = lax.dynamic_slice_in_dim(w_down, ctx * 4 * TILE, 4 * TILE, 0)
        out_piece = lax.dynamic_slice_in_dim(w_out, ctx * TILE, TILE, 0)
        count_here = jnp.sum(valid).astype(BF16)
        piece = jnp.concatenate(
            [
                up_piece,
                down_piece.reshape(4, TILE, CHUNK),
                out_piece[None],
                jnp.full((1, TILE, CHUNK), count_here, BF16),
            ],
            axis=0,
        )
        piece, _ = lax.optimization_barrier((piece, q))
        stack = jnp.stack([piece] + [plan.swap(piece, (0, m)) for m in range(1, n_wt)])
        planes = [2 * p for p in range(n_ctx // 2)]
        stacks = [stack] + [plan.swap(stack, (p, 0)) for p in planes[1:]]
        stacks = stacks + [plan.swap(s, core) for s in stacks]
        piece_ids = planes + [p + 1 for p in planes]
        weights = stacks
        count = jnp.zeros((1,), F32)
    else:
        piece_ids = []
        up_full = lax.all_gather(w_up, "wt", axis=0, tiled=True)
        down_full = lax.all_gather(w_down, "wt", axis=0, tiled=True)
        out_full = lax.all_gather(w_out, "wt", axis=0, tiled=True)
        weights = [
            up_full.reshape(width, nq, CHUNK).transpose(1, 0, 2),
            down_full.reshape(nq, CHUNK, width),
            out_full,
        ]
        count = lax.psum(jnp.sum(valid).astype(F32), ("ctx", "wt")).reshape(1)

    pairs = ns * nb * ns // 4
    o, of32, lse = call(
        attend_body(plan, blk, nseq),
        "attend",
        [info, deal, lengths, codes, q] + kvs,
        [SMEM] * 4 + [VMEM] + [ANY] * nb,
        [
            sds((ns, blk, 2 * HEAD), BF16),
            sds((ns, blk, 2 * HEAD), F32),
            sds((ns, 1, blk), F32),
        ],
        scratch=[
            pltpu.VMEM((nb * ns, blk, 2 * HEAD), BF16),
            pltpu.SMEM((n_ctx * n_wt,), jnp.int32),
            pltpu.VMEM((2 * HEAD, blk), F32),
            pltpu.VMEM((1, blk), F32),
            pltpu.VMEM((1, blk), F32),
            pltpu.SemaphoreType.DMA((nb,)),
        ],
        flops=pairs * 4 * blk * blk * 128,
        trans=pairs * blk * blk,
    )
    mixed = o[:nj] + plan.swap(o[nj:], core)
    att = [mixed[0]] + [plan.swap(mixed[j], plan.peers[j]) for j in range(1, nj)]

    mlp_in = [info, words, teacher, valid[:, None], vecs, count] + att + weights
    specs = [SMEM] + [VMEM] * 4 + [SMEM] + [VMEM] * nj
    specs += [ANY] * len(weights) if packed else [VMEM] * len(weights)
    scratch = [pltpu.VMEM((nq, blk, CHUNK), F32), pltpu.VMEM((blk, width), F32)]
    if packed:
        scratch = [
            pltpu.VMEM((nq, n_wt, n_ctx, TILE, CHUNK), BF16),
            pltpu.VMEM((n_wt, n_ctx * 4, TILE, CHUNK), BF16),
            pltpu.VMEM((n_wt, n_ctx, TILE, CHUNK), BF16),
            pltpu.VMEM((n_wt, n_ctx, TILE, CHUNK), BF16),
            *scratch,
            pltpu.SemaphoreType.DMA((4,)),
        ]
    layer_out, square, grad_one, gatt, act, gpre, n2, gb, ga, gvec = call(
        mlp_body(plan, width, ff, blk, packed, piece_ids),
        "mlp",
        mlp_in,
        specs,
        [
            sds((blk, width), BF16),
            sds((8, 128), F32),
            sds((blk, width), F32),
            sds((nj, blk, 2 * HEAD), BF16),
            sds((nq, blk, CHUNK), BF16),
            sds((nq, blk, CHUNK), BF16),
            sds((blk, width), BF16),
            sds((blk, width), BF16),
            sds((blk, width), BF16),
            sds((8, width), F32),
        ],
        scratch=scratch,
        flops=8 * blk * width * ff,
        trans=2 * blk * ff,
    )
    g_own = [gatt[0]] + [plan.swap(gatt[j], plan.peers[j]) for j in range(1, nj)]
    g_sib = plan.swap(jnp.stack(g_own), core)

    grads_in = [info, act, gpre, n2, gb, ga, gvec, square] + att
    if packed:
        grads_out = [sds((n_ctx, n_wt, nq + 6, TILE, CHUNK), BF16)]
    else:
        grads_out = [
            sds((nq, width, CHUNK), BF16),
            sds((nq, CHUNK, width), BF16),
            sds((width, width), BF16),
        ]
    weight_grads = call(
        mlp_grads_body(plan, width, ff, blk, packed),
        "mlp_grads",
        grads_in,
        [SMEM] + [VMEM] * (7 + nj),
        grads_out,
        flops=4 * blk * width * ff,
    )

    back = call(
        attend_back_body(plan, blk, nseq),
        "attend_back",
        [info, deal, lengths, codes, q, of32, lse] + g_own + [g_sib] + kvs,
        [SMEM] * 4 + [VMEM] * (3 + nj + 1) + [ANY] * nb,
        [sds((ns, blk, 2 * HEAD), BF16)] + [sds((ns, blk, 2 * HEAD), BF16)] * nb,
        scratch=[
            pltpu.VMEM((nb * ns, blk, 2 * HEAD), BF16),
            pltpu.SMEM((n_ctx * n_wt,), jnp.int32),
            pltpu.VMEM((nb * ns, blk, 2 * HEAD), F32),
            pltpu.VMEM((2 * HEAD, blk), F32),
            pltpu.VMEM((ns, blk, 2 * HEAD), BF16),
            pltpu.VMEM((ns, 1, blk), F32),
            pltpu.SemaphoreType.DMA((nb,)),
        ],
        flops=pairs * 10 * blk * blk * 128,
        trans=pairs * blk * blk,
    )
    dq, dkvs = back[0], back[1:]
    parts = [dkvs[0]] + [plan.swap(dkvs[b], plan.groups[b]) for b in range(1, nb)]

    outs = call(
        head_grads_body(plan, blk, width, shard),
        "head_grads",
        [info, dq, w_head, normed] + xs + parts,
        [SMEM] + [VMEM] * (3 + ns + nb),
        [sds((nj, blk, width), BF16)] * 2 + [sds((shard, 4 * HEAD), BF16)] * n_wt,
        scratch=[pltpu.VMEM((width, 4 * HEAD), F32)],
        flops=4 * ns * blk * width * 4 * HEAD,
    )
    own_rows, sib_rows, dw = outs[0], outs[1], outs[2:]
    rows = (own_rows.astype(F32) + plan.swap(sib_rows, core).astype(F32)).astype(BF16)
    up_rows = [rows[0]] + [plan.swap(rows[j], plan.peers[j]) for j in range(1, nj)]
    grad_words = call(
        words_body(nj),
        "words_grad",
        [words, vecs, grad_one] + up_rows,
        [VMEM] * (3 + nj),
        [sds((blk, width), F32)],
    )[0]

    dw = [dw[0]] + [plan.swap(dw[m], (0, m)) for m in range(1, n_wt)]
    merged = []
    for a in range(WT_HEADS):
        total = dw[a].astype(F32)
        for m in range(a + WT_HEADS, n_wt, WT_HEADS):
            total = total + dw[m].astype(F32)
        merged.append(total)
    heads = jnp.stack(merged).astype(BF16)
    step = CTX_HEADS
    while step < n_ctx:
        heads = (heads.astype(F32) + plan.swap(heads, (step, 0)).astype(F32)).astype(BF16)
        step *= 2
    cols = [heads]
    for mc in range(2, CTX_HEADS, 2):
        cols.append(plan.swap(heads, (mc, 0)))
    own_heads = jnp.stack(cols, axis=1)
    sib_heads = plan.swap(own_heads, core)
    srcs = [own_heads[a, p] for a in range(WT_HEADS) for p in range(CTX_HEADS // 2)]
    srcs += [sib_heads[a, p] for a in range(WT_HEADS) for p in range(CTX_HEADS // 2)]
    g_qkv, gvec_attn = call(
        head_out_body(plan, shard),
        "head_out",
        [info] + srcs,
        [SMEM] + [VMEM] * H,
        [sds((shard, 3 * width), F32), sds((8, shard), F32)],
    )

    if packed:
        g_all = weight_grads[0].reshape(n_ctx // 2, 2, n_wt, nq + 6, TILE, CHUNK)
        half = (g_all[:, 0].astype(F32) + plan.swap(g_all[:, 1], core).astype(F32)).astype(BF16)
        total = half[0].astype(F32)
        for p in range(1, n_ctx // 2):
            total = total + plan.swap(half[p], (2 * p, 0)).astype(F32)
        total = total.astype(BF16)
        final = total[0].astype(F32)
        for m in range(1, n_wt):
            final = final + plan.swap(total[m], (0, m)).astype(F32)
        final = final.astype(BF16)
        finals = [final] + [plan.swap(final, (p, 0)) for p in planes[1:]]
        finals_sib = plan.swap(jnp.stack(finals), core)
        finals = finals + [finals_sib[p] for p in range(n_ctx // 2)]
        g_up, g_down, g_out, meta = call(
            unpack_body(plan, width, ff, piece_ids),
            "unpack",
            [info] + finals,
            [SMEM] + [VMEM] * len(finals),
            [
                sds((shard, ff), F32),
                sds((ff // n_wt, width), F32),
                sds((shard, width), F32),
                sds((TILE, CHUNK), F32),
            ],
        )
        square_all = jnp.sum(meta[0])
        g_gain, g_shift = meta[1, :shard], meta[2, :shard]
        count_all = square[1, 0]
    else:
        g_up, g_down, g_out = weight_grads
        g_up = g_up.transpose(1, 0, 2).reshape(width, ff)
        g_down = g_down.reshape(ff, width)

        def reduce_rows(g):
            part = lax.psum_scatter(g.astype(BF16), "wt", scatter_dimension=0, tiled=True)
            return lax.psum(part, "ctx").astype(F32)

        g_up, g_down, g_out = reduce_rows(g_up), reduce_rows(g_down), reduce_rows(g_out)
        both = lax.psum(gvec[:2], ("ctx", "wt"))
        both = lax.dynamic_slice_in_dim(both, wt * shard, shard, 1)
        g_gain, g_shift = both[0], both[1]
        count_all = count[0]
        square_all = lax.psum(square[0, 0], ("ctx", "wt"))
    loss = square_all / (count_all * width)
    return (
        layer_out,
        loss,
        grad_words,
        gvec_attn[0],
        gvec_attn[1],
        g_qkv,
        g_out,
        g_gain,
        g_shift,
        g_up,
        g_down,
    )


def solution(mesh):
    placed = (
        P(("ctx", "wt"), None),
        P(("ctx", "wt"), None),
        P(("ctx", "wt")),
        P(),
        P(),
        P("wt"),
        P("wt"),
        P("wt", None),
        P("wt", None),
        P("wt"),
        P("wt"),
        P("wt", None),
        P("wt", None),
    )
    return jax.shard_map(
        per_device,
        mesh=mesh,
        in_specs=placed,
        out_specs=(
            P(("ctx", "wt"), None),
            P(),
            P(("ctx", "wt"), None),
            P("wt"),
            P("wt"),
            P("wt", None),
            P("wt", None),
            P("wt"),
            P("wt"),
            P("wt", None),
            P("wt", None),
        ),
        check_vma=False,
    )
```

time: 687 us -> 334 us (0.49); the launches traced: 680 us -> 336 us
  blocking collectives: 157 us -> 0 us
  matrix products: 124 us -> 0 us
  waiting for transfers between devices: 240 us -> 134 us
  Pallas kernels: 0 us -> 94.7 us
  starting transfers between devices: 9.25 us -> 70.1 us
  other arithmetic: 64.5 us -> 11.8 us
  local copies, waits for them, and re-layouts: 65.7 us -> 21.5 us
  between operations: 18.4 us -> 4.3 us
    reduce_scatter x5 -> x0, waiting for transfers between devices: 152 us -> none  [the longest x1 45.5 us: per_device(): lax.psum_scatter(grad_down.astype(jnp.bfloat16), 'wt', scatter_dimension=...]
    ppermute x0 -> x55, waiting for transfers between devices: none -> 134 us  [swap(): return lax.ppermute(x, ('ctx', 'wt'), perm)]
    dot_general x68 -> x0, matrix products: 124 us -> none  [the longest x16 32 us: scores_of(): jnp.einsum('qhd,khd->hqk', queries, kv_piece[:, :, 0], preferred_element_...]
    pallas_call x0 -> x9, Pallas kernels: none -> 94.7 us  [call(): pl.pallas_call(body, name=name, out_shape=list(outs), in_specs=in_specs,...]
    ppermute x0 -> x55, starting transfers between devices: none -> 70.1 us  [swap(): return lax.ppermute(x, ('ctx', 'wt'), perm)]
    all_gather x5 -> x0, blocking collectives: 54.7 us -> none  [the longest x1 15.2 us: per_device(): lax.all_gather(w_out, 'wt', axis=0, tiled=True)]
    psum x2 -> x0, blocking collectives: 50.8 us -> none  [the longest x1 38.9 us: per_device(): lax.psum((jnp.sum(valid_float), jnp.sum(valid_float * jnp.sum(distance *...]
    all_gather x4 -> x0, waiting for transfers between devices: 45.4 us -> none  [the longest x1 26.7 us: per_device(): lax.all_gather(key_values, 'ctx', axis=0, tiled=True)]
  transfers between devices with their start and end apart: 12 -> 55, of which waited for: 8 -> 26; matrix products, arithmetic and copies ran while one was open for 20% -> 7% of each run, Pallas kernels for 0% -> 22%
where the time goes in v1:
time: 334 us; the launch traced here: 336 us
  waiting for transfers between devices  134 us (40%)
  Pallas kernels  94.7 us (28%)
  starting transfers between devices  70.1 us (21%)
  local copies, waits for them, and re-layouts  21.5 us (6%)
  other arithmetic  11.8 us (4%)
  between operations  4.3 us (1%)
    ppermute x55, waiting for transfers between devices, swap(): return lax.ppermute(x, ('ctx', 'wt'), perm)  134 us
    pallas_call x9, Pallas kernels, call(): pl.pallas_call(body, name=name, out_shape=list(outs), in_specs=in_specs,...  94.7 us
    ppermute x55, starting transfers between devices, swap(): return lax.ppermute(x, ('ctx', 'wt'), perm)  70.1 us
  transfers between devices with their start and end apart: 55, of which 26 were waited for; matrix products, arithmetic and copies ran while one was open for 7% of the time, Pallas kernels for 22%

profile of v1, /device:TPU:0, one launch (start us, length us, event | category | flops | bytes accessed | tf_op | source)
XLA Modules:
  0.0 336.2 jit_solution(8755103938653047219)
XLA Ops:
  1.2 3.6 %collective-permute-start.2 = (bf16[192,512]{1,0:T(8,128)(2,1)}, bf16[192,512]{1,0:T(8,128)(2,1)S(1)}, u32[]{:S(2)}, u32[]{:S(2)}) collective-permute-start(bf16[192,512]{1,0:T(8,128)(2,1)} %x_ref.1), channel_id=1, source_target_pairs={{0,9},{1,8},{2,11},{3,10},{4,13},{5,12},{6,15},{7,14},{8,1},{9,0},... | collective-permute-start | bytes 589832 | tf_op jit(solution)/shard_map/ppermute | solution.py:86
  8.2 3.9 %collective-permute-start.9 = (bf16[128,256]{1,0:T(8,128)(2,1)S(1)}, bf16[128,256]{1,0:T(8,128)(2,1)S(1)}, u32[]{:S(2)}, u32[]{:S(2)}) collective-permute-start(bf16[128,256]{1,0:T(8,128)(2,1)S(1)} %get-tuple-element.120), channel_id=1, source_target_pairs={{0,3},{1,2},{2,1},{3,0},{4,7},{5,6},{6,5},{7,4},{8,11},{9,10},{10,... | collective-permute-start | bytes 196616 | tf_op jit(solution)/shard_map/ppermute | solution.py:86
  15.1 3.3 collective-permute-done.9.refs_11_
  19.7 2.8 collective-permute-done.7.refs_9_
  23.2 4.7 %collective-permute-done.8.refs_10_ = bf16[128,256]{1,0:T(8,128)(2,1)S(1)} collective-permute-done((bf16[128,256]{1,0:T(8,128)(2,1)S(1)}, bf16[128,256]{1,0:T(8,128)(2,1)S(1)}, u32[]{:S(2)}, u32[]{:S(2)}) %collective-permute-start.8) | collective-permute-done | bytes 65568 | tf_op jit(solution)/shard_map/ppermute | solution.py:86
  28.8 4.5 %project.1 = (bf16[8,192,128]{2,1,0:T(8,128)(2,1)}, bf16[8,192,128]{2,1,0:T(8,128)(2,1)}, bf16[8,192,512]{2,1,0:T(8,128)(2,1)}, bf16[512,256]{1,0:T(8,128)(2,1)}, f32[8,512]{1,0:T(8,128)}) custom-call(s32[2]{0:T(128)} %pad_add_fusion.info, bf16[192,512]{1,0:T(8,128)(2,1)} %x_ref.1, bf16[192,512]{1,0:T(8,128)(2,1)} %copy-done.5, bf16[192,512]{1,0:T(8,128)(2,1)} %copy-done.4, ...), custom_call_target="tpu_custom_call" | custom-call | flops 402653184 | bytes 4472840 | tf_op jit(solution)/shard_map/project/pallas_call | solution.py:51
  39.4 10.9 %collective-permute-done.19 = bf16[10,16,512]{2,1,0:T(8,128)(2,1)S(1)} collective-permute-done((bf16[10,16,512]{2,1,0:T(8,128)(2,1)S(1)}, bf16[10,16,512]{2,1,0:T(8,128)(2,1)S(1)}, u32[]{:S(2)}, u32[]{:S(2)}) %collective-permute-start.19) | collective-permute-done | bytes 163872 | tf_op jit(solution)/shard_map/ppermute | solution.py:86
  50.3 13.5 %collective-permute-start.10 = (bf16[8,192,128]{2,1,0:T(8,128)(2,1)}, bf16[8,192,128]{2,1,0:T(8,128)(2,1)S(1)}, u32[]{:S(2)}, u32[]{:S(2)}) collective-permute-start(bf16[8,192,128]{2,1,0:T(8,128)(2,1)} %get-tuple-element.49.refs_0_.refs_5_), channel_id=1, source_target_pairs={{0,2},{1,3},{2,0},{3,1},{4,6},{5,7},{6,4},{7,5},{8,10},{9,11},{10,... | collective-permute-start | bytes 1179656 | tf_op jit(solution)/shard_map/ppermute | solution.py:86
  63.8 3.0 collective-permute-done.18
  70.4 13.1 %collective-permute-done.10.refs_1_.refs_6_ = bf16[8,192,128]{2,1,0:T(8,128)(2,1)S(1)} collective-permute-done((bf16[8,192,128]{2,1,0:T(8,128)(2,1)}, bf16[8,192,128]{2,1,0:T(8,128)(2,1)S(1)}, u32[]{:S(2)}, u32[]{:S(2)}) %collective-permute-start.10) | collective-permute-done | bytes 393248 | tf_op jit(solution)/shard_map/ppermute | solution.py:86
  84.3 31.5 %attend.1 = (bf16[8,192,128]{2,1,0:T(8,128)(2,1)}, f32[8,192,128]{2,1,0:T(8,128)}, f32[8,1,192]{2,1,0:T(1,128)}) custom-call(s32[2]{0:T(128)} %pad_add_fusion.info, s32[32]{0:T(128)} %deal.3, s32[4]{0:T(128)} %lengths.3, s32[8]{0:T(128)} %constant.80.clone.codes, bf16[8,192,128]{2,1,0:T(8,128)(2,1)} %get-tuple-element.48.q_ref, ...), custom_call_target="tpu_custom_call" | custom-call | flops 1207959552 | bytes 3152056 | tf_op jit(solution)/shard_map/attend/pallas_call | solution.py:51
  119.9 5.0 %collective-permute-done.16.refs_8_.refs_3_ = bf16[192,128]{1,0:T(8,128)(2,1)S(1)} collective-permute-done((bf16[192,128]{1,0:T(8,128)(2,1)S(1)}, bf16[192,128]{1,0:T(8,128)(2,1)S(1)}, u32[]{:S(2)}, u32[]{:S(2)}) %collective-permute-start.16) | collective-permute-done | bytes 49184 | tf_op jit(solution)/shard_map/ppermute | solution.py:86
  124.8 4.1 %collective-permute-done.15.refs_7_.refs_2_ = bf16[192,128]{1,0:T(8,128)(2,1)S(1)} collective-permute-done((bf16[192,128]{1,0:T(8,128)(2,1)S(1)}, bf16[192,128]{1,0:T(8,128)(2,1)S(1)}, u32[]{:S(2)}, u32[]{:S(2)}) %collective-permute-start.15) | collective-permute-done | bytes 49184 | tf_op jit(solution)/shard_map/ppermute | solution.py:86
  130.2 2.8 collective-permute-done.14.refs_6_.refs_1_
  133.6 9.0 %mlp.1 = (bf16[192,512]{1,0:T(8,128)(2,1)}, f32[8,128]{1,0:T(8,128)}, f32[192,512]{1,0:T(8,128)}, bf16[4,192,128]{2,1,0:T(8,128)(2,1)}, bf16[4,192,512]{2,1,0:T(...) custom-call(s32[2]{0:T(128)} %pad_add_fusion.info, ...), custom_call_target="tpu_custom_call" | custom-call | flops 1610612736 | bytes 8819468 | tf_op jit(solution)/shard_map/mlp/pallas_call | solution.py:51
  142.6 5.5 %mlp_grads.1 = bf16[8,4,10,16,512]{4,3,2,1,0:T(8,128)(2,1)} custom-call(s32[2]{0:T(128)} %pad_add_fusion.info, bf16[4,192,512]{2,1,0:T(8,128)(2,1)} %get-tuple-element.53.act_ref, bf16[4,192,512]{2,1,0:T(8,128)(2,1)} %get-tuple-element.54.gpre_ref, bf16[192,512]{1,0:T(8,128)(2,1)} %get-tuple-element.55.n2_ref, bf16[192,512]{1,0:T(8,128)(2,1)} %get-tuple-element.56.gb_ref, ...), custom_call_target="tpu_custom_call" | custom-call | flops 805306368 | bytes 7622664 | tf_op jit(solution)/shard_map/mlp_grads/pallas_call | solution.py:51
  148.1 3.6 %slice_bitcast_fusion = bf16[4,4,10,16,512]{4,3,2,1,0:T(8,128)(2,1)} fusion(bf16[4,2,4,10,16,512]{5,4,3,2,1,0:T(8,128)(2,1)} %bitcast.129), kind=kLoop, calls=%fused_computation.2 | loop fusion | bytes 5242880 | tf_op jit(solution)/shard_map/squeeze | solution.py:789
  160.6 30.8 %attend_back.1 = (bf16[8,192,128]{2,1,0:T(8,128)(2,1)}, bf16[8,192,128]{2,1,0:T(8,128)(2,1)}, bf16[8,192,128]{2,1,0:T(8,128)(2,1)}, bf16[8,192,128]{2,1,0:T(8,128)(2,1)}, bf16[8,192,128]{2,1,0:T(8,128)(2,1)}) custom-call(s32[2]{0:T(128)} %pad_add_fusion.info, s32[32]{0:T(128)} %deal.3, s32[4]{0:T(128)} %lengths.3, s32[8]{0:T(128)} %constant.80.clone.codes, ...), custom_call_target="tpu_custom_call" | custom-call | flops 3019898880 | bytes 5118136 | tf_op jit(solution)/shard_map/attend_back/pallas_call | solution.py:51
  191.6 4.3 %collective-permute-start.44 = (bf16[8,192,128]{2,1,0:T(8,128)(2,1)}, bf16[8,192,128]{2,1,0:T(8,128)(2,1)}, u32[]{:S(2)}, u32[]{:S(2)}) collective-permute-start(bf16[8,192,128]{2,1,0:T(8,128)(2,1)} %get-tuple-element.71), channel_id=1, source_target_pairs={{0,18},{1,19},{2,16},{3,17},{4,22},{5,23},{6,20},{7,21},{8,26},{9,... | collective-permute-start | bytes 1179656 | tf_op jit(solution)/shard_map/ppermute | solution.py:86
  195.9 24.3 %collective-permute-done.42.refs_9_ = bf16[8,192,128]{2,1,0:T(8,128)(2,1)S(1)} collective-permute-done((bf16[8,192,128]{2,1,0:T(8,128)(2,1)}, bf16[8,192,128]{2,1,0:T(8,128)(2,1)S(1)}, u32[]{:S(2)}, u32[]{:S(2)}) %collective-permute-start.42) | collective-permute-done | bytes 393248 | tf_op jit(solution)/shard_map/ppermute | solution.py:86
  220.9 5.8 %head_grads.1 = (bf16[4,192,512]{2,1,0:T(8,128)(2,1)}, bf16[4,192,512]{2,1,0:T(8,128)(2,1)}, bf16[128,256]{1,0:T(8,128)(2,1)}, bf16[128,256]{1,0:T(8,128)(2,1)},...) custom-call(s32[2]{0:T(128)} %pad_add_fusion.info, bf16[8,192,128]{2,1,0:T(8,128)(2,1)} %get-tuple-element.65.dq_ref, ...), custom_call_target="tpu_custom_call" | custom-call | flops 805306368 | bytes 7208968 | tf_op jit(solution)/shard_map/head_grads/pallas_call | solution.py:51
  226.7 7.3 %collective-permute-start.49 = (bf16[128,256]{1,0:T(8,128)(2,1)}, bf16[128,256]{1,0:T(8,128)(2,1)S(1)}, u32[]{:S(2)}, u32[]{:S(2)}) collective-permute-start(bf16[128,256]{1,0:T(8,128)(2,1)} %get-tuple-element.75), channel_id=1, source_target_pairs={{0,2},{1,3},{2,0},{3,1},{4,6},{5,7},{6,4},{7,5},{8,10},{9,11},{10,... | collective-permute-start | bytes 196616 | tf_op jit(solution)/shard_map/ppermute | solution.py:86
  242.4 3.2 collective-permute-start.52
  245.7 3.0 fusion
  254.8 26.1 %collective-permute-done.53 = bf16[2,128,256]{2,1,0:T(8,128)(2,1)S(1)} collective-permute-done((bf16[2,128,256]{2,1,0:T(8,128)(2,1)S(1)}, bf16[2,128,256]{2,1,0:T(8,128)(2,1)S(1)}, u32[]{:S(2)}, u32[]{:S(2)}) %collective-permute-start.53) | collective-permute-done | bytes 131104 | tf_op jit(solution)/shard_map/ppermute | solution.py:86
  281.6 2.8 collective-permute-start.33
  288.2 4.8 %collective-permute-done.33 = bf16[10,16,512]{2,1,0:T(8,128)(2,1)S(1)} collective-permute-done((bf16[10,16,512]{2,1,0:T(8,128)(2,1)S(1)}, bf16[10,16,512]{2,1,0:T(8,128)(2,1)S(1)}, u32[]{:S(2)}, u32[]{:S(2)}) %collective-permute-start.33) | collective-permute-done | bytes 163872 | tf_op jit(solution)/shard_map/ppermute | solution.py:86
  292.9 7.0 %collective-permute-done.32 = bf16[10,16,512]{2,1,0:T(8,128)(2,1)S(1)} collective-permute-done((bf16[10,16,512]{2,1,0:T(8,128)(2,1)S(1)}, bf16[10,16,512]{2,1,0:T(8,128)(2,1)S(1)}, u32[]{:S(2)}, u32[]{:S(2)}) %collective-permute-start.32) | collective-permute-done | bytes 163872 | tf_op jit(solution)/shard_map/ppermute | solution.py:86
  317.2 3.9 %collective-permute-done.48.refs_3_ = bf16[192,512]{1,0:T(8,128)(2,1)S(1)} collective-permute-done((bf16[192,512]{1,0:T(8,128)(2,1)S(1)}, bf16[192,512]{1,0:T(8,128)(2,1)S(1)}, u32[]{:S(2)}, u32[]{:S(2)}) %collective-permute-start.48) | collective-permute-done | bytes 196640 | tf_op jit(solution)/shard_map/ppermute | solution.py:86
  321.1 3.0 collective-permute-done.47.refs_2_
  325.5 2.5 words_grad.1
  328.9 2.9 unpack.1
  (206 shorter events, 75.7 us)
Async XLA Ops:
  0.7 27.3 %collective-permute-start.3 = (bf16[192,512]{1,0:T(8,128)(2,1)}, bf16[192,512]{1,0:T(8,128)(2,1)S(1)}, u32[]{:S(2)}, u32[]{:S(2)}) collective-permute-start(bf16[192,512]{1,0:T(8,128)(2,1)} %x_ref.1), channel_id=1, source_target_pairs={{0,4},{1,5},{2,6},{3,7},{4,0},{5,1},{6,2},{7,3},{8,12},{9,13},{10,... | collective-permute-start | bytes 589832 | tf_op jit(solution)/shard_map/ppermute | solution.py:86
  1.2 17.2 %collective-permute-start.2 = (bf16[192,512]{1,0:T(8,128)(2,1)}, bf16[192,512]{1,0:T(8,128)(2,1)S(1)}, u32[]{:S(2)}, u32[]{:S(2)}) collective-permute-start(bf16[192,512]{1,0:T(8,128)(2,1)} %x_ref.1), channel_id=1, source_target_pairs={{0,9},{1,8},{2,11},{3,10},{4,13},{5,12},{6,15},{7,14},{8,1},{9,0},... | collective-permute-start | bytes 589832 | tf_op jit(solution)/shard_map/ppermute | solution.py:86
  4.8 13.7 %collective-permute-start.1 = (bf16[192,512]{1,0:T(8,128)(2,1)}, bf16[192,512]{1,0:T(8,128)(2,1)S(1)}, u32[]{:S(2)}, u32[]{:S(2)}) collective-permute-start(bf16[192,512]{1,0:T(8,128)(2,1)} %x_ref.1), channel_id=1, source_target_pairs={{0,1},{1,0},{2,3},{3,2},{4,5},{5,4},{6,7},{7,6},{8,9},{9,8},{10,11... | collective-permute-start | bytes 589832 | tf_op jit(solution)/shard_map/ppermute | solution.py:86
  5.2 13.7 %collective-permute-start = (bf16[192,512]{1,0:T(8,128)(2,1)}, bf16[192,512]{1,0:T(8,128)(2,1)S(1)}, u32[]{:S(2)}, u32[]{:S(2)}) collective-permute-start(bf16[192,512]{1,0:T(8,128)(2,1)} %x_ref.1), channel_id=1, source_target_pairs={{0,8},{1,9},{2,10},{3,11},{4,12},{5,13},{6,14},{7,15},{8,0},{9,1},... | collective-permute-start | bytes 589832 | tf_op jit(solution)/shard_map/ppermute | solution.py:86
  33.3 35.6 %collective-permute-start.12 = (bf16[8,192,128]{2,1,0:T(8,128)(2,1)}, bf16[8,192,128]{2,1,0:T(8,128)(2,1)S(1)}, u32[]{:S(2)}, u32[]{:S(2)}) collective-permute-start(bf16[8,192,128]{2,1,0:T(8,128)(2,1)} %get-tuple-element.49.refs_0_.refs_5_), channel_id=1, source_target_pairs={{0,18},{1,19},{2,16},{3,17},{4,22},{5,23},{6,20},{7,21},{8,26},{9,... | collective-permute-start | bytes 1179656 | tf_op jit(solution)/shard_map/ppermute | solution.py:86
  34.3 16.1 %collective-permute-start.19 = (bf16[10,16,512]{2,1,0:T(8,128)(2,1)S(1)}, bf16[10,16,512]{2,1,0:T(8,128)(2,1)S(1)}, u32[]{:S(2)}, u32[]{:S(2)}) collective-permute-start(bf16[10,16,512]{2,1,0:T(8,128)(2,1)S(1)} %maximum_maximum_fusion), channel_id=1, source_target_pairs={{0,3},{1,2},{2,1},{3,0},{4,7},{5,6},{6,5},{7,4},{8,11},{9,10},{10,... | collective-permute-start | bytes 491528 | tf_op jit(solution)/shard_map/ppermute | solution.py:86
  36.7 30.1 %collective-permute-start.18 = (bf16[10,16,512]{2,1,0:T(8,128)(2,1)S(1)}, bf16[10,16,512]{2,1,0:T(8,128)(2,1)S(1)}, u32[]{:S(2)}, u32[]{:S(2)}) collective-permute-start(bf16[10,16,512]{2,1,0:T(8,128)(2,1)S(1)} %maximum_maximum_fusion), channel_id=1, source_target_pairs={{0,2},{1,3},{2,0},{3,1},{4,6},{5,7},{6,4},{7,5},{8,10},{9,11},{10,... | collective-permute-start | bytes 491528 | tf_op jit(solution)/shard_map/ppermute | solution.py:86
  37.9 28.8 %collective-permute-start.17 = (bf16[10,16,512]{2,1,0:T(8,128)(2,1)S(1)}, bf16[10,16,512]{2,1,0:T(8,128)(2,1)S(1)}, u32[]{:S(2)}, u32[]{:S(2)}) collective-permute-start(bf16[10,16,512]{2,1,0:T(8,128)(2,1)S(1)} %maximum_maximum_fusion), channel_id=1, source_target_pairs={{0,1},{1,0},{2,3},{3,2},{4,5},{5,4},{6,7},{7,6},{8,9},{9,8},{10,11... | collective-permute-start | bytes 491528 | tf_op jit(solution)/shard_map/ppermute | solution.py:86
  38.7 31.7 %collective-permute-start.11 = (bf16[8,192,128]{2,1,0:T(8,128)(2,1)}, bf16[8,192,128]{2,1,0:T(8,128)(2,1)S(1)}, u32[]{:S(2)}, u32[]{:S(2)}) collective-permute-start(bf16[8,192,128]{2,1,0:T(8,128)(2,1)} %get-tuple-element.49.refs_0_.refs_5_), channel_id=1, source_target_pairs={{0,16},{1,17},{2,18},{3,19},{4,20},{5,21},{6,22},{7,23},{8,24},{9,... | collective-permute-start | bytes 1179656 | tf_op jit(solution)/shard_map/ppermute | solution.py:86
  50.3 33.2 %collective-permute-start.10 = (bf16[8,192,128]{2,1,0:T(8,128)(2,1)}, bf16[8,192,128]{2,1,0:T(8,128)(2,1)S(1)}, u32[]{:S(2)}, u32[]{:S(2)}) collective-permute-start(bf16[8,192,128]{2,1,0:T(8,128)(2,1)} %get-tuple-element.49.refs_0_.refs_5_), channel_id=1, source_target_pairs={{0,2},{1,3},{2,0},{3,1},{4,6},{5,7},{6,4},{7,5},{8,10},{9,11},{10,... | collective-permute-start | bytes 1179656 | tf_op jit(solution)/shard_map/ppermute | solution.py:86
  66.9 50.4 %collective-permute-start.22 = (bf16[4,10,16,512]{3,2,1,0:T(8,128)(2,1)S(1)}, bf16[4,10,16,512]{3,2,1,0:T(8,128)(2,1)S(1)}, u32[]{:S(2)}, u32[]{:S(2)}) collective-permute-start(bf16[4,10,16,512]{3,2,1,0:T(8,128)(2,1)S(1)} %pad_maximum_fusion.refs_9_), channel_id=1, source_target_pairs={{0,24},{1,25},{2,26},{3,27},{4,28},{5,29},{6,30},{7,31},{8,16},{9,... | collective-permute-start | bytes 1966088 | tf_op jit(solution)/shard_map/ppermute | solution.py:86
  67.4 50.0 %collective-permute-start.21 = (bf16[4,10,16,512]{3,2,1,0:T(8,128)(2,1)S(1)}, bf16[4,10,16,512]{3,2,1,0:T(8,128)(2,1)S(1)}, u32[]{:S(2)}, u32[]{:S(2)}) collective-permute-start(bf16[4,10,16,512]{3,2,1,0:T(8,128)(2,1)S(1)} %pad_maximum_fusion.refs_9_), channel_id=1, source_target_pairs={{0,16},{1,17},{2,18},{3,19},{4,20},{5,21},{6,22},{7,23},{8,24},{9,... | collective-permute-start | bytes 1966088 | tf_op jit(solution)/shard_map/ppermute | solution.py:86
  68.9 48.9 %collective-permute-start.20 = (bf16[4,10,16,512]{3,2,1,0:T(8,128)(2,1)S(1)}, bf16[4,10,16,512]{3,2,1,0:T(8,128)(2,1)S(1)}, u32[]{:S(2)}, u32[]{:S(2)}) collective-permute-start(bf16[4,10,16,512]{3,2,1,0:T(8,128)(2,1)S(1)} %pad_maximum_fusion.refs_9_), channel_id=1, source_target_pairs={{0,8},{1,9},{2,10},{3,11},{4,12},{5,13},{6,14},{7,15},{8,0},{9,1},... | collective-permute-start | bytes 1966088 | tf_op jit(solution)/shard_map/ppermute | solution.py:86
  116.8 16.2 %collective-permute-start.23 = (bf16[4,10,16,512]{3,2,1,0:T(8,128)(2,1)S(1)}, bf16[4,10,16,512]{3,2,1,0:T(8,128)(2,1)}, u32[]{:S(2)}, u32[]{:S(2)}) collective-permute-start(bf16[4,10,16,512]{3,2,1,0:T(8,128)(2,1)S(1)} %pad_maximum_fusion.refs_9_), channel_id=1, source_target_pairs={{0,4},{1,5},{2,6},{3,7},{4,0},{5,1},{6,2},{7,3},{8,12},{9,13},{10,... | collective-permute-start | bytes 1966088 | tf_op jit(solution)/shard_map/ppermute | solution.py:86
  117.3 15.7 %collective-permute-start.26 = (bf16[4,10,16,512]{3,2,1,0:T(8,128)(2,1)S(1)}, bf16[4,10,16,512]{3,2,1,0:T(8,128)(2,1)}, u32[]{:S(2)}, u32[]{:S(2)}) collective-permute-start(bf16[4,10,16,512]{3,2,1,0:T(8,128)(2,1)S(1)} %collective-permute-done.22.refs_12_), channel_id=1, source_target_pairs={{0,4},{1,5},{2,6},{3,7},{4,0},{5,1},{6,2},{7,3},{8,12},{9,13},{10,... | collective-permute-start | bytes 1966088 | tf_op jit(solution)/shard_map/ppermute | solution.py:86
  117.4 15.6 %collective-permute-start.25 = (bf16[4,10,16,512]{3,2,1,0:T(8,128)(2,1)S(1)}, bf16[4,10,16,512]{3,2,1,0:T(8,128)(2,1)}, u32[]{:S(2)}, u32[]{:S(2)}) collective-permute-start(bf16[4,10,16,512]{3,2,1,0:T(8,128)(2,1)S(1)} %collective-permute-done.21.refs_11_), channel_id=1, source_target_pairs={{0,4},{1,5},{2,6},{3,7},{4,0},{5,1},{6,2},{7,3},{8,12},{9,13},{10,... | collective-permute-start | bytes 1966088 | tf_op jit(solution)/shard_map/ppermute | solution.py:86
  117.8 15.2 %collective-permute-start.24 = (bf16[4,10,16,512]{3,2,1,0:T(8,128)(2,1)S(1)}, bf16[4,10,16,512]{3,2,1,0:T(8,128)(2,1)}, u32[]{:S(2)}, u32[]{:S(2)}) collective-permute-start(bf16[4,10,16,512]{3,2,1,0:T(8,128)(2,1)S(1)} %collective-permute-done.20.refs_10_), channel_id=1, source_target_pairs={{0,4},{1,5},{2,6},{3,7},{4,0},{5,1},{6,2},{7,3},{8,12},{9,13},{10,... | collective-permute-start | bytes 1966088 | tf_op jit(solution)/shard_map/ppermute | solution.py:86
  151.7 94.0 %collective-permute-start.27 = (bf16[4,4,10,16,512]{4,3,2,1,0:T(8,128)(2,1)}, bf16[4,4,10,16,512]{4,3,2,1,0:T(8,128)(2,1)}, u32[]{:S(2)}, u32[]{:S(2)}) collective-permute-start(bf16[4,4,10,16,512]{4,3,2,1,0:T(8,128)(2,1)} %slice_bitcast_fusion), channel_id=1, source_target_pairs={{0,4},{1,5},{2,6},{3,7},{4,0},{5,1},{6,2},{7,3},{8,12},{9,13},{10,... | collective-permute-start | bytes 7864328 | tf_op jit(solution)/shard_map/ppermute | solution.py:86
  191.5 28.7 %collective-permute-start.42 = (bf16[8,192,128]{2,1,0:T(8,128)(2,1)}, bf16[8,192,128]{2,1,0:T(8,128)(2,1)S(1)}, u32[]{:S(2)}, u32[]{:S(2)}) collective-permute-start(bf16[8,192,128]{2,1,0:T(8,128)(2,1)} %get-tuple-element.69), channel_id=1, source_target_pairs={{0,2},{1,3},{2,0},{3,1},{4,6},{5,7},{6,4},{7,5},{8,10},{9,11},{10,... | collective-permute-start | bytes 1179656 | tf_op jit(solution)/shard_map/ppermute | solution.py:86
  191.5 28.6 %collective-permute-start.43 = (bf16[8,192,128]{2,1,0:T(8,128)(2,1)}, bf16[8,192,128]{2,1,0:T(8,128)(2,1)}, u32[]{:S(2)}, u32[]{:S(2)}) collective-permute-start(bf16[8,192,128]{2,1,0:T(8,128)(2,1)} %get-tuple-element.70), channel_id=1, source_target_pairs={{0,16},{1,17},{2,18},{3,19},{4,20},{5,21},{6,22},{7,23},{8,24},{9,... | collective-permute-start | bytes 1179656 | tf_op jit(solution)/shard_map/ppermute | solution.py:86
  191.6 28.6 %collective-permute-start.44 = (bf16[8,192,128]{2,1,0:T(8,128)(2,1)}, bf16[8,192,128]{2,1,0:T(8,128)(2,1)}, u32[]{:S(2)}, u32[]{:S(2)}) collective-permute-start(bf16[8,192,128]{2,1,0:T(8,128)(2,1)} %get-tuple-element.71), channel_id=1, source_target_pairs={{0,18},{1,19},{2,16},{3,17},{4,22},{5,23},{6,20},{7,21},{8,26},{9,... | collective-permute-start | bytes 1179656 | tf_op jit(solution)/shard_map/ppermute | solution.py:86
  226.7 10.8 %collective-permute-start.49 = (bf16[128,256]{1,0:T(8,128)(2,1)}, bf16[128,256]{1,0:T(8,128)(2,1)S(1)}, u32[]{:S(2)}, u32[]{:S(2)}) collective-permute-start(bf16[128,256]{1,0:T(8,128)(2,1)} %get-tuple-element.75), channel_id=1, source_target_pairs={{0,2},{1,3},{2,0},{3,1},{4,6},{5,7},{6,4},{7,5},{8,10},{9,11},{10,... | collective-permute-start | bytes 196616 | tf_op jit(solution)/shard_map/ppermute | solution.py:86
  237.4 72.9 %collective-permute-start.45 = (bf16[4,192,512]{2,1,0:T(8,128)(2,1)}, bf16[4,192,512]{2,1,0:T(8,128)(2,1)}, u32[]{:S(2)}, u32[]{:S(2)}) collective-permute-start(bf16[4,192,512]{2,1,0:T(8,128)(2,1)} %get-tuple-element.73), channel_id=1, source_target_pairs={{0,4},{1,5},{2,6},{3,7},{4,0},{5,1},{6,2},{7,3},{8,12},{9,13},{10,... | collective-permute-start | bytes 2359304 | tf_op jit(solution)/shard_map/ppermute | solution.py:86
  249.0 32.0 %collective-permute-start.28 = (bf16[4,10,16,512]{3,2,1,0:T(8,128)(2,1)S(1)}, bf16[4,10,16,512]{3,2,1,0:T(8,128)(2,1)S(1)}, u32[]{:S(2)}, u32[]{:S(2)}) collective-permute-start(bf16[4,10,16,512]{3,2,1,0:T(8,128)(2,1)S(1)} %get-tuple-element.83), channel_id=1, source_target_pairs={{0,8},{1,9},{2,10},{3,11},{4,12},{5,13},{6,14},{7,15},{8,0},{9,1},... | collective-permute-start | bytes 1966088 | tf_op jit(solution)/shard_map/ppermute | solution.py:86
  250.5 30.5 %collective-permute-start.30 = (bf16[4,10,16,512]{3,2,1,0:T(8,128)(2,1)S(1)}, bf16[4,10,16,512]{3,2,1,0:T(8,128)(2,1)S(1)}, u32[]{:S(2)}, u32[]{:S(2)}) collective-permute-start(bf16[4,10,16,512]{3,2,1,0:T(8,128)(2,1)S(1)} %get-tuple-element.84), channel_id=1, source_target_pairs={{0,24},{1,25},{2,26},{3,27},{4,28},{5,29},{6,30},{7,31},{8,16},{9,... | collective-permute-start | bytes 1966088 | tf_op jit(solution)/shard_map/ppermute | solution.py:86
  250.5 30.5 %collective-permute-start.29 = (bf16[4,10,16,512]{3,2,1,0:T(8,128)(2,1)S(1)}, bf16[4,10,16,512]{3,2,1,0:T(8,128)(2,1)S(1)}, u32[]{:S(2)}, u32[]{:S(2)}) collective-permute-start(bf16[4,10,16,512]{3,2,1,0:T(8,128)(2,1)S(1)} %get-tuple-element.85), channel_id=1, source_target_pairs={{0,16},{1,17},{2,18},{3,19},{4,20},{5,21},{6,22},{7,23},{8,24},{9,... | collective-permute-start | bytes 1966088 | tf_op jit(solution)/shard_map/ppermute | solution.py:86
  252.5 28.3 %collective-permute-start.53 = (bf16[2,128,256]{2,1,0:T(8,128)(2,1)S(1)}, bf16[2,128,256]{2,1,0:T(8,128)(2,1)S(1)}, u32[]{:S(2)}, u32[]{:S(2)}) collective-permute-start(bf16[2,128,256]{2,1,0:T(8,128)(2,1)S(1)} %add_convert_fusion.1), channel_id=1, source_target_pairs={{0,8},{1,9},{2,10},{3,11},{4,12},{5,13},{6,14},{7,15},{8,0},{9,1},... | collective-permute-start | bytes 393224 | tf_op jit(solution)/shard_map/ppermute | solution.py:86
  280.9 22.7 %collective-permute-start.54 = (bf16[2,2,128,256]{3,2,1,0:T(8,128)(2,1)S(1)}, bf16[2,2,128,256]{3,2,1,0:T(8,128)(2,1)S(1)}, u32[]{:S(2)}, u32[]{:S(2)}) collective-permute-start(bf16[2,2,128,256]{3,2,1,0:T(8,128)(2,1)S(1)} %pad_maximum_fusion.2), channel_id=1, source_target_pairs={{0,4},{1,5},{2,6},{3,7},{4,0},{5,1},{6,2},{7,3},{8,12},{9,13},{10,... | collective-permute-start | bytes 786440 | tf_op jit(solution)/shard_map/ppermute | solution.py:86
  281.6 11.3 %collective-permute-start.33 = (bf16[10,16,512]{2,1,0:T(8,128)(2,1)S(1)}, bf16[10,16,512]{2,1,0:T(8,128)(2,1)S(1)}, u32[]{:S(2)}, u32[]{:S(2)}) collective-permute-start(bf16[10,16,512]{2,1,0:T(8,128)(2,1)S(1)} %get-tuple-element.95), channel_id=1, source_target_pairs={{0,3},{1,2},{2,1},{3,0},{4,7},{5,6},{6,5},{7,4},{8,11},{9,10},{10,... | collective-permute-start | bytes 491528 | tf_op jit(solution)/shard_map/ppermute | solution.py:86
  284.4 15.6 %collective-permute-start.32 = (bf16[10,16,512]{2,1,0:T(8,128)(2,1)S(1)}, bf16[10,16,512]{2,1,0:T(8,128)(2,1)S(1)}, u32[]{:S(2)}, u32[]{:S(2)}) collective-permute-start(bf16[10,16,512]{2,1,0:T(8,128)(2,1)S(1)} %get-tuple-element.96), channel_id=1, source_target_pairs={{0,2},{1,3},{2,0},{3,1},{4,6},{5,7},{6,4},{7,5},{8,10},{9,11},{10,... | collective-permute-start | bytes 491528 | tf_op jit(solution)/shard_map/ppermute | solution.py:86
  310.2 17.9 %collective-permute-start.37 = (bf16[4,10,16,512]{3,2,1,0:T(8,128)(2,1)S(1)}, bf16[4,10,16,512]{3,2,1,0:T(8,128)(2,1)S(1)}, u32[]{:S(2)}, u32[]{:S(2)}) collective-permute-start(bf16[4,10,16,512]{3,2,1,0:T(8,128)(2,1)S(1)} %pad_maximum_fusion.1), channel_id=1, source_target_pairs={{0,4},{1,5},{2,6},{3,7},{4,0},{5,1},{6,2},{7,3},{8,12},{9,13},{10,... | collective-permute-start | bytes 1966088 | tf_op jit(solution)/shard_map/ppermute | solution.py:86
  312.5 11.6 %collective-permute-start.47 = (bf16[192,512]{1,0:T(8,128)(2,1)S(1)}, bf16[192,512]{1,0:T(8,128)(2,1)S(1)}, u32[]{:S(2)}, u32[]{:S(2)}) collective-permute-start(bf16[192,512]{1,0:T(8,128)(2,1)S(1)} %get-tuple-element.87), channel_id=1, source_target_pairs={{0,1},{1,0},{2,3},{3,2},{4,5},{5,4},{6,7},{7,6},{8,9},{9,8},{10,11... | collective-permute-start | bytes 589832 | tf_op jit(solution)/shard_map/ppermute | solution.py:86
  (61 other events, 649.5 us)

commit v2 on v1

--- a/solution.py
+++ b/solution.py
@@ -9,8 +9,8 @@
 HEAD = 64
 EPS = 1e-05
 LOSS_SCALE = 262144.0
-CTX_HEADS = 4
-WT_HEADS = 2
+CTX_HEADS = 2
+WT_HEADS = 4
 CHUNK = 512
 TILE = 16
 F32 = jnp.float32
@@ -72,7 +72,13 @@
         self.peers = [(mc, mw) for mw in range(aw) for mc in range(0, ac, 2)]
         self.slots = [(mc | k, mw) for k in (0, 1) for mc, mw in self.peers]
         self.groups = [(mc, mw) for mc in range(0, n_ctx, ac) for mw in range(0, n_wt, aw)]
-        self.all_slots = [(gc ^ sc, gw ^ sw) for gc, gw in self.groups for sc, sw in self.slots]
+        self.square = n_ctx == 8 and n_wt == aw
+
+    def near(self, core):
+        return [0, 2 + 2 * core, 4 - 2 * core, 6]
+
+    def group_masks(self, core):
+        return [(m, 0) for m in self.near(core)] if self.square else self.groups
 
     def head(self, ctx, wt):
         return (wt % WT_HEADS) * CTX_HEADS + ctx % CTX_HEADS
@@ -85,9 +91,47 @@
         ]
         return lax.ppermute(x, ("ctx", "wt"), perm)
 
+    def turn(self, x, first):
+        n = self.n_wt
+        masks = (2, 4) if first else (4, 2)
+        perm = [
+            (c * n + w, (c ^ masks[c % 2]) * n + w) for c in range(self.n_ctx) for w in range(n)
+        ]
+        return lax.ppermute(x, ("ctx", "wt"), perm)
+
+    def gather_square(self, x):
+        one = self.turn(x, True)
+        return [x, one, self.turn(x, False), self.turn(one, False)]
+
+    def gather_groups(self, x):
+        if self.square:
+            return self.gather_square(x)
+        return [x] + [self.swap(x, m) for m in self.groups[1:]]
+
+
+def pack_body(plan, shard, blk):
+    nw, half = plan.n_wt, shard // 2
+
+    def body(info, words_ref, w_ref, vec_ref, *outs):
+        odd = (info[0] % 2) == 1
+        vec = vec_ref[...].astype(F32)
+        lane = lane_iota((shard, 4 * HEAD))
+        for m in range(nw):
+            pair = plan.head(info[0], info[1] ^ m) // 2
+            col = pl.multiple_of(pair * (6 * HEAD), 2 * HEAD)
+            both = w_ref[:, pl.ds(col, 6 * HEAD)].astype(F32)
+            turned = pltpu.roll(both, 3 * HEAD, 1)
+            cols = jnp.where(odd, turned[:, : 4 * HEAD], both[:, : 4 * HEAD])
+            cols = jnp.where(lane < 3 * HEAD, cols, vec).astype(BF16)
+            outs[m][:blk, :] = words_ref[...]
+            outs[m][blk:, : 4 * HEAD] = cols[:half]
+            outs[m][blk:, 4 * HEAD :] = cols[half:]
+
+    return body
+
 
 def project_body(plan, shard, blk):
-    ns, nw = len(plan.slots), plan.n_wt
+    ns, nw, half = len(plan.slots), plan.n_wt, shard // 2
 
     def body(info, *refs):
         xs, wps = refs[:ns], refs[ns : ns + nw]
@@ -95,7 +139,8 @@
         wt = info[1]
         for m in range(nw):
             row = pl.multiple_of((wt ^ m) * shard, shard)
-            wh_ref[pl.ds(row, shard), :] = wps[m][...]
+            wh_ref[pl.ds(row, half), :] = wps[m][blk:, : 4 * HEAD]
+            wh_ref[pl.ds(row + half, half), :] = wps[m][blk:, 4 * HEAD :]
         weight = wh_ref[...]
         rows = lax.broadcasted_iota(jnp.int32, (8, 4 * HEAD), 0)
         pick = jnp.where(lane_iota((8, 4 * HEAD)) == rows + 3 * HEAD, 1.0, 0.0).astype(BF16)
@@ -104,7 +149,7 @@
         gain, shift = vecs[0:1], vecs[1:2]
         low = lane_iota((blk, 2 * HEAD)) < HEAD
         for s in range(ns):
-            unit, _ = norm_stats(xs[s][...].astype(F32))
+            unit, _ = norm_stats(xs[s][:blk, :].astype(F32))
             normed = (unit * gain + shift).astype(BF16)
             normed_ref[s] = normed
             y = mm(normed, weight)
@@ -117,8 +162,10 @@
 
 
 def fill_slots(plan, info, deal, slot_of):
-    for s, (mc, mw) in enumerate(plan.all_slots):
-        slot_of[deal[(info[0] ^ mc) * plan.n_wt + (info[1] ^ mw)]] = s
+    for g, (gc, gw) in enumerate(plan.group_masks(info[0] % 2)):
+        for s, (mc, mw) in enumerate(plan.slots):
+            at = (info[0] ^ gc ^ mc) * plan.n_wt + (info[1] ^ gw ^ mw)
+            slot_of[deal[at]] = g * len(plan.slots) + s
 
 
 def slot_range(plan, info, deal, lengths, codes, i, blk, nseq):
@@ -133,129 +180,252 @@
     return first, here
 
 
-def load_kv(kv_refs, kvs, sem, ns):
-    copies = [
-        pltpu.make_async_copy(ref, kvs.at[pl.ds(b * ns, ns)], sem.at[b])
-        for b, ref in enumerate(kv_refs)
-    ]
-    for c in copies:
-        c.start()
-    for c in copies:
-        c.wait()
-
-
-def attend_body(plan, blk, nseq):
-    ns, nb = len(plan.slots), len(plan.groups)
+def list_pairs(plan, info, deal, lengths, codes, blk, nseq, slot_of, pairs, low, high):
+    fill_slots(plan, info, deal, slot_of)
+
+    def one_block(i, n):
+        first, here = slot_range(plan, info, deal, lengths, codes, i, blk, nseq)
+
+        def one_key(b, n):
+            slot = slot_of[b]
+            inside = (slot >= low) & (slot < high)
+            pairs[n] = i * 1024 + slot - low
+            return n + inside.astype(jnp.int32)
+
+        return lax.fori_loop(first, here, one_key, n)
+
+    n = lax.fori_loop(0, len(plan.slots), one_block, jnp.int32(0))
+    pairs[n] = pairs[jnp.maximum(n - 1, 0)]
+    return n
+
+
+def attend_body(plan, blk, nseq, lo, hi, last):
+    ns, nb = len(plan.slots), hi - lo
 
     def body(info, deal, lengths, codes, q_ref, *refs):
-        kv_refs = refs[:nb]
-        o_ref, of_ref, lse_ref = refs[nb : nb + 3]
-        kvs, slot_of, acc_ref, m_ref, l_ref, sem = refs[nb + 3 :]
-        load_kv(kv_refs, kvs, sem, ns)
-        fill_slots(plan, info, deal, slot_of)
-        core = info[0] % 2
-        tri = lax.broadcasted_iota(jnp.int32, (blk, blk), 0) <= lane_iota((blk, blk))
-
-        def one_block(i, _):
-            first, here = slot_range(plan, info, deal, lengths, codes, i, blk, nseq)
-            q = q_ref[i]
-            kv = kvs[slot_of[here]]
-            s = jnp.where(tri, mm(kv, q, NT), NEG)
-            m = jnp.max(s, axis=0, keepdims=True)
-            p = jnp.exp(s - m)
-            m_ref[...] = m
-            l_ref[...] = jnp.sum(p, axis=0, keepdims=True)
-            acc_ref[...] = mm(kv, p.astype(BF16), TN)
-
-            def step(b, _):
-                kv = kvs[slot_of[b]]
-                s = mm(kv, q, NT)
-                m_old = m_ref[...]
+        kv_refs, refs = refs[:nb], refs[nb:]
+        if lo:
+            olds, refs = refs[:3], refs[3:]
+        (m_ref, l_ref, acc_ref), refs = refs[:3], refs[3:]
+        if last:
+            (o_ref, of_ref, lse_ref), refs = refs[:3], refs[3:]
+        kvs, slot_of, pairs, sem = refs
+        copies = [
+            pltpu.make_async_copy(ref, kvs.at[pl.ds(b * ns, ns)], sem.at[b])
+            for b, ref in enumerate(kv_refs)
+        ]
+        for c in copies:
+            c.start()
+        n = list_pairs(
+            plan, info, deal, lengths, codes, blk, nseq, slot_of, pairs, lo * ns, hi * ns
+        )
+        if lo:
+            for new, old in zip((m_ref, l_ref, acc_ref), olds):
+                new[...] = old[...]
+        for c in copies:
+            c.wait()
+        if not lo:
+            tri = lax.broadcasted_iota(jnp.int32, (blk, blk), 0) <= lane_iota((blk, blk))
+
+            def diagonal(h, _):
+                scores = [mm(kvs[h * 2 + k], q_ref[h * 2 + k], NT) for k in (0, 1)]
+                for k in (0, 1):
+                    i = h * 2 + k
+                    s = jnp.where(tri, scores[k], NEG)
+                    m = jnp.max(s, axis=0, keepdims=True)
+                    p = jnp.exp(s - m)
+                    m_ref[i] = m
+                    l_ref[i] = jnp.sum(p, axis=0, keepdims=True)
+                    acc_ref[i] = mm(kvs[i], p.astype(BF16), TN)
+                return 0
+
+            lax.fori_loop(0, ns // 2, diagonal, 0)
+
+        def step(h, _):
+            codes2 = [pairs[h * 2], pairs[h * 2 + 1]]
+            rows = [c // 1024 for c in codes2]
+            cols = [c % 1024 for c in codes2]
+            scores = [mm(kvs[cols[k]], q_ref[rows[k]], NT) for k in (0, 1)]
+            scores[1] = jnp.where(h * 2 + 1 < n, scores[1], NEG)
+            for k in (0, 1):
+                i, s = rows[k], scores[k]
+                m_old = m_ref[i]
                 m = jnp.maximum(m_old, jnp.max(s, axis=0, keepdims=True))
                 p = jnp.exp(s - m)
                 factor = jnp.exp(m_old - m)
-                m_ref[...] = m
-                l_ref[...] = l_ref[...] * factor + jnp.sum(p, axis=0, keepdims=True)
-                acc_ref[...] = acc_ref[...] * factor + mm(kv, p.astype(BF16), TN)
+                m_ref[i] = m
+                l_ref[i] = l_ref[i] * factor + jnp.sum(p, axis=0, keepdims=True)
+                acc_ref[i] = acc_ref[i] * factor + mm(kvs[cols[k]], p.astype(BF16), TN)
+            return 0
+
+        lax.fori_loop(0, (n + 1) // 2, step, 0)
+        if last:
+            core = info[0] % 2
+
+            def finish(i, _):
+                total = l_ref[i]
+                lse_ref[i] = m_ref[i] + jnp.log(total)
+                out = acc_ref[i, HEAD:, :] / total
+                zero = jnp.zeros_like(out)
+                placed = jnp.concatenate(
+                    [jnp.where(core == 0, out, zero), jnp.where(core == 1, out, zero)], axis=0
+                )
+                wide = placed.T
+                of_ref[i] = wide
+                o_ref[i] = wide.astype(BF16)
                 return 0
 
-            lax.fori_loop(first, here, step, 0)
-            total = l_ref[...]
-            lse_ref[i] = m_ref[...] + jnp.log(total)
-            out = acc_ref[HEAD:, :] / total
-            zero = jnp.zeros_like(out)
-            placed = jnp.concatenate(
-                [jnp.where(core == 0, out, zero), jnp.where(core == 1, out, zero)], axis=0
+            lax.fori_loop(0, ns, finish, 0)
+
+    return body
+
+
+def attend_part(plan, blk, nseq, lo, hi, last, scalars, q, kvs, olds):
+    ns, nb = len(plan.slots), hi - lo
+    outs = [sds((ns, 1, blk), F32), sds((ns, 1, blk), F32), sds((ns, 2 * HEAD, blk), F32)]
+    if last:
+        outs += [
+            sds((ns, blk, 2 * HEAD), BF16),
+            sds((ns, blk, 2 * HEAD), F32),
+            sds((ns, 1, blk), F32),
+        ]
+    n_dev = plan.n_ctx * plan.n_wt
+    pairs = 14 * nb
+    return call(
+        attend_body(plan, blk, nseq, lo, hi, last),
+        "attend",
+        list(scalars) + [q] + list(kvs[lo:hi]) + list(olds),
+        [SMEM] * 4 + [VMEM] + [ANY] * nb + [VMEM] * len(olds),
+        outs,
+        scratch=[
+            pltpu.VMEM((nb * ns, blk, 2 * HEAD), BF16),
+            pltpu.SMEM((n_dev,), jnp.int32),
+            pltpu.SMEM((ns * n_dev + 1,), jnp.int32),
+            pltpu.SemaphoreType.DMA((nb,)),
+        ],
+        flops=pairs * 4 * blk * blk * 128 * 8,
+        trans=pairs * blk * blk,
+    )
+
+
+def attend_back_body(plan, blk, nseq, lo, hi, first, last):
+    ns, nb, nj = len(plan.slots), hi - lo, len(plan.peers)
+
+    def body(info, deal, lengths, codes, q_ref, lse_ref, *refs):
+        kv_refs, refs = refs[:nb], refs[nb:]
+        if first:
+            of_ref, g_refs, gs_ref, refs = refs[0], refs[1 : 1 + nj], refs[1 + nj], refs[2 + nj :]
+        else:
+            g_ext, delta_ref, old_dq, refs = refs[0], refs[1], refs[2], refs[3:]
+        dkv_refs, refs = refs[:nb], refs[nb:]
+        dq_acc, refs = refs[0], refs[1:]
+        if first:
+            g_ext, delta_ref, refs = refs[0], refs[1], refs[2:]
+        if last:
+            dq_ref, refs = refs[0], refs[1:]
+        kvs, dkvs, slot_of, pairs, sem = refs
+        copies = [
+            pltpu.make_async_copy(ref, kvs.at[pl.ds(b * ns, ns)], sem.at[b])
+            for b, ref in enumerate(kv_refs)
+        ]
+        for c in copies:
+            c.start()
+        n = list_pairs(
+            plan, info, deal, lengths, codes, blk, nseq, slot_of, pairs, lo * ns, hi * ns
+        )
+        core = info[0] % 2
+        high = lane_iota((blk, 2 * HEAD)) >= HEAD
+        if first:
+            own_half = (lane_iota((blk, 2 * HEAD)) // HEAD) == core
+            for s in range(ns):
+                g = (g_refs[s][...] if s < nj else gs_ref[s - nj]).astype(F32)
+                g = jnp.where(own_half, g, 0.0)
+                delta_ref[s] = jnp.sum((g * of_ref[s]).T, axis=0, keepdims=True)
+                turned = pltpu.roll(g, HEAD, 1)
+                g_ext[s] = jnp.where(high, jnp.where(core == 1, g, turned), 0.0).astype(BF16)
+            dq_acc[...] = jnp.zeros_like(dq_acc)
+        else:
+            dq_acc[...] = old_dq[...]
+        dkvs[...] = jnp.zeros_like(dkvs)
+        for c in copies:
+            c.wait()
+
+        def pair_terms(rows, cols, mask):
+            scores = [mm(kvs[c], q_ref[i], NT) for i, c in zip(rows, cols)]
+            slopes = [mm(kvs[c], g_ext[i], NT) for i, c in zip(rows, cols)]
+            for k, (i, c) in enumerate(zip(rows, cols)):
+                p = jnp.exp(scores[k] - lse_ref[i])
+                p = mask(k, p)
+                ds = (p * (slopes[k] - delta_ref[i])).astype(BF16)
+                dkvs[c] += mm(ds, q_ref[i]) + mm(p.astype(BF16), g_ext[i])
+                dq_acc[i] += mm(kvs[c], ds, TN)
+
+        if not lo:
+            tri = lax.broadcasted_iota(jnp.int32, (blk, blk), 0) <= lane_iota((blk, blk))
+
+            def diagonal(h, _):
+                at = [h * 2, h * 2 + 1]
+                pair_terms(at, at, lambda k, p: jnp.where(tri, p, 0.0))
+                return 0
+
+            lax.fori_loop(0, ns // 2, diagonal, 0)
+
+        def step(h, _):
+            codes2 = [pairs[h * 2], pairs[h * 2 + 1]]
+            pair_terms(
+                [c // 1024 for c in codes2],
+                [c % 1024 for c in codes2],
+                lambda k, p: jnp.where(h * 2 + 1 < n, p, 0.0) if k else p,
             )
-            wide = placed.T
-            of_ref[i] = wide
-            o_ref[i] = wide.astype(BF16)
             return 0
 
-        lax.fori_loop(0, ns, one_block, 0)
-
-    return body
-
-
-def attend_back_body(plan, blk, nseq):
-    ns, nb, nj = len(plan.slots), len(plan.groups), len(plan.peers)
-
-    def body(info, deal, lengths, codes, q_ref, of_ref, lse_ref, *refs):
-        g_refs, gs_ref = refs[:nj], refs[nj]
-        kv_refs = refs[nj + 1 : nj + 1 + nb]
-        outs = refs[nj + 1 + nb :]
-        dq_ref, dkv_refs = outs[0], outs[1 : 1 + nb]
-        kvs, slot_of, dkvs, dq_acc, g_ext, delta_ref, sem = outs[1 + nb :]
-        load_kv(kv_refs, kvs, sem, ns)
-        fill_slots(plan, info, deal, slot_of)
-        core = info[0] % 2
-        tri = lax.broadcasted_iota(jnp.int32, (blk, blk), 0) <= lane_iota((blk, blk))
-        high = lane_iota((blk, 2 * HEAD)) >= HEAD
-        own_half = (lane_iota((blk, 2 * HEAD)) // HEAD) == core
-        for s in range(ns):
-            g = (g_refs[s][...] if s < nj else gs_ref[s - nj]).astype(F32)
-            g = jnp.where(own_half, g, 0.0)
-            delta_ref[s] = jnp.sum((g * of_ref[s]).T, axis=0, keepdims=True)
-            turned = pltpu.roll(g, HEAD, 1)
-            g_ext[s] = jnp.where(high, jnp.where(core == 1, g, turned), 0.0).astype(BF16)
-        dkvs[...] = jnp.zeros_like(dkvs)
-
-        def one_block(i, _):
-            first, here = slot_range(plan, info, deal, lengths, codes, i, blk, nseq)
-            q = q_ref[i]
-            g = g_ext[i]
-            lse = lse_ref[i]
-            delta = delta_ref[i]
-
-            def pair(b, mask):
-                slot = slot_of[b]
-                kv = kvs[slot]
-                p = jnp.exp(mm(kv, q, NT) - lse)
-                if mask:
-                    p = jnp.where(tri, p, 0.0)
-                ds = (p * (mm(kv, g, NT) - delta)).astype(BF16)
-                dkvs[slot] += mm(ds, q) + mm(p.astype(BF16), g)
-                return mm(kv, ds, TN)
-
-            dq_acc[...] = pair(here, True)
-
-            def step(b, _):
-                dq_acc[...] += pair(b, False)
+        lax.fori_loop(0, (n + 1) // 2, step, 0)
+        if last:
+
+            def finish(i, _):
+                wide = dq_acc[i].T * HEAD**-0.5
+                dq_ref[i] = jnp.where(high, 0.0, wide).astype(BF16)
                 return 0
 
-            lax.fori_loop(first, here, step, 0)
-            wide = dq_acc[...].T * HEAD**-0.5
-            dq_ref[i] = jnp.where(high, 0.0, wide).astype(BF16)
-            return 0
-
-        lax.fori_loop(0, ns, one_block, 0)
+            lax.fori_loop(0, ns, finish, 0)
         for b in range(nb):
             dkv_refs[b][...] = dkvs[b * ns : (b + 1) * ns].astype(BF16)
 
     return body
 
 
-def mlp_body(plan, width, ff, blk, packed, pieces):
+def attend_back_part(plan, blk, nseq, lo, hi, first, last, scalars, q, lse, kvs, extra):
+    ns, nb = len(plan.slots), hi - lo
+    rows = sds((ns, blk, 2 * HEAD), BF16)
+    outs = [rows] * nb + [sds((ns, 2 * HEAD, blk), F32)]
+    if first:
+        outs += [rows, sds((ns, 1, blk), F32)]
+    if last:
+        outs += [rows]
+    n_dev = plan.n_ctx * plan.n_wt
+    pairs = 14 * nb
+    return call(
+        attend_back_body(plan, blk, nseq, lo, hi, first, last),
+        "attend_back",
+        list(scalars) + [q, lse] + list(kvs[lo:hi]) + list(extra),
+        [SMEM] * 4 + [VMEM] * 2 + [ANY] * nb + [VMEM] * len(extra),
+        outs,
+        scratch=[
+            pltpu.VMEM((nb * ns, blk, 2 * HEAD), BF16),
+            pltpu.VMEM((nb * ns, blk, 2 * HEAD), F32),
+            pltpu.SMEM((n_dev,), jnp.int32),
+            pltpu.SMEM((ns * n_dev + 1,), jnp.int32),
+            pltpu.SemaphoreType.DMA((nb,)),
+        ],
+        flops=pairs * 10 * blk * blk * 128 * 8,
+        trans=pairs * blk * blk,
+    )
+
+
+Z_ORDER = (0, 2, 1, 3)
+
+
+def mlp_body(plan, width, ff, blk, packed):
     nj, nw, nc = len(plan.peers), plan.n_wt, plan.n_ctx
     nq = ff // CHUNK
 
@@ -264,7 +434,7 @@
         x_ref, teacher_ref, valid_ref, vec_ref, count_ref = refs[:5]
         att = refs[5 : 5 + nj]
         rest = refs[5 + nj :]
-        nwt_in = len(pieces) if packed else 3
+        nwt_in = nc if packed else 3
         w_in, rest = rest[:nwt_in], rest[nwt_in:]
         (lo_ref, sq_ref, g1_ref, gatt_ref, act_ref, gpre_ref, n2_ref, gb_ref, ga_ref, gv_ref) = (
             rest[:10]
@@ -272,10 +442,12 @@
         if packed:
             wup, wdown, wout, meta, slope_ref, acc_ref, sem = rest[10:]
             copies = []
-            for n, (jc, src) in enumerate(zip(pieces, w_in)):
-                c = info[0] ^ jc
+            here = info[0] % 2
+            owners = [info[0] ^ m for m in plan.near(here)]
+            owners += [info[0] ^ 1 ^ m for m in plan.near(1 - here)]
+            for c, src in zip(owners, w_in):
                 for m in range(nw):
-                    w = info[1] ^ m
+                    w = info[1] ^ Z_ORDER[m]
                     copies += [
                         pltpu.make_async_copy(
                             src.at[m, pl.ds(nq + 4, 1)], wout.at[w, pl.ds(c, 1)], sem.at[0]
@@ -374,10 +546,7 @@
         att, outs = refs[:nj], refs[nj:]
         n2, gb, ga = n2_ref[...], gb_ref[...], ga_ref[...]
         ctx, wt = info[0], info[1]
-        if packed:
-            out_ref = outs[0]
-            rows_up = width // (nw * nc)
-
+        rows_up = width // (nw * nc)
         for q in range(nq):
             up = mm(n2, gpre_ref[q], TN).astype(BF16)
             down = mm(act_ref[q], gb, TN).astype(BF16)
@@ -386,10 +555,10 @@
                 down_t = down.reshape(nc, 4, TILE, width)
                 for w in range(nw):
                     for c in range(nc):
-                        put_tile(out_ref, info, c, w, q, up_t[w, c])
+                        put_tile(outs, info, c, w, q, up_t[w, c])
                 for c in range(nc):
                     for t in range(4):
-                        put_tile(out_ref, info, c, q, nq + t, down_t[c, t])
+                        put_tile(outs, info, c, q, nq + t, down_t[c, t])
             else:
                 outs[0][q] = up
                 outs[1][q] = down
@@ -403,7 +572,7 @@
                 for t in range(2 * HEAD // TILE):
                     at = base + t
                     w, c = at // nc, at % nc
-                    put_tile(out_ref, info, c, w, nq + 4, part_t[t])
+                    put_tile(outs, info, c, w, nq + 4, part_t[t])
             else:
                 row = pl.multiple_of((head // 2) * (2 * HEAD), 2 * HEAD)
                 outs[2][pl.ds(row, 2 * HEAD), :] = part
@@ -423,18 +592,23 @@
                 tile = jnp.concatenate([line, vec, jnp.zeros((TILE - 3, CHUNK), F32)], axis=0)
                 tile = tile.astype(BF16)
                 for c in range(nc):
-                    put_tile(out_ref, info, c, w, nq + 5, tile)
+                    put_tile(outs, info, c, w, nq + 5, tile)
 
     return body
 
 
-def put_tile(out_ref, info, c, w, tile, value):
-    jc = c ^ info[0]
-    out_ref[jc, w ^ info[1], tile] = value
-
-
-def head_grads_body(plan, blk, width, shard):
-    ns, nb, nw, nj = len(plan.slots), len(plan.groups), plan.n_wt, len(plan.peers)
+def put_tile(outs, info, c, w, tile, value):
+    plane = (c ^ info[0]) // 2
+    core = c % 2
+    middle = (plane == 1) | (plane == 2)
+    place = jnp.where(middle & (core == 1), 3 - plane, plane)
+    zed = w ^ info[1]
+    zed = jnp.where((zed == 1) | (zed == 2), 3 - zed, zed)
+    outs[0][core ^ (info[0] % 2), place, zed, tile] = value
+
+
+def head_grads_body(plan, blk, width, shard, nb):
+    ns, nw, nj = len(plan.slots), plan.n_wt, len(plan.peers)
 
     def body(info, dq_ref, wh_ref, normed_ref, *refs):
         xs = refs[:ns]
@@ -458,7 +632,7 @@
                 own_ref[s] = back.astype(BF16)
             else:
                 sib_ref[s - nj] = back.astype(BF16)
-            unit, _ = norm_stats(xs[s][...].astype(F32))
+            unit, _ = norm_stats(xs[s][:blk, :].astype(F32))
             gsum = gsum + jnp.sum(back * unit, axis=0, keepdims=True)
             ssum = ssum + jnp.sum(back, axis=0, keepdims=True)
             dw = mm(normed_ref[s], gh, TN)
@@ -489,14 +663,16 @@
     return body
 
 
-def unpack_body(plan, width, ff, pieces):
+def unpack_body(plan, width, ff):
     nq, nw, nc = ff // CHUNK, plan.n_wt, plan.n_ctx
 
     def body(info, *refs):
-        srcs, outs = refs[: len(pieces)], refs[len(pieces) :]
+        srcs, outs = refs[:nc], refs[nc:]
         up_ref, down_ref, out_ref, meta_ref = outs
-        for jc, src in zip(pieces, srcs):
-            c = info[0] ^ jc
+        here = info[0] % 2
+        owners = [info[0] ^ m for m in plan.near(here)]
+        owners += [info[0] ^ 1 ^ m for m in plan.near(1 - here)]
+        for c, src in zip(owners, srcs):
             row = pl.multiple_of(c * TILE, TILE)
             for q in range(nq):
                 up_ref[pl.ds(row, TILE), q * CHUNK : (q + 1) * CHUNK] = src[q].astype(F32)
@@ -566,28 +742,27 @@
     nq = ff // CHUNK
     nseq = lengths.shape[0]
     ns, nb, nj = len(plan.slots), len(plan.groups), len(plan.peers)
-    packed = width == CHUNK and width % (n_wt * n_ctx * TILE) == 0 and n_wt * CHUNK == ff
+    packed = plan.square and width == CHUNK and width % (n_wt * n_ctx * TILE) == 0 and n_wt * CHUNK == ff
     info = jnp.stack([ctx, wt]).astype(jnp.int32)
     codes = jnp.array([mc * n_wt + mw for mc, mw in plan.slots], jnp.int32)
     core = (1, 0)
 
-    xs = [words] + [plan.swap(words, m) for m in plan.peers[1:]]
     vec_cols = jnp.stack([gain_attn, shift_attn, gain_mlp, shift_mlp], axis=1)
-    vec_cols = jnp.pad(vec_cols, ((0, 0), (0, HEAD - 4)))
-
-    def head_cols(m):
-        head = plan.head(ctx, wt ^ m)
-        cols = lax.dynamic_slice_in_dim(w_qkv, head * 3 * HEAD, 3 * HEAD, 1)
-        return jnp.concatenate([cols, vec_cols], axis=1)
-
-    w_parts = [plan.swap(head_cols(m), (0, m)) for m in range(1, n_wt)]
-    w_parts = [head_cols(0)] + w_parts
-    xs = xs + [plan.swap(x, core) for x in xs]
+    vec_cols = jnp.pad(vec_cols, ((0, 0), (3 * HEAD, HEAD - 4)))
+    load = call(
+        pack_body(plan, shard, blk),
+        "pack",
+        [info, words, w_qkv, vec_cols],
+        [SMEM] + [VMEM] * 3,
+        [sds((blk + shard // 2, width), BF16)] * n_wt,
+    )
+    loads = [load[0]] + [plan.swap(load[m], (0, m)) for m in range(1, n_wt)]
+    xs = loads[:nj] + [plan.swap(x, core) for x in loads[:nj]]
 
     q, kv, normed, w_head, vecs = call(
         project_body(plan, shard, blk),
         "project",
-        [info] + xs + w_parts,
+        [info] + xs + loads,
         [SMEM] + [VMEM] * (ns + n_wt),
         [
             sds((ns, blk, 2 * HEAD), BF16),
@@ -598,7 +773,7 @@
         ],
         flops=2 * ns * blk * width * 4 * HEAD,
     )
-    kvs = [kv] + [plan.swap(kv, m) for m in plan.groups[1:]]
+    kvs = plan.gather_groups(kv)
 
     if packed:
         rows_up = width // (n_wt * n_ctx)
@@ -617,15 +792,15 @@
             axis=0,
         )
         piece, _ = lax.optimization_barrier((piece, q))
-        stack = jnp.stack([piece] + [plan.swap(piece, (0, m)) for m in range(1, n_wt)])
-        planes = [2 * p for p in range(n_ctx // 2)]
-        stacks = [stack] + [plan.swap(stack, (p, 0)) for p in planes[1:]]
+        two = jnp.stack([piece, plan.swap(piece, (0, 2))])
+        two, _ = lax.optimization_barrier((two, kvs[1]))
+        stack = jnp.concatenate([two, plan.swap(two, (0, 1))])
+        stack, _ = lax.optimization_barrier((stack, kvs[3]))
+        stacks = plan.gather_square(stack)
         stacks = stacks + [plan.swap(s, core) for s in stacks]
-        piece_ids = planes + [p + 1 for p in planes]
         weights = stacks
         count = jnp.zeros((1,), F32)
     else:
-        piece_ids = []
         up_full = lax.all_gather(w_up, "wt", axis=0, tiled=True)
         down_full = lax.all_gather(w_down, "wt", axis=0, tiled=True)
         out_full = lax.all_gather(w_out, "wt", axis=0, tiled=True)
@@ -636,28 +811,12 @@
         ]
         count = lax.psum(jnp.sum(valid).astype(F32), ("ctx", "wt")).reshape(1)
 
-    pairs = ns * nb * ns // 4
-    o, of32, lse = call(
-        attend_body(plan, blk, nseq),
-        "attend",
-        [info, deal, lengths, codes, q] + kvs,
-        [SMEM] * 4 + [VMEM] + [ANY] * nb,
-        [
-            sds((ns, blk, 2 * HEAD), BF16),
-            sds((ns, blk, 2 * HEAD), F32),
-            sds((ns, 1, blk), F32),
-        ],
-        scratch=[
-            pltpu.VMEM((nb * ns, blk, 2 * HEAD), BF16),
-            pltpu.SMEM((n_ctx * n_wt,), jnp.int32),
-            pltpu.VMEM((2 * HEAD, blk), F32),
-            pltpu.VMEM((1, blk), F32),
-            pltpu.VMEM((1, blk), F32),
-            pltpu.SemaphoreType.DMA((nb,)),
-        ],
-        flops=pairs * 4 * blk * blk * 128,
-        trans=pairs * blk * blk,
-    )
+    scalars = [info, deal, lengths, codes]
+    state = []
+    cuts = [(0, 1), (1, 3), (3, 4)] if plan.square else [(0, nb)]
+    for lo, hi in cuts:
+        state = attend_part(plan, blk, nseq, lo, hi, hi == nb, scalars, q, kvs, state)
+    o, of32, lse = state[3:]
     mixed = o[:nj] + plan.swap(o[nj:], core)
     att = [mixed[0]] + [plan.swap(mixed[j], plan.peers[j]) for j in range(1, nj)]
 
@@ -675,7 +834,7 @@
             pltpu.SemaphoreType.DMA((4,)),
         ]
     layer_out, square, grad_one, gatt, act, gpre, n2, gb, ga, gvec = call(
-        mlp_body(plan, width, ff, blk, packed, piece_ids),
+        mlp_body(plan, width, ff, blk, packed),
         "mlp",
         mlp_in,
         specs,
@@ -700,7 +859,7 @@
 
     grads_in = [info, act, gpre, n2, gb, ga, gvec, square] + att
     if packed:
-        grads_out = [sds((n_ctx, n_wt, nq + 6, TILE, CHUNK), BF16)]
+        grads_out = [sds((2, n_ctx // 2, n_wt, nq + 6, TILE, CHUNK), BF16)]
     else:
         grads_out = [
             sds((nq, width, CHUNK), BF16),
@@ -716,32 +875,29 @@
         flops=4 * blk * width * ff,
     )
 
-    back = call(
-        attend_back_body(plan, blk, nseq),
-        "attend_back",
-        [info, deal, lengths, codes, q, of32, lse] + g_own + [g_sib] + kvs,
-        [SMEM] * 4 + [VMEM] * (3 + nj + 1) + [ANY] * nb,
-        [sds((ns, blk, 2 * HEAD), BF16)] + [sds((ns, blk, 2 * HEAD), BF16)] * nb,
-        scratch=[
-            pltpu.VMEM((nb * ns, blk, 2 * HEAD), BF16),
-            pltpu.SMEM((n_ctx * n_wt,), jnp.int32),
-            pltpu.VMEM((nb * ns, blk, 2 * HEAD), F32),
-            pltpu.VMEM((2 * HEAD, blk), F32),
-            pltpu.VMEM((ns, blk, 2 * HEAD), BF16),
-            pltpu.VMEM((ns, 1, blk), F32),
-            pltpu.SemaphoreType.DMA((nb,)),
-        ],
-        flops=pairs * 10 * blk * blk * 128,
-        trans=pairs * blk * blk,
-    )
-    dq, dkvs = back[0], back[1:]
-    parts = [dkvs[0]] + [plan.swap(dkvs[b], plan.groups[b]) for b in range(1, nb)]
+    extra = [of32] + g_own + [g_sib]
+    if plan.square:
+        part = attend_back_part(plan, blk, nseq, 2, 4, True, False, scalars, q, lse, kvs, extra)
+        dkv2, dkv3, dq_part, g_ext, delta = part
+        far = [plan.turn(d, False) for d in (dkv3, dkv2)]
+        dkv1, dq_part = attend_back_part(
+            plan, blk, nseq, 1, 2, False, False, scalars, q, lse, kvs, [g_ext, delta, dq_part]
+        )
+        mid = plan.turn((dkv1.astype(F32) + far[0].astype(F32)).astype(BF16), True)
+        dkv0, _, dq = attend_back_part(
+            plan, blk, nseq, 0, 1, False, True, scalars, q, lse, kvs, [g_ext, delta, dq_part]
+        )
+        parts = [dkv0, far[1], mid]
+    else:
+        part = attend_back_part(plan, blk, nseq, 0, nb, True, True, scalars, q, lse, kvs, extra)
+        dq = part[-1]
+        parts = [part[0]] + [plan.swap(part[b], plan.groups[b]) for b in range(1, nb)]
 
     outs = call(
-        head_grads_body(plan, blk, width, shard),
+        head_grads_body(plan, blk, width, shard, len(parts)),
         "head_grads",
         [info, dq, w_head, normed] + xs + parts,
-        [SMEM] + [VMEM] * (3 + ns + nb),
+        [SMEM] + [VMEM] * (3 + ns + len(parts)),
         [sds((nj, blk, width), BF16)] * 2 + [sds((shard, 4 * HEAD), BF16)] * n_wt,
         scratch=[pltpu.VMEM((width, 4 * HEAD), F32)],
         flops=4 * ns * blk * width * 4 * HEAD,
@@ -770,8 +926,6 @@
         heads = (heads.astype(F32) + plan.swap(heads, (step, 0)).astype(F32)).astype(BF16)
         step *= 2
     cols = [heads]
-    for mc in range(2, CTX_HEADS, 2):
-        cols.append(plan.swap(heads, (mc, 0)))
     own_heads = jnp.stack(cols, axis=1)
     sib_heads = plan.swap(own_heads, core)
     srcs = [own_heads[a, p] for a in range(WT_HEADS) for p in range(CTX_HEADS // 2)]
@@ -785,21 +939,21 @@
     )
 
     if packed:
-        g_all = weight_grads[0].reshape(n_ctx // 2, 2, n_wt, nq + 6, TILE, CHUNK)
-        half = (g_all[:, 0].astype(F32) + plan.swap(g_all[:, 1], core).astype(F32)).astype(BF16)
-        total = half[0].astype(F32)
-        for p in range(1, n_ctx // 2):
-            total = total + plan.swap(half[p], (2 * p, 0)).astype(F32)
-        total = total.astype(BF16)
-        final = total[0].astype(F32)
-        for m in range(1, n_wt):
-            final = final + plan.swap(total[m], (0, m)).astype(F32)
-        final = final.astype(BF16)
-        finals = [final] + [plan.swap(final, (p, 0)) for p in planes[1:]]
-        finals_sib = plan.swap(jnp.stack(finals), core)
-        finals = finals + [finals_sib[p] for p in range(n_ctx // 2)]
+        g_all = weight_grads[0]
+        g_core = plan.swap(g_all[1], core)
+        far = (g_all[0, 2:].astype(F32) + g_core[2:].astype(F32)).astype(BF16)
+        far = plan.turn(far, False)
+        mid = g_all[0, 1].astype(F32) + g_core[1].astype(F32) + far[1].astype(F32)
+        mid = plan.turn(mid.astype(BF16), True)
+        near = g_all[0, 0].astype(F32) + g_core[0].astype(F32) + far[0].astype(F32)
+        near = (near + mid.astype(F32)).astype(BF16)
+        far = plan.swap(near[2:], (0, 1))
+        two = (near[:2].astype(F32) + far.astype(F32)).astype(BF16)
+        final = (two[0].astype(F32) + plan.swap(two[1], (0, 2)).astype(F32)).astype(BF16)
+        finals = plan.gather_square(final)
+        finals = finals + [plan.swap(f, core) for f in finals]
         g_up, g_down, g_out, meta = call(
-            unpack_body(plan, width, ff, piece_ids),
+            unpack_body(plan, width, ff),
             "unpack",
             [info] + finals,
             [SMEM] + [VMEM] * len(finals),

time: 334 us -> 271 us (0.81)
  waiting for transfers between devices: 134 us -> 93.8 us
  Pallas kernels: 94.7 us -> 75.3 us
  starting transfers between devices: 70.1 us -> 61.3 us
    ppermute x55 -> x38, waiting for transfers between devices: 134 us -> 88.1 us  [swap(): return lax.ppermute(x, ('ctx', 'wt'), perm)]
    ppermute x55 -> x38, starting transfers between devices: 70.1 us -> 30.3 us  [swap(): return lax.ppermute(x, ('ctx', 'wt'), perm)]
    ppermute x0 -> x14, starting transfers between devices: none -> 31.1 us  [turn(): return lax.ppermute(x, ('ctx', 'wt'), perm)]
    pallas_call x9 -> x14, Pallas kernels: 94.7 us -> 75.3 us  [call(): pl.pallas_call(body, name=name, out_shape=list(outs), in_specs=in_specs,...]
    ppermute x0 -> x14, waiting for transfers between devices: none -> 5.63 us  [turn(): return lax.ppermute(x, ('ctx', 'wt'), perm)]
    convert_element_type x3 -> x6, other arithmetic: 3.58 us -> 8.45 us  [the longest x1 2.96 us: per_device(): far = (g_all[0, 2:].astype(F32) + g_core[2:].astype(F32)).astype(BF16)]
  transfers between devices with their start and end apart: 55 -> 52, of which waited for: 26 -> 21; matrix products, arithmetic and copies ran while one was open for 7% -> 8% of each run, Pallas kernels for 22% -> 18%
where the time goes in v2:
time: 271 us
  waiting for transfers between devices  93.8 us (35%)
  Pallas kernels  75.3 us (28%)
  starting transfers between devices  61.3 us (23%)
  local copies, waits for them, and re-layouts  21.9 us (8%)
  other arithmetic  14 us (5%)
  between operations  4.41 us (2%)
    ppermute x38, waiting for transfers between devices, swap(): return lax.ppermute(x, ('ctx', 'wt'), perm)  88.1 us
    pallas_call x14, Pallas kernels, call(): pl.pallas_call(body, name=name, out_shape=list(outs), in_specs=in_specs,...  75.3 us
    ppermute x14, starting transfers between devices, turn(): return lax.ppermute(x, ('ctx', 'wt'), perm)  31.1 us
    ppermute x38, starting transfers between devices, swap(): return lax.ppermute(x, ('ctx', 'wt'), perm)  30.3 us
    unnamed x84, local copies, waits for them, and re-layouts  6.42 us
    ppermute x14, waiting for transfers between devices, turn(): return lax.ppermute(x, ('ctx', 'wt'), perm)  5.63 us
  transfers between devices with their start and end apart: 52, of which 21 were waited for; matrix products, arithmetic and copies ran while one was open for 8% of the time, Pallas kernels for 18%

profile of v2, /device:TPU:0, one launch (start us, length us, event | category | flops | bytes accessed | tf_op | source)
XLA Modules:
  0.0 270.8 jit_solution(11876478515528012995)
XLA Ops:
  5.1 3.0 %collective-permute-start = (bf16[256,512]{1,0:T(8,128)(2,1)}, bf16[256,512]{1,0:T(8,128)(2,1)S(1)}, u32[]{:S(2)}, u32[]{:S(2)}) collective-permute-start(bf16[256,512]{1,0:T(8,128)(2,1)} %get-tuple-element.64), channel_id=1, source_target_pairs={{0,1},{1,0},{2,3},{3,2},{4,5},{5,4},{6,7},{7,6},{8,9},{9,8},{10,11... | collective-permute-start | bytes 786440 | tf_op jit(solution)/shard_map/ppermute | solution.py:92
  8.1 2.6 collective-permute-start.1
  10.7 8.8 %collective-permute-done.refs_1_.refs_9_ = bf16[256,512]{1,0:T(8,128)(2,1)S(1)} collective-permute-done((bf16[256,512]{1,0:T(8,128)(2,1)}, bf16[256,512]{1,0:T(8,128)(2,1)S(1)}, u32[]{:S(2)}, u32[]{:S(2)}) %collective-permute-start) | collective-permute-done | bytes 262176 | tf_op jit(solution)/shard_map/ppermute | solution.py:92
  19.5 10.2 %collective-permute-done.1.refs_2_.refs_10_ = bf16[256,512]{1,0:T(8,128)(2,1)S(1)} collective-permute-done((bf16[256,512]{1,0:T(8,128)(2,1)}, bf16[256,512]{1,0:T(8,128)(2,1)S(1)}, u32[]{:S(2)}, u32[]{:S(2)}) %collective-permute-start.1) | collective-permute-done | bytes 262176 | tf_op jit(solution)/shard_map/ppermute | solution.py:92
  35.5 4.9 %project.1 = (bf16[8,192,128]{2,1,0:T(8,128)(2,1)}, bf16[8,192,128]{2,1,0:T(8,128)(2,1)}, bf16[8,192,512]{2,1,0:T(8,128)(2,1)}, bf16[512,256]{1,0:T(8,128)(2,1)}, f32[8,512]{1,0:T(8,128)}) custom-call(s32[2]{0:T(128)} %pad_add_fusion.info, bf16[256,512]{1,0:T(8,128)(2,1)} %get-tuple-element.63.refs_0_.refs_8_, bf16[256,512]{1,0:T(8,128)(2,1)} %copy-done.1, ...), custom_call_target="tpu_custom_call" | custom-call | flops 402653184 | bytes 5783560 | tf_op jit(solution)/shard_map/project/pallas_call | solution.py:51
  42.0 5.4 %collective-permute-start.14 = (bf16[10,16,512]{2,1,0:T(8,128)(2,1)S(1)}, bf16[10,16,512]{2,1,0:T(8,128)(2,1)S(1)}, u32[]{:S(2)}, u32[]{:S(2)}) collective-permute-start(bf16[10,16,512]{2,1,0:T(8,128)(2,1)S(1)} %maximum_maximum_fusion), channel_id=1, source_target_pairs={{0,2},{1,3},{2,0},{3,1},{4,6},{5,7},{6,4},{7,5},{8,10},{9,11},{10,... | collective-permute-start | bytes 491528 | tf_op jit(solution)/shard_map/ppermute | solution.py:92
  47.4 8.1 %collective-permute-done.14 = bf16[10,16,512]{2,1,0:T(8,128)(2,1)S(1)} collective-permute-done((bf16[10,16,512]{2,1,0:T(8,128)(2,1)S(1)}, bf16[10,16,512]{2,1,0:T(8,128)(2,1)S(1)}, u32[]{:S(2)}, u32[]{:S(2)}) %collective-permute-start.14) | collective-permute-done | bytes 163872 | tf_op jit(solution)/shard_map/ppermute | solution.py:92
  56.1 8.7 %collective-permute-done.15 = bf16[2,10,16,512]{3,2,1,0:T(8,128)(2,1)S(1)} collective-permute-done((bf16[2,10,16,512]{3,2,1,0:T(8,128)(2,1)S(1)}, bf16[2,10,16,512]{3,2,1,0:T(8,128)(2,1)S(1)}, u32[]{:S(2)}, u32[]{:S(2)}) %collective-permute-start.15) | collective-permute-done | bytes 327712 | tf_op jit(solution)/shard_map/ppermute | solution.py:92
  67.5 6.8 %attend.3 = (f32[8,1,192]{2,1,0:T(1,128)}, f32[8,1,192]{2,1,0:T(1,128)}, f32[8,128,192]{2,1,0:T(8,128)}) custom-call(s32[2]{0:T(128)} %pad_add_fusion.info, s32[32]{0:T(128)} %deal.11, s32[4]{0:T(128)} %lengths.11, s32[8]{0:T(128)} %call_exported.0.codes, bf16[8,192,128]{2,1,0:T(8,128)(2,1)} %get-tuple-element.68.q_ref, ...), custom_call_target="tpu_custom_call" | custom-call | flops 2113929216 | bytes 1585336 | tf_op jit(solution)/shard_map/attend/pallas_call | solution.py:51
  75.6 4.9 %collective-permute-done.16.refs_10_ = bf16[4,10,16,512]{3,2,1,0:T(8,128)(2,1)S(1)} collective-permute-done((bf16[4,10,16,512]{3,2,1,0:T(8,128)(2,1)S(1)}, bf16[4,10,16,512]{3,2,1,0:T(8,128)(2,1)S(1)}, u32[]{:S(2)}, u32[]{:S(2)}) %collective-permute-start.16) | collective-permute-done | bytes 655392 | tf_op jit(solution)/shard_map/ppermute | solution.py:100
  82.5 5.5 %attend.4 = (f32[8,1,192]{2,1,0:T(1,128)}, f32[8,1,192]{2,1,0:T(1,128)}, f32[8,128,192]{2,1,0:T(8,128)}) custom-call(s32[2]{0:T(128)} %pad_add_fusion.info, s32[32]{0:T(128)} %deal.11, s32[4]{0:T(128)} %lengths.11, s32[8]{0:T(128)} %call_exported.0.codes, bf16[8,192,128]{2,1,0:T(8,128)(2,1)} %get-tuple-element.68.q_ref, bf16[8,192,128]{2,1,0:T(8,128)(2,1)} %copy-done.36, ...), custom_call_target="tpu_custom_call" | custom-call | flops 4227858432 | bytes 2777272 | tf_op jit(solution)/shard_map/attend/pallas_call | solution.py:51
  88.0 6.7 %attend.5 = (f32[8,1,192]{2,1,0:T(1,128)}, f32[8,1,192]{2,1,0:T(1,128)}, f32[8,128,192]{2,1,0:T(8,128)}, bf16[8,192,128]{2,1,0:T(8,128)(2,1)}, f32[8,192,128]{2,1,0:T(8,128)}, /*index=5*/f32[8,1,192]{2,1,0:T(1,128)}) custom-call(s32[2]{0:T(128)} %pad_add_fusion.info, s32[32]{0:T(128)} %deal.11, s32[4]{0:T(128)} %lengths.11, s32[8]{0:T(128)} %call_exported.0.codes, ...), custom_call_target="tpu_custom_call" | custom-call | flops 2113929216 | bytes 3569848 | tf_op jit(solution)/shard_map/attend/pallas_call | solution.py:51
  100.1 4.5 %collective-permute-done.13.refs_8_.refs_3_ = bf16[192,128]{1,0:T(8,128)(2,1)S(1)} collective-permute-done((bf16[192,128]{1,0:T(8,128)(2,1)S(1)}, bf16[192,128]{1,0:T(8,128)(2,1)S(1)}, u32[]{:S(2)}, u32[]{:S(2)}) %collective-permute-start.13) | collective-permute-done | bytes 49184 | tf_op jit(solution)/shard_map/ppermute | solution.py:92
  104.6 5.0 %collective-permute-done.12.refs_7_.refs_2_ = bf16[192,128]{1,0:T(8,128)(2,1)S(1)} collective-permute-done((bf16[192,128]{1,0:T(8,128)(2,1)S(1)}, bf16[192,128]{1,0:T(8,128)(2,1)S(1)}, u32[]{:S(2)}, u32[]{:S(2)}) %collective-permute-start.12) | collective-permute-done | bytes 49184 | tf_op jit(solution)/shard_map/ppermute | solution.py:92
  110.4 3.3 %collective-permute-done.11.refs_6_.refs_1_ = bf16[192,128]{1,0:T(8,128)(2,1)S(1)} collective-permute-done((bf16[192,128]{1,0:T(8,128)(2,1)S(1)}, bf16[192,128]{1,0:T(8,128)(2,1)S(1)}, u32[]{:S(2)}, u32[]{:S(2)}) %collective-permute-start.11) | collective-permute-done | bytes 49184 | tf_op jit(solution)/shard_map/ppermute | solution.py:92
  114.3 9.0 %mlp.1 = (bf16[192,512]{1,0:T(8,128)(2,1)}, f32[8,128]{1,0:T(8,128)}, f32[192,512]{1,0:T(8,128)}, bf16[4,192,128]{2,1,0:T(8,128)(2,1)}, bf16[4,192,512]{2,1,0:T(...) custom-call(s32[2]{0:T(128)} %pad_add_fusion.info, ...), custom_call_target="tpu_custom_call" | custom-call | flops 1610612736 | bytes 8819468 | tf_op jit(solution)/shard_map/mlp/pallas_call | solution.py:51
  123.3 6.4 %mlp_grads.1 = bf16[2,4,4,10,16,512]{5,4,3,2,1,0:T(8,128)(2,1)} custom-call(s32[2]{0:T(128)} %pad_add_fusion.info, bf16[4,192,512]{2,1,0:T(8,128)(2,1)} %get-tuple-element.81.act_ref, bf16[4,192,512]{2,1,0:T(8,128)(2,1)} %get-tuple-element.82.gpre_ref, bf16[192,512]{1,0:T(8,128)(2,1)} %get-tuple-element.83.n2_ref, ...), custom_call_target="tpu_custom_call" | custom-call | flops 805306368 | bytes 7622664 | tf_op jit(solution)/shard_map/mlp_grads/pallas_call | solution.py:51
  129.7 3.6 %slice_bitcast_fusion = bf16[4,4,10,16,512]{4,3,2,1,0:T(8,128)(2,1)} fusion(bf16[2,4,4,10,16,512]{5,4,3,2,1,0:T(8,128)(2,1)} %mlp_grads.1), kind=kLoop, calls=%fused_computation | loop fusion | bytes 5242880 | tf_op jit(solution)/shard_map/squeeze | solution.py:943
  135.4 2.9 %collective-permute-start.35 = (bf16[192,128]{1,0:T(8,128)(2,1)S(1)}, bf16[192,128]{1,0:T(8,128)(2,1)S(1)}, u32[]{:S(2)}, u32[]{:S(2)}) collective-permute-start(bf16[192,128]{1,0:T(8,128)(2,1)S(1)} %get-tuple-element.131), channel_id=1, source_target_pairs={{0,1},{1,0},{2,3},{3,2},{4,5},{5,4},{6,7},{7,6},{8,9},{9,8},{10,11... | collective-permute-start | bytes 147464 | tf_op jit(solution)/shard_map/ppermute | solution.py:92
  144.2 7.1 %attend_back.3 = (bf16[8,192,128]{2,1,0:T(8,128)(2,1)}, bf16[8,192,128]{2,1,0:T(8,128)(2,1)}, f32[8,128,192]{2,1,0:T(8,128)}, bf16[8,192,128]{2,1,0:T(8,128)(2,1)}, f32[8,1,192]{2,1,0:T(1,128)}) custom-call(s32[2]{0:T(128)} %pad_add_fusion.info, s32[32]{0:T(128)} %deal.11, s32[4]{0:T(128)} %lengths.11, s32[8]{0:T(128)} %call_exported.0.codes, ...), custom_call_target="tpu_custom_call" | custom-call | flops 10569646080 | bytes 4337848 | tf_op jit(solution)/shard_map/attend_back/pallas_call | solution.py:51
  151.3 14.2 %collective-permute-start.39 = (bf16[8,192,128]{2,1,0:T(8,128)(2,1)}, bf16[8,192,128]{2,1,0:T(8,128)(2,1)S(1)}, u32[]{:S(2)}, u32[]{:S(2)}) collective-permute-start(bf16[8,192,128]{2,1,0:T(8,128)(2,1)} %get-tuple-element.101), channel_id=1, source_target_pairs={{0,16},{1,17},{2,18},{3,19},{4,12},{5,13},{6,14},{7,15},{8,24},{9,... | collective-permute-start | bytes 1179656 | tf_op jit(solution)/shard_map/ppermute | solution.py:100
  165.6 3.0 %fusion = bf16[2,4,10,16,512]{4,3,2,1,0:T(8,128)(2,1)} fusion(bf16[4,4,10,16,512]{4,3,2,1,0:T(8,128)(2,1)} %collective-permute-done.23, bf16[2,4,4,10,16,512]{5,4,3,2,1,0:T(8,128)(2,1)S(1)} %bitcast.122), kind=kLoop, calls=%fused_computation.2 | loop fusion | flops 2621440 | bytes 3932160 | tf_op jit(solution)/shard_map/convert_element_type | solution.py:944
  170.5 4.6 %attend_back.4 = (bf16[8,192,128]{2,1,0:T(8,128)(2,1)}, f32[8,128,192]{2,1,0:T(8,128)}) custom-call(s32[2]{0:T(128)} %pad_add_fusion.info, s32[32]{0:T(128)} %deal.11, s32[4]{0:T(128)} %lengths.11, s32[8]{0:T(128)} %call_exported.0.codes, bf16[8,192,128]{2,1,0:T(8,128)(2,1)} %get-tuple-element.68.q_ref, f32[8,1,192]{2,1,0:T(1,128)} %get-tuple-element.90.lse_ref, ...), custom_call_target="tpu_custom_call" | custom-call | flops 5284823040 | bytes 3158200 | tf_op jit(solution)/shard_map/attend_back/pallas_call | solution.py:51
  177.7 4.9 %collective-permute-start.41 = (bf16[8,192,128]{2,1,0:T(8,128)(2,1)}, bf16[8,192,128]{2,1,0:T(8,128)(2,1)}, u32[]{:S(2)}, u32[]{:S(2)}) collective-permute-start(bf16[8,192,128]{2,1,0:T(8,128)(2,1)} %add_convert_fusion.1), channel_id=1, source_target_pairs={{0,8},{1,9},{2,10},{3,11},{4,20},{5,21},{6,22},{7,23},{8,0},{9,1},... | collective-permute-start | bytes 1179656 | tf_op jit(solution)/shard_map/ppermute | solution.py:100
  182.6 8.7 %attend_back.5 = (bf16[8,192,128]{2,1,0:T(8,128)(2,1)}, f32[8,128,192]{2,1,0:T(8,128)}, bf16[8,192,128]{2,1,0:T(8,128)(2,1)}) custom-call(s32[2]{0:T(128)} %pad_add_fusion.info, s32[32]{0:T(128)} %deal.11, s32[4]{0:T(128)} %lengths.11, s32[8]{0:T(128)} %call_exported.0.codes, bf16[8,192,128]{2,1,0:T(8,128)(2,1)} %get-tuple-element.68.q_ref, ...), custom_call_target="tpu_custom_call" | custom-call | flops 5284823040 | bytes 3551416 | tf_op jit(solution)/shard_map/attend_back/pallas_call | solution.py:51
  192.1 5.7 %head_grads.1 = (bf16[4,192,512]{2,1,0:T(8,128)(2,1)}, bf16[4,192,512]{2,1,0:T(8,128)(2,1)}, bf16[128,256]{1,0:T(8,128)(2,1)}, bf16[128,256]{1,0:T(8,128)(2,1)},...) custom-call(s32[2]{0:T(128)} %pad_add_fusion.info, bf16[8,192,128]{2,1,0:T(8,128)(2,1)} %get-tuple-element.97.dq_ref, ...), custom_call_target="tpu_custom_call" | custom-call | flops 805306368 | bytes 7340040 | tf_op jit(solution)/shard_map/head_grads/pallas_call | solution.py:51
  208.6 11.0 %collective-permute-done.49 = bf16[4,128,256]{2,1,0:T(8,128)(2,1)S(1)} collective-permute-done((bf16[4,128,256]{2,1,0:T(8,128)(2,1)S(1)}, bf16[4,128,256]{2,1,0:T(8,128)(2,1)S(1)}, u32[]{:S(2)}, u32[]{:S(2)}) %collective-permute-start.49) | collective-permute-done | bytes 262176 | tf_op jit(solution)/shard_map/ppermute | solution.py:92
  223.2 2.9 %collective-permute-done.50 = bf16[4,128,256]{2,1,0:T(8,128)(2,1)S(1)} collective-permute-done((bf16[4,128,256]{2,1,0:T(8,128)(2,1)S(1)}, bf16[4,128,256]{2,1,0:T(8,128)(2,1)S(1)}, u32[]{:S(2)}, u32[]{:S(2)}) %collective-permute-start.50) | collective-permute-done | bytes 262176 | tf_op jit(solution)/shard_map/ppermute | solution.py:92
  227.0 3.2 %collective-permute-done.26 = bf16[2,10,16,512]{3,2,1,0:T(8,128)(2,1)S(1)} collective-permute-done((bf16[2,10,16,512]{3,2,1,0:T(8,128)(2,1)S(1)}, bf16[2,10,16,512]{3,2,1,0:T(8,128)(2,1)S(1)}, u32[]{:S(2)}, u32[]{:S(2)}) %collective-permute-start.26) | collective-permute-done | bytes 327712 | tf_op jit(solution)/shard_map/ppermute | solution.py:92
  230.7 7.2 %collective-permute-done.27 = bf16[10,16,512]{2,1,0:T(8,128)(2,1)S(1)} collective-permute-done((bf16[10,16,512]{2,1,0:T(8,128)(2,1)S(1)}, bf16[10,16,512]{2,1,0:T(8,128)(2,1)S(1)}, u32[]{:S(2)}, u32[]{:S(2)}) %collective-permute-start.27) | collective-permute-done | bytes 163872 | tf_op jit(solution)/shard_map/ppermute | solution.py:92
  249.6 7.3 %collective-permute-done.44.refs_2_ = bf16[192,512]{1,0:T(8,128)(2,1)S(1)} collective-permute-done((bf16[192,512]{1,0:T(8,128)(2,1)S(1)}, bf16[192,512]{1,0:T(8,128)(2,1)S(1)}, u32[]{:S(2)}, u32[]{:S(2)}) %collective-permute-start.44) | collective-permute-done | bytes 196640 | tf_op jit(solution)/shard_map/ppermute | solution.py:92
  263.4 3.0 %unpack.1 = (f32[128,2048]{1,0:T(8,128)}, f32[512,512]{1,0:T(8,128)}, f32[128,512]{1,0:T(8,128)}, f32[16,512]{1,0:T(8,128)}) custom-call(s32[2]{0:T(128)} %pad_add_fusion.info, bf16[10,16,512]{2,1,0:T(8,128)(2,1)} %copy-done.10, bf16[10,16,512]{2,1,0:T(8,128)(2,1)} %copy-done.17, bf16[10,16,512]{2,1,0:T(8,128)(2,1)} %copy-done.18, ...), custom_call_target="tpu_custom_call" | custom-call | bytes 3702792 | tf_op jit(solution)/shard_map/unpack/pallas_call | solution.py:51
  (211 shorter events, 73.4 us)
Async XLA Ops:
  5.1 14.4 %collective-permute-start = (bf16[256,512]{1,0:T(8,128)(2,1)}, bf16[256,512]{1,0:T(8,128)(2,1)S(1)}, u32[]{:S(2)}, u32[]{:S(2)}) collective-permute-start(bf16[256,512]{1,0:T(8,128)(2,1)} %get-tuple-element.64), channel_id=1, source_target_pairs={{0,1},{1,0},{2,3},{3,2},{4,5},{5,4},{6,7},{7,6},{8,9},{9,8},{10,11... | collective-permute-start | bytes 786440 | tf_op jit(solution)/shard_map/ppermute | solution.py:92
  8.1 21.6 %collective-permute-start.1 = (bf16[256,512]{1,0:T(8,128)(2,1)}, bf16[256,512]{1,0:T(8,128)(2,1)S(1)}, u32[]{:S(2)}, u32[]{:S(2)}) collective-permute-start(bf16[256,512]{1,0:T(8,128)(2,1)} %get-tuple-element.65), channel_id=1, source_target_pairs={{0,2},{1,3},{2,0},{3,1},{4,6},{5,7},{6,4},{7,5},{8,10},{9,11},{10,... | collective-permute-start | bytes 786440 | tf_op jit(solution)/shard_map/ppermute | solution.py:92
  10.7 19.0 %collective-permute-start.2 = (bf16[256,512]{1,0:T(8,128)(2,1)}, bf16[256,512]{1,0:T(8,128)(2,1)S(1)}, u32[]{:S(2)}, u32[]{:S(2)}) collective-permute-start(bf16[256,512]{1,0:T(8,128)(2,1)} %get-tuple-element.66), channel_id=1, source_target_pairs={{0,3},{1,2},{2,1},{3,0},{4,7},{5,6},{6,5},{7,4},{8,11},{9,10},{10,... | collective-permute-start | bytes 786440 | tf_op jit(solution)/shard_map/ppermute | solution.py:92
  10.7 23.1 %collective-permute-start.3 = (bf16[256,512]{1,0:T(8,128)(2,1)}, bf16[256,512]{1,0:T(8,128)(2,1)S(1)}, u32[]{:S(2)}, u32[]{:S(2)}) collective-permute-start(bf16[256,512]{1,0:T(8,128)(2,1)} %get-tuple-element.63.refs_0_.refs_8_), channel_id=1, source_target_pairs={{0,4},{1,5},{2,6},{3,7},{4,0},{5,1},{6,2},{7,3},{8,12},{9,13},{10,... | collective-permute-start | bytes 786440 | tf_op jit(solution)/shard_map/ppermute | solution.py:92
  19.5 14.4 %collective-permute-start.4 = (bf16[256,512]{1,0:T(8,128)(2,1)S(1)}, bf16[256,512]{1,0:T(8,128)(2,1)S(1)}, u32[]{:S(2)}, u32[]{:S(2)}) collective-permute-start(bf16[256,512]{1,0:T(8,128)(2,1)S(1)} %collective-permute-done.refs_1_.refs_9_), channel_id=1, source_target_pairs={{0,4},{1,5},{2,6},{3,7},{4,0},{5,1},{6,2},{7,3},{8,12},{9,13},{10,... | collective-permute-start | bytes 786440 | tf_op jit(solution)/shard_map/ppermute | solution.py:92
  40.3 15.1 %collective-permute-start.7 = (bf16[8,192,128]{2,1,0:T(8,128)(2,1)}, bf16[8,192,128]{2,1,0:T(8,128)(2,1)S(1)}, u32[]{:S(2)}, u32[]{:S(2)}) collective-permute-start(bf16[8,192,128]{2,1,0:T(8,128)(2,1)} %get-tuple-element.69.refs_0_), channel_id=1, source_target_pairs={{0,8},{1,9},{2,10},{3,11},{4,20},{5,21},{6,22},{7,23},{8,0},{9,1},... | collective-permute-start | bytes 1179656 | tf_op jit(solution)/shard_map/ppermute | solution.py:100
  42.0 13.5 %collective-permute-start.14 = (bf16[10,16,512]{2,1,0:T(8,128)(2,1)S(1)}, bf16[10,16,512]{2,1,0:T(8,128)(2,1)S(1)}, u32[]{:S(2)}, u32[]{:S(2)}) collective-permute-start(bf16[10,16,512]{2,1,0:T(8,128)(2,1)S(1)} %maximum_maximum_fusion), channel_id=1, source_target_pairs={{0,2},{1,3},{2,0},{3,1},{4,6},{5,7},{6,4},{7,5},{8,10},{9,11},{10,... | collective-permute-start | bytes 491528 | tf_op jit(solution)/shard_map/ppermute | solution.py:92
  55.5 9.4 %collective-permute-start.15 = (bf16[2,10,16,512]{3,2,1,0:T(8,128)(2,1)S(1)}, bf16[2,10,16,512]{3,2,1,0:T(8,128)(2,1)S(1)}, u32[]{:S(2)}, u32[]{:S(2)}) collective-permute-start(bf16[2,10,16,512]{3,2,1,0:T(8,128)(2,1)S(1)} %pad_maximum_fusion.1), channel_id=1, source_target_pairs={{0,1},{1,0},{2,3},{3,2},{4,5},{5,4},{6,7},{7,6},{8,9},{9,8},{10,11... | collective-permute-start | bytes 983048 | tf_op jit(solution)/shard_map/ppermute | solution.py:92
  55.6 9.4 %collective-permute-start.8 = (bf16[8,192,128]{2,1,0:T(8,128)(2,1)S(1)}, bf16[8,192,128]{2,1,0:T(8,128)(2,1)S(1)}, u32[]{:S(2)}, u32[]{:S(2)}) collective-permute-start(bf16[8,192,128]{2,1,0:T(8,128)(2,1)S(1)} %collective-permute-done.7.refs_0_), channel_id=1, source_target_pairs={{0,16},{1,17},{2,18},{3,19},{4,12},{5,13},{6,14},{7,15},{8,24},{9,... | collective-permute-start | bytes 1179656 | tf_op jit(solution)/shard_map/ppermute | solution.py:100
  65.0 15.6 %collective-permute-start.16 = (bf16[4,10,16,512]{3,2,1,0:T(8,128)(2,1)S(1)}, bf16[4,10,16,512]{3,2,1,0:T(8,128)(2,1)S(1)}, u32[]{:S(2)}, u32[]{:S(2)}) collective-permute-start(bf16[4,10,16,512]{3,2,1,0:T(8,128)(2,1)S(1)} %pad_maximum_fusion.refs_9_), channel_id=1, source_target_pairs={{0,8},{1,9},{2,10},{3,11},{4,20},{5,21},{6,22},{7,23},{8,0},{9,1},... | collective-permute-start | bytes 1966088 | tf_op jit(solution)/shard_map/ppermute | solution.py:100
  66.2 15.5 %collective-permute-start.9 = (bf16[8,192,128]{2,1,0:T(8,128)(2,1)S(1)}, bf16[8,192,128]{2,1,0:T(8,128)(2,1)S(1)}, u32[]{:S(2)}, u32[]{:S(2)}) collective-permute-start(bf16[8,192,128]{2,1,0:T(8,128)(2,1)S(1)} %copy-done.35), channel_id=1, source_target_pairs={{0,16},{1,17},{2,18},{3,19},{4,12},{5,13},{6,14},{7,15},{8,24},{9,... | collective-permute-start | bytes 1179656 | tf_op jit(solution)/shard_map/ppermute | solution.py:100
  74.3 22.0 %collective-permute-start.17 = (bf16[4,10,16,512]{3,2,1,0:T(8,128)(2,1)S(1)}, bf16[4,10,16,512]{3,2,1,0:T(8,128)(2,1)S(1)}, u32[]{:S(2)}, u32[]{:S(2)}) collective-permute-start(bf16[4,10,16,512]{3,2,1,0:T(8,128)(2,1)S(1)} %pad_maximum_fusion.refs_9_), channel_id=1, source_target_pairs={{0,16},{1,17},{2,18},{3,19},{4,12},{5,13},{6,14},{7,15},{8,24},{9,... | collective-permute-start | bytes 1966088 | tf_op jit(solution)/shard_map/ppermute | solution.py:100
  80.6 16.2 %collective-permute-start.18 = (bf16[4,10,16,512]{3,2,1,0:T(8,128)(2,1)S(1)}, bf16[4,10,16,512]{3,2,1,0:T(8,128)(2,1)S(1)}, u32[]{:S(2)}, u32[]{:S(2)}) collective-permute-start(bf16[4,10,16,512]{3,2,1,0:T(8,128)(2,1)S(1)} %collective-permute-done.16.refs_10_), channel_id=1, source_target_pairs={{0,16},{1,17},{2,18},{3,19},{4,12},{5,13},{6,14},{7,15},{8,24},{9,... | collective-permute-start | bytes 1966088 | tf_op jit(solution)/shard_map/ppermute | solution.py:100
  95.7 18.0 %collective-permute-start.19 = (bf16[4,10,16,512]{3,2,1,0:T(8,128)(2,1)S(1)}, bf16[4,10,16,512]{3,2,1,0:T(8,128)(2,1)}, u32[]{:S(2)}, u32[]{:S(2)}) collective-permute-start(bf16[4,10,16,512]{3,2,1,0:T(8,128)(2,1)S(1)} %pad_maximum_fusion.refs_9_), channel_id=1, source_target_pairs={{0,4},{1,5},{2,6},{3,7},{4,0},{5,1},{6,2},{7,3},{8,12},{9,13},{10,... | collective-permute-start | bytes 1966088 | tf_op jit(solution)/shard_map/ppermute | solution.py:92
  96.2 17.5 %collective-permute-start.20 = (bf16[4,10,16,512]{3,2,1,0:T(8,128)(2,1)S(1)}, bf16[4,10,16,512]{3,2,1,0:T(8,128)(2,1)}, u32[]{:S(2)}, u32[]{:S(2)}) collective-permute-start(bf16[4,10,16,512]{3,2,1,0:T(8,128)(2,1)S(1)} %collective-permute-done.16.refs_10_), channel_id=1, source_target_pairs={{0,4},{1,5},{2,6},{3,7},{4,0},{5,1},{6,2},{7,3},{8,12},{9,13},{10,... | collective-permute-start | bytes 1966088 | tf_op jit(solution)/shard_map/ppermute | solution.py:92
  96.3 17.4 %collective-permute-start.21 = (bf16[4,10,16,512]{3,2,1,0:T(8,128)(2,1)S(1)}, bf16[4,10,16,512]{3,2,1,0:T(8,128)(2,1)}, u32[]{:S(2)}, u32[]{:S(2)}) collective-permute-start(bf16[4,10,16,512]{3,2,1,0:T(8,128)(2,1)S(1)} %collective-permute-done.17.refs_11_), channel_id=1, source_target_pairs={{0,4},{1,5},{2,6},{3,7},{4,0},{5,1},{6,2},{7,3},{8,12},{9,13},{10,... | collective-permute-start | bytes 1966088 | tf_op jit(solution)/shard_map/ppermute | solution.py:92
  96.7 17.0 %collective-permute-start.22 = (bf16[4,10,16,512]{3,2,1,0:T(8,128)(2,1)S(1)}, bf16[4,10,16,512]{3,2,1,0:T(8,128)(2,1)}, u32[]{:S(2)}, u32[]{:S(2)}) collective-permute-start(bf16[4,10,16,512]{3,2,1,0:T(8,128)(2,1)S(1)} %collective-permute-done.18.refs_12_), channel_id=1, source_target_pairs={{0,4},{1,5},{2,6},{3,7},{4,0},{5,1},{6,2},{7,3},{8,12},{9,13},{10,... | collective-permute-start | bytes 1966088 | tf_op jit(solution)/shard_map/ppermute | solution.py:92
  133.3 32.3 %collective-permute-start.23 = (bf16[4,4,10,16,512]{4,3,2,1,0:T(8,128)(2,1)}, bf16[4,4,10,16,512]{4,3,2,1,0:T(8,128)(2,1)}, u32[]{:S(2)}, u32[]{:S(2)}) collective-permute-start(bf16[4,4,10,16,512]{4,3,2,1,0:T(8,128)(2,1)} %slice_bitcast_fusion), channel_id=1, source_target_pairs={{0,4},{1,5},{2,6},{3,7},{4,0},{5,1},{6,2},{7,3},{8,12},{9,13},{10,... | collective-permute-start | bytes 7864328 | tf_op jit(solution)/shard_map/ppermute | solution.py:92
  151.3 40.1 %collective-permute-start.39 = (bf16[8,192,128]{2,1,0:T(8,128)(2,1)}, bf16[8,192,128]{2,1,0:T(8,128)(2,1)S(1)}, u32[]{:S(2)}, u32[]{:S(2)}) collective-permute-start(bf16[8,192,128]{2,1,0:T(8,128)(2,1)} %get-tuple-element.101), channel_id=1, source_target_pairs={{0,16},{1,17},{2,18},{3,19},{4,12},{5,13},{6,14},{7,15},{8,24},{9,... | collective-permute-start | bytes 1179656 | tf_op jit(solution)/shard_map/ppermute | solution.py:100
  165.5 10.3 %collective-permute-start.40 = (bf16[8,192,128]{2,1,0:T(8,128)(2,1)}, bf16[8,192,128]{2,1,0:T(8,128)(2,1)}, u32[]{:S(2)}, u32[]{:S(2)}) collective-permute-start(bf16[8,192,128]{2,1,0:T(8,128)(2,1)} %get-tuple-element.103), channel_id=1, source_target_pairs={{0,16},{1,17},{2,18},{3,19},{4,12},{5,13},{6,14},{7,15},{8,24},{9,... | collective-permute-start | bytes 1179656 | tf_op jit(solution)/shard_map/ppermute | solution.py:100
  168.5 33.8 %collective-permute-start.24 = (bf16[2,4,10,16,512]{4,3,2,1,0:T(8,128)(2,1)}, bf16[2,4,10,16,512]{4,3,2,1,0:T(8,128)(2,1)}, u32[]{:S(2)}, u32[]{:S(2)}) collective-permute-start(bf16[2,4,10,16,512]{4,3,2,1,0:T(8,128)(2,1)} %fusion), channel_id=1, source_target_pairs={{0,16},{1,17},{2,18},{3,19},{4,12},{5,13},{6,14},{7,15},{8,24},{9,... | collective-permute-start | bytes 3932168 | tf_op jit(solution)/shard_map/ppermute | solution.py:100
  177.7 13.7 %collective-permute-start.41 = (bf16[8,192,128]{2,1,0:T(8,128)(2,1)}, bf16[8,192,128]{2,1,0:T(8,128)(2,1)}, u32[]{:S(2)}, u32[]{:S(2)}) collective-permute-start(bf16[8,192,128]{2,1,0:T(8,128)(2,1)} %add_convert_fusion.1), channel_id=1, source_target_pairs={{0,8},{1,9},{2,10},{3,11},{4,20},{5,21},{6,22},{7,23},{8,0},{9,1},... | collective-permute-start | bytes 1179656 | tf_op jit(solution)/shard_map/ppermute | solution.py:100
  204.0 17.3 %collective-permute-start.25 = (bf16[4,10,16,512]{3,2,1,0:T(8,128)(2,1)S(1)}, bf16[4,10,16,512]{3,2,1,0:T(8,128)(2,1)S(1)}, u32[]{:S(2)}, u32[]{:S(2)}) collective-permute-start(bf16[4,10,16,512]{3,2,1,0:T(8,128)(2,1)S(1)} %fusion.1), channel_id=1, source_target_pairs={{0,8},{1,9},{2,10},{3,11},{4,20},{5,21},{6,22},{7,23},{8,0},{9,1},... | collective-permute-start | bytes 1966088 | tf_op jit(solution)/shard_map/ppermute | solution.py:100
  206.4 13.3 %collective-permute-start.49 = (bf16[4,128,256]{2,1,0:T(8,128)(2,1)S(1)}, bf16[4,128,256]{2,1,0:T(8,128)(2,1)S(1)}, u32[]{:S(2)}, u32[]{:S(2)}) collective-permute-start(bf16[4,128,256]{2,1,0:T(8,128)(2,1)S(1)} %pad_maximum_fusion.2), channel_id=1, source_target_pairs={{0,8},{1,9},{2,10},{3,11},{4,12},{5,13},{6,14},{7,15},{8,0},{9,1},... | collective-permute-start | bytes 786440 | tf_op jit(solution)/shard_map/ppermute | solution.py:92
  208.6 21.9 %collective-permute-start.42 = (bf16[4,192,512]{2,1,0:T(8,128)(2,1)S(1)}, bf16[4,192,512]{2,1,0:T(8,128)(2,1)S(1)}, u32[]{:S(2)}, u32[]{:S(2)}) collective-permute-start(bf16[4,192,512]{2,1,0:T(8,128)(2,1)S(1)} %copy-done.31), channel_id=1, source_target_pairs={{0,4},{1,5},{2,6},{3,7},{4,0},{5,1},{6,2},{7,3},{8,12},{9,13},{10,... | collective-permute-start | bytes 2359304 | tf_op jit(solution)/shard_map/ppermute | solution.py:92
  226.2 18.1 %collective-permute-start.51 = (bf16[4,1,128,256]{3,2,1,0:T(8,128)(2,1)S(1)}, bf16[4,1,128,256]{3,2,1,0:T(8,128)(2,1)S(1)}, u32[]{:S(2)}, u32[]{:S(2)}) collective-permute-start(bf16[4,1,128,256]{3,2,1,0:T(8,128)(2,1)S(1)} %bitcast.123), channel_id=1, source_target_pairs={{0,4},{1,5},{2,6},{3,7},{4,0},{5,1},{6,2},{7,3},{8,12},{9,13},{10,... | collective-permute-start | bytes 786440 | tf_op jit(solution)/shard_map/ppermute | solution.py:92
  240.0 9.6 %collective-permute-start.45 = (bf16[192,512]{1,0:T(8,128)(2,1)S(1)}, bf16[192,512]{1,0:T(8,128)(2,1)S(1)}, u32[]{:S(2)}, u32[]{:S(2)}) collective-permute-start(bf16[192,512]{1,0:T(8,128)(2,1)S(1)} %get-tuple-element.115), channel_id=1, source_target_pairs={{0,3},{1,2},{2,1},{3,0},{4,7},{5,6},{6,5},{7,4},{8,11},{9,10},{10,... | collective-permute-start | bytes 589832 | tf_op jit(solution)/shard_map/ppermute | solution.py:92
  241.9 15.0 %collective-permute-start.44 = (bf16[192,512]{1,0:T(8,128)(2,1)S(1)}, bf16[192,512]{1,0:T(8,128)(2,1)S(1)}, u32[]{:S(2)}, u32[]{:S(2)}) collective-permute-start(bf16[192,512]{1,0:T(8,128)(2,1)S(1)} %get-tuple-element.116), channel_id=1, source_target_pairs={{0,2},{1,3},{2,0},{3,1},{4,6},{5,7},{6,4},{7,5},{8,10},{9,11},{10,... | collective-permute-start | bytes 589832 | tf_op jit(solution)/shard_map/ppermute | solution.py:92
  241.9 16.9 %collective-permute-start.43 = (bf16[192,512]{1,0:T(8,128)(2,1)S(1)}, bf16[192,512]{1,0:T(8,128)(2,1)S(1)}, u32[]{:S(2)}, u32[]{:S(2)}) collective-permute-start(bf16[192,512]{1,0:T(8,128)(2,1)S(1)} %get-tuple-element.117), channel_id=1, source_target_pairs={{0,1},{1,0},{2,3},{3,2},{4,5},{5,4},{6,7},{7,6},{8,9},{9,8},{10,11... | collective-permute-start | bytes 589832 | tf_op jit(solution)/shard_map/ppermute | solution.py:92
  244.4 12.5 %collective-permute-start.29 = (bf16[10,16,512]{2,1,0:T(8,128)(2,1)S(1)}, bf16[10,16,512]{2,1,0:T(8,128)(2,1)S(1)}, u32[]{:S(2)}, u32[]{:S(2)}) collective-permute-start(bf16[10,16,512]{2,1,0:T(8,128)(2,1)S(1)} %fusion.4.refs_0_), channel_id=1, source_target_pairs={{0,16},{1,17},{2,18},{3,19},{4,12},{5,13},{6,14},{7,15},{8,24},{9,... | collective-permute-start | bytes 491528 | tf_op jit(solution)/shard_map/ppermute | solution.py:100
  245.7 11.7 %collective-permute-start.30 = (bf16[10,16,512]{2,1,0:T(8,128)(2,1)S(1)}, bf16[10,16,512]{2,1,0:T(8,128)(2,1)S(1)}, u32[]{:S(2)}, u32[]{:S(2)}) collective-permute-start(bf16[10,16,512]{2,1,0:T(8,128)(2,1)S(1)} %collective-permute-done.28.refs_1_), channel_id=1, source_target_pairs={{0,16},{1,17},{2,18},{3,19},{4,12},{5,13},{6,14},{7,15},{8,24},{9,... | collective-permute-start | bytes 491528 | tf_op jit(solution)/shard_map/ppermute | solution.py:100
  249.6 12.3 %collective-permute-start.31 = (bf16[10,16,512]{2,1,0:T(8,128)(2,1)S(1)}, bf16[10,16,512]{2,1,0:T(8,128)(2,1)S(1)}, u32[]{:S(2)}, u32[]{:S(2)}) collective-permute-start(bf16[10,16,512]{2,1,0:T(8,128)(2,1)S(1)} %fusion.4.refs_0_), channel_id=1, source_target_pairs={{0,4},{1,5},{2,6},{3,7},{4,0},{5,1},{6,2},{7,3},{8,12},{9,13},{10,... | collective-permute-start | bytes 491528 | tf_op jit(solution)/shard_map/ppermute | solution.py:92
  (62 other events, 469.0 us)

commit v3 on v2

--- a/solution.py
+++ b/solution.py
@@ -60,6 +60,10 @@
     )(*ins)
 
 
+def after(value, *earlier):
+    return lax.optimization_barrier((value, *earlier))[0]
+
+
 def sds(shape, dtype):
     return jax.ShapeDtypeStruct(shape, dtype)
 
@@ -114,7 +118,9 @@
 
     def body(info, words_ref, w_ref, vec_ref, *outs):
         odd = (info[0] % 2) == 1
-        vec = vec_ref[...].astype(F32)
+        rows = lax.broadcasted_iota(jnp.int32, (4, 4 * HEAD), 0)
+        pick = jnp.where(lane_iota((4, 4 * HEAD)) == rows + 3 * HEAD, 1.0, 0.0).astype(BF16)
+        vec = mm(vec_ref[...], pick, TN)
         lane = lane_iota((shard, 4 * HEAD))
         for m in range(nw):
             pair = plan.head(info[0], info[1] ^ m) // 2
@@ -208,7 +214,7 @@
             olds, refs = refs[:3], refs[3:]
         (m_ref, l_ref, acc_ref), refs = refs[:3], refs[3:]
         if last:
-            (o_ref, of_ref, lse_ref), refs = refs[:3], refs[3:]
+            (o_ref, o_sib_ref, of_ref, lse_ref), refs = refs[:4], refs[4:]
         kvs, slot_of, pairs, sem = refs
         copies = [
             pltpu.make_async_copy(ref, kvs.at[pl.ds(b * ns, ns)], sem.at[b])
@@ -272,7 +278,15 @@
                 )
                 wide = placed.T
                 of_ref[i] = wide
-                o_ref[i] = wide.astype(BF16)
+
+                @pl.when(i < ns // 2)
+                def _():
+                    o_ref[i] = wide.astype(BF16)
+
+                @pl.when(i >= ns // 2)
+                def _():
+                    o_sib_ref[i - ns // 2] = wide.astype(BF16)
+
                 return 0
 
             lax.fori_loop(0, ns, finish, 0)
@@ -285,7 +299,8 @@
     outs = [sds((ns, 1, blk), F32), sds((ns, 1, blk), F32), sds((ns, 2 * HEAD, blk), F32)]
     if last:
         outs += [
-            sds((ns, blk, 2 * HEAD), BF16),
+            sds((ns // 2, blk, 2 * HEAD), BF16),
+            sds((ns // 2, blk, 2 * HEAD), BF16),
             sds((ns, blk, 2 * HEAD), F32),
             sds((ns, 1, blk), F32),
         ]
@@ -434,18 +449,22 @@
         x_ref, teacher_ref, valid_ref, vec_ref, count_ref = refs[:5]
         att = refs[5 : 5 + nj]
         rest = refs[5 + nj :]
-        nwt_in = nc if packed else 3
+        nwt_in = 6 if packed else 3
         w_in, rest = rest[:nwt_in], rest[nwt_in:]
-        (lo_ref, sq_ref, g1_ref, gatt_ref, act_ref, gpre_ref, n2_ref, gb_ref, ga_ref, gv_ref) = (
-            rest[:10]
-        )
+        lo_ref, sq_ref, g1_ref = rest[:3]
+        gatt_refs, rest = rest[3 : 3 + nj], rest[3 + nj :]
+        act_ref, gpre_ref, n2_ref, gb_ref, ga_ref, gv_ref = rest[:6]
+        rest = rest[6:]
         if packed:
-            wup, wdown, wout, meta, slope_ref, acc_ref, sem = rest[10:]
+            wup, wdown, wout, meta, slope_ref, acc_ref, sem = rest
             copies = []
             here = info[0] % 2
             owners = [info[0] ^ m for m in plan.near(here)]
             owners += [info[0] ^ 1 ^ m for m in plan.near(1 - here)]
-            for c, src in zip(owners, w_in):
+            sources = []
+            for head, pair, tail in (w_in[:3], w_in[3:]):
+                sources += [head, pair.at[0], pair.at[1], tail]
+            for c, src in zip(owners, sources):
                 for m in range(nw):
                     w = info[1] ^ Z_ORDER[m]
                     copies += [
@@ -472,7 +491,7 @@
             w_out = lambda row: wout_flat[pl.ds(row, pair_rows), :]
             count = jnp.sum(meta[:, :, 0:1, 0:1].astype(F32))
         else:
-            slope_ref, acc_ref = rest[10:]
+            slope_ref, acc_ref = rest
             w_up = lambda q: w_in[0][q]
             w_down = lambda q: w_in[1][q]
             w_out = lambda row: w_in[2][pl.ds(row, 2 * HEAD), :]
@@ -533,7 +552,7 @@
         ga = g1.astype(BF16)
         ga_ref[...] = ga
         for j in range(nj):
-            gatt_ref[j] = mm(ga, w_out(rows[j]), NT).astype(BF16)
+            gatt_refs[j][...] = mm(ga, w_out(rows[j]), NT).astype(BF16)
 
     return body
 
@@ -544,21 +563,36 @@
 
     def body(info, act_ref, gpre_ref, n2_ref, gb_ref, ga_ref, gv_ref, sq_ref, *refs):
         att, outs = refs[:nj], refs[nj:]
+        if packed:
+            outs, (ups, downs, attn, metas, sem) = outs[:2], outs[2:]
         n2, gb, ga = n2_ref[...], gb_ref[...], ga_ref[...]
         ctx, wt = info[0], info[1]
         rows_up = width // (nw * nc)
+
+        def put(c, w, tile, value):
+            plane = (c ^ ctx) // 2
+            middle = (plane == 1) | (plane == 2)
+            place = jnp.where(middle, 3 - plane, plane) if c % 2 else plane
+            zed = w ^ wt
+            zed = jnp.where((zed == 1) | (zed == 2), 3 - zed, zed)
+            for k in (0, 1):
+
+                @pl.when(ctx % 2 == k)
+                def _():
+                    target = outs[(c % 2) ^ k].at[place, zed, pl.ds(tile, value.shape[0])]
+                    pltpu.make_async_copy(value, target, sem.at[0]).start()
+
         for q in range(nq):
             up = mm(n2, gpre_ref[q], TN).astype(BF16)
             down = mm(act_ref[q], gb, TN).astype(BF16)
             if packed:
-                up_t = up.reshape(nw, nc, rows_up, CHUNK)
-                down_t = down.reshape(nc, 4, TILE, width)
+                ups[q] = up.reshape(nw * nc, rows_up, CHUNK)
+                downs[q] = down.reshape(nc * 4, TILE, width)
                 for w in range(nw):
                     for c in range(nc):
-                        put_tile(outs, info, c, w, q, up_t[w, c])
+                        put(c, w, q, ups.at[q, pl.ds(w * nc + c, 1)])
                 for c in range(nc):
-                    for t in range(4):
-                        put_tile(outs, info, c, q, nq + t, down_t[c, t])
+                    put(c, q, nq, downs.at[q, pl.ds(4 * c, 4)])
             else:
                 outs[0][q] = up
                 outs[1][q] = down
@@ -566,13 +600,9 @@
             head = plan.head(ctx ^ mc, wt ^ mw)
             part = mm(att[j][...], ga, TN).astype(BF16)
             if packed:
-                per = width // nw
-                part_t = part.reshape(2 * HEAD // TILE, TILE, width)
-                base = (head // 2) * (2 * HEAD // TILE)
+                attn[j] = part.reshape(2 * HEAD // TILE, TILE, width)
                 for t in range(2 * HEAD // TILE):
-                    at = base + t
-                    w, c = at // nc, at % nc
-                    put_tile(outs, info, c, w, nq + 4, part_t[t])
+                    put(t, head // 2, nq + 4, attn.at[j, pl.ds(t, 1)])
             else:
                 row = pl.multiple_of((head // 2) * (2 * HEAD), 2 * HEAD)
                 outs[2][pl.ds(row, 2 * HEAD), :] = part
@@ -590,21 +620,13 @@
                 vec = gv_ref[0:2, per * w : per * (w + 1)]
                 vec = jnp.concatenate([vec, jnp.zeros((2, CHUNK - per), F32)], axis=1)
                 tile = jnp.concatenate([line, vec, jnp.zeros((TILE - 3, CHUNK), F32)], axis=0)
-                tile = tile.astype(BF16)
+                metas[w, 0] = tile.astype(BF16)
                 for c in range(nc):
-                    put_tile(outs, info, c, w, nq + 5, tile)
+                    put(c, w, nq + 5, metas.at[w])
+            for ref in outs:
+                pltpu.make_async_copy(ref, ref, sem.at[0]).wait()
 
     return body
-
-
-def put_tile(outs, info, c, w, tile, value):
-    plane = (c ^ info[0]) // 2
-    core = c % 2
-    middle = (plane == 1) | (plane == 2)
-    place = jnp.where(middle & (core == 1), 3 - plane, plane)
-    zed = w ^ info[1]
-    zed = jnp.where((zed == 1) | (zed == 2), 3 - zed, zed)
-    outs[0][core ^ (info[0] % 2), place, zed, tile] = value
 
 
 def head_grads_body(plan, blk, width, shard, nb):
@@ -614,8 +636,8 @@
         xs = refs[:ns]
         parts = refs[ns : ns + nb]
         outs = refs[ns + nb :]
-        own_ref, sib_ref, dw_refs = outs[0], outs[1], outs[2 : 2 + nw]
-        acc = outs[2 + nw]
+        own_ref, sib_ref, dw_ref, acc = outs
+        half = shard // 2
         weight = wh_ref[...]
         gsum = jnp.zeros((1, width), F32)
         ssum = jnp.zeros((1, width), F32)
@@ -646,7 +668,23 @@
         acc[...] += mm(vecs, pick, TN)
         for m in range(nw):
             row = pl.multiple_of((info[1] ^ m) * shard, shard)
-            dw_refs[m][...] = acc[pl.ds(row, shard), :].astype(BF16)
+            block = acc[pl.ds(row, shard), :].astype(BF16)
+            dw_ref[m, :, : 4 * HEAD] = block[:half]
+            dw_ref[m, :, 4 * HEAD :] = block[half:]
+
+    return body
+
+
+def merge_body(nj, nw, blk):
+    def body(own_ref, sib_ref, dw_ref, more_ref, *outs):
+        for m in range(nw):
+            dw = (dw_ref[m].astype(F32) + more_ref[m].astype(F32)).astype(BF16)
+            if m < nj:
+                rows = own_ref[m].astype(F32) + sib_ref[m].astype(F32)
+                outs[m][:blk, :] = rows.astype(BF16)
+                outs[m][blk:, :] = dw
+            else:
+                outs[m][...] = dw
 
     return body
 
@@ -654,9 +692,9 @@
 def words_body(nj):
     def body(x_ref, vec_ref, g1_ref, *refs):
         parts, sibs, out_ref = refs[:nj], refs[nj : 2 * nj], refs[-1]
-        up = parts[0][...].astype(F32)
+        up = parts[0][: x_ref.shape[0], :].astype(F32)
         for p in parts[1:]:
-            up = up + p[...].astype(F32)
+            up = up + p[: up.shape[0], :].astype(F32)
         unit, inverse = norm_stats(x_ref[...].astype(F32))
         out_ref[...] = g1_ref[...] + norm_back(up, unit, inverse, vec_ref[0:1, :])
 
@@ -666,9 +704,9 @@
 def unpack_body(plan, width, ff):
     nq, nw, nc = ff // CHUNK, plan.n_wt, plan.n_ctx
 
-    def body(info, *refs):
-        srcs, outs = refs[:nc], refs[nc:]
-        up_ref, down_ref, out_ref, meta_ref = outs
+    def body(info, sq_ref, own, sib, *outs):
+        srcs = [r.at[n] for r in (own, sib) for n in range(nc // 2)]
+        up_ref, down_ref, out_ref, loss_ref, gain_ref, shift_ref = outs
         here = info[0] % 2
         owners = [info[0] ^ m for m in plan.near(here)]
         owners += [info[0] ^ 1 ^ m for m in plan.near(1 - here)]
@@ -682,38 +720,44 @@
                 ].astype(F32)
             out_ref[pl.ds(row, TILE), :] = src[nq + 4].astype(F32)
         meta = srcs[0][nq + 5].astype(F32)
-        meta_ref[...] = meta
+        count = jnp.max(sq_ref[1:2, :], axis=1, keepdims=True)
+        loss_ref[...] = jnp.sum(meta[0:1], axis=1, keepdims=True) / (count * width)
+        gain_ref[...] = meta[1:2, : width // nw]
+        shift_ref[...] = meta[2:3, : width // nw]
 
     return body
 
 
 def head_out_body(plan, shard):
-    def body(info, *refs):
-        srcs, (out_ref, vec_ref) = refs[:H], refs[H:]
+    nj, half = len(plan.peers), shard // 2
+
+    def body(info, own_ref, sib_ref, out_ref, gain_ref, shift_ref):
         core = info[0] % 2
-        total = srcs[0][...].astype(F32)
-        for s in srcs[1:]:
-            total = total + s[...].astype(F32)
         rows = lax.broadcasted_iota(jnp.int32, (8, 4 * HEAD), 0)
         pick = jnp.where(lane_iota((8, 4 * HEAD)) == rows + 3 * HEAD, 1.0, 0.0)
-        vec_ref[...] = lax.dot_general(
-            pick, total, NT, precision=lax.Precision.HIGHEST, preferred_element_type=F32
-        )
-        nj = len(plan.peers)
-        for j, (mc, mw) in enumerate(plan.peers):
-            head = plan.head(info[0] ^ mc, info[1] ^ mw)
-            own = srcs[j][...].astype(F32)
-            sib = srcs[nj + j][...].astype(F32)
-            even = jnp.where(core == 0, own, sib)
-            odd = jnp.where(core == 0, sib, own)
-            turned = pltpu.roll(odd, 3 * HEAD, 1)
-            lane = lane_iota((shard, 2 * HEAD))
-            mid = jnp.where(lane < HEAD, even[:, 2 * HEAD :], turned[:, 2 * HEAD :])
-            last = turned[:, : 2 * HEAD]
-            col = pl.multiple_of((head // 2) * (6 * HEAD), 2 * HEAD)
-            out_ref[:, pl.ds(col, 2 * HEAD)] = even[:, : 2 * HEAD]
-            out_ref[:, pl.ds(col + 2 * HEAD, 2 * HEAD)] = mid
-            out_ref[:, pl.ds(col + 4 * HEAD, 2 * HEAD)] = last
+        lane = lane_iota((half, 2 * HEAD))
+        for side in (0, 1):
+            at = slice(side * 4 * HEAD, (side + 1) * 4 * HEAD)
+            here = slice(side * half, (side + 1) * half)
+            total = jnp.zeros((half, 4 * HEAD), F32)
+            for j, (mc, mw) in enumerate(plan.peers):
+                head = plan.head(info[0] ^ mc, info[1] ^ mw)
+                own = own_ref[j, :, at].astype(F32)
+                sib = sib_ref[j, :, at].astype(F32)
+                total = total + own + sib
+                even = jnp.where(core == 0, own, sib)
+                odd = jnp.where(core == 0, sib, own)
+                turned = pltpu.roll(odd, 3 * HEAD, 1)
+                mid = jnp.where(lane < HEAD, even[:, 2 * HEAD :], turned[:, 2 * HEAD :])
+                col = pl.multiple_of((head // 2) * (6 * HEAD), 2 * HEAD)
+                out_ref[here, pl.ds(col, 2 * HEAD)] = even[:, : 2 * HEAD]
+                out_ref[here, pl.ds(col + 2 * HEAD, 2 * HEAD)] = mid
+                out_ref[here, pl.ds(col + 4 * HEAD, 2 * HEAD)] = turned[:, : 2 * HEAD]
+            both = lax.dot_general(
+                pick, total, NT, precision=lax.Precision.HIGHEST, preferred_element_type=F32
+            )
+            gain_ref[:, here] = both[0:1]
+            shift_ref[:, here] = both[1:2]
 
     return body
 
@@ -742,17 +786,17 @@
     nq = ff // CHUNK
     nseq = lengths.shape[0]
     ns, nb, nj = len(plan.slots), len(plan.groups), len(plan.peers)
-    packed = plan.square and width == CHUNK and width % (n_wt * n_ctx * TILE) == 0 and n_wt * CHUNK == ff
+    packed = plan.square and width == CHUNK and width % (n_wt * n_ctx * TILE) == 0
+    packed = packed and n_wt * CHUNK == ff and 2 * HEAD // TILE == n_ctx
     info = jnp.stack([ctx, wt]).astype(jnp.int32)
     codes = jnp.array([mc * n_wt + mw for mc, mw in plan.slots], jnp.int32)
     core = (1, 0)
 
-    vec_cols = jnp.stack([gain_attn, shift_attn, gain_mlp, shift_mlp], axis=1)
-    vec_cols = jnp.pad(vec_cols, ((0, 0), (3 * HEAD, HEAD - 4)))
+    vecs_here = jnp.stack([gain_attn, shift_attn, gain_mlp, shift_mlp])
     load = call(
         pack_body(plan, shard, blk),
         "pack",
-        [info, words, w_qkv, vec_cols],
+        [info, words, w_qkv, vecs_here],
         [SMEM] + [VMEM] * 3,
         [sds((blk + shard // 2, width), BF16)] * n_wt,
     )
@@ -791,14 +835,7 @@
             ],
             axis=0,
         )
-        piece, _ = lax.optimization_barrier((piece, q))
-        two = jnp.stack([piece, plan.swap(piece, (0, 2))])
-        two, _ = lax.optimization_barrier((two, kvs[1]))
-        stack = jnp.concatenate([two, plan.swap(two, (0, 1))])
-        stack, _ = lax.optimization_barrier((stack, kvs[3]))
-        stacks = plan.gather_square(stack)
-        stacks = stacks + [plan.swap(s, core) for s in stacks]
-        weights = stacks
+        piece = after(piece, kvs[1])
         count = jnp.zeros((1,), F32)
     else:
         up_full = lax.all_gather(w_up, "wt", axis=0, tiled=True)
@@ -813,12 +850,33 @@
 
     scalars = [info, deal, lengths, codes]
     state = []
-    cuts = [(0, 1), (1, 3), (3, 4)] if plan.square else [(0, nb)]
-    for lo, hi in cuts:
-        state = attend_part(plan, blk, nseq, lo, hi, hi == nb, scalars, q, kvs, state)
-    o, of32, lse = state[3:]
-    mixed = o[:nj] + plan.swap(o[nj:], core)
+    if not plan.square:
+        state = attend_part(plan, blk, nseq, 0, nb, True, scalars, q, kvs, state)
+    else:
+        state = attend_part(plan, blk, nseq, 0, 1, False, scalars, q, kvs, state)
+        if packed:
+            two = jnp.stack([piece, plan.swap(piece, (0, 2))])
+            two = after(two, state[0])
+            other = plan.swap(two, (0, 1))
+        state = [after(state[0], kvs[3]), *state[1:]]
+        state = attend_part(plan, blk, nseq, 1, 3, False, scalars, q, kvs, state)
+        if packed:
+            stack = jnp.concatenate([two, other])
+            stack = after(stack, state[0])
+            one, side = plan.turn(stack, True), plan.turn(stack, False)
+            stack_sib = plan.swap(stack, core)
+        state = attend_part(plan, blk, nseq, 3, 4, True, scalars, q, kvs, state)
+    o, o_sib, of32, lse = state[3:]
+    o_sib = plan.swap(o_sib, core)
+    if packed:
+        one = after(one, o_sib)
+        last = plan.turn(one, False)
+        pair = jnp.stack([one, side])
+        weights = [stack, pair, last, stack_sib, plan.swap(pair, core)]
+    mixed = o + o_sib
     att = [mixed[0]] + [plan.swap(mixed[j], plan.peers[j]) for j in range(1, nj)]
+    if packed:
+        weights += [plan.swap(after(last, *att[1:]), core)]
 
     mlp_in = [info, words, teacher, valid[:, None], vecs, count] + att + weights
     specs = [SMEM] + [VMEM] * 4 + [SMEM] + [VMEM] * nj
@@ -833,7 +891,7 @@
             *scratch,
             pltpu.SemaphoreType.DMA((4,)),
         ]
-    layer_out, square, grad_one, gatt, act, gpre, n2, gb, ga, gvec = call(
+    layer_out, square, grad_one, *rest = call(
         mlp_body(plan, width, ff, blk, packed),
         "mlp",
         mlp_in,
@@ -842,7 +900,7 @@
             sds((blk, width), BF16),
             sds((8, 128), F32),
             sds((blk, width), F32),
-            sds((nj, blk, 2 * HEAD), BF16),
+            *[sds((blk, 2 * HEAD), BF16)] * nj,
             sds((nq, blk, CHUNK), BF16),
             sds((nq, blk, CHUNK), BF16),
             sds((blk, width), BF16),
@@ -854,29 +912,45 @@
         flops=8 * blk * width * ff,
         trans=2 * blk * ff,
     )
+    gatt, (act, gpre, n2, gb, ga, gvec) = rest[:nj], rest[nj:]
     g_own = [gatt[0]] + [plan.swap(gatt[j], plan.peers[j]) for j in range(1, nj)]
     g_sib = plan.swap(jnp.stack(g_own), core)
 
     grads_in = [info, act, gpre, n2, gb, ga, gvec, square] + att
     if packed:
-        grads_out = [sds((2, n_ctx // 2, n_wt, nq + 6, TILE, CHUNK), BF16)]
+        grads_out = [sds((n_ctx // 2, n_wt, nq + 6, TILE, CHUNK), BF16)] * 2
+        grads_scratch = [
+            pltpu.VMEM((nq, n_wt * n_ctx, TILE, CHUNK), BF16),
+            pltpu.VMEM((nq, n_ctx * 4, TILE, CHUNK), BF16),
+            pltpu.VMEM((nj, n_ctx, TILE, CHUNK), BF16),
+            pltpu.VMEM((n_wt, 1, TILE, CHUNK), BF16),
+            pltpu.SemaphoreType.DMA((1,)),
+        ]
     else:
         grads_out = [
             sds((nq, width, CHUNK), BF16),
             sds((nq, CHUNK, width), BF16),
             sds((width, width), BF16),
         ]
+        grads_scratch = []
     weight_grads = call(
         mlp_grads_body(plan, width, ff, blk, packed),
         "mlp_grads",
         grads_in,
         [SMEM] + [VMEM] * (7 + nj),
         grads_out,
+        scratch=grads_scratch,
+        out_specs=[ANY if packed else VMEM] * len(grads_out),
         flops=4 * blk * width * ff,
     )
 
     extra = [of32] + g_own + [g_sib]
     if plan.square:
+        if packed:
+            g_all, g_core = weight_grads[0], plan.swap(weight_grads[1], core)
+            g_far = (g_all[2:].astype(F32) + g_core[2:].astype(F32)).astype(BF16)
+            extra = [after(of32, g_far)] + extra[1:]
+            g_far = plan.turn(g_far, False)
         part = attend_back_part(plan, blk, nseq, 2, 4, True, False, scalars, q, lse, kvs, extra)
         dkv2, dkv3, dq_part, g_ext, delta = part
         far = [plan.turn(d, False) for d in (dkv3, dkv2)]
@@ -884,89 +958,82 @@
             plan, blk, nseq, 1, 2, False, False, scalars, q, lse, kvs, [g_ext, delta, dq_part]
         )
         mid = plan.turn((dkv1.astype(F32) + far[0].astype(F32)).astype(BF16), True)
+        if packed:
+            g_far = after(g_far, dkv1)
+            g_mid = g_all[1].astype(F32) + g_core[1].astype(F32) + g_far[1].astype(F32)
+            g_mid = g_mid.astype(BF16)
+            dq_part = after(dq_part, g_mid)
+            g_mid = plan.turn(g_mid, True)
         dkv0, _, dq = attend_back_part(
             plan, blk, nseq, 0, 1, False, True, scalars, q, lse, kvs, [g_ext, delta, dq_part]
         )
+        if packed:
+            g_mid = after(g_mid, dkv0)
+            g_near = g_all[0].astype(F32) + g_core[0].astype(F32) + g_far[0].astype(F32)
+            g_near = (g_near + g_mid.astype(F32)).astype(BF16)
+            dq = after(dq, g_near)
+            g_other = plan.swap(g_near[2:], (0, 1))
         parts = [dkv0, far[1], mid]
     else:
         part = attend_back_part(plan, blk, nseq, 0, nb, True, True, scalars, q, lse, kvs, extra)
         dq = part[-1]
         parts = [part[0]] + [plan.swap(part[b], plan.groups[b]) for b in range(1, nb)]
 
-    outs = call(
+    head_outs = call(
         head_grads_body(plan, blk, width, shard, len(parts)),
         "head_grads",
         [info, dq, w_head, normed] + xs + parts,
         [SMEM] + [VMEM] * (3 + ns + len(parts)),
-        [sds((nj, blk, width), BF16)] * 2 + [sds((shard, 4 * HEAD), BF16)] * n_wt,
+        [sds((nj, blk, width), BF16)] * 2 + [sds((n_wt, shard // 2, width), BF16)],
         scratch=[pltpu.VMEM((width, 4 * HEAD), F32)],
         flops=4 * ns * blk * width * 4 * HEAD,
     )
-    own_rows, sib_rows, dw = outs[0], outs[1], outs[2:]
-    rows = (own_rows.astype(F32) + plan.swap(sib_rows, core).astype(F32)).astype(BF16)
-    up_rows = [rows[0]] + [plan.swap(rows[j], plan.peers[j]) for j in range(1, nj)]
-    grad_words = call(
-        words_body(nj),
-        "words_grad",
-        [words, vecs, grad_one] + up_rows,
-        [VMEM] * (3 + nj),
-        [sds((blk, width), F32)],
-    )[0]
-
-    dw = [dw[0]] + [plan.swap(dw[m], (0, m)) for m in range(1, n_wt)]
-    merged = []
-    for a in range(WT_HEADS):
-        total = dw[a].astype(F32)
-        for m in range(a + WT_HEADS, n_wt, WT_HEADS):
-            total = total + dw[m].astype(F32)
-        merged.append(total)
-    heads = jnp.stack(merged).astype(BF16)
-    step = CTX_HEADS
-    while step < n_ctx:
-        heads = (heads.astype(F32) + plan.swap(heads, (step, 0)).astype(F32)).astype(BF16)
-        step *= 2
-    cols = [heads]
-    own_heads = jnp.stack(cols, axis=1)
-    sib_heads = plan.swap(own_heads, core)
-    srcs = [own_heads[a, p] for a in range(WT_HEADS) for p in range(CTX_HEADS // 2)]
-    srcs += [sib_heads[a, p] for a in range(WT_HEADS) for p in range(CTX_HEADS // 2)]
-    g_qkv, gvec_attn = call(
-        head_out_body(plan, shard),
-        "head_out",
-        [info] + srcs,
-        [SMEM] + [VMEM] * H,
-        [sds((shard, 3 * width), F32), sds((8, shard), F32)],
+    own_rows, sib_rows, dw = head_outs
+    if packed:
+        g_two = (g_near[:2].astype(F32) + g_other.astype(F32)).astype(BF16)
+        g_last = plan.swap(g_two[1], (0, 2))
+    sib_rows = plan.swap(sib_rows, core)
+
+    if plan.square:
+        dw = (dw.astype(F32) + plan.turn(dw, True).astype(F32)).astype(BF16)
+        dw_more = plan.turn(dw, False)
+    else:
+        step = CTX_HEADS
+        while step < n_ctx:
+            dw_more = plan.swap(dw, (step, 0))
+            step *= 2
+            if step < n_ctx:
+                dw = (dw.astype(F32) + dw_more.astype(F32)).astype(BF16)
+    load = call(
+        merge_body(nj, n_wt, blk),
+        "merge",
+        [own_rows, sib_rows, dw, dw_more],
+        [VMEM] * 4,
+        [sds((blk + shard // 2, width), BF16)] * nj
+        + [sds((shard // 2, width), BF16)] * (n_wt - nj),
     )
-
+    loads = [load[0]] + [plan.swap(load[m], (0, m)) for m in range(1, n_wt)]
     if packed:
-        g_all = weight_grads[0]
-        g_core = plan.swap(g_all[1], core)
-        far = (g_all[0, 2:].astype(F32) + g_core[2:].astype(F32)).astype(BF16)
-        far = plan.turn(far, False)
-        mid = g_all[0, 1].astype(F32) + g_core[1].astype(F32) + far[1].astype(F32)
-        mid = plan.turn(mid.astype(BF16), True)
-        near = g_all[0, 0].astype(F32) + g_core[0].astype(F32) + far[0].astype(F32)
-        near = (near + mid.astype(F32)).astype(BF16)
-        far = plan.swap(near[2:], (0, 1))
-        two = (near[:2].astype(F32) + far.astype(F32)).astype(BF16)
-        final = (two[0].astype(F32) + plan.swap(two[1], (0, 2)).astype(F32)).astype(BF16)
+        g_last = after(g_last, load[0])
+        final = (g_two[0].astype(F32) + g_last.astype(F32)).astype(BF16)
         finals = plan.gather_square(final)
-        finals = finals + [plan.swap(f, core) for f in finals]
-        g_up, g_down, g_out, meta = call(
+        finals = jnp.stack(finals)
+        finals = [finals, plan.swap(finals, core)]
+        g_up, g_down, g_out, loss, g_gain, g_shift = call(
             unpack_body(plan, width, ff),
             "unpack",
-            [info] + finals,
-            [SMEM] + [VMEM] * len(finals),
+            [info, square] + finals,
+            [SMEM] + [VMEM] * 3,
             [
                 sds((shard, ff), F32),
                 sds((ff // n_wt, width), F32),
                 sds((shard, width), F32),
-                sds((TILE, CHUNK), F32),
+                sds((1, 1), F32),
+                sds((1, shard), F32),
+                sds((1, shard), F32),
             ],
         )
-        square_all = jnp.sum(meta[0])
-        g_gain, g_shift = meta[1, :shard], meta[2, :shard]
-        count_all = square[1, 0]
+        loss, g_gain, g_shift = loss[0, 0], g_gain.reshape(shard), g_shift.reshape(shard)
     else:
         g_up, g_down, g_out = weight_grads
         g_up = g_up.transpose(1, 0, 2).reshape(width, ff)
@@ -980,15 +1047,34 @@
         both = lax.psum(gvec[:2], ("ctx", "wt"))
         both = lax.dynamic_slice_in_dim(both, wt * shard, shard, 1)
         g_gain, g_shift = both[0], both[1]
-        count_all = count[0]
-        square_all = lax.psum(square[0, 0], ("ctx", "wt"))
-    loss = square_all / (count_all * width)
+        loss = lax.psum(square[0, 0], ("ctx", "wt")) / (count[0] * width)
+    if packed:
+        loads = loads[:3] + [after(loads[3], g_up)]
+    own_heads = jnp.stack([x[blk:] for x in loads[:nj]])
+    if n_wt > nj:
+        own_heads = (own_heads.astype(F32) + jnp.stack(loads[nj:]).astype(F32)).astype(BF16)
+    sib_heads = plan.swap(own_heads, core)
+    grad_words = call(
+        words_body(nj),
+        "words_grad",
+        [words, vecs, grad_one] + loads[:nj],
+        [VMEM] * (3 + nj),
+        [sds((blk, width), F32)],
+    )[0]
+    g_qkv, gain_one, shift_one = call(
+        head_out_body(plan, shard),
+        "head_out",
+        [info, own_heads, sib_heads],
+        [SMEM] + [VMEM] * 2,
+        [sds((shard, 3 * width), F32), sds((1, shard), F32), sds((1, shard), F32)],
+    )
+
     return (
         layer_out,
         loss,
         grad_words,
-        gvec_attn[0],
-        gvec_attn[1],
+        gain_one.reshape(shard),
+        shift_one.reshape(shard),
         g_qkv,
         g_out,
         g_gain,

time: 271 us -> 235 us (0.87); the launches traced: 271 us -> 231 us
  waiting for transfers between devices: 93.8 us -> 65.6 us
  local copies, waits for them, and re-layouts: 21.9 us -> 12.3 us
    ppermute x38 -> x29, waiting for transfers between devices: 88.1 us -> 43.2 us  [swap(): return lax.ppermute(x, ('ctx', 'wt'), perm)]
    ppermute x14 -> x16, waiting for transfers between devices: 5.63 us -> 22.4 us  [turn(): return lax.ppermute(x, ('ctx', 'wt'), perm)]
    squeeze x7 -> x1, local copies, waits for them, and re-layouts: 8.24 us -> 0.01 us  [per_device(): g_last = plan.swap(g_two[1], (0, 2))]
    slice x4 -> x1, local copies, waits for them, and re-layouts: 2.79 us -> 0.02 us  [per_device(): g_other = plan.swap(g_near[2:], (0, 1))]
    pallas_call x14 -> x15, Pallas kernels: 75.3 us -> 77.9 us  [call(): pl.pallas_call(body, name=name, out_shape=list(outs), in_specs=in_specs,...]
    convert_element_type x8 -> x6, other arithmetic: 6.87 us -> 9.01 us  [the longest x1 2.94 us: per_device(): g_far = (g_all[2:].astype(F32) + g_core[2:].astype(F32)).astype(BF16)]
    ppermute x38 -> x29, starting transfers between devices: 30.3 us -> 28.5 us  [swap(): return lax.ppermute(x, ('ctx', 'wt'), perm)]
    ppermute x14 -> x16, starting transfers between devices: 31.1 us -> 30.4 us  [turn(): return lax.ppermute(x, ('ctx', 'wt'), perm)]
  transfers between devices with their start and end apart: 52 -> 45, of which waited for: 21 -> 19; matrix products, arithmetic and copies ran while one was open for 8% -> 7% of each run, Pallas kernels for 18% -> 21%
where the time goes in v3:
time: 235 us; the launch traced here: 231 us
  Pallas kernels  77.9 us (33%)
  waiting for transfers between devices  65.6 us (28%)
  starting transfers between devices  58.9 us (25%)
  other arithmetic  14.6 us (6%)
  local copies, waits for them, and re-layouts  12.3 us (5%)
    pallas_call x15, Pallas kernels, call(): pl.pallas_call(body, name=name, out_shape=list(outs), in_specs=in_specs,...  77.9 us
    ppermute x29, waiting for transfers between devices, swap(): return lax.ppermute(x, ('ctx', 'wt'), perm)  43.2 us
    ppermute x16, starting transfers between devices, turn(): return lax.ppermute(x, ('ctx', 'wt'), perm)  30.4 us
    ppermute x29, starting transfers between devices, swap(): return lax.ppermute(x, ('ctx', 'wt'), perm)  28.5 us
    ppermute x16, waiting for transfers between devices, turn(): return lax.ppermute(x, ('ctx', 'wt'), perm)  22.4 us
    unnamed x84, local copies, waits for them, and re-layouts  7.67 us
  transfers between devices with their start and end apart: 45, of which 19 were waited for; matrix products, arithmetic and copies ran while one was open for 7% of the time, Pallas kernels for 21%

profile of v3, /device:TPU:0, one launch (start us, length us, event | category | flops | bytes accessed | tf_op | source)
XLA Modules:
  0.0 231.3 jit_solution(13041414621775459777)
XLA Ops:
  4.8 3.0 %collective-permute-start = (bf16[256,512]{1,0:T(8,128)(2,1)}, bf16[256,512]{1,0:T(8,128)(2,1)S(1)}, u32[]{:S(2)}, u32[]{:S(2)}) collective-permute-start(bf16[256,512]{1,0:T(8,128)(2,1)} %get-tuple-element.84), channel_id=1, source_target_pairs={{0,1},{1,0},{2,3},{3,2},{4,5},{5,4},{6,7},{7,6},{8,9},{9,8},{10,11... | collective-permute-start | bytes 786440 | tf_op jit(solution)/shard_map/ppermute | solution.py:96
  7.8 2.6 %collective-permute-start.1 = (bf16[256,512]{1,0:T(8,128)(2,1)}, bf16[256,512]{1,0:T(8,128)(2,1)S(1)}, u32[]{:S(2)}, u32[]{:S(2)}) collective-permute-start(bf16[256,512]{1,0:T(8,128)(2,1)} %get-tuple-element.85), channel_id=1, source_target_pairs={{0,2},{1,3},{2,0},{3,1},{4,6},{5,7},{6,4},{7,5},{8,10},{9,11},{10,... | collective-permute-start | bytes 786440 | tf_op jit(solution)/shard_map/ppermute | solution.py:96
  10.4 8.8 %collective-permute-done.refs_1_.refs_9_ = bf16[256,512]{1,0:T(8,128)(2,1)S(1)} collective-permute-done((bf16[256,512]{1,0:T(8,128)(2,1)}, bf16[256,512]{1,0:T(8,128)(2,1)S(1)}, u32[]{:S(2)}, u32[]{:S(2)}) %collective-permute-start) | collective-permute-done | bytes 262176 | tf_op jit(solution)/shard_map/ppermute | solution.py:96
  19.2 10.2 %collective-permute-done.1.refs_2_.refs_10_ = bf16[256,512]{1,0:T(8,128)(2,1)S(1)} collective-permute-done((bf16[256,512]{1,0:T(8,128)(2,1)}, bf16[256,512]{1,0:T(8,128)(2,1)S(1)}, u32[]{:S(2)}, u32[]{:S(2)}) %collective-permute-start.1) | collective-permute-done | bytes 262176 | tf_op jit(solution)/shard_map/ppermute | solution.py:96
  33.6 4.8 %project.1 = (bf16[8,192,128]{2,1,0:T(8,128)(2,1)}, bf16[8,192,128]{2,1,0:T(8,128)(2,1)}, bf16[8,192,512]{2,1,0:T(8,128)(2,1)}, bf16[512,256]{1,0:T(8,128)(2,1)}, f32[8,512]{1,0:T(8,128)}) custom-call(s32[2]{0:T(128)} %pad_add_fusion.info, bf16[256,512]{1,0:T(8,128)(2,1)} %get-tuple-element.83.refs_0_.refs_8_, bf16[256,512]{1,0:T(8,128)(2,1)} %copy-done.4, ...), custom_call_target="tpu_custom_call" | custom-call | flops 402653184 | bytes 5783560 | tf_op jit(solution)/shard_map/project/pallas_call | solution.py:51
  43.0 5.4 %collective-permute-done.7.refs_0_ = bf16[8,192,128]{2,1,0:T(8,128)(2,1)S(1)} collective-permute-done((bf16[8,192,128]{2,1,0:T(8,128)(2,1)}, bf16[8,192,128]{2,1,0:T(8,128)(2,1)S(1)}, u32[]{:S(2)}, u32[]{:S(2)}) %collective-permute-start.7) | collective-permute-done | bytes 393248 | tf_op jit(solution)/shard_map/ppermute | solution.py:104
  48.4 2.6 %collective-permute-start.8 = (bf16[8,192,128]{2,1,0:T(8,128)(2,1)S(1)}, bf16[8,192,128]{2,1,0:T(8,128)(2,1)S(1)}, u32[]{:S(2)}, u32[]{:S(2)}) collective-permute-start(bf16[8,192,128]{2,1,0:T(8,128)(2,1)S(1)} %collective-permute-done.7.refs_0_), channel_id=1, source_target_pairs={{0,16},{1,17},{2,18},{3,19},{4,12},{5,13},{6,14},{7,15},{8,24},{9,... | collective-permute-start | bytes 1179656 | tf_op jit(solution)/shard_map/ppermute | solution.py:104
  51.1 4.9 %collective-permute-start.14 = (bf16[10,16,512]{2,1,0:T(8,128)(2,1)S(1)}, bf16[10,16,512]{2,1,0:T(8,128)(2,1)S(1)}, u32[]{:S(2)}, u32[]{:S(2)}) collective-permute-start(bf16[10,16,512]{2,1,0:T(8,128)(2,1)S(1)} %maximum_maximum_fusion), channel_id=1, source_target_pairs={{0,2},{1,3},{2,0},{3,1},{4,6},{5,7},{6,4},{7,5},{8,10},{9,11},{10,... | collective-permute-start | bytes 491528 | tf_op jit(solution)/shard_map/ppermute | solution.py:96
  56.6 6.8 %attend.3 = (f32[8,1,192]{2,1,0:T(1,128)}, f32[8,1,192]{2,1,0:T(1,128)}, f32[8,128,192]{2,1,0:T(8,128)}) custom-call(s32[2]{0:T(128)} %pad_add_fusion.info, s32[32]{0:T(128)} %deal.11, s32[4]{0:T(128)} %lengths.11, s32[8]{0:T(128)} %call_exported.0.codes, bf16[8,192,128]{2,1,0:T(8,128)(2,1)} %get-tuple-element.88.q_ref, ...), custom_call_target="tpu_custom_call" | custom-call | flops 2113929216 | bytes 1585336 | tf_op jit(solution)/shard_map/attend/pallas_call | solution.py:51
  64.4 6.5 %attend.4 = (f32[8,1,192]{2,1,0:T(1,128)}, f32[8,1,192]{2,1,0:T(1,128)}, f32[8,128,192]{2,1,0:T(8,128)}) custom-call(s32[2]{0:T(128)} %pad_add_fusion.info, s32[32]{0:T(128)} %deal.11, s32[4]{0:T(128)} %lengths.11, s32[8]{0:T(128)} %call_exported.0.codes, bf16[8,192,128]{2,1,0:T(8,128)(2,1)} %get-tuple-element.88.q_ref, bf16[8,192,128]{2,1,0:T(8,128)(2,1)} %copy-done.31, ...), custom_call_target="tpu_custom_call" | custom-call | flops 4227858432 | bytes 2777272 | tf_op jit(solution)/shard_map/attend/pallas_call | solution.py:51
  71.0 4.5 %collective-permute-start.16 = (bf16[4,10,16,512]{3,2,1,0:T(8,128)(2,1)S(1)}, bf16[4,10,16,512]{3,2,1,0:T(8,128)(2,1)S(1)}, u32[]{:S(2)}, u32[]{:S(2)}) collective-permute-start(bf16[4,10,16,512]{3,2,1,0:T(8,128)(2,1)S(1)} %pad_maximum_fusion.1.refs_9_), channel_id=1, source_target_pairs={{0,8},{1,9},{2,10},{3,11},{4,20},{5,21},{6,22},{7,23},{8,0},{9,1},... | collective-permute-start | bytes 1966088 | tf_op jit(solution)/shard_map/ppermute | solution.py:104
  77.9 6.8 %attend.5 = (f32[8,1,192]{2,1,0:T(1,128)}, f32[8,1,192]{2,1,0:T(1,128)}, f32[8,128,192]{2,1,0:T(8,128)}, bf16[4,192,128]{2,1,0:T(8,128)(2,1)}, bf16[4,192,128]{2...) custom-call(s32[2]{0:T(128)} %pad_add_fusion.info, s32[32]{0:T(128)} %deal.11, s32[4]{0:T(128)} %lengths.11, ...), custom_call_target="tpu_custom_call" | custom-call | flops 2113929216 | bytes 3569848 | tf_op jit(solution)/shard_map/attend/pallas_call | solution.py:51
  86.5 4.5 %collective-permute-done.16 = bf16[4,10,16,512]{3,2,1,0:T(8,128)(2,1)S(1)} collective-permute-done((bf16[4,10,16,512]{3,2,1,0:T(8,128)(2,1)S(1)}, bf16[4,10,16,512]{3,2,1,0:T(8,128)(2,1)S(1)}, u32[]{:S(2)}, u32[]{:S(2)}) %collective-permute-start.16) | collective-permute-done | bytes 655392 | tf_op jit(solution)/shard_map/ppermute | solution.py:104
  103.8 9.0 %mlp.1 = (bf16[192,512]{1,0:T(8,128)(2,1)}, f32[8,128]{1,0:T(8,128)}, f32[192,512]{1,0:T(8,128)}, bf16[192,128]{1,0:T(8,128)(2,1)}, bf16[192,128]{1,0:T(8,128)(2...) custom-call(s32[2]{0:T(128)} %pad_add_fusion.info, ...), custom_call_target="tpu_custom_call" | custom-call | flops 1610612736 | bytes 8819468 | tf_op jit(solution)/shard_map/mlp/pallas_call | solution.py:51
  112.9 4.4 %mlp_grads.1 = (bf16[4,4,10,16,512]{4,3,2,1,0:T(8,128)(2,1)}, bf16[4,4,10,16,512]{4,3,2,1,0:T(8,128)(2,1)}) custom-call(s32[2]{0:T(128)} %pad_add_fusion.info, bf16[4,192,512]{2,1,0:T(8,128)(2,1)} %get-tuple-element.106.act_ref, bf16[4,192,512]{2,1,0:T(8,128)(2,1)} %get-tuple-element.107.gpre_ref, bf16[192,512]{1,0:T(8,128)(2,1)} %get-tuple-element.108.n2_ref, ...), custom_call_target="tpu_custom_call" | custom-call | flops 805306368 | bytes 7622664 | tf_op jit(solution)/shard_map/mlp_grads/pallas_call | solution.py:51
  121.9 4.2 %collective-permute-done.25.refs_5_ = bf16[192,128]{1,0:T(8,128)(2,1)S(1)} collective-permute-done((bf16[192,128]{1,0:T(8,128)(2,1)S(1)}, bf16[192,128]{1,0:T(8,128)(2,1)S(1)}, u32[]{:S(2)}, u32[]{:S(2)}) %collective-permute-start.25) | collective-permute-done | bytes 49184 | tf_op jit(solution)/shard_map/ppermute | solution.py:96
  126.3 2.9 %add_convert_fusion = bf16[2,4,10,16,512]{4,3,2,1,0:T(8,128)(2,1)} fusion(bf16[4,4,10,16,512]{4,3,2,1,0:T(8,128)(2,1)S(1)} %collective-permute-done.22, bf16[4,4,10,16,512]{4,3,2,1,0:T(8,128)(2,1)} %get-tuple-element.112), kind=kLoop, calls=%fused_computation | loop fusion | flops 2621440 | bytes 3932160 | tf_op jit(solution)/shard_map/convert_element_type | solution.py:951
  130.7 8.1 %attend_back.3 = (bf16[8,192,128]{2,1,0:T(8,128)(2,1)}, bf16[8,192,128]{2,1,0:T(8,128)(2,1)}, f32[8,128,192]{2,1,0:T(8,128)}, bf16[8,192,128]{2,1,0:T(8,128)(2,1)}, f32[8,1,192]{2,1,0:T(1,128)}) custom-call(s32[2]{0:T(128)} %pad_add_fusion.info, s32[32]{0:T(128)} %deal.11, s32[4]{0:T(128)} %lengths.11, s32[8]{0:T(128)} %call_exported.0.codes, ...), custom_call_target="tpu_custom_call" | custom-call | flops 10569646080 | bytes 4337848 | tf_op jit(solution)/shard_map/attend_back/pallas_call | solution.py:51
  138.7 4.0 %collective-permute-start.31 = (bf16[8,192,128]{2,1,0:T(8,128)(2,1)}, bf16[8,192,128]{2,1,0:T(8,128)(2,1)S(1)}, u32[]{:S(2)}, u32[]{:S(2)}) collective-permute-start(bf16[8,192,128]{2,1,0:T(8,128)(2,1)} %get-tuple-element.134), channel_id=1, source_target_pairs={{0,16},{1,17},{2,18},{3,19},{4,12},{5,13},{6,14},{7,15},{8,24},{9,... | collective-permute-start | bytes 1179656 | tf_op jit(solution)/shard_map/ppermute | solution.py:104
  142.8 4.8 %attend_back.4 = (bf16[8,192,128]{2,1,0:T(8,128)(2,1)}, f32[8,128,192]{2,1,0:T(8,128)}) custom-call(s32[2]{0:T(128)} %pad_add_fusion.info, s32[32]{0:T(128)} %deal.11, s32[4]{0:T(128)} %lengths.11, s32[8]{0:T(128)} %call_exported.0.codes, bf16[8,192,128]{2,1,0:T(8,128)(2,1)} %get-tuple-element.88.q_ref, f32[8,1,192]{2,1,0:T(1,128)} %get-tuple-element.114.lse_ref, ...), custom_call_target="tpu_custom_call" | custom-call | flops 5284823040 | bytes 3158200 | tf_op jit(solution)/shard_map/attend_back/pallas_call | solution.py:51
  149.9 5.7 %collective-permute-start.28 = (bf16[4,10,16,512]{3,2,1,0:T(8,128)(2,1)}, bf16[4,10,16,512]{3,2,1,0:T(8,128)(2,1)}, u32[]{:S(2)}, u32[]{:S(2)}) collective-permute-start(bf16[4,10,16,512]{3,2,1,0:T(8,128)(2,1)} %fusion.1), channel_id=1, source_target_pairs={{0,8},{1,9},{2,10},{3,11},{4,20},{5,21},{6,22},{7,23},{8,0},{9,1},... | collective-permute-start | bytes 1966088 | tf_op jit(solution)/shard_map/ppermute | solution.py:104
  159.6 8.7 %attend_back.5 = (bf16[8,192,128]{2,1,0:T(8,128)(2,1)}, f32[8,128,192]{2,1,0:T(8,128)}, bf16[8,192,128]{2,1,0:T(8,128)(2,1)}) custom-call(s32[2]{0:T(128)} %pad_add_fusion.info, s32[32]{0:T(128)} %deal.11, s32[4]{0:T(128)} %lengths.11, s32[8]{0:T(128)} %call_exported.0.codes, bf16[8,192,128]{2,1,0:T(8,128)(2,1)} %get-tuple-element.88.q_ref, ...), custom_call_target="tpu_custom_call" | custom-call | flops 5284823040 | bytes 3551416 | tf_op jit(solution)/shard_map/attend_back/pallas_call | solution.py:51
  168.3 2.6 %fusion = bf16[4,10,16,512]{3,2,1,0:T(8,128)(2,1)} fusion(bf16[4,10,16,512]{3,2,1,0:T(8,128)(2,1)} %collective-permute-done.28, bf16[4,4,10,16,512]{4,3,2,1,0:T(8,128)(2,1)S(1)} %collective-permute-done.22, bf16[2,4,10,16,512]{4,3,2,1,0:T(8,128)(2,1)} %collective-permute-done.23, bf16[4,4,10,16,512]{4,3,2,1,0:T(8,128)(2,1)S(1)} %copy-done.2), kind=kLoop, calls=%fused_computation.3 | loop fusion | flops 2621440 | bytes 3276800 | tf_op jit(solution)/shard_map/convert_element_type | solution.py:973
  171.6 5.8 %head_grads.1 = (bf16[4,192,512]{2,1,0:T(8,128)(2,1)}, bf16[4,192,512]{2,1,0:T(8,128)(2,1)}, bf16[4,64,512]{2,1,0:T(8,128)(2,1)}) custom-call(s32[2]{0:T(128)} %pad_add_fusion.info, bf16[8,192,128]{2,1,0:T(8,128)(2,1)} %get-tuple-element.131.dq_ref, bf16[512,256]{1,0:T(8,128)(2,1)} %get-tuple-element.132.wh_ref, ...), custom_call_target="tpu_custom_call" | custom-call | flops 805306368 | bytes 7340040 | tf_op jit(solution)/shard_map/head_grads/pallas_call | solution.py:51
  179.2 4.8 %collective-permute-done.35 = bf16[4,64,512]{2,1,0:T(8,128)(2,1)S(1)} collective-permute-done((bf16[4,64,512]{2,1,0:T(8,128)(2,1)}, bf16[4,64,512]{2,1,0:T(8,128)(2,1)S(1)}, u32[]{:S(2)}, u32[]{:S(2)}) %collective-permute-start.35) | collective-permute-done | bytes 262176 | tf_op jit(solution)/shard_map/ppermute | solution.py:104
  188.3 3.1 %collective-permute-done.36.more_ref = bf16[4,64,512]{2,1,0:T(8,128)(2,1)S(1)} collective-permute-done((bf16[4,64,512]{2,1,0:T(8,128)(2,1)S(1)}, bf16[4,64,512]{2,1,0:T(8,128)(2,1)S(1)}, u32[]{:S(2)}, u32[]{:S(2)}) %collective-permute-start.36) | collective-permute-done | bytes 262176 | tf_op jit(solution)/shard_map/ppermute | solution.py:104
  192.4 2.5 %merge.1 = (bf16[256,512]{1,0:T(8,128)(2,1)}, bf16[256,512]{1,0:T(8,128)(2,1)}, bf16[256,512]{1,0:T(8,128)(2,1)}, bf16[256,512]{1,0:T(8,128)(2,1)}) custom-call(bf16[4,192,512]{2,1,0:T(8,128)(2,1)} %get-tuple-element.136.own_ref, bf16[4,192,512]{2,1,0:T(8,128)(2,1)} %copy-done.14, bf16[4,64,512]{2,1,0:T(8,128)(2,1)} %copy-done.13, bf16[4,64,512]{2,1,0:T(8,128)(2,1)} %copy-done.23), custom_call_target="tpu_custom_call" | custom-call | bytes 3145728 | tf_op jit(solution)/shard_map/merge/pallas_call | solution.py:51
  197.9 3.2 %collective-permute-done.37 = bf16[10,16,512]{2,1,0:T(8,128)(2,1)S(1)} collective-permute-done((bf16[10,16,512]{2,1,0:T(8,128)(2,1)S(1)}, bf16[10,16,512]{2,1,0:T(8,128)(2,1)S(1)}, u32[]{:S(2)}, u32[]{:S(2)}) %collective-permute-start.37) | collective-permute-done | bytes 163872 | tf_op jit(solution)/shard_map/ppermute | solution.py:104
  209.6 4.5 %collective-permute-done.41.refs_1_ = bf16[256,512]{1,0:T(8,128)(2,1)S(1)} collective-permute-done((bf16[256,512]{1,0:T(8,128)(2,1)}, bf16[256,512]{1,0:T(8,128)(2,1)S(1)}, u32[]{:S(2)}, u32[]{:S(2)}) %collective-permute-start.41) | collective-permute-done | bytes 262176 | tf_op jit(solution)/shard_map/ppermute | solution.py:96
  214.1 7.4 %collective-permute-done.42.refs_2_ = bf16[256,512]{1,0:T(8,128)(2,1)S(1)} collective-permute-done((bf16[256,512]{1,0:T(8,128)(2,1)}, bf16[256,512]{1,0:T(8,128)(2,1)S(1)}, u32[]{:S(2)}, u32[]{:S(2)}) %collective-permute-start.42) | collective-permute-done | bytes 262176 | tf_op jit(solution)/shard_map/ppermute | solution.py:96
  222.4 2.8 %unpack.1 = (f32[128,2048]{1,0:T(8,128)}, f32[512,512]{1,0:T(8,128)}, f32[128,512]{1,0:T(8,128)}, f32[1,1]{1,0:T(1,128)}, f32[1,128]{1,0:T(1,128)}, /*index=5*/f32[1,128]{1,0:T(1,128)}) custom-call(s32[2]{0:T(128)} %pad_add_fusion.info, f32[8,128]{1,0:T(8,128)} %get-tuple-element.105.sq_ref, bf16[4,10,16,512]{3,2,1,0:T(8,128)(2,1)} %copy-done.1, ...), custom_call_target="tpu_custom_call" | custom-call | bytes 3675148 | tf_op jit(solution)/shard_map/unpack/pallas_call | solution.py:51
  225.9 2.5 %words_grad.1 = f32[192,512]{1,0:T(8,128)} custom-call(bf16[192,512]{1,0:T(8,128)(2,1)} %x_ref.1, f32[8,512]{1,0:T(8,128)} %get-tuple-element.87.refs_3_.vec_ref, f32[192,512]{1,0:T(8,128)} %get-tuple-element.142.g1_ref, bf16[256,512]{1,0:T(8,128)(2,1)} %get-tuple-element.139.refs_0_, bf16[256,512]{1,0:T(8,128)(2,1)} %copy-done.17, ...), custom_call_target="tpu_custom_call" | custom-call | bytes 2048000 | tf_op jit(solution)/shard_map/words_grad/pallas_call | solution.py:51
  (189 shorter events, 67.0 us)
Async XLA Ops:
  4.8 14.4 %collective-permute-start = (bf16[256,512]{1,0:T(8,128)(2,1)}, bf16[256,512]{1,0:T(8,128)(2,1)S(1)}, u32[]{:S(2)}, u32[]{:S(2)}) collective-permute-start(bf16[256,512]{1,0:T(8,128)(2,1)} %get-tuple-element.84), channel_id=1, source_target_pairs={{0,1},{1,0},{2,3},{3,2},{4,5},{5,4},{6,7},{7,6},{8,9},{9,8},{10,11... | collective-permute-start | bytes 786440 | tf_op jit(solution)/shard_map/ppermute | solution.py:96
  7.8 21.6 %collective-permute-start.1 = (bf16[256,512]{1,0:T(8,128)(2,1)}, bf16[256,512]{1,0:T(8,128)(2,1)S(1)}, u32[]{:S(2)}, u32[]{:S(2)}) collective-permute-start(bf16[256,512]{1,0:T(8,128)(2,1)} %get-tuple-element.85), channel_id=1, source_target_pairs={{0,2},{1,3},{2,0},{3,1},{4,6},{5,7},{6,4},{7,5},{8,10},{9,11},{10,... | collective-permute-start | bytes 786440 | tf_op jit(solution)/shard_map/ppermute | solution.py:96
  10.4 19.0 %collective-permute-start.2 = (bf16[256,512]{1,0:T(8,128)(2,1)}, bf16[256,512]{1,0:T(8,128)(2,1)S(1)}, u32[]{:S(2)}, u32[]{:S(2)}) collective-permute-start(bf16[256,512]{1,0:T(8,128)(2,1)} %get-tuple-element.86), channel_id=1, source_target_pairs={{0,3},{1,2},{2,1},{3,0},{4,7},{5,6},{6,5},{7,4},{8,11},{9,10},{10,... | collective-permute-start | bytes 786440 | tf_op jit(solution)/shard_map/ppermute | solution.py:96
  10.4 21.5 %collective-permute-start.3 = (bf16[256,512]{1,0:T(8,128)(2,1)}, bf16[256,512]{1,0:T(8,128)(2,1)S(1)}, u32[]{:S(2)}, u32[]{:S(2)}) collective-permute-start(bf16[256,512]{1,0:T(8,128)(2,1)} %get-tuple-element.83.refs_0_.refs_8_), channel_id=1, source_target_pairs={{0,4},{1,5},{2,6},{3,7},{4,0},{5,1},{6,2},{7,3},{8,12},{9,13},{10,... | collective-permute-start | bytes 786440 | tf_op jit(solution)/shard_map/ppermute | solution.py:96
  19.2 12.7 %collective-permute-start.4 = (bf16[256,512]{1,0:T(8,128)(2,1)S(1)}, bf16[256,512]{1,0:T(8,128)(2,1)S(1)}, u32[]{:S(2)}, u32[]{:S(2)}) collective-permute-start(bf16[256,512]{1,0:T(8,128)(2,1)S(1)} %collective-permute-done.refs_1_.refs_9_), channel_id=1, source_target_pairs={{0,4},{1,5},{2,6},{3,7},{4,0},{5,1},{6,2},{7,3},{8,12},{9,13},{10,... | collective-permute-start | bytes 786440 | tf_op jit(solution)/shard_map/ppermute | solution.py:96
  38.4 10.1 %collective-permute-start.7 = (bf16[8,192,128]{2,1,0:T(8,128)(2,1)}, bf16[8,192,128]{2,1,0:T(8,128)(2,1)S(1)}, u32[]{:S(2)}, u32[]{:S(2)}) collective-permute-start(bf16[8,192,128]{2,1,0:T(8,128)(2,1)} %get-tuple-element.89.refs_0_), channel_id=1, source_target_pairs={{0,8},{1,9},{2,10},{3,11},{4,20},{5,21},{6,22},{7,23},{8,0},{9,1},... | collective-permute-start | bytes 1179656 | tf_op jit(solution)/shard_map/ppermute | solution.py:104
  41.5 22.1 %collective-permute-start.9 = (bf16[8,192,128]{2,1,0:T(8,128)(2,1)}, bf16[8,192,128]{2,1,0:T(8,128)(2,1)S(1)}, u32[]{:S(2)}, u32[]{:S(2)}) collective-permute-start(bf16[8,192,128]{2,1,0:T(8,128)(2,1)} %get-tuple-element.89.refs_0_), channel_id=1, source_target_pairs={{0,16},{1,17},{2,18},{3,19},{4,12},{5,13},{6,14},{7,15},{8,24},{9,... | collective-permute-start | bytes 1179656 | tf_op jit(solution)/shard_map/ppermute | solution.py:104
  48.4 15.1 %collective-permute-start.8 = (bf16[8,192,128]{2,1,0:T(8,128)(2,1)S(1)}, bf16[8,192,128]{2,1,0:T(8,128)(2,1)S(1)}, u32[]{:S(2)}, u32[]{:S(2)}) collective-permute-start(bf16[8,192,128]{2,1,0:T(8,128)(2,1)S(1)} %collective-permute-done.7.refs_0_), channel_id=1, source_target_pairs={{0,16},{1,17},{2,18},{3,19},{4,12},{5,13},{6,14},{7,15},{8,24},{9,... | collective-permute-start | bytes 1179656 | tf_op jit(solution)/shard_map/ppermute | solution.py:104
  51.1 12.3 %collective-permute-start.14 = (bf16[10,16,512]{2,1,0:T(8,128)(2,1)S(1)}, bf16[10,16,512]{2,1,0:T(8,128)(2,1)S(1)}, u32[]{:S(2)}, u32[]{:S(2)}) collective-permute-start(bf16[10,16,512]{2,1,0:T(8,128)(2,1)S(1)} %maximum_maximum_fusion), channel_id=1, source_target_pairs={{0,2},{1,3},{2,0},{3,1},{4,6},{5,7},{6,4},{7,5},{8,10},{9,11},{10,... | collective-permute-start | bytes 491528 | tf_op jit(solution)/shard_map/ppermute | solution.py:96
  63.5 7.4 %collective-permute-start.15 = (bf16[2,10,16,512]{3,2,1,0:T(8,128)(2,1)S(1)}, bf16[2,10,16,512]{3,2,1,0:T(8,128)(2,1)S(1)}, u32[]{:S(2)}, u32[]{:S(2)}) collective-permute-start(bf16[2,10,16,512]{3,2,1,0:T(8,128)(2,1)S(1)} %pad_maximum_fusion.3), channel_id=1, source_target_pairs={{0,1},{1,0},{2,3},{3,2},{4,5},{5,4},{6,7},{7,6},{8,9},{9,8},{10,11... | collective-permute-start | bytes 983048 | tf_op jit(solution)/shard_map/ppermute | solution.py:96
  71.0 20.0 %collective-permute-start.16 = (bf16[4,10,16,512]{3,2,1,0:T(8,128)(2,1)S(1)}, bf16[4,10,16,512]{3,2,1,0:T(8,128)(2,1)S(1)}, u32[]{:S(2)}, u32[]{:S(2)}) collective-permute-start(bf16[4,10,16,512]{3,2,1,0:T(8,128)(2,1)S(1)} %pad_maximum_fusion.1.refs_9_), channel_id=1, source_target_pairs={{0,8},{1,9},{2,10},{3,11},{4,20},{5,21},{6,22},{7,23},{8,0},{9,1},... | collective-permute-start | bytes 1966088 | tf_op jit(solution)/shard_map/ppermute | solution.py:104
  75.5 15.7 %collective-permute-start.17 = (bf16[4,10,16,512]{3,2,1,0:T(8,128)(2,1)S(1)}, bf16[4,10,16,512]{3,2,1,0:T(8,128)(2,1)S(1)}, u32[]{:S(2)}, u32[]{:S(2)}) collective-permute-start(bf16[4,10,16,512]{3,2,1,0:T(8,128)(2,1)S(1)} %pad_maximum_fusion.1.refs_9_), channel_id=1, source_target_pairs={{0,16},{1,17},{2,18},{3,19},{4,12},{5,13},{6,14},{7,15},{8,24},{9,... | collective-permute-start | bytes 1966088 | tf_op jit(solution)/shard_map/ppermute | solution.py:104
  91.0 10.6 %collective-permute-start.18 = (bf16[4,10,16,512]{3,2,1,0:T(8,128)(2,1)S(1)}, bf16[4,10,16,512]{3,2,1,0:T(8,128)(2,1)S(1)}, u32[]{:S(2)}, u32[]{:S(2)}) collective-permute-start(bf16[4,10,16,512]{3,2,1,0:T(8,128)(2,1)S(1)} %collective-permute-done.16), channel_id=1, source_target_pairs={{0,16},{1,17},{2,18},{3,19},{4,12},{5,13},{6,14},{7,15},{8,24},{9,... | collective-permute-start | bytes 1966088 | tf_op jit(solution)/shard_map/ppermute | solution.py:104
  91.3 12.5 %collective-permute-start.20 = (bf16[2,4,10,16,512]{4,3,2,1,0:T(8,128)(2,1)S(1)}, bf16[2,4,10,16,512]{4,3,2,1,0:T(8,128)(2,1)}, u32[]{:S(2)}, u32[]{:S(2)}) collective-permute-start(bf16[2,4,10,16,512]{4,3,2,1,0:T(8,128)(2,1)S(1)} %pad_maximum_fusion.refs_10_), channel_id=1, source_target_pairs={{0,4},{1,5},{2,6},{3,7},{4,0},{5,1},{6,2},{7,3},{8,12},{9,13},{10,... | collective-permute-start | bytes 3932168 | tf_op jit(solution)/shard_map/ppermute | solution.py:96
  94.2 6.5 %collective-permute-start.12 = (bf16[192,128]{1,0:T(8,128)(2,1)S(1)}, bf16[192,128]{1,0:T(8,128)(2,1)S(1)}, u32[]{:S(2)}, u32[]{:S(2)}) collective-permute-start(bf16[192,128]{1,0:T(8,128)(2,1)S(1)} %get-tuple-element.156), channel_id=1, source_target_pairs={{0,2},{1,3},{2,0},{3,1},{4,6},{5,7},{6,4},{7,5},{8,10},{9,11},{10,... | collective-permute-start | bytes 147464 | tf_op jit(solution)/shard_map/ppermute | solution.py:96
  117.3 9.0 %collective-permute-start.22 = (bf16[4,4,10,16,512]{4,3,2,1,0:T(8,128)(2,1)}, bf16[4,4,10,16,512]{4,3,2,1,0:T(8,128)(2,1)S(1)}, u32[]{:S(2)}, u32[]{:S(2)}) collective-permute-start(bf16[4,4,10,16,512]{4,3,2,1,0:T(8,128)(2,1)} %get-tuple-element.113), channel_id=1, source_target_pairs={{0,4},{1,5},{2,6},{3,7},{4,0},{5,1},{6,2},{7,3},{8,12},{9,13},{10,... | collective-permute-start | bytes 7864328 | tf_op jit(solution)/shard_map/ppermute | solution.py:96
  119.5 6.6 %collective-permute-start.25 = (bf16[192,128]{1,0:T(8,128)(2,1)S(1)}, bf16[192,128]{1,0:T(8,128)(2,1)S(1)}, u32[]{:S(2)}, u32[]{:S(2)}) collective-permute-start(bf16[192,128]{1,0:T(8,128)(2,1)S(1)} %copy-done.40), channel_id=1, source_target_pairs={{0,2},{1,3},{2,0},{3,1},{4,6},{5,7},{6,4},{7,5},{8,10},{9,11},{10,... | collective-permute-start | bytes 147464 | tf_op jit(solution)/shard_map/ppermute | solution.py:96
  119.5 6.6 %collective-permute-start.26 = (bf16[192,128]{1,0:T(8,128)(2,1)S(1)}, bf16[192,128]{1,0:T(8,128)(2,1)S(1)}, u32[]{:S(2)}, u32[]{:S(2)}) collective-permute-start(bf16[192,128]{1,0:T(8,128)(2,1)S(1)} %copy-done.39), channel_id=1, source_target_pairs={{0,3},{1,2},{2,1},{3,0},{4,7},{5,6},{6,5},{7,4},{8,11},{9,10},{10,... | collective-permute-start | bytes 147464 | tf_op jit(solution)/shard_map/ppermute | solution.py:96
  129.2 18.4 %collective-permute-start.23 = (bf16[2,4,10,16,512]{4,3,2,1,0:T(8,128)(2,1)}, bf16[2,4,10,16,512]{4,3,2,1,0:T(8,128)(2,1)}, u32[]{:S(2)}, u32[]{:S(2)}) collective-permute-start(bf16[2,4,10,16,512]{4,3,2,1,0:T(8,128)(2,1)} %add_convert_fusion), channel_id=1, source_target_pairs={{0,16},{1,17},{2,18},{3,19},{4,12},{5,13},{6,14},{7,15},{8,24},{9,... | collective-permute-start | bytes 3932168 | tf_op jit(solution)/shard_map/ppermute | solution.py:104
  138.7 32.1 %collective-permute-start.31 = (bf16[8,192,128]{2,1,0:T(8,128)(2,1)}, bf16[8,192,128]{2,1,0:T(8,128)(2,1)S(1)}, u32[]{:S(2)}, u32[]{:S(2)}) collective-permute-start(bf16[8,192,128]{2,1,0:T(8,128)(2,1)} %get-tuple-element.134), channel_id=1, source_target_pairs={{0,16},{1,17},{2,18},{3,19},{4,12},{5,13},{6,14},{7,15},{8,24},{9,... | collective-permute-start | bytes 1179656 | tf_op jit(solution)/shard_map/ppermute | solution.py:104
  142.7 12.9 %collective-permute-start.32 = (bf16[8,192,128]{2,1,0:T(8,128)(2,1)}, bf16[8,192,128]{2,1,0:T(8,128)(2,1)}, u32[]{:S(2)}, u32[]{:S(2)}) collective-permute-start(bf16[8,192,128]{2,1,0:T(8,128)(2,1)} %get-tuple-element.135), channel_id=1, source_target_pairs={{0,16},{1,17},{2,18},{3,19},{4,12},{5,13},{6,14},{7,15},{8,24},{9,... | collective-permute-start | bytes 1179656 | tf_op jit(solution)/shard_map/ppermute | solution.py:104
  149.9 18.4 %collective-permute-start.28 = (bf16[4,10,16,512]{3,2,1,0:T(8,128)(2,1)}, bf16[4,10,16,512]{3,2,1,0:T(8,128)(2,1)}, u32[]{:S(2)}, u32[]{:S(2)}) collective-permute-start(bf16[4,10,16,512]{3,2,1,0:T(8,128)(2,1)} %fusion.1), channel_id=1, source_target_pairs={{0,8},{1,9},{2,10},{3,11},{4,20},{5,21},{6,22},{7,23},{8,0},{9,1},... | collective-permute-start | bytes 1966088 | tf_op jit(solution)/shard_map/ppermute | solution.py:104
  157.5 13.4 %collective-permute-start.33 = (bf16[8,192,128]{2,1,0:T(8,128)(2,1)}, bf16[8,192,128]{2,1,0:T(8,128)(2,1)}, u32[]{:S(2)}, u32[]{:S(2)}) collective-permute-start(bf16[8,192,128]{2,1,0:T(8,128)(2,1)} %add_convert_fusion.2), channel_id=1, source_target_pairs={{0,8},{1,9},{2,10},{3,11},{4,20},{5,21},{6,22},{7,23},{8,0},{9,1},... | collective-permute-start | bytes 1179656 | tf_op jit(solution)/shard_map/ppermute | solution.py:104
  177.4 6.6 %collective-permute-start.35 = (bf16[4,64,512]{2,1,0:T(8,128)(2,1)}, bf16[4,64,512]{2,1,0:T(8,128)(2,1)S(1)}, u32[]{:S(2)}, u32[]{:S(2)}) collective-permute-start(bf16[4,64,512]{2,1,0:T(8,128)(2,1)} %get-tuple-element.138), channel_id=1, source_target_pairs={{0,8},{1,9},{2,10},{3,11},{4,20},{5,21},{6,22},{7,23},{8,0},{9,1},... | collective-permute-start | bytes 786440 | tf_op jit(solution)/shard_map/ppermute | solution.py:104
  177.5 9.0 %collective-permute-start.29 = (bf16[2,10,16,512]{3,2,1,0:T(8,128)(2,1)S(1)}, bf16[2,10,16,512]{3,2,1,0:T(8,128)(2,1)S(1)}, u32[]{:S(2)}, u32[]{:S(2)}) collective-permute-start(bf16[2,10,16,512]{3,2,1,0:T(8,128)(2,1)S(1)} %slice.88), channel_id=1, source_target_pairs={{0,1},{1,0},{2,3},{3,2},{4,5},{5,4},{6,7},{7,6},{8,9},{9,8},{10,11... | collective-permute-start | bytes 983048 | tf_op jit(solution)/shard_map/ppermute | solution.py:96
  179.2 12.2 %collective-permute-start.34 = (bf16[4,192,512]{2,1,0:T(8,128)(2,1)}, bf16[4,192,512]{2,1,0:T(8,128)(2,1)S(1)}, u32[]{:S(2)}, u32[]{:S(2)}) collective-permute-start(bf16[4,192,512]{2,1,0:T(8,128)(2,1)} %get-tuple-element.137), channel_id=1, source_target_pairs={{0,4},{1,5},{2,6},{3,7},{4,0},{5,1},{6,2},{7,3},{8,12},{9,13},{10,... | collective-permute-start | bytes 2359304 | tf_op jit(solution)/shard_map/ppermute | solution.py:96
  186.6 9.0 %collective-permute-start.30 = (bf16[10,16,512]{2,1,0:T(8,128)(2,1)S(1)}, bf16[10,16,512]{2,1,0:T(8,128)(2,1)S(1)}, u32[]{:S(2)}, u32[]{:S(2)}) collective-permute-start(bf16[10,16,512]{2,1,0:T(8,128)(2,1)S(1)} %slice_bitcast_fusion), channel_id=1, source_target_pairs={{0,2},{1,3},{2,0},{3,1},{4,6},{5,7},{6,4},{7,5},{8,10},{9,11},{10,... | collective-permute-start | bytes 491528 | tf_op jit(solution)/shard_map/ppermute | solution.py:96
  197.2 8.5 %collective-permute-start.38 = (bf16[10,16,512]{2,1,0:T(8,128)(2,1)S(1)}, bf16[10,16,512]{2,1,0:T(8,128)(2,1)S(1)}, u32[]{:S(2)}, u32[]{:S(2)}) collective-permute-start(bf16[10,16,512]{2,1,0:T(8,128)(2,1)S(1)} %fusion.2), channel_id=1, source_target_pairs={{0,16},{1,17},{2,18},{3,19},{4,12},{5,13},{6,14},{7,15},{8,24},{9,... | collective-permute-start | bytes 491528 | tf_op jit(solution)/shard_map/ppermute | solution.py:104
  203.2 10.9 %collective-permute-start.41 = (bf16[256,512]{1,0:T(8,128)(2,1)}, bf16[256,512]{1,0:T(8,128)(2,1)S(1)}, u32[]{:S(2)}, u32[]{:S(2)}) collective-permute-start(bf16[256,512]{1,0:T(8,128)(2,1)} %get-tuple-element.143), channel_id=1, source_target_pairs={{0,1},{1,0},{2,3},{3,2},{4,5},{5,4},{6,7},{7,6},{8,9},{9,8},{10,11... | collective-permute-start | bytes 786440 | tf_op jit(solution)/shard_map/ppermute | solution.py:96
  203.6 17.9 %collective-permute-start.42 = (bf16[256,512]{1,0:T(8,128)(2,1)}, bf16[256,512]{1,0:T(8,128)(2,1)S(1)}, u32[]{:S(2)}, u32[]{:S(2)}) collective-permute-start(bf16[256,512]{1,0:T(8,128)(2,1)} %get-tuple-element.144), channel_id=1, source_target_pairs={{0,2},{1,3},{2,0},{3,1},{4,6},{5,7},{6,4},{7,5},{8,10},{9,11},{10,... | collective-permute-start | bytes 786440 | tf_op jit(solution)/shard_map/ppermute | solution.py:96
  206.6 14.9 %collective-permute-start.40 = (bf16[4,10,16,512]{3,2,1,0:T(8,128)(2,1)S(1)}, bf16[4,10,16,512]{3,2,1,0:T(8,128)(2,1)S(1)}, u32[]{:S(2)}, u32[]{:S(2)}) collective-permute-start(bf16[4,10,16,512]{3,2,1,0:T(8,128)(2,1)S(1)} %pad_maximum_fusion.2.own), channel_id=1, source_target_pairs={{0,4},{1,5},{2,6},{3,7},{4,0},{5,1},{6,2},{7,3},{8,12},{9,13},{10,... | collective-permute-start | bytes 1966088 | tf_op jit(solution)/shard_map/ppermute | solution.py:96
  207.6 17.6 %collective-permute-start.43 = (bf16[256,512]{1,0:T(8,128)(2,1)S(1)}, bf16[256,512]{1,0:T(8,128)(2,1)S(1)}, u32[]{:S(2)}, u32[]{:S(2)}) collective-permute-start(bf16[256,512]{1,0:T(8,128)(2,1)S(1)} %copy-done.34), channel_id=1, source_target_pairs={{0,3},{1,2},{2,1},{3,0},{4,7},{5,6},{6,5},{7,4},{8,11},{9,10},{10,... | collective-permute-start | bytes 786440 | tf_op jit(solution)/shard_map/ppermute | solution.py:96
  (55 other events, 321.1 us)

commit v4 on v3

--- a/solution.py
+++ b/solution.py
@@ -13,6 +13,8 @@
 WT_HEADS = 4
 CHUNK = 512
 TILE = 16
+WIDE = 4
+WIDE_BACK = 4
 F32 = jnp.float32
 BF16 = jnp.bfloat16
 NEG = -1e30
@@ -186,45 +188,56 @@
     return first, here
 
 
-def list_pairs(plan, info, deal, lengths, codes, blk, nseq, slot_of, pairs, low, high):
-    fill_slots(plan, info, deal, slot_of)
-
-    def one_block(i, n):
-        first, here = slot_range(plan, info, deal, lengths, codes, i, blk, nseq)
-
-        def one_key(b, n):
-            slot = slot_of[b]
-            inside = (slot >= low) & (slot < high)
-            pairs[n] = i * 1024 + slot - low
-            return n + inside.astype(jnp.int32)
-
-        return lax.fori_loop(first, here, one_key, n)
-
-    n = lax.fori_loop(0, len(plan.slots), one_block, jnp.int32(0))
-    pairs[n] = pairs[jnp.maximum(n - 1, 0)]
-    return n
-
-
-def attend_body(plan, blk, nseq, lo, hi, last):
+def lists_body(plan, blk, nseq, sets):
+    ns = len(plan.slots)
+
+    def body(info, deal, lengths, codes, *refs):
+        outs, slot_of = refs[:-1], refs[-1]
+        fill_slots(plan, info, deal, slot_of)
+
+        def one_block(i, counts):
+            first, here = slot_range(plan, info, deal, lengths, codes, i, blk, nseq)
+
+            def one_key(b, counts):
+                slot = slot_of[b]
+                more = []
+                for out, n, (lo, hi) in zip(outs, counts, sets):
+                    inside = (slot >= lo * ns) & (slot < hi * ns)
+                    out[n] = i * 1024 + slot - lo * ns
+                    more.append(n + inside.astype(jnp.int32))
+                return tuple(more)
+
+            return lax.fori_loop(first, here, one_key, counts)
+
+        start = tuple(jnp.int32(1) for _ in sets)
+        counts = lax.fori_loop(0, ns, one_block, start)
+        for out, n in zip(outs, counts):
+            spare = jnp.where(n > 1, out[jnp.maximum(n - 1, 1)], 0)
+            for t in range(max(WIDE, WIDE_BACK) - 1):
+                out[n + t] = spare
+            out[0] = n - 1
+
+    return body
+
+
+def attend_body(plan, blk, lo, hi, last):
     ns, nb = len(plan.slots), hi - lo
 
-    def body(info, deal, lengths, codes, q_ref, *refs):
+    def body(info, pairs, q_ref, *refs):
         kv_refs, refs = refs[:nb], refs[nb:]
         if lo:
             olds, refs = refs[:3], refs[3:]
         (m_ref, l_ref, acc_ref), refs = refs[:3], refs[3:]
         if last:
             (o_ref, o_sib_ref, of_ref, lse_ref), refs = refs[:4], refs[4:]
-        kvs, slot_of, pairs, sem = refs
+        kvs, sem = refs
         copies = [
             pltpu.make_async_copy(ref, kvs.at[pl.ds(b * ns, ns)], sem.at[b])
             for b, ref in enumerate(kv_refs)
         ]
         for c in copies:
             c.start()
-        n = list_pairs(
-            plan, info, deal, lengths, codes, blk, nseq, slot_of, pairs, lo * ns, hi * ns
-        )
+        n = pairs[0]
         if lo:
             for new, old in zip((m_ref, l_ref, acc_ref), olds):
                 new[...] = old[...]
@@ -234,9 +247,9 @@
             tri = lax.broadcasted_iota(jnp.int32, (blk, blk), 0) <= lane_iota((blk, blk))
 
             def diagonal(h, _):
-                scores = [mm(kvs[h * 2 + k], q_ref[h * 2 + k], NT) for k in (0, 1)]
-                for k in (0, 1):
-                    i = h * 2 + k
+                scores = [mm(kvs[h * WIDE + k], q_ref[h * WIDE + k], NT) for k in range(WIDE)]
+                for k in range(WIDE):
+                    i = h * WIDE + k
                     s = jnp.where(tri, scores[k], NEG)
                     m = jnp.max(s, axis=0, keepdims=True)
                     p = jnp.exp(s - m)
@@ -245,15 +258,16 @@
                     acc_ref[i] = mm(kvs[i], p.astype(BF16), TN)
                 return 0
 
-            lax.fori_loop(0, ns // 2, diagonal, 0)
+            lax.fori_loop(0, ns // WIDE, diagonal, 0)
 
         def step(h, _):
-            codes2 = [pairs[h * 2], pairs[h * 2 + 1]]
+            codes2 = [pairs[h * WIDE + 1 + k] for k in range(WIDE)]
             rows = [c // 1024 for c in codes2]
             cols = [c % 1024 for c in codes2]
-            scores = [mm(kvs[cols[k]], q_ref[rows[k]], NT) for k in (0, 1)]
-            scores[1] = jnp.where(h * 2 + 1 < n, scores[1], NEG)
-            for k in (0, 1):
+            scores = [mm(kvs[cols[k]], q_ref[rows[k]], NT) for k in range(WIDE)]
+            for k in range(1, WIDE):
+                scores[k] = jnp.where(h * WIDE + k < n, scores[k], NEG)
+            for k in range(WIDE):
                 i, s = rows[k], scores[k]
                 m_old = m_ref[i]
                 m = jnp.maximum(m_old, jnp.max(s, axis=0, keepdims=True))
@@ -264,7 +278,7 @@
                 acc_ref[i] = acc_ref[i] * factor + mm(kvs[cols[k]], p.astype(BF16), TN)
             return 0
 
-        lax.fori_loop(0, (n + 1) // 2, step, 0)
+        lax.fori_loop(0, (n + WIDE - 1) // WIDE, step, 0)
         if last:
             core = info[0] % 2
 
@@ -294,7 +308,7 @@
     return body
 
 
-def attend_part(plan, blk, nseq, lo, hi, last, scalars, q, kvs, olds):
+def attend_part(plan, blk, lo, hi, last, info, lists, q, kvs, olds):
     ns, nb = len(plan.slots), hi - lo
     outs = [sds((ns, 1, blk), F32), sds((ns, 1, blk), F32), sds((ns, 2 * HEAD, blk), F32)]
     if last:
@@ -304,18 +318,15 @@
             sds((ns, blk, 2 * HEAD), F32),
             sds((ns, 1, blk), F32),
         ]
-    n_dev = plan.n_ctx * plan.n_wt
     pairs = 14 * nb
     return call(
-        attend_body(plan, blk, nseq, lo, hi, last),
+        attend_body(plan, blk, lo, hi, last),
         "attend",
-        list(scalars) + [q] + list(kvs[lo:hi]) + list(olds),
-        [SMEM] * 4 + [VMEM] + [ANY] * nb + [VMEM] * len(olds),
+        [info, lists[lo, hi], q] + list(kvs[lo:hi]) + list(olds),
+        [SMEM] * 2 + [VMEM] + [ANY] * nb + [VMEM] * len(olds),
         outs,
         scratch=[
             pltpu.VMEM((nb * ns, blk, 2 * HEAD), BF16),
-            pltpu.SMEM((n_dev,), jnp.int32),
-            pltpu.SMEM((ns * n_dev + 1,), jnp.int32),
             pltpu.SemaphoreType.DMA((nb,)),
         ],
         flops=pairs * 4 * blk * blk * 128 * 8,
@@ -323,10 +334,10 @@
     )
 
 
-def attend_back_body(plan, blk, nseq, lo, hi, first, last):
+def attend_back_body(plan, blk, lo, hi, first, last):
     ns, nb, nj = len(plan.slots), hi - lo, len(plan.peers)
 
-    def body(info, deal, lengths, codes, q_ref, lse_ref, *refs):
+    def body(info, pairs, q_ref, lse_ref, *refs):
         kv_refs, refs = refs[:nb], refs[nb:]
         if first:
             of_ref, g_refs, gs_ref, refs = refs[0], refs[1 : 1 + nj], refs[1 + nj], refs[2 + nj :]
@@ -338,16 +349,14 @@
             g_ext, delta_ref, refs = refs[0], refs[1], refs[2:]
         if last:
             dq_ref, refs = refs[0], refs[1:]
-        kvs, dkvs, slot_of, pairs, sem = refs
+        kvs, dkvs, sem = refs
         copies = [
             pltpu.make_async_copy(ref, kvs.at[pl.ds(b * ns, ns)], sem.at[b])
             for b, ref in enumerate(kv_refs)
         ]
         for c in copies:
             c.start()
-        n = list_pairs(
-            plan, info, deal, lengths, codes, blk, nseq, slot_of, pairs, lo * ns, hi * ns
-        )
+        n = pairs[0]
         core = info[0] % 2
         high = lane_iota((blk, 2 * HEAD)) >= HEAD
         if first:
@@ -379,22 +388,22 @@
             tri = lax.broadcasted_iota(jnp.int32, (blk, blk), 0) <= lane_iota((blk, blk))
 
             def diagonal(h, _):
-                at = [h * 2, h * 2 + 1]
+                at = [h * WIDE_BACK + k for k in range(WIDE_BACK)]
                 pair_terms(at, at, lambda k, p: jnp.where(tri, p, 0.0))
                 return 0
 
-            lax.fori_loop(0, ns // 2, diagonal, 0)
+            lax.fori_loop(0, ns // WIDE_BACK, diagonal, 0)
 
         def step(h, _):
-            codes2 = [pairs[h * 2], pairs[h * 2 + 1]]
+            codes2 = [pairs[h * WIDE_BACK + 1 + k] for k in range(WIDE_BACK)]
             pair_terms(
                 [c // 1024 for c in codes2],
                 [c % 1024 for c in codes2],
-                lambda k, p: jnp.where(h * 2 + 1 < n, p, 0.0) if k else p,
+                lambda k, p: jnp.where(h * WIDE_BACK + k < n, p, 0.0) if k else p,
             )
             return 0
 
-        lax.fori_loop(0, (n + 1) // 2, step, 0)
+        lax.fori_loop(0, (n + WIDE_BACK - 1) // WIDE_BACK, step, 0)
         if last:
 
             def finish(i, _):
@@ -409,7 +418,7 @@
     return body
 
 
-def attend_back_part(plan, blk, nseq, lo, hi, first, last, scalars, q, lse, kvs, extra):
+def attend_back_part(plan, blk, lo, hi, first, last, info, lists, q, lse, kvs, extra):
     ns, nb = len(plan.slots), hi - lo
     rows = sds((ns, blk, 2 * HEAD), BF16)
     outs = [rows] * nb + [sds((ns, 2 * HEAD, blk), F32)]
@@ -417,19 +426,16 @@
         outs += [rows, sds((ns, 1, blk), F32)]
     if last:
         outs += [rows]
-    n_dev = plan.n_ctx * plan.n_wt
     pairs = 14 * nb
     return call(
-        attend_back_body(plan, blk, nseq, lo, hi, first, last),
+        attend_back_body(plan, blk, lo, hi, first, last),
         "attend_back",
-        list(scalars) + [q, lse] + list(kvs[lo:hi]) + list(extra),
-        [SMEM] * 4 + [VMEM] * 2 + [ANY] * nb + [VMEM] * len(extra),
+        [info, lists[lo, hi], q, lse] + list(kvs[lo:hi]) + list(extra),
+        [SMEM] * 2 + [VMEM] * 2 + [ANY] * nb + [VMEM] * len(extra),
         outs,
         scratch=[
             pltpu.VMEM((nb * ns, blk, 2 * HEAD), BF16),
             pltpu.VMEM((nb * ns, blk, 2 * HEAD), F32),
-            pltpu.SMEM((n_dev,), jnp.int32),
-            pltpu.SMEM((ns * n_dev + 1,), jnp.int32),
             pltpu.SemaphoreType.DMA((nb,)),
         ],
         flops=pairs * 10 * blk * blk * 128 * 8,
@@ -801,7 +807,19 @@
         [sds((blk + shard // 2, width), BF16)] * n_wt,
     )
     loads = [load[0]] + [plan.swap(load[m], (0, m)) for m in range(1, n_wt)]
-    xs = loads[:nj] + [plan.swap(x, core) for x in loads[:nj]]
+    sets = [(0, 1), (1, 3), (3, 4), (2, 4), (1, 2)] if plan.square else [(0, nb)]
+    lists = call(
+        lists_body(plan, blk, nseq, sets),
+        "lists",
+        [after(info, load[1]), deal, lengths, codes],
+        [SMEM] * 4,
+        [sds((ns * n_ctx * n_wt + WIDE + WIDE_BACK,), jnp.int32)] * len(sets),
+        scratch=[pltpu.SMEM((n_ctx * n_wt,), jnp.int32)],
+        out_specs=[SMEM] * len(sets),
+    )
+    lists = dict(zip(sets, lists))
+    late = [loads[0], after(loads[1], lists[sets[0]])] + loads[2:]
+    xs = loads[:nj] + [plan.swap(x, core) for x in late[:nj]]
 
     q, kv, normed, w_head, vecs = call(
         project_body(plan, shard, blk),
@@ -835,7 +853,10 @@
             ],
             axis=0,
         )
-        piece = after(piece, kvs[1])
+        piece = after(piece, loads[2])
+        two = jnp.stack([piece, plan.swap(piece, (0, 2))])
+        two = after(two, kvs[1])
+        near = plan.swap(two, (0, 1))
         count = jnp.zeros((1,), F32)
     else:
         up_full = lax.all_gather(w_up, "wt", axis=0, tiled=True)
@@ -848,24 +869,21 @@
         ]
         count = lax.psum(jnp.sum(valid).astype(F32), ("ctx", "wt")).reshape(1)
 
-    scalars = [info, deal, lengths, codes]
     state = []
     if not plan.square:
-        state = attend_part(plan, blk, nseq, 0, nb, True, scalars, q, kvs, state)
+        state = attend_part(plan, blk, 0, nb, True, info, lists, q, kvs, state)
     else:
-        state = attend_part(plan, blk, nseq, 0, 1, False, scalars, q, kvs, state)
+        state = attend_part(plan, blk, 0, 1, False, info, lists, q, kvs, state)
         if packed:
-            two = jnp.stack([piece, plan.swap(piece, (0, 2))])
-            two = after(two, state[0])
-            other = plan.swap(two, (0, 1))
+            stack = jnp.concatenate([two, near])
+            stack = after(stack, kvs[3])
+            kvs = kvs[:3] + [after(kvs[3], stack)]
         state = [after(state[0], kvs[3]), *state[1:]]
-        state = attend_part(plan, blk, nseq, 1, 3, False, scalars, q, kvs, state)
+        state = attend_part(plan, blk, 1, 3, False, info, lists, q, kvs, state)
         if packed:
-            stack = jnp.concatenate([two, other])
-            stack = after(stack, state[0])
             one, side = plan.turn(stack, True), plan.turn(stack, False)
             stack_sib = plan.swap(stack, core)
-        state = attend_part(plan, blk, nseq, 3, 4, True, scalars, q, kvs, state)
+        state = attend_part(plan, blk, 3, 4, True, info, lists, q, kvs, state)
     o, o_sib, of32, lse = state[3:]
     o_sib = plan.swap(o_sib, core)
     if packed:
@@ -951,11 +969,11 @@
             g_far = (g_all[2:].astype(F32) + g_core[2:].astype(F32)).astype(BF16)
             extra = [after(of32, g_far)] + extra[1:]
             g_far = plan.turn(g_far, False)
-        part = attend_back_part(plan, blk, nseq, 2, 4, True, False, scalars, q, lse, kvs, extra)
+        part = attend_back_part(plan, blk, 2, 4, True, False, info, lists, q, lse, kvs, extra)
         dkv2, dkv3, dq_part, g_ext, delta = part
         far = [plan.turn(d, False) for d in (dkv3, dkv2)]
         dkv1, dq_part = attend_back_part(
-            plan, blk, nseq, 1, 2, False, False, scalars, q, lse, kvs, [g_ext, delta, dq_part]
+            plan, blk, 1, 2, False, False, info, lists, q, lse, kvs, [g_ext, delta, dq_part]
         )
         mid = plan.turn((dkv1.astype(F32) + far[0].astype(F32)).astype(BF16), True)
         if packed:
@@ -965,7 +983,7 @@
             dq_part = after(dq_part, g_mid)
             g_mid = plan.turn(g_mid, True)
         dkv0, _, dq = attend_back_part(
-            plan, blk, nseq, 0, 1, False, True, scalars, q, lse, kvs, [g_ext, delta, dq_part]
+            plan, blk, 0, 1, False, True, info, lists, q, lse, kvs, [g_ext, delta, dq_part]
         )
         if packed:
             g_mid = after(g_mid, dkv0)
@@ -975,7 +993,7 @@
             g_other = plan.swap(g_near[2:], (0, 1))
         parts = [dkv0, far[1], mid]
     else:
-        part = attend_back_part(plan, blk, nseq, 0, nb, True, True, scalars, q, lse, kvs, extra)
+        part = attend_back_part(plan, blk, 0, nb, True, True, info, lists, q, lse, kvs, extra)
         dq = part[-1]
         parts = [part[0]] + [plan.swap(part[b], plan.groups[b]) for b in range(1, nb)]
 
@@ -1048,8 +1066,6 @@
         both = lax.dynamic_slice_in_dim(both, wt * shard, shard, 1)
         g_gain, g_shift = both[0], both[1]
         loss = lax.psum(square[0, 0], ("ctx", "wt")) / (count[0] * width)
-    if packed:
-        loads = loads[:3] + [after(loads[3], g_up)]
     own_heads = jnp.stack([x[blk:] for x in loads[:nj]])
     if n_wt > nj:
         own_heads = (own_heads.astype(F32) + jnp.stack(loads[nj:]).astype(F32)).astype(BF16)

time: 235 us -> 224 us (0.953); the launches traced: 231 us -> 223 us
  starting transfers between devices: 58.9 us -> 47.3 us
    ppermute x16, starting transfers between devices: 30.4 us -> 19.4 us  [turn(): return lax.ppermute(x, ('ctx', 'wt'), perm)]
    ppermute x29, waiting for transfers between devices: 43.2 us -> 47.1 us  [swap(): return lax.ppermute(x, ('ctx', 'wt'), perm)]
    pallas_call x15 -> x16, Pallas kernels: 77.9 us -> 79.3 us  [call(): pl.pallas_call(body, name=name, out_shape=list(outs), in_specs=in_specs,...]
    unnamed x84 -> x82, local copies, waits for them, and re-layouts: 7.67 us -> 7.51 us
  transfers between devices with their start and end apart: 45 -> 45, of which waited for: 19 -> 18; matrix products, arithmetic and copies ran while one was open for 7% -> 8% of each run, Pallas kernels for 21% -> 23%
where the time goes in v4:
time: 224 us; the launch traced here: 223 us
  Pallas kernels  79.3 us (35%)
  waiting for transfers between devices  67.8 us (30%)
  starting transfers between devices  47.3 us (21%)
  other arithmetic  14.6 us (7%)
  local copies, waits for them, and re-layouts  12 us (5%)
    pallas_call x16, Pallas kernels, call(): pl.pallas_call(body, name=name, out_shape=list(outs), in_specs=in_specs,...  79.3 us
    ppermute x29, waiting for transfers between devices, swap(): return lax.ppermute(x, ('ctx', 'wt'), perm)  47.1 us
    ppermute x29, starting transfers between devices, swap(): return lax.ppermute(x, ('ctx', 'wt'), perm)  27.9 us
    ppermute x16, waiting for transfers between devices, turn(): return lax.ppermute(x, ('ctx', 'wt'), perm)  20.8 us
    ppermute x16, starting transfers between devices, turn(): return lax.ppermute(x, ('ctx', 'wt'), perm)  19.4 us
    unnamed x82, local copies, waits for them, and re-layouts  7.51 us
  transfers between devices with their start and end apart: 45, of which 18 were waited for; matrix products, arithmetic and copies ran while one was open for 8% of the time, Pallas kernels for 23%

profile of v4, /device:TPU:0, one launch (start us, length us, event | category | flops | bytes accessed | tf_op | source)
XLA Modules:
  0.0 223.0 jit_solution(15367303159477473318)
XLA Ops:
  4.9 3.0 %collective-permute-start = (bf16[256,512]{1,0:T(8,128)(2,1)}, bf16[256,512]{1,0:T(8,128)(2,1)S(1)}, u32[]{:S(2)}, u32[]{:S(2)}) collective-permute-start(bf16[256,512]{1,0:T(8,128)(2,1)} %get-tuple-element.91), channel_id=1, source_target_pairs={{0,1},{1,0},{2,3},{3,2},{4,5},{5,4},{6,7},{7,6},{8,9},{9,8},{10,11... | collective-permute-start | bytes 786440 | tf_op jit(solution)/shard_map/ppermute | solution.py:98
  7.9 2.6 %collective-permute-start.1 = (bf16[256,512]{1,0:T(8,128)(2,1)}, bf16[256,512]{1,0:T(8,128)(2,1)S(1)}, u32[]{:S(2)}, u32[]{:S(2)}) collective-permute-start(bf16[256,512]{1,0:T(8,128)(2,1)} %get-tuple-element.92), channel_id=1, source_target_pairs={{0,2},{1,3},{2,0},{3,1},{4,6},{5,7},{6,4},{7,5},{8,10},{9,11},{10,... | collective-permute-start | bytes 786440 | tf_op jit(solution)/shard_map/ppermute | solution.py:98
  11.0 2.6 %lists.1 = (s32[264]{0:T(512)}, s32[264]{0:T(512)}, s32[264]{0:T(512)}, s32[264]{0:T(512)}, s32[264]{0:T(512)}) custom-call(s32[2]{0:T(128)} %pad_add_fusion.info, s32[32]{0:T(128)} %deal.1, s32[4]{0:T(128)} %lengths.1, s32[8]{0:T(128)} %call_exported.0.codes), custom_call_target="tpu_custom_call" | custom-call | bytes 5464 | tf_op jit(solution)/shard_map/lists/pallas_call | solution.py:53
  13.6 5.7 %collective-permute-done.refs_1_.refs_9_ = bf16[256,512]{1,0:T(8,128)(2,1)S(1)} collective-permute-done((bf16[256,512]{1,0:T(8,128)(2,1)}, bf16[256,512]{1,0:T(8,128)(2,1)S(1)}, u32[]{:S(2)}, u32[]{:S(2)}) %collective-permute-start) | collective-permute-done | bytes 262176 | tf_op jit(solution)/shard_map/ppermute | solution.py:98
  19.3 10.2 %collective-permute-done.1.refs_2_.refs_10_ = bf16[256,512]{1,0:T(8,128)(2,1)S(1)} collective-permute-done((bf16[256,512]{1,0:T(8,128)(2,1)}, bf16[256,512]{1,0:T(8,128)(2,1)S(1)}, u32[]{:S(2)}, u32[]{:S(2)}) %collective-permute-start.1) | collective-permute-done | bytes 262176 | tf_op jit(solution)/shard_map/ppermute | solution.py:98
  35.3 4.8 %project.1 = (bf16[8,192,128]{2,1,0:T(8,128)(2,1)}, bf16[8,192,128]{2,1,0:T(8,128)(2,1)}, bf16[8,192,512]{2,1,0:T(8,128)(2,1)}, bf16[512,256]{1,0:T(8,128)(2,1)}, f32[8,512]{1,0:T(8,128)}) custom-call(s32[2]{0:T(128)} %pad_add_fusion.info, bf16[256,512]{1,0:T(8,128)(2,1)} %get-tuple-element.90.refs_0_.refs_8_, bf16[256,512]{1,0:T(8,128)(2,1)} %copy-done.4, ...), custom_call_target="tpu_custom_call" | custom-call | flops 402653184 | bytes 5783560 | tf_op jit(solution)/shard_map/project/pallas_call | solution.py:53
  41.7 5.4 %collective-permute-start.9 = (bf16[10,16,512]{2,1,0:T(8,128)(2,1)S(1)}, bf16[10,16,512]{2,1,0:T(8,128)(2,1)S(1)}, u32[]{:S(2)}, u32[]{:S(2)}) collective-permute-start(bf16[10,16,512]{2,1,0:T(8,128)(2,1)S(1)} %maximum_maximum_fusion), channel_id=1, source_target_pairs={{0,2},{1,3},{2,0},{3,1},{4,6},{5,7},{6,4},{7,5},{8,10},{9,11},{10,... | collective-permute-start | bytes 491528 | tf_op jit(solution)/shard_map/ppermute | solution.py:98
  47.0 8.1 %collective-permute-done.9 = bf16[10,16,512]{2,1,0:T(8,128)(2,1)S(1)} collective-permute-done((bf16[10,16,512]{2,1,0:T(8,128)(2,1)S(1)}, bf16[10,16,512]{2,1,0:T(8,128)(2,1)S(1)}, u32[]{:S(2)}, u32[]{:S(2)}) %collective-permute-start.9) | collective-permute-done | bytes 163872 | tf_op jit(solution)/shard_map/ppermute | solution.py:98
  57.3 5.4 %attend.3 = (f32[8,1,192]{2,1,0:T(1,128)}, f32[8,1,192]{2,1,0:T(1,128)}, f32[8,128,192]{2,1,0:T(8,128)}) custom-call(s32[2]{0:T(128)} %pad_add_fusion.info, s32[264]{0:T(512)} %get-tuple-element.95.pairs, bf16[8,192,128]{2,1,0:T(8,128)(2,1)} %get-tuple-element.99.q_ref, bf16[8,192,128]{2,1,0:T(8,128)(2,1)} %get-tuple-element.100.refs_0_), custom_call_target="tpu_custom_call" | custom-call | flops 2113929216 | bytes 1586216 | tf_op jit(solution)/shard_map/attend/pallas_call | solution.py:53
  68.1 7.1 %attend.4 = (f32[8,1,192]{2,1,0:T(1,128)}, f32[8,1,192]{2,1,0:T(1,128)}, f32[8,128,192]{2,1,0:T(8,128)}) custom-call(s32[2]{0:T(128)} %pad_add_fusion.info, s32[264]{0:T(512)} %get-tuple-element.105.pairs, bf16[8,192,128]{2,1,0:T(8,128)(2,1)} %get-tuple-element.99.q_ref, bf16[8,192,128]{2,1,0:T(8,128)(2,1)} %copy-done.31, bf16[8,192,128]{2,1,0:T(8,128)(2,1)} %copy-done.33, ...), custom_call_target="tpu_custom_call" | custom-call | flops 4227858432 | bytes 2778152 | tf_op jit(solution)/shard_map/attend/pallas_call | solution.py:53
  75.2 6.6 %attend.5 = (f32[8,1,192]{2,1,0:T(1,128)}, f32[8,1,192]{2,1,0:T(1,128)}, f32[8,128,192]{2,1,0:T(8,128)}, bf16[4,192,128]{2,1,0:T(8,128)(2,1)}, bf16[4,192,128]{2...) custom-call(s32[2]{0:T(128)} %pad_add_fusion.info, s32[264]{0:T(512)} %get-tuple-element.98.pairs, ...), custom_call_target="tpu_custom_call" | custom-call | flops 2113929216 | bytes 3570728 | tf_op jit(solution)/shard_map/attend/pallas_call | solution.py:53
  86.5 3.2 %collective-permute-start.14 = (bf16[192,128]{1,0:T(8,128)(2,1)S(1)}, bf16[192,128]{1,0:T(8,128)(2,1)S(1)}, u32[]{:S(2)}, u32[]{:S(2)}) collective-permute-start(bf16[192,128]{1,0:T(8,128)(2,1)S(1)} %get-tuple-element.170), channel_id=1, source_target_pairs={{0,2},{1,3},{2,0},{3,1},{4,6},{5,7},{6,4},{7,5},{8,10},{9,11},{10,... | collective-permute-start | bytes 147464 | tf_op jit(solution)/shard_map/ppermute | solution.py:98
  91.2 2.9 %collective-permute-done.14.refs_7_.refs_2_ = bf16[192,128]{1,0:T(8,128)(2,1)S(1)} collective-permute-done((bf16[192,128]{1,0:T(8,128)(2,1)S(1)}, bf16[192,128]{1,0:T(8,128)(2,1)S(1)}, u32[]{:S(2)}, u32[]{:S(2)}) %collective-permute-start.14) | collective-permute-done | bytes 49184 | tf_op jit(solution)/shard_map/ppermute | solution.py:98
  96.8 9.0 %mlp.1 = (bf16[192,512]{1,0:T(8,128)(2,1)}, f32[8,128]{1,0:T(8,128)}, f32[192,512]{1,0:T(8,128)}, bf16[192,128]{1,0:T(8,128)(2,1)}, bf16[192,128]{1,0:T(8,128)(2...) custom-call(s32[2]{0:T(128)} %pad_add_fusion.info, ...), custom_call_target="tpu_custom_call" | custom-call | flops 1610612736 | bytes 8819468 | tf_op jit(solution)/shard_map/mlp/pallas_call | solution.py:53
  105.9 4.4 %mlp_grads.1 = (bf16[4,4,10,16,512]{4,3,2,1,0:T(8,128)(2,1)}, bf16[4,4,10,16,512]{4,3,2,1,0:T(8,128)(2,1)}) custom-call(s32[2]{0:T(128)} %pad_add_fusion.info, bf16[4,192,512]{2,1,0:T(8,128)(2,1)} %get-tuple-element.119.act_ref, bf16[4,192,512]{2,1,0:T(8,128)(2,1)} %get-tuple-element.120.gpre_ref, bf16[192,512]{1,0:T(8,128)(2,1)} %get-tuple-element.121.n2_ref, ...), custom_call_target="tpu_custom_call" | custom-call | flops 805306368 | bytes 7622664 | tf_op jit(solution)/shard_map/mlp_grads/pallas_call | solution.py:53
  110.4 2.6 %collective-permute-start.24 = (bf16[192,128]{1,0:T(8,128)(2,1)S(1)}, bf16[192,128]{1,0:T(8,128)(2,1)S(1)}, u32[]{:S(2)}, u32[]{:S(2)}) collective-permute-start(bf16[192,128]{1,0:T(8,128)(2,1)S(1)} %copy-done.40), channel_id=1, source_target_pairs={{0,1},{1,0},{2,3},{3,2},{4,5},{5,4},{6,7},{7,6},{8,9},{9,8},{10,11... | collective-permute-start | bytes 147464 | tf_op jit(solution)/shard_map/ppermute | solution.py:98
  115.4 4.2 %collective-permute-done.25.refs_5_ = bf16[192,128]{1,0:T(8,128)(2,1)S(1)} collective-permute-done((bf16[192,128]{1,0:T(8,128)(2,1)S(1)}, bf16[192,128]{1,0:T(8,128)(2,1)S(1)}, u32[]{:S(2)}, u32[]{:S(2)}) %collective-permute-start.25) | collective-permute-done | bytes 49184 | tf_op jit(solution)/shard_map/ppermute | solution.py:98
  119.7 2.9 %add_convert_fusion = bf16[2,4,10,16,512]{4,3,2,1,0:T(8,128)(2,1)} fusion(bf16[4,4,10,16,512]{4,3,2,1,0:T(8,128)(2,1)S(1)} %collective-permute-done.22, bf16[4,4,10,16,512]{4,3,2,1,0:T(8,128)(2,1)} %get-tuple-element.125), kind=kLoop, calls=%fused_computation | loop fusion | flops 2621440 | bytes 3932160 | tf_op jit(solution)/shard_map/convert_element_type | solution.py:969
  122.7 2.8 %collective-permute-start.23 = (bf16[2,4,10,16,512]{4,3,2,1,0:T(8,128)(2,1)}, bf16[2,4,10,16,512]{4,3,2,1,0:T(8,128)(2,1)}, u32[]{:S(2)}, u32[]{:S(2)}) collective-permute-start(bf16[2,4,10,16,512]{4,3,2,1,0:T(8,128)(2,1)} %add_convert_fusion), channel_id=1, source_target_pairs={{0,16},{1,17},{2,18},{3,19},{4,12},{5,13},{6,14},{7,15},{8,24},{9,... | collective-permute-start | bytes 3932168 | tf_op jit(solution)/shard_map/ppermute | solution.py:106
  126.2 8.1 %attend_back.3 = (bf16[8,192,128]{2,1,0:T(8,128)(2,1)}, bf16[8,192,128]{2,1,0:T(8,128)(2,1)}, f32[8,128,192]{2,1,0:T(8,128)}, bf16[8,192,128]{2,1,0:T(8,128)(2,1)}, f32[8,1,192]{2,1,0:T(1,128)}) custom-call(s32[2]{0:T(128)} %pad_add_fusion.info, s32[264]{0:T(512)} %get-tuple-element.129.pairs, bf16[8,192,128]{2,1,0:T(8,128)(2,1)} %get-tuple-element.99.q_ref, ...), custom_call_target="tpu_custom_call" | custom-call | flops 10569646080 | bytes 4338728 | tf_op jit(solution)/shard_map/attend_back/pallas_call | solution.py:53
  136.4 5.8 %attend_back.4 = (bf16[8,192,128]{2,1,0:T(8,128)(2,1)}, f32[8,128,192]{2,1,0:T(8,128)}) custom-call(s32[2]{0:T(128)} %pad_add_fusion.info, s32[264]{0:T(512)} %get-tuple-element.127.pairs, bf16[8,192,128]{2,1,0:T(8,128)(2,1)} %get-tuple-element.99.q_ref, f32[8,1,192]{2,1,0:T(1,128)} %get-tuple-element.128.lse_ref, bf16[8,192,128]{2,1,0:T(8,128)(2,1)} %copy-done.31, ...), custom_call_target="tpu_custom_call" | custom-call | flops 5284823040 | bytes 3159080 | tf_op jit(solution)/shard_map/attend_back/pallas_call | solution.py:53
  146.8 5.5 %collective-permute-done.32 = bf16[8,192,128]{2,1,0:T(8,128)(2,1)} collective-permute-done((bf16[8,192,128]{2,1,0:T(8,128)(2,1)}, bf16[8,192,128]{2,1,0:T(8,128)(2,1)}, u32[]{:S(2)}, u32[]{:S(2)}) %collective-permute-start.32) | collective-permute-done | bytes 393248 | tf_op jit(solution)/shard_map/ppermute | solution.py:106
  154.2 3.2 %collective-permute-start.33 = (bf16[8,192,128]{2,1,0:T(8,128)(2,1)}, bf16[8,192,128]{2,1,0:T(8,128)(2,1)}, u32[]{:S(2)}, u32[]{:S(2)}) collective-permute-start(bf16[8,192,128]{2,1,0:T(8,128)(2,1)} %add_convert_fusion.2), channel_id=1, source_target_pairs={{0,8},{1,9},{2,10},{3,11},{4,20},{5,21},{6,22},{7,23},{8,0},{9,1},... | collective-permute-start | bytes 1179656 | tf_op jit(solution)/shard_map/ppermute | solution.py:106
  157.4 7.5 %attend_back.5 = (bf16[8,192,128]{2,1,0:T(8,128)(2,1)}, f32[8,128,192]{2,1,0:T(8,128)}, bf16[8,192,128]{2,1,0:T(8,128)(2,1)}) custom-call(s32[2]{0:T(128)} %pad_add_fusion.info, s32[264]{0:T(512)} %get-tuple-element.95.pairs, bf16[8,192,128]{2,1,0:T(8,128)(2,1)} %get-tuple-element.99.q_ref, f32[8,1,192]{2,1,0:T(1,128)} %get-tuple-element.128.lse_ref, ...), custom_call_target="tpu_custom_call" | custom-call | flops 5284823040 | bytes 3552296 | tf_op jit(solution)/shard_map/attend_back/pallas_call | solution.py:53
  164.9 2.6 %fusion = bf16[4,10,16,512]{3,2,1,0:T(8,128)(2,1)} fusion(bf16[4,10,16,512]{3,2,1,0:T(8,128)(2,1)} %collective-permute-done.28, bf16[4,4,10,16,512]{4,3,2,1,0:T(8,128)(2,1)S(1)} %collective-permute-done.22, bf16[2,4,10,16,512]{4,3,2,1,0:T(8,128)(2,1)} %collective-permute-done.23, bf16[4,4,10,16,512]{4,3,2,1,0:T(8,128)(2,1)S(1)} %copy-done.2), kind=kLoop, calls=%fused_computation.3 | loop fusion | flops 2621440 | bytes 3276800 | tf_op jit(solution)/shard_map/convert_element_type | solution.py:991
  168.2 5.8 %head_grads.1 = (bf16[4,192,512]{2,1,0:T(8,128)(2,1)}, bf16[4,192,512]{2,1,0:T(8,128)(2,1)}, bf16[4,64,512]{2,1,0:T(8,128)(2,1)}) custom-call(s32[2]{0:T(128)} %pad_add_fusion.info, bf16[8,192,128]{2,1,0:T(8,128)(2,1)} %get-tuple-element.146.dq_ref, bf16[512,256]{1,0:T(8,128)(2,1)} %get-tuple-element.147.wh_ref, ...), custom_call_target="tpu_custom_call" | custom-call | flops 805306368 | bytes 7340040 | tf_op jit(solution)/shard_map/head_grads/pallas_call | solution.py:53
  174.8 6.0 %collective-permute-done.35 = bf16[4,64,512]{2,1,0:T(8,128)(2,1)S(1)} collective-permute-done((bf16[4,64,512]{2,1,0:T(8,128)(2,1)}, bf16[4,64,512]{2,1,0:T(8,128)(2,1)S(1)}, u32[]{:S(2)}, u32[]{:S(2)}) %collective-permute-start.35) | collective-permute-done | bytes 262176 | tf_op jit(solution)/shard_map/ppermute | solution.py:106
  184.6 3.6 %collective-permute-done.36.more_ref = bf16[4,64,512]{2,1,0:T(8,128)(2,1)S(1)} collective-permute-done((bf16[4,64,512]{2,1,0:T(8,128)(2,1)S(1)}, bf16[4,64,512]{2,1,0:T(8,128)(2,1)S(1)}, u32[]{:S(2)}, u32[]{:S(2)}) %collective-permute-start.36) | collective-permute-done | bytes 262176 | tf_op jit(solution)/shard_map/ppermute | solution.py:106
  194.2 2.5 %collective-permute-start.42 = (bf16[256,512]{1,0:T(8,128)(2,1)}, bf16[256,512]{1,0:T(8,128)(2,1)S(1)}, u32[]{:S(2)}, u32[]{:S(2)}) collective-permute-start(bf16[256,512]{1,0:T(8,128)(2,1)} %get-tuple-element.159), channel_id=1, source_target_pairs={{0,2},{1,3},{2,0},{3,1},{4,6},{5,7},{6,4},{7,5},{8,10},{9,11},{10,... | collective-permute-start | bytes 786440 | tf_op jit(solution)/shard_map/ppermute | solution.py:98
  202.8 2.8 %collective-permute-done.39 = bf16[10,16,512]{2,1,0:T(8,128)(2,1)S(1)} collective-permute-done((bf16[10,16,512]{2,1,0:T(8,128)(2,1)S(1)}, bf16[10,16,512]{2,1,0:T(8,128)(2,1)S(1)}, u32[]{:S(2)}, u32[]{:S(2)}) %collective-permute-start.39) | collective-permute-done | bytes 163872 | tf_op jit(solution)/shard_map/ppermute | solution.py:106
  205.8 7.4 %collective-permute-done.42.refs_2_ = bf16[256,512]{1,0:T(8,128)(2,1)S(1)} collective-permute-done((bf16[256,512]{1,0:T(8,128)(2,1)}, bf16[256,512]{1,0:T(8,128)(2,1)S(1)}, u32[]{:S(2)}, u32[]{:S(2)}) %collective-permute-start.42) | collective-permute-done | bytes 262176 | tf_op jit(solution)/shard_map/ppermute | solution.py:98
  220.2 2.8 %unpack.1 = (f32[128,2048]{1,0:T(8,128)}, f32[512,512]{1,0:T(8,128)}, f32[128,512]{1,0:T(8,128)}, f32[1,1]{1,0:T(1,128)}, f32[1,128]{1,0:T(1,128)}, /*index=5*/f32[1,128]{1,0:T(1,128)}) custom-call(s32[2]{0:T(128)} %pad_add_fusion.info, f32[8,128]{1,0:T(8,128)} %get-tuple-element.118.sq_ref, bf16[4,10,16,512]{3,2,1,0:T(8,128)(2,1)} %copy-done.1, ...), custom_call_target="tpu_custom_call" | custom-call | bytes 3675148 | tf_op jit(solution)/shard_map/unpack/pallas_call | solution.py:53
  (188 shorter events, 64.0 us)
Async XLA Ops:
  4.9 14.4 %collective-permute-start = (bf16[256,512]{1,0:T(8,128)(2,1)}, bf16[256,512]{1,0:T(8,128)(2,1)S(1)}, u32[]{:S(2)}, u32[]{:S(2)}) collective-permute-start(bf16[256,512]{1,0:T(8,128)(2,1)} %get-tuple-element.91), channel_id=1, source_target_pairs={{0,1},{1,0},{2,3},{3,2},{4,5},{5,4},{6,7},{7,6},{8,9},{9,8},{10,11... | collective-permute-start | bytes 786440 | tf_op jit(solution)/shard_map/ppermute | solution.py:98
  7.9 21.6 %collective-permute-start.1 = (bf16[256,512]{1,0:T(8,128)(2,1)}, bf16[256,512]{1,0:T(8,128)(2,1)S(1)}, u32[]{:S(2)}, u32[]{:S(2)}) collective-permute-start(bf16[256,512]{1,0:T(8,128)(2,1)} %get-tuple-element.92), channel_id=1, source_target_pairs={{0,2},{1,3},{2,0},{3,1},{4,6},{5,7},{6,4},{7,5},{8,10},{9,11},{10,... | collective-permute-start | bytes 786440 | tf_op jit(solution)/shard_map/ppermute | solution.py:98
  10.5 19.0 %collective-permute-start.2 = (bf16[256,512]{1,0:T(8,128)(2,1)}, bf16[256,512]{1,0:T(8,128)(2,1)S(1)}, u32[]{:S(2)}, u32[]{:S(2)}) collective-permute-start(bf16[256,512]{1,0:T(8,128)(2,1)} %get-tuple-element.93), channel_id=1, source_target_pairs={{0,3},{1,2},{2,1},{3,0},{4,7},{5,6},{6,5},{7,4},{8,11},{9,10},{10,... | collective-permute-start | bytes 786440 | tf_op jit(solution)/shard_map/ppermute | solution.py:98
  10.5 23.1 %collective-permute-start.3 = (bf16[256,512]{1,0:T(8,128)(2,1)}, bf16[256,512]{1,0:T(8,128)(2,1)S(1)}, u32[]{:S(2)}, u32[]{:S(2)}) collective-permute-start(bf16[256,512]{1,0:T(8,128)(2,1)} %get-tuple-element.90.refs_0_.refs_8_), channel_id=1, source_target_pairs={{0,4},{1,5},{2,6},{3,7},{4,0},{5,1},{6,2},{7,3},{8,12},{9,13},{10,... | collective-permute-start | bytes 786440 | tf_op jit(solution)/shard_map/ppermute | solution.py:98
  19.3 14.4 %collective-permute-start.4 = (bf16[256,512]{1,0:T(8,128)(2,1)S(1)}, bf16[256,512]{1,0:T(8,128)(2,1)S(1)}, u32[]{:S(2)}, u32[]{:S(2)}) collective-permute-start(bf16[256,512]{1,0:T(8,128)(2,1)S(1)} %collective-permute-done.refs_1_.refs_9_), channel_id=1, source_target_pairs={{0,4},{1,5},{2,6},{3,7},{4,0},{5,1},{6,2},{7,3},{8,12},{9,13},{10,... | collective-permute-start | bytes 786440 | tf_op jit(solution)/shard_map/ppermute | solution.py:98
  40.1 15.1 %collective-permute-start.7 = (bf16[8,192,128]{2,1,0:T(8,128)(2,1)}, bf16[8,192,128]{2,1,0:T(8,128)(2,1)S(1)}, u32[]{:S(2)}, u32[]{:S(2)}) collective-permute-start(bf16[8,192,128]{2,1,0:T(8,128)(2,1)} %get-tuple-element.100.refs_0_), channel_id=1, source_target_pairs={{0,8},{1,9},{2,10},{3,11},{4,20},{5,21},{6,22},{7,23},{8,0},{9,1},... | collective-permute-start | bytes 1179656 | tf_op jit(solution)/shard_map/ppermute | solution.py:106
  41.7 13.5 %collective-permute-start.9 = (bf16[10,16,512]{2,1,0:T(8,128)(2,1)S(1)}, bf16[10,16,512]{2,1,0:T(8,128)(2,1)S(1)}, u32[]{:S(2)}, u32[]{:S(2)}) collective-permute-start(bf16[10,16,512]{2,1,0:T(8,128)(2,1)S(1)} %maximum_maximum_fusion), channel_id=1, source_target_pairs={{0,2},{1,3},{2,0},{3,1},{4,6},{5,7},{6,4},{7,5},{8,10},{9,11},{10,... | collective-permute-start | bytes 491528 | tf_op jit(solution)/shard_map/ppermute | solution.py:98
  55.2 9.4 %collective-permute-start.10 = (bf16[2,10,16,512]{3,2,1,0:T(8,128)(2,1)S(1)}, bf16[2,10,16,512]{3,2,1,0:T(8,128)(2,1)S(1)}, u32[]{:S(2)}, u32[]{:S(2)}) collective-permute-start(bf16[2,10,16,512]{3,2,1,0:T(8,128)(2,1)S(1)} %pad_maximum_fusion.3), channel_id=1, source_target_pairs={{0,1},{1,0},{2,3},{3,2},{4,5},{5,4},{6,7},{7,6},{8,9},{9,8},{10,11... | collective-permute-start | bytes 983048 | tf_op jit(solution)/shard_map/ppermute | solution.py:98
  55.2 9.4 %collective-permute-start.8 = (bf16[8,192,128]{2,1,0:T(8,128)(2,1)S(1)}, bf16[8,192,128]{2,1,0:T(8,128)(2,1)S(1)}, u32[]{:S(2)}, u32[]{:S(2)}) collective-permute-start(bf16[8,192,128]{2,1,0:T(8,128)(2,1)S(1)} %collective-permute-done.7.refs_0_), channel_id=1, source_target_pairs={{0,16},{1,17},{2,18},{3,19},{4,12},{5,13},{6,14},{7,15},{8,24},{9,... | collective-permute-start | bytes 1179656 | tf_op jit(solution)/shard_map/ppermute | solution.py:106
  55.8 11.5 %collective-permute-start.11 = (bf16[8,192,128]{2,1,0:T(8,128)(2,1)}, bf16[8,192,128]{2,1,0:T(8,128)(2,1)S(1)}, u32[]{:S(2)}, u32[]{:S(2)}) collective-permute-start(bf16[8,192,128]{2,1,0:T(8,128)(2,1)} %get-tuple-element.100.refs_0_), channel_id=1, source_target_pairs={{0,16},{1,17},{2,18},{3,19},{4,12},{5,13},{6,14},{7,15},{8,24},{9,... | collective-permute-start | bytes 1179656 | tf_op jit(solution)/shard_map/ppermute | solution.py:106
  64.7 18.9 %collective-permute-start.17 = (bf16[4,10,16,512]{3,2,1,0:T(8,128)(2,1)S(1)}, bf16[4,10,16,512]{3,2,1,0:T(8,128)(2,1)S(1)}, u32[]{:S(2)}, u32[]{:S(2)}) collective-permute-start(bf16[4,10,16,512]{3,2,1,0:T(8,128)(2,1)S(1)} %pad_maximum_fusion.1.refs_9_), channel_id=1, source_target_pairs={{0,16},{1,17},{2,18},{3,19},{4,12},{5,13},{6,14},{7,15},{8,24},{9,... | collective-permute-start | bytes 1966088 | tf_op jit(solution)/shard_map/ppermute | solution.py:106
  64.7 18.8 %collective-permute-start.16 = (bf16[4,10,16,512]{3,2,1,0:T(8,128)(2,1)S(1)}, bf16[4,10,16,512]{3,2,1,0:T(8,128)(2,1)S(1)}, u32[]{:S(2)}, u32[]{:S(2)}) collective-permute-start(bf16[4,10,16,512]{3,2,1,0:T(8,128)(2,1)S(1)} %pad_maximum_fusion.1.refs_9_), channel_id=1, source_target_pairs={{0,8},{1,9},{2,10},{3,11},{4,20},{5,21},{6,22},{7,23},{8,0},{9,1},... | collective-permute-start | bytes 1966088 | tf_op jit(solution)/shard_map/ppermute | solution.py:106
  83.5 10.9 %collective-permute-start.18 = (bf16[4,10,16,512]{3,2,1,0:T(8,128)(2,1)S(1)}, bf16[4,10,16,512]{3,2,1,0:T(8,128)(2,1)S(1)}, u32[]{:S(2)}, u32[]{:S(2)}) collective-permute-start(bf16[4,10,16,512]{3,2,1,0:T(8,128)(2,1)S(1)} %collective-permute-done.16), channel_id=1, source_target_pairs={{0,16},{1,17},{2,18},{3,19},{4,12},{5,13},{6,14},{7,15},{8,24},{9,... | collective-permute-start | bytes 1966088 | tf_op jit(solution)/shard_map/ppermute | solution.py:106
  83.7 13.1 %collective-permute-start.20 = (bf16[2,4,10,16,512]{4,3,2,1,0:T(8,128)(2,1)S(1)}, bf16[2,4,10,16,512]{4,3,2,1,0:T(8,128)(2,1)}, u32[]{:S(2)}, u32[]{:S(2)}) collective-permute-start(bf16[2,4,10,16,512]{4,3,2,1,0:T(8,128)(2,1)S(1)} %pad_maximum_fusion.refs_10_), channel_id=1, source_target_pairs={{0,4},{1,5},{2,6},{3,7},{4,0},{5,1},{6,2},{7,3},{8,12},{9,13},{10,... | collective-permute-start | bytes 3932168 | tf_op jit(solution)/shard_map/ppermute | solution.py:98
  86.5 7.6 %collective-permute-start.14 = (bf16[192,128]{1,0:T(8,128)(2,1)S(1)}, bf16[192,128]{1,0:T(8,128)(2,1)S(1)}, u32[]{:S(2)}, u32[]{:S(2)}) collective-permute-start(bf16[192,128]{1,0:T(8,128)(2,1)S(1)} %get-tuple-element.170), channel_id=1, source_target_pairs={{0,2},{1,3},{2,0},{3,1},{4,6},{5,7},{6,4},{7,5},{8,10},{9,11},{10,... | collective-permute-start | bytes 147464 | tf_op jit(solution)/shard_map/ppermute | solution.py:98
  110.2 9.5 %collective-permute-start.22 = (bf16[4,4,10,16,512]{4,3,2,1,0:T(8,128)(2,1)}, bf16[4,4,10,16,512]{4,3,2,1,0:T(8,128)(2,1)S(1)}, u32[]{:S(2)}, u32[]{:S(2)}) collective-permute-start(bf16[4,4,10,16,512]{4,3,2,1,0:T(8,128)(2,1)} %get-tuple-element.126), channel_id=1, source_target_pairs={{0,4},{1,5},{2,6},{3,7},{4,0},{5,1},{6,2},{7,3},{8,12},{9,13},{10,... | collective-permute-start | bytes 7864328 | tf_op jit(solution)/shard_map/ppermute | solution.py:98
  113.0 6.6 %collective-permute-start.25 = (bf16[192,128]{1,0:T(8,128)(2,1)S(1)}, bf16[192,128]{1,0:T(8,128)(2,1)S(1)}, u32[]{:S(2)}, u32[]{:S(2)}) collective-permute-start(bf16[192,128]{1,0:T(8,128)(2,1)S(1)} %copy-done.39), channel_id=1, source_target_pairs={{0,2},{1,3},{2,0},{3,1},{4,6},{5,7},{6,4},{7,5},{8,10},{9,11},{10,... | collective-permute-start | bytes 147464 | tf_op jit(solution)/shard_map/ppermute | solution.py:98
  113.0 6.6 %collective-permute-start.26 = (bf16[192,128]{1,0:T(8,128)(2,1)S(1)}, bf16[192,128]{1,0:T(8,128)(2,1)S(1)}, u32[]{:S(2)}, u32[]{:S(2)}) collective-permute-start(bf16[192,128]{1,0:T(8,128)(2,1)S(1)} %copy-done.38), channel_id=1, source_target_pairs={{0,3},{1,2},{2,1},{3,0},{4,7},{5,6},{6,5},{7,4},{8,11},{9,10},{10,... | collective-permute-start | bytes 147464 | tf_op jit(solution)/shard_map/ppermute | solution.py:98
  122.7 19.5 %collective-permute-start.23 = (bf16[2,4,10,16,512]{4,3,2,1,0:T(8,128)(2,1)}, bf16[2,4,10,16,512]{4,3,2,1,0:T(8,128)(2,1)}, u32[]{:S(2)}, u32[]{:S(2)}) collective-permute-start(bf16[2,4,10,16,512]{4,3,2,1,0:T(8,128)(2,1)} %add_convert_fusion), channel_id=1, source_target_pairs={{0,16},{1,17},{2,18},{3,19},{4,12},{5,13},{6,14},{7,15},{8,24},{9,... | collective-permute-start | bytes 3932168 | tf_op jit(solution)/shard_map/ppermute | solution.py:106
  134.3 33.2 %collective-permute-start.31 = (bf16[8,192,128]{2,1,0:T(8,128)(2,1)}, bf16[8,192,128]{2,1,0:T(8,128)(2,1)S(1)}, u32[]{:S(2)}, u32[]{:S(2)}) collective-permute-start(bf16[8,192,128]{2,1,0:T(8,128)(2,1)} %get-tuple-element.149), channel_id=1, source_target_pairs={{0,16},{1,17},{2,18},{3,19},{4,12},{5,13},{6,14},{7,15},{8,24},{9,... | collective-permute-start | bytes 1179656 | tf_op jit(solution)/shard_map/ppermute | solution.py:106
  135.1 17.2 %collective-permute-start.32 = (bf16[8,192,128]{2,1,0:T(8,128)(2,1)}, bf16[8,192,128]{2,1,0:T(8,128)(2,1)}, u32[]{:S(2)}, u32[]{:S(2)}) collective-permute-start(bf16[8,192,128]{2,1,0:T(8,128)(2,1)} %get-tuple-element.150), channel_id=1, source_target_pairs={{0,16},{1,17},{2,18},{3,19},{4,12},{5,13},{6,14},{7,15},{8,24},{9,... | collective-permute-start | bytes 1179656 | tf_op jit(solution)/shard_map/ppermute | solution.py:106
  144.5 20.3 %collective-permute-start.28 = (bf16[4,10,16,512]{3,2,1,0:T(8,128)(2,1)}, bf16[4,10,16,512]{3,2,1,0:T(8,128)(2,1)}, u32[]{:S(2)}, u32[]{:S(2)}) collective-permute-start(bf16[4,10,16,512]{3,2,1,0:T(8,128)(2,1)} %fusion.1), channel_id=1, source_target_pairs={{0,8},{1,9},{2,10},{3,11},{4,20},{5,21},{6,22},{7,23},{8,0},{9,1},... | collective-permute-start | bytes 1966088 | tf_op jit(solution)/shard_map/ppermute | solution.py:106
  154.2 13.3 %collective-permute-start.33 = (bf16[8,192,128]{2,1,0:T(8,128)(2,1)}, bf16[8,192,128]{2,1,0:T(8,128)(2,1)}, u32[]{:S(2)}, u32[]{:S(2)}) collective-permute-start(bf16[8,192,128]{2,1,0:T(8,128)(2,1)} %add_convert_fusion.2), channel_id=1, source_target_pairs={{0,8},{1,9},{2,10},{3,11},{4,20},{5,21},{6,22},{7,23},{8,0},{9,1},... | collective-permute-start | bytes 1179656 | tf_op jit(solution)/shard_map/ppermute | solution.py:106
  174.0 6.8 %collective-permute-start.35 = (bf16[4,64,512]{2,1,0:T(8,128)(2,1)}, bf16[4,64,512]{2,1,0:T(8,128)(2,1)S(1)}, u32[]{:S(2)}, u32[]{:S(2)}) collective-permute-start(bf16[4,64,512]{2,1,0:T(8,128)(2,1)} %get-tuple-element.153), channel_id=1, source_target_pairs={{0,8},{1,9},{2,10},{3,11},{4,20},{5,21},{6,22},{7,23},{8,0},{9,1},... | collective-permute-start | bytes 786440 | tf_op jit(solution)/shard_map/ppermute | solution.py:106
  174.0 8.7 %collective-permute-start.29 = (bf16[2,10,16,512]{3,2,1,0:T(8,128)(2,1)S(1)}, bf16[2,10,16,512]{3,2,1,0:T(8,128)(2,1)S(1)}, u32[]{:S(2)}, u32[]{:S(2)}) collective-permute-start(bf16[2,10,16,512]{3,2,1,0:T(8,128)(2,1)S(1)} %slice.88), channel_id=1, source_target_pairs={{0,1},{1,0},{2,3},{3,2},{4,5},{5,4},{6,7},{7,6},{8,9},{9,8},{10,11... | collective-permute-start | bytes 983048 | tf_op jit(solution)/shard_map/ppermute | solution.py:98
  174.7 13.5 %collective-permute-start.34 = (bf16[4,192,512]{2,1,0:T(8,128)(2,1)}, bf16[4,192,512]{2,1,0:T(8,128)(2,1)S(1)}, u32[]{:S(2)}, u32[]{:S(2)}) collective-permute-start(bf16[4,192,512]{2,1,0:T(8,128)(2,1)} %get-tuple-element.152), channel_id=1, source_target_pairs={{0,4},{1,5},{2,6},{3,7},{4,0},{5,1},{6,2},{7,3},{8,12},{9,13},{10,... | collective-permute-start | bytes 2359304 | tf_op jit(solution)/shard_map/ppermute | solution.py:98
  182.9 8.8 %collective-permute-start.30 = (bf16[10,16,512]{2,1,0:T(8,128)(2,1)S(1)}, bf16[10,16,512]{2,1,0:T(8,128)(2,1)S(1)}, u32[]{:S(2)}, u32[]{:S(2)}) collective-permute-start(bf16[10,16,512]{2,1,0:T(8,128)(2,1)S(1)} %slice_bitcast_fusion), channel_id=1, source_target_pairs={{0,2},{1,3},{2,0},{3,1},{4,6},{5,7},{6,4},{7,5},{8,10},{9,11},{10,... | collective-permute-start | bytes 491528 | tf_op jit(solution)/shard_map/ppermute | solution.py:98
  191.7 11.0 %collective-permute-start.41 = (bf16[256,512]{1,0:T(8,128)(2,1)}, bf16[256,512]{1,0:T(8,128)(2,1)S(1)}, u32[]{:S(2)}, u32[]{:S(2)}) collective-permute-start(bf16[256,512]{1,0:T(8,128)(2,1)} %get-tuple-element.158), channel_id=1, source_target_pairs={{0,1},{1,0},{2,3},{3,2},{4,5},{5,4},{6,7},{7,6},{8,9},{9,8},{10,11... | collective-permute-start | bytes 786440 | tf_op jit(solution)/shard_map/ppermute | solution.py:98
  192.2 10.5 %collective-permute-start.38 = (bf16[10,16,512]{2,1,0:T(8,128)(2,1)S(1)}, bf16[10,16,512]{2,1,0:T(8,128)(2,1)S(1)}, u32[]{:S(2)}, u32[]{:S(2)}) collective-permute-start(bf16[10,16,512]{2,1,0:T(8,128)(2,1)S(1)} %fusion.2), channel_id=1, source_target_pairs={{0,16},{1,17},{2,18},{3,19},{4,12},{5,13},{6,14},{7,15},{8,24},{9,... | collective-permute-start | bytes 491528 | tf_op jit(solution)/shard_map/ppermute | solution.py:106
  194.2 18.9 %collective-permute-start.42 = (bf16[256,512]{1,0:T(8,128)(2,1)}, bf16[256,512]{1,0:T(8,128)(2,1)S(1)}, u32[]{:S(2)}, u32[]{:S(2)}) collective-permute-start(bf16[256,512]{1,0:T(8,128)(2,1)} %get-tuple-element.159), channel_id=1, source_target_pairs={{0,2},{1,3},{2,0},{3,1},{4,6},{5,7},{6,4},{7,5},{8,10},{9,11},{10,... | collective-permute-start | bytes 786440 | tf_op jit(solution)/shard_map/ppermute | solution.py:98
  196.7 16.4 %collective-permute-start.43 = (bf16[256,512]{1,0:T(8,128)(2,1)}, bf16[256,512]{1,0:T(8,128)(2,1)S(1)}, u32[]{:S(2)}, u32[]{:S(2)}) collective-permute-start(bf16[256,512]{1,0:T(8,128)(2,1)} %get-tuple-element.160), channel_id=1, source_target_pairs={{0,3},{1,2},{2,1},{3,0},{4,7},{5,6},{6,5},{7,4},{8,11},{9,10},{10,... | collective-permute-start | bytes 786440 | tf_op jit(solution)/shard_map/ppermute | solution.py:98
  205.7 13.7 %collective-permute-start.40 = (bf16[4,10,16,512]{3,2,1,0:T(8,128)(2,1)S(1)}, bf16[4,10,16,512]{3,2,1,0:T(8,128)(2,1)S(1)}, u32[]{:S(2)}, u32[]{:S(2)}) collective-permute-start(bf16[4,10,16,512]{3,2,1,0:T(8,128)(2,1)S(1)} %pad_maximum_fusion.2.own), channel_id=1, source_target_pairs={{0,4},{1,5},{2,6},{3,7},{4,0},{5,1},{6,2},{7,3},{8,12},{9,13},{10,... | collective-permute-start | bytes 1966088 | tf_op jit(solution)/shard_map/ppermute | solution.py:98
  (54 other events, 302.8 us)

commit v5 on v4

--- a/solution.py
+++ b/solution.py
@@ -382,7 +382,7 @@
                 p = mask(k, p)
                 ds = (p * (slopes[k] - delta_ref[i])).astype(BF16)
                 dkvs[c] += mm(ds, q_ref[i]) + mm(p.astype(BF16), g_ext[i])
-                dq_acc[i] += mm(kvs[c], ds, TN)
+                dq_acc[i] += mm(kvs[c][:, :HEAD], ds, TN)
 
         if not lo:
             tri = lax.broadcasted_iota(jnp.int32, (blk, blk), 0) <= lane_iota((blk, blk))
@@ -407,8 +407,9 @@
         if last:
 
             def finish(i, _):
-                wide = dq_acc[i].T * HEAD**-0.5
-                dq_ref[i] = jnp.where(high, 0.0, wide).astype(BF16)
+                thin = dq_acc[i] * HEAD**-0.5
+                wide = jnp.concatenate([thin, jnp.zeros_like(thin)], axis=0).T
+                dq_ref[i] = wide.astype(BF16)
                 return 0
 
             lax.fori_loop(0, ns, finish, 0)
@@ -421,7 +422,7 @@
 def attend_back_part(plan, blk, lo, hi, first, last, info, lists, q, lse, kvs, extra):
     ns, nb = len(plan.slots), hi - lo
     rows = sds((ns, blk, 2 * HEAD), BF16)
-    outs = [rows] * nb + [sds((ns, 2 * HEAD, blk), F32)]
+    outs = [rows] * nb + [sds((ns, HEAD, blk), F32)]
     if first:
         outs += [rows, sds((ns, 1, blk), F32)]
     if last:
@@ -485,10 +486,16 @@
                             src.at[m, pl.ds(nq + 5, 1)], meta.at[w, pl.ds(c, 1)], sem.at[3]
                         ),
                     ]
-            for cp in copies:
-                cp.start()
-            for cp in copies:
-                cp.wait()
+            for part in (0, 3, 1, 2):
+                for cp in copies[part::4]:
+                    cp.start()
+
+            def arrived(*parts):
+                for part in parts:
+                    for cp in copies[part::4]:
+                        cp.wait()
+
+            arrived(0, 3)
             w_up = lambda q: wup[q].reshape(width, CHUNK)
             w_down = lambda q: wdown[q].reshape(CHUNK, width)
             out_rows = width // nw
@@ -498,6 +505,7 @@
             count = jnp.sum(meta[:, :, 0:1, 0:1].astype(F32))
         else:
             slope_ref, acc_ref = rest
+            arrived = lambda *parts: None
             w_up = lambda q: w_in[0][q]
             w_down = lambda q: w_in[1][q]
             w_out = lambda row: w_in[2][pl.ds(row, 2 * HEAD), :]
@@ -515,8 +523,12 @@
         unit, inverse = norm_stats(res)
         n2 = (unit * gain + shift).astype(BF16)
         n2_ref[...] = n2
+        arrived(1)
         for q in range(nq):
-            pre = mm(n2, w_up(q))
+            if q == 0:
+                first = mm(n2, w_up(q))
+                arrived(2)
+            pre = first if q == 0 else mm(n2, w_up(q))
             cdf = 0.5 * (1.0 + lax.erf(pre * 0.7071067811865476))
             pdf = jnp.exp(-0.5 * pre * pre) * 0.3989422804014327
             act = (pre * cdf).astype(BF16)
@@ -768,6 +780,19 @@
     return body
 
 
+def last_body(plan, shard, nj, width, ff, n_more):
+    def body(info, own_ref, sib_ref, x_ref, vec_ref, g1_ref, *refs):
+        loads, refs = refs[:nj], refs[nj:]
+        more, refs = refs[:n_more], refs[n_more:]
+        words_ref, out_ref, gain_ref, shift_ref = refs[:4]
+        words_body(nj)(x_ref, vec_ref, g1_ref, *loads, *loads, words_ref)
+        head_out_body(plan, shard)(info, own_ref, sib_ref, out_ref, gain_ref, shift_ref)
+        if n_more:
+            unpack_body(plan, width, ff)(info, *more, *refs[4:])
+
+    return body
+
+
 def per_device(
     words,
     teacher,
@@ -818,25 +843,7 @@
         out_specs=[SMEM] * len(sets),
     )
     lists = dict(zip(sets, lists))
-    late = [loads[0], after(loads[1], lists[sets[0]])] + loads[2:]
-    xs = loads[:nj] + [plan.swap(x, core) for x in late[:nj]]
-
-    q, kv, normed, w_head, vecs = call(
-        project_body(plan, shard, blk),
-        "project",
-        [info] + xs + loads,
-        [SMEM] + [VMEM] * (ns + n_wt),
-        [
-            sds((ns, blk, 2 * HEAD), BF16),
-            sds((ns, blk, 2 * HEAD), BF16),
-            sds((ns, blk, width), BF16),
-            sds((width, 4 * HEAD), BF16),
-            sds((8, width), F32),
-        ],
-        flops=2 * ns * blk * width * 4 * HEAD,
-    )
-    kvs = plan.gather_groups(kv)
-
+    piece = info
     if packed:
         rows_up = width // (n_wt * n_ctx)
         up_piece = lax.dynamic_slice_in_dim(w_up, ctx * rows_up, rows_up, 0)
@@ -853,6 +860,26 @@
             ],
             axis=0,
         )
+    late = [loads[0], after(loads[1], lists[sets[0]], piece)] + loads[2:]
+    xs = loads[:nj] + [plan.swap(x, core) for x in late[:nj]]
+
+    q, kv, normed, w_head, vecs = call(
+        project_body(plan, shard, blk),
+        "project",
+        [info] + xs + loads,
+        [SMEM] + [VMEM] * (ns + n_wt),
+        [
+            sds((ns, blk, 2 * HEAD), BF16),
+            sds((ns, blk, 2 * HEAD), BF16),
+            sds((ns, blk, width), BF16),
+            sds((width, 4 * HEAD), BF16),
+            sds((8, width), F32),
+        ],
+        flops=2 * ns * blk * width * 4 * HEAD,
+    )
+    kvs = plan.gather_groups(kv)
+
+    if packed:
         piece = after(piece, loads[2])
         two = jnp.stack([piece, plan.swap(piece, (0, 2))])
         two = after(two, kvs[1])
@@ -1037,21 +1064,6 @@
         finals = plan.gather_square(final)
         finals = jnp.stack(finals)
         finals = [finals, plan.swap(finals, core)]
-        g_up, g_down, g_out, loss, g_gain, g_shift = call(
-            unpack_body(plan, width, ff),
-            "unpack",
-            [info, square] + finals,
-            [SMEM] + [VMEM] * 3,
-            [
-                sds((shard, ff), F32),
-                sds((ff // n_wt, width), F32),
-                sds((shard, width), F32),
-                sds((1, 1), F32),
-                sds((1, shard), F32),
-                sds((1, shard), F32),
-            ],
-        )
-        loss, g_gain, g_shift = loss[0, 0], g_gain.reshape(shard), g_shift.reshape(shard)
     else:
         g_up, g_down, g_out = weight_grads
         g_up = g_up.transpose(1, 0, 2).reshape(width, ff)
@@ -1070,21 +1082,33 @@
     if n_wt > nj:
         own_heads = (own_heads.astype(F32) + jnp.stack(loads[nj:]).astype(F32)).astype(BF16)
     sib_heads = plan.swap(own_heads, core)
-    grad_words = call(
-        words_body(nj),
-        "words_grad",
-        [words, vecs, grad_one] + loads[:nj],
-        [VMEM] * (3 + nj),
-        [sds((blk, width), F32)],
-    )[0]
-    g_qkv, gain_one, shift_one = call(
-        head_out_body(plan, shard),
-        "head_out",
-        [info, own_heads, sib_heads],
-        [SMEM] + [VMEM] * 2,
-        [sds((shard, 3 * width), F32), sds((1, shard), F32), sds((1, shard), F32)],
-    )
-
+    more_in = [square, *finals] if packed else []
+    more_out = []
+    if packed:
+        more_out = [
+            sds((shard, ff), F32),
+            sds((ff // n_wt, width), F32),
+            sds((shard, width), F32),
+            sds((1, 1), F32),
+            sds((1, shard), F32),
+            sds((1, shard), F32),
+        ]
+    grad_words, g_qkv, gain_one, shift_one, *more = call(
+        last_body(plan, shard, nj, width, ff, len(more_in)),
+        "last",
+        [info, own_heads, sib_heads, words, vecs, grad_one] + loads[:nj] + more_in,
+        [SMEM] + [VMEM] * (5 + nj + len(more_in)),
+        [
+            sds((blk, width), F32),
+            sds((shard, 3 * width), F32),
+            sds((1, shard), F32),
+            sds((1, shard), F32),
+        ]
+        + more_out,
+    )
+    if packed:
+        g_up, g_down, g_out, loss, g_gain, g_shift = more
+        loss, g_gain, g_shift = loss[0, 0], g_gain.reshape(shard), g_shift.reshape(shard)
     return (
         layer_out,
         loss,

time: 224 us -> 217 us (0.969)
  Pallas kernels: 79.3 us -> 66.2 us
  starting transfers between devices: 47.3 us -> 56.8 us
    pallas_call x16 -> x14, Pallas kernels: 79.3 us -> 66.2 us  [call(): pl.pallas_call(body, name=name, out_shape=list(outs), in_specs=in_specs,...]
    ppermute x16, starting transfers between devices: 19.4 us -> 29.1 us  [turn(): return lax.ppermute(x, ('ctx', 'wt'), perm)]
  transfers between devices with their start and end apart: 45 -> 45, of which waited for: 18 -> 23; matrix products, arithmetic and copies ran while one was open for 8% -> 8% of each run, Pallas kernels for 23% -> 17%
where the time goes in v5:
time: 217 us; the launch traced here: 216 us
  Pallas kernels  66.2 us (31%)
  waiting for transfers between devices  65.7 us (30%)
  starting transfers between devices  56.8 us (26%)
  other arithmetic  14.5 us (7%)
  local copies, waits for them, and re-layouts  10.4 us (5%)
    pallas_call x14, Pallas kernels, call(): pl.pallas_call(body, name=name, out_shape=list(outs), in_specs=in_specs,...  66.2 us
    ppermute x29, waiting for transfers between devices, swap(): return lax.ppermute(x, ('ctx', 'wt'), perm)  45.3 us
    ppermute x16, starting transfers between devices, turn(): return lax.ppermute(x, ('ctx', 'wt'), perm)  29.1 us
    ppermute x29, starting transfers between devices, swap(): return lax.ppermute(x, ('ctx', 'wt'), perm)  27.7 us
    ppermute x16, waiting for transfers between devices, turn(): return lax.ppermute(x, ('ctx', 'wt'), perm)  20.4 us
    unnamed x82, local copies, waits for them, and re-layouts  5.87 us
  transfers between devices with their start and end apart: 45, of which 23 were waited for; matrix products, arithmetic and copies ran while one was open for 8% of the time, Pallas kernels for 17%

profile of v5, /device:TPU:0, one launch (start us, length us, event | category | flops | bytes accessed | tf_op | source)
XLA Modules:
  0.0 215.7 jit_solution(4054409688583977579)
XLA Ops:
  4.8 4.0 %collective-permute-start.1 = (bf16[256,512]{1,0:T(8,128)(2,1)}, bf16[256,512]{1,0:T(8,128)(2,1)S(1)}, u32[]{:S(2)}, u32[]{:S(2)}) collective-permute-start(bf16[256,512]{1,0:T(8,128)(2,1)} %get-tuple-element.93), channel_id=1, source_target_pairs={{0,2},{1,3},{2,0},{3,1},{4,6},{5,7},{6,4},{7,5},{8,10},{9,11},{10,... | collective-permute-start | bytes 786440 | tf_op jit(solution)/shard_map/ppermute | solution.py:98
  16.8 11.1 %collective-permute-done.refs_1_.refs_9_ = bf16[256,512]{1,0:T(8,128)(2,1)S(1)} collective-permute-done((bf16[256,512]{1,0:T(8,128)(2,1)}, bf16[256,512]{1,0:T(8,128)(2,1)S(1)}, u32[]{:S(2)}, u32[]{:S(2)}) %collective-permute-start) | collective-permute-done | bytes 262176 | tf_op jit(solution)/shard_map/ppermute | solution.py:98
  31.3 4.8 %project.1 = (bf16[8,192,128]{2,1,0:T(8,128)(2,1)}, bf16[8,192,128]{2,1,0:T(8,128)(2,1)}, bf16[8,192,512]{2,1,0:T(8,128)(2,1)}, bf16[512,256]{1,0:T(8,128)(2,1)}, f32[8,512]{1,0:T(8,128)}) custom-call(s32[2]{0:T(128)} %pad_add_fusion.info, bf16[256,512]{1,0:T(8,128)(2,1)} %get-tuple-element.91.refs_0_.refs_8_, bf16[256,512]{1,0:T(8,128)(2,1)} %copy-done.6, ...), custom_call_target="tpu_custom_call" | custom-call | flops 402653184 | bytes 5783560 | tf_op jit(solution)/shard_map/project/pallas_call | solution.py:53
  37.7 6.4 %collective-permute-start.9 = (bf16[10,16,512]{2,1,0:T(8,128)(2,1)S(1)}, bf16[10,16,512]{2,1,0:T(8,128)(2,1)S(1)}, u32[]{:S(2)}, u32[]{:S(2)}) collective-permute-start(bf16[10,16,512]{2,1,0:T(8,128)(2,1)S(1)} %maximum_maximum_fusion), channel_id=1, source_target_pairs={{0,2},{1,3},{2,0},{3,1},{4,6},{5,7},{6,4},{7,5},{8,10},{9,11},{10,... | collective-permute-start | bytes 491528 | tf_op jit(solution)/shard_map/ppermute | solution.py:98
  44.1 7.8 %collective-permute-done.9 = bf16[10,16,512]{2,1,0:T(8,128)(2,1)S(1)} collective-permute-done((bf16[10,16,512]{2,1,0:T(8,128)(2,1)S(1)}, bf16[10,16,512]{2,1,0:T(8,128)(2,1)S(1)}, u32[]{:S(2)}, u32[]{:S(2)}) %collective-permute-start.9) | collective-permute-done | bytes 163872 | tf_op jit(solution)/shard_map/ppermute | solution.py:98
  54.1 5.4 %attend.3 = (f32[8,1,192]{2,1,0:T(1,128)}, f32[8,1,192]{2,1,0:T(1,128)}, f32[8,128,192]{2,1,0:T(8,128)}) custom-call(s32[2]{0:T(128)} %pad_add_fusion.info, s32[264]{0:T(512)} %get-tuple-element.96.pairs, bf16[8,192,128]{2,1,0:T(8,128)(2,1)} %get-tuple-element.100.q_ref, bf16[8,192,128]{2,1,0:T(8,128)(2,1)} %get-tuple-element.101.refs_0_), custom_call_target="tpu_custom_call" | custom-call | flops 2113929216 | bytes 1586216 | tf_op jit(solution)/shard_map/attend/pallas_call | solution.py:53
  64.8 4.7 %attend.4 = (f32[8,1,192]{2,1,0:T(1,128)}, f32[8,1,192]{2,1,0:T(1,128)}, f32[8,128,192]{2,1,0:T(8,128)}) custom-call(s32[2]{0:T(128)} %pad_add_fusion.info, s32[264]{0:T(512)} %get-tuple-element.106.pairs, bf16[8,192,128]{2,1,0:T(8,128)(2,1)} %get-tuple-element.100.q_ref, bf16[8,192,128]{2,1,0:T(8,128)(2,1)} %copy-done.31, bf16[8,192,128]{2,1,0:T(8,128)(2,1)} %copy-done.33, ...), custom_call_target="tpu_custom_call" | custom-call | flops 4227858432 | bytes 2778152 | tf_op jit(solution)/shard_map/attend/pallas_call | solution.py:53
  69.5 5.4 %attend.5 = (f32[8,1,192]{2,1,0:T(1,128)}, f32[8,1,192]{2,1,0:T(1,128)}, f32[8,128,192]{2,1,0:T(8,128)}, bf16[4,192,128]{2,1,0:T(8,128)(2,1)}, bf16[4,192,128]{2...) custom-call(s32[2]{0:T(128)} %pad_add_fusion.info, s32[264]{0:T(512)} %get-tuple-element.99.pairs, ...), custom_call_target="tpu_custom_call" | custom-call | flops 2113929216 | bytes 3570728 | tf_op jit(solution)/shard_map/attend/pallas_call | solution.py:53
  77.2 4.1 %collective-permute-start.18 = (bf16[4,10,16,512]{3,2,1,0:T(8,128)(2,1)S(1)}, bf16[4,10,16,512]{3,2,1,0:T(8,128)(2,1)S(1)}, u32[]{:S(2)}, u32[]{:S(2)}) collective-permute-start(bf16[4,10,16,512]{3,2,1,0:T(8,128)(2,1)S(1)} %collective-permute-done.16), channel_id=1, source_target_pairs={{0,16},{1,17},{2,18},{3,19},{4,12},{5,13},{6,14},{7,15},{8,24},{9,... | collective-permute-start | bytes 1966088 | tf_op jit(solution)/shard_map/ppermute | solution.py:106
  83.5 3.2 %collective-permute-start.14 = (bf16[192,128]{1,0:T(8,128)(2,1)S(1)}, bf16[192,128]{1,0:T(8,128)(2,1)S(1)}, u32[]{:S(2)}, u32[]{:S(2)}) collective-permute-start(bf16[192,128]{1,0:T(8,128)(2,1)S(1)} %get-tuple-element.172), channel_id=1, source_target_pairs={{0,2},{1,3},{2,0},{3,1},{4,6},{5,7},{6,4},{7,5},{8,10},{9,11},{10,... | collective-permute-start | bytes 147464 | tf_op jit(solution)/shard_map/ppermute | solution.py:98
  94.0 8.3 %mlp.1 = (bf16[192,512]{1,0:T(8,128)(2,1)}, f32[8,128]{1,0:T(8,128)}, f32[192,512]{1,0:T(8,128)}, bf16[192,128]{1,0:T(8,128)(2,1)}, bf16[192,128]{1,0:T(8,128)(2...) custom-call(s32[2]{0:T(128)} %pad_add_fusion.info, ...), custom_call_target="tpu_custom_call" | custom-call | flops 1610612736 | bytes 8819468 | tf_op jit(solution)/shard_map/mlp/pallas_call | solution.py:53
  102.3 4.4 %mlp_grads.1 = (bf16[4,4,10,16,512]{4,3,2,1,0:T(8,128)(2,1)}, bf16[4,4,10,16,512]{4,3,2,1,0:T(8,128)(2,1)}) custom-call(s32[2]{0:T(128)} %pad_add_fusion.info, bf16[4,192,512]{2,1,0:T(8,128)(2,1)} %get-tuple-element.122.act_ref, bf16[4,192,512]{2,1,0:T(8,128)(2,1)} %get-tuple-element.123.gpre_ref, bf16[192,512]{1,0:T(8,128)(2,1)} %get-tuple-element.124.n2_ref, ...), custom_call_target="tpu_custom_call" | custom-call | flops 805306368 | bytes 7622664 | tf_op jit(solution)/shard_map/mlp_grads/pallas_call | solution.py:53
  108.0 3.2 %collective-permute-start.25 = (bf16[192,128]{1,0:T(8,128)(2,1)S(1)}, bf16[192,128]{1,0:T(8,128)(2,1)S(1)}, u32[]{:S(2)}, u32[]{:S(2)}) collective-permute-start(bf16[192,128]{1,0:T(8,128)(2,1)S(1)} %copy-done.38), channel_id=1, source_target_pairs={{0,3},{1,2},{2,1},{3,0},{4,7},{5,6},{6,5},{7,4},{8,11},{9,10},{10,... | collective-permute-start | bytes 147464 | tf_op jit(solution)/shard_map/ppermute | solution.py:98
  111.3 3.5 %collective-permute-done.24.refs_5_ = bf16[192,128]{1,0:T(8,128)(2,1)S(1)} collective-permute-done((bf16[192,128]{1,0:T(8,128)(2,1)S(1)}, bf16[192,128]{1,0:T(8,128)(2,1)S(1)}, u32[]{:S(2)}, u32[]{:S(2)}) %collective-permute-start.24) | collective-permute-done | bytes 49184 | tf_op jit(solution)/shard_map/ppermute | solution.py:98
  114.9 2.9 %add_convert_fusion = bf16[2,4,10,16,512]{4,3,2,1,0:T(8,128)(2,1)} fusion(bf16[4,4,10,16,512]{4,3,2,1,0:T(8,128)(2,1)S(1)} %collective-permute-done.22, bf16[4,4,10,16,512]{4,3,2,1,0:T(8,128)(2,1)} %get-tuple-element.129), kind=kLoop, calls=%fused_computation | loop fusion | flops 2621440 | bytes 3932160 | tf_op jit(solution)/shard_map/convert_element_type | solution.py:996
  117.8 4.1 %collective-permute-start.27 = (bf16[2,4,10,16,512]{4,3,2,1,0:T(8,128)(2,1)}, bf16[2,4,10,16,512]{4,3,2,1,0:T(8,128)(2,1)}, u32[]{:S(2)}, u32[]{:S(2)}) collective-permute-start(bf16[2,4,10,16,512]{4,3,2,1,0:T(8,128)(2,1)} %add_convert_fusion), channel_id=1, source_target_pairs={{0,16},{1,17},{2,18},{3,19},{4,12},{5,13},{6,14},{7,15},{8,24},{9,... | collective-permute-start | bytes 3932168 | tf_op jit(solution)/shard_map/ppermute | solution.py:106
  122.6 5.1 %attend_back.3 = (bf16[8,192,128]{2,1,0:T(8,128)(2,1)}, bf16[8,192,128]{2,1,0:T(8,128)(2,1)}, f32[8,64,192]{2,1,0:T(8,128)}, bf16[8,192,128]{2,1,0:T(8,128)(2,1)}, f32[8,1,192]{2,1,0:T(1,128)}) custom-call(s32[2]{0:T(128)} %pad_add_fusion.info, s32[264]{0:T(512)} %get-tuple-element.120.pairs, bf16[8,192,128]{2,1,0:T(8,128)(2,1)} %get-tuple-element.100.q_ref, ...), custom_call_target="tpu_custom_call" | custom-call | flops 10569646080 | bytes 3945512 | tf_op jit(solution)/shard_map/attend_back/pallas_call | solution.py:53
  127.7 4.1 %collective-permute-start.29 = (bf16[8,192,128]{2,1,0:T(8,128)(2,1)}, bf16[8,192,128]{2,1,0:T(8,128)(2,1)S(1)}, u32[]{:S(2)}, u32[]{:S(2)}) collective-permute-start(bf16[8,192,128]{2,1,0:T(8,128)(2,1)} %get-tuple-element.150), channel_id=1, source_target_pairs={{0,16},{1,17},{2,18},{3,19},{4,12},{5,13},{6,14},{7,15},{8,24},{9,... | collective-permute-start | bytes 1179656 | tf_op jit(solution)/shard_map/ppermute | solution.py:106
  132.0 4.1 %attend_back.4 = (bf16[8,192,128]{2,1,0:T(8,128)(2,1)}, f32[8,64,192]{2,1,0:T(8,128)}) custom-call(s32[2]{0:T(128)} %pad_add_fusion.info, s32[264]{0:T(512)} %get-tuple-element.138.pairs, bf16[8,192,128]{2,1,0:T(8,128)(2,1)} %get-tuple-element.100.q_ref, f32[8,1,192]{2,1,0:T(1,128)} %get-tuple-element.119.lse_ref, bf16[8,192,128]{2,1,0:T(8,128)(2,1)} %copy-done.31, ...), custom_call_target="tpu_custom_call" | custom-call | flops 5284823040 | bytes 2372648 | tf_op jit(solution)/shard_map/attend_back/pallas_call | solution.py:53
  137.9 2.3 %fusion.1 = bf16[4,10,16,512]{3,2,1,0:T(8,128)(2,1)} fusion(bf16[4,4,10,16,512]{4,3,2,1,0:T(8,128)(2,1)S(1)} %collective-permute-done.22, bf16[2,4,10,16,512]{4,3,2,1,0:T(8,128)(2,1)} %collective-permute-done.27, bf16[4,4,10,16,512]{4,3,2,1,0:T(8,128)(2,1)S(1)} %copy-done.1), kind=kLoop, calls=%fused_computation.6 | loop fusion | flops 1966080 | bytes 2621440 | tf_op jit(solution)/shard_map/convert_element_type | solution.py:1009
  140.2 3.8 %collective-permute-start.28 = (bf16[4,10,16,512]{3,2,1,0:T(8,128)(2,1)}, bf16[4,10,16,512]{3,2,1,0:T(8,128)(2,1)}, u32[]{:S(2)}, u32[]{:S(2)}) collective-permute-start(bf16[4,10,16,512]{3,2,1,0:T(8,128)(2,1)} %fusion.1), channel_id=1, source_target_pairs={{0,8},{1,9},{2,10},{3,11},{4,20},{5,21},{6,22},{7,23},{8,0},{9,1},... | collective-permute-start | bytes 1966088 | tf_op jit(solution)/shard_map/ppermute | solution.py:106
  144.0 3.8 %collective-permute-done.30 = bf16[8,192,128]{2,1,0:T(8,128)(2,1)} collective-permute-done((bf16[8,192,128]{2,1,0:T(8,128)(2,1)}, bf16[8,192,128]{2,1,0:T(8,128)(2,1)}, u32[]{:S(2)}, u32[]{:S(2)}) %collective-permute-start.30) | collective-permute-done | bytes 393248 | tf_op jit(solution)/shard_map/ppermute | solution.py:106
  149.6 4.1 %collective-permute-start.31 = (bf16[8,192,128]{2,1,0:T(8,128)(2,1)}, bf16[8,192,128]{2,1,0:T(8,128)(2,1)}, u32[]{:S(2)}, u32[]{:S(2)}) collective-permute-start(bf16[8,192,128]{2,1,0:T(8,128)(2,1)} %add_convert_fusion.2), channel_id=1, source_target_pairs={{0,8},{1,9},{2,10},{3,11},{4,20},{5,21},{6,22},{7,23},{8,0},{9,1},... | collective-permute-start | bytes 1179656 | tf_op jit(solution)/shard_map/ppermute | solution.py:106
  153.8 7.0 %attend_back.5 = (bf16[8,192,128]{2,1,0:T(8,128)(2,1)}, f32[8,64,192]{2,1,0:T(8,128)}, bf16[8,192,128]{2,1,0:T(8,128)(2,1)}) custom-call(s32[2]{0:T(128)} %pad_add_fusion.info, s32[264]{0:T(512)} %get-tuple-element.96.pairs, bf16[8,192,128]{2,1,0:T(8,128)(2,1)} %get-tuple-element.100.q_ref, f32[8,1,192]{2,1,0:T(1,128)} %get-tuple-element.119.lse_ref, ...), custom_call_target="tpu_custom_call" | custom-call | flops 5284823040 | bytes 2765864 | tf_op jit(solution)/shard_map/attend_back/pallas_call | solution.py:53
  160.8 2.6 %fusion = bf16[4,10,16,512]{3,2,1,0:T(8,128)(2,1)} fusion(bf16[4,10,16,512]{3,2,1,0:T(8,128)(2,1)} %collective-permute-done.28, bf16[4,4,10,16,512]{4,3,2,1,0:T(8,128)(2,1)S(1)} %collective-permute-done.22, bf16[2,4,10,16,512]{4,3,2,1,0:T(8,128)(2,1)} %collective-permute-done.27, bf16[4,4,10,16,512]{4,3,2,1,0:T(8,128)(2,1)S(1)} %copy-done.1), kind=kLoop, calls=%fused_computation.3 | loop fusion | flops 2621440 | bytes 3276800 | tf_op jit(solution)/shard_map/convert_element_type | solution.py:1018
  164.2 5.8 %head_grads.1 = (bf16[4,192,512]{2,1,0:T(8,128)(2,1)}, bf16[4,192,512]{2,1,0:T(8,128)(2,1)}, bf16[4,64,512]{2,1,0:T(8,128)(2,1)}) custom-call(s32[2]{0:T(128)} %pad_add_fusion.info, bf16[8,192,128]{2,1,0:T(8,128)(2,1)} %get-tuple-element.147.dq_ref, bf16[512,256]{1,0:T(8,128)(2,1)} %get-tuple-element.148.wh_ref, ...), custom_call_target="tpu_custom_call" | custom-call | flops 805306368 | bytes 7340040 | tf_op jit(solution)/shard_map/head_grads/pallas_call | solution.py:53
  170.7 6.5 %collective-permute-done.33 = bf16[4,64,512]{2,1,0:T(8,128)(2,1)S(1)} collective-permute-done((bf16[4,64,512]{2,1,0:T(8,128)(2,1)}, bf16[4,64,512]{2,1,0:T(8,128)(2,1)S(1)}, u32[]{:S(2)}, u32[]{:S(2)}) %collective-permute-start.33) | collective-permute-done | bytes 262176 | tf_op jit(solution)/shard_map/ppermute | solution.py:106
  180.9 3.8 %collective-permute-done.34.more_ref = bf16[4,64,512]{2,1,0:T(8,128)(2,1)S(1)} collective-permute-done((bf16[4,64,512]{2,1,0:T(8,128)(2,1)S(1)}, bf16[4,64,512]{2,1,0:T(8,128)(2,1)S(1)}, u32[]{:S(2)}, u32[]{:S(2)}) %collective-permute-start.34) | collective-permute-done | bytes 262176 | tf_op jit(solution)/shard_map/ppermute | solution.py:106
  185.6 2.5 %merge.1 = (bf16[256,512]{1,0:T(8,128)(2,1)}, bf16[256,512]{1,0:T(8,128)(2,1)}, bf16[256,512]{1,0:T(8,128)(2,1)}, bf16[256,512]{1,0:T(8,128)(2,1)}) custom-call(bf16[4,192,512]{2,1,0:T(8,128)(2,1)} %get-tuple-element.152.own_ref, bf16[4,192,512]{2,1,0:T(8,128)(2,1)} %copy-done.14, bf16[4,64,512]{2,1,0:T(8,128)(2,1)} %copy-done.13, bf16[4,64,512]{2,1,0:T(8,128)(2,1)} %copy-done.23), custom_call_target="tpu_custom_call" | custom-call | bytes 3145728 | tf_op jit(solution)/shard_map/merge/pallas_call | solution.py:53
  196.4 3.8 %collective-permute-done.35.refs_1_ = bf16[256,512]{1,0:T(8,128)(2,1)S(1)} collective-permute-done((bf16[256,512]{1,0:T(8,128)(2,1)}, bf16[256,512]{1,0:T(8,128)(2,1)S(1)}, u32[]{:S(2)}, u32[]{:S(2)}) %collective-permute-start.35) | collective-permute-done | bytes 262176 | tf_op jit(solution)/shard_map/ppermute | solution.py:98
  201.8 6.7 %collective-permute-done.36.refs_2_ = bf16[256,512]{1,0:T(8,128)(2,1)S(1)} collective-permute-done((bf16[256,512]{1,0:T(8,128)(2,1)}, bf16[256,512]{1,0:T(8,128)(2,1)S(1)}, u32[]{:S(2)}, u32[]{:S(2)}) %collective-permute-start.36) | collective-permute-done | bytes 262176 | tf_op jit(solution)/shard_map/ppermute | solution.py:98
  211.2 4.4 %last.1 = (f32[192,512]{1,0:T(8,128)}, f32[128,1536]{1,0:T(8,128)}, f32[1,128]{1,0:T(1,128)}, f32[1,128]{1,0:T(1,128)}, f32[128,2048]{1,0:T(8,128)}, /*index=5*/...) custom-call(s32[2]{0:T(128)} %pad_add_fusion.info, ...), custom_call_target="tpu_custom_call" | custom-call | bytes 7034892 | tf_op jit(solution)/shard_map/last/pallas_call | solution.py:53
  (186 shorter events, 59.8 us)
Async XLA Ops:
  4.8 23.2 %collective-permute-start.1 = (bf16[256,512]{1,0:T(8,128)(2,1)}, bf16[256,512]{1,0:T(8,128)(2,1)S(1)}, u32[]{:S(2)}, u32[]{:S(2)}) collective-permute-start(bf16[256,512]{1,0:T(8,128)(2,1)} %get-tuple-element.93), channel_id=1, source_target_pairs={{0,2},{1,3},{2,0},{3,1},{4,6},{5,7},{6,4},{7,5},{8,10},{9,11},{10,... | collective-permute-start | bytes 786440 | tf_op jit(solution)/shard_map/ppermute | solution.py:98
  8.8 19.2 %collective-permute-start.2 = (bf16[256,512]{1,0:T(8,128)(2,1)}, bf16[256,512]{1,0:T(8,128)(2,1)S(1)}, u32[]{:S(2)}, u32[]{:S(2)}) collective-permute-start(bf16[256,512]{1,0:T(8,128)(2,1)} %get-tuple-element.94), channel_id=1, source_target_pairs={{0,3},{1,2},{2,1},{3,0},{4,7},{5,6},{6,5},{7,4},{8,11},{9,10},{10,... | collective-permute-start | bytes 786440 | tf_op jit(solution)/shard_map/ppermute | solution.py:98
  10.2 17.8 %collective-permute-start = (bf16[256,512]{1,0:T(8,128)(2,1)}, bf16[256,512]{1,0:T(8,128)(2,1)S(1)}, u32[]{:S(2)}, u32[]{:S(2)}) collective-permute-start(bf16[256,512]{1,0:T(8,128)(2,1)} %get-tuple-element.92), channel_id=1, source_target_pairs={{0,1},{1,0},{2,3},{3,2},{4,5},{5,4},{6,7},{7,6},{8,9},{9,8},{10,11... | collective-permute-start | bytes 786440 | tf_op jit(solution)/shard_map/ppermute | solution.py:98
  10.4 18.2 %collective-permute-start.3 = (bf16[256,512]{1,0:T(8,128)(2,1)}, bf16[256,512]{1,0:T(8,128)(2,1)S(1)}, u32[]{:S(2)}, u32[]{:S(2)}) collective-permute-start(bf16[256,512]{1,0:T(8,128)(2,1)} %get-tuple-element.91.refs_0_.refs_8_), channel_id=1, source_target_pairs={{0,4},{1,5},{2,6},{3,7},{4,0},{5,1},{6,2},{7,3},{8,12},{9,13},{10,... | collective-permute-start | bytes 786440 | tf_op jit(solution)/shard_map/ppermute | solution.py:98
  36.1 15.8 %collective-permute-start.7 = (bf16[8,192,128]{2,1,0:T(8,128)(2,1)}, bf16[8,192,128]{2,1,0:T(8,128)(2,1)S(1)}, u32[]{:S(2)}, u32[]{:S(2)}) collective-permute-start(bf16[8,192,128]{2,1,0:T(8,128)(2,1)} %get-tuple-element.101.refs_0_), channel_id=1, source_target_pairs={{0,8},{1,9},{2,10},{3,11},{4,20},{5,21},{6,22},{7,23},{8,0},{9,1},... | collective-permute-start | bytes 1179656 | tf_op jit(solution)/shard_map/ppermute | solution.py:106
  37.7 14.2 %collective-permute-start.9 = (bf16[10,16,512]{2,1,0:T(8,128)(2,1)S(1)}, bf16[10,16,512]{2,1,0:T(8,128)(2,1)S(1)}, u32[]{:S(2)}, u32[]{:S(2)}) collective-permute-start(bf16[10,16,512]{2,1,0:T(8,128)(2,1)S(1)} %maximum_maximum_fusion), channel_id=1, source_target_pairs={{0,2},{1,3},{2,0},{3,1},{4,6},{5,7},{6,4},{7,5},{8,10},{9,11},{10,... | collective-permute-start | bytes 491528 | tf_op jit(solution)/shard_map/ppermute | solution.py:98
  51.9 9.5 %collective-permute-start.10 = (bf16[2,10,16,512]{3,2,1,0:T(8,128)(2,1)S(1)}, bf16[2,10,16,512]{3,2,1,0:T(8,128)(2,1)S(1)}, u32[]{:S(2)}, u32[]{:S(2)}) collective-permute-start(bf16[2,10,16,512]{3,2,1,0:T(8,128)(2,1)S(1)} %pad_maximum_fusion.3), channel_id=1, source_target_pairs={{0,1},{1,0},{2,3},{3,2},{4,5},{5,4},{6,7},{7,6},{8,9},{9,8},{10,11... | collective-permute-start | bytes 983048 | tf_op jit(solution)/shard_map/ppermute | solution.py:98
  52.0 9.4 %collective-permute-start.8 = (bf16[8,192,128]{2,1,0:T(8,128)(2,1)S(1)}, bf16[8,192,128]{2,1,0:T(8,128)(2,1)S(1)}, u32[]{:S(2)}, u32[]{:S(2)}) collective-permute-start(bf16[8,192,128]{2,1,0:T(8,128)(2,1)S(1)} %collective-permute-done.7.refs_0_), channel_id=1, source_target_pairs={{0,16},{1,17},{2,18},{3,19},{4,12},{5,13},{6,14},{7,15},{8,24},{9,... | collective-permute-start | bytes 1179656 | tf_op jit(solution)/shard_map/ppermute | solution.py:106
  52.6 11.5 %collective-permute-start.11 = (bf16[8,192,128]{2,1,0:T(8,128)(2,1)}, bf16[8,192,128]{2,1,0:T(8,128)(2,1)S(1)}, u32[]{:S(2)}, u32[]{:S(2)}) collective-permute-start(bf16[8,192,128]{2,1,0:T(8,128)(2,1)} %get-tuple-element.101.refs_0_), channel_id=1, source_target_pairs={{0,16},{1,17},{2,18},{3,19},{4,12},{5,13},{6,14},{7,15},{8,24},{9,... | collective-permute-start | bytes 1179656 | tf_op jit(solution)/shard_map/ppermute | solution.py:106
  61.5 19.9 %collective-permute-start.17 = (bf16[4,10,16,512]{3,2,1,0:T(8,128)(2,1)S(1)}, bf16[4,10,16,512]{3,2,1,0:T(8,128)(2,1)S(1)}, u32[]{:S(2)}, u32[]{:S(2)}) collective-permute-start(bf16[4,10,16,512]{3,2,1,0:T(8,128)(2,1)S(1)} %pad_maximum_fusion.1.refs_9_), channel_id=1, source_target_pairs={{0,16},{1,17},{2,18},{3,19},{4,12},{5,13},{6,14},{7,15},{8,24},{9,... | collective-permute-start | bytes 1966088 | tf_op jit(solution)/shard_map/ppermute | solution.py:106
  61.9 15.3 %collective-permute-start.16 = (bf16[4,10,16,512]{3,2,1,0:T(8,128)(2,1)S(1)}, bf16[4,10,16,512]{3,2,1,0:T(8,128)(2,1)S(1)}, u32[]{:S(2)}, u32[]{:S(2)}) collective-permute-start(bf16[4,10,16,512]{3,2,1,0:T(8,128)(2,1)S(1)} %pad_maximum_fusion.1.refs_9_), channel_id=1, source_target_pairs={{0,8},{1,9},{2,10},{3,11},{4,20},{5,21},{6,22},{7,23},{8,0},{9,1},... | collective-permute-start | bytes 1966088 | tf_op jit(solution)/shard_map/ppermute | solution.py:106
  77.2 14.4 %collective-permute-start.18 = (bf16[4,10,16,512]{3,2,1,0:T(8,128)(2,1)S(1)}, bf16[4,10,16,512]{3,2,1,0:T(8,128)(2,1)S(1)}, u32[]{:S(2)}, u32[]{:S(2)}) collective-permute-start(bf16[4,10,16,512]{3,2,1,0:T(8,128)(2,1)S(1)} %collective-permute-done.16), channel_id=1, source_target_pairs={{0,16},{1,17},{2,18},{3,19},{4,12},{5,13},{6,14},{7,15},{8,24},{9,... | collective-permute-start | bytes 1966088 | tf_op jit(solution)/shard_map/ppermute | solution.py:106
  81.5 12.5 %collective-permute-start.20 = (bf16[2,4,10,16,512]{4,3,2,1,0:T(8,128)(2,1)S(1)}, bf16[2,4,10,16,512]{4,3,2,1,0:T(8,128)(2,1)}, u32[]{:S(2)}, u32[]{:S(2)}) collective-permute-start(bf16[2,4,10,16,512]{4,3,2,1,0:T(8,128)(2,1)S(1)} %pad_maximum_fusion.refs_10_), channel_id=1, source_target_pairs={{0,4},{1,5},{2,6},{3,7},{4,0},{5,1},{6,2},{7,3},{8,12},{9,13},{10,... | collective-permute-start | bytes 3932168 | tf_op jit(solution)/shard_map/ppermute | solution.py:98
  83.5 7.9 %collective-permute-start.14 = (bf16[192,128]{1,0:T(8,128)(2,1)S(1)}, bf16[192,128]{1,0:T(8,128)(2,1)S(1)}, u32[]{:S(2)}, u32[]{:S(2)}) collective-permute-start(bf16[192,128]{1,0:T(8,128)(2,1)S(1)} %get-tuple-element.172), channel_id=1, source_target_pairs={{0,2},{1,3},{2,0},{3,1},{4,6},{5,7},{6,4},{7,5},{8,10},{9,11},{10,... | collective-permute-start | bytes 147464 | tf_op jit(solution)/shard_map/ppermute | solution.py:98
  106.7 8.2 %collective-permute-start.22 = (bf16[4,4,10,16,512]{4,3,2,1,0:T(8,128)(2,1)}, bf16[4,4,10,16,512]{4,3,2,1,0:T(8,128)(2,1)S(1)}, u32[]{:S(2)}, u32[]{:S(2)}) collective-permute-start(bf16[4,4,10,16,512]{4,3,2,1,0:T(8,128)(2,1)} %get-tuple-element.130), channel_id=1, source_target_pairs={{0,4},{1,5},{2,6},{3,7},{4,0},{5,1},{6,2},{7,3},{8,12},{9,13},{10,... | collective-permute-start | bytes 7864328 | tf_op jit(solution)/shard_map/ppermute | solution.py:98
  107.5 7.3 %collective-permute-start.24 = (bf16[192,128]{1,0:T(8,128)(2,1)S(1)}, bf16[192,128]{1,0:T(8,128)(2,1)S(1)}, u32[]{:S(2)}, u32[]{:S(2)}) collective-permute-start(bf16[192,128]{1,0:T(8,128)(2,1)S(1)} %copy-done.39), channel_id=1, source_target_pairs={{0,2},{1,3},{2,0},{3,1},{4,6},{5,7},{6,4},{7,5},{8,10},{9,11},{10,... | collective-permute-start | bytes 147464 | tf_op jit(solution)/shard_map/ppermute | solution.py:98
  108.0 6.7 %collective-permute-start.25 = (bf16[192,128]{1,0:T(8,128)(2,1)S(1)}, bf16[192,128]{1,0:T(8,128)(2,1)S(1)}, u32[]{:S(2)}, u32[]{:S(2)}) collective-permute-start(bf16[192,128]{1,0:T(8,128)(2,1)S(1)} %copy-done.38), channel_id=1, source_target_pairs={{0,3},{1,2},{2,1},{3,0},{4,7},{5,6},{6,5},{7,4},{8,11},{9,10},{10,... | collective-permute-start | bytes 147464 | tf_op jit(solution)/shard_map/ppermute | solution.py:98
  114.8 7.2 %collective-permute-start.26 = (bf16[4,192,128]{2,1,0:T(8,128)(2,1)S(1)}, bf16[4,192,128]{2,1,0:T(8,128)(2,1)S(1)}, u32[]{:S(2)}, u32[]{:S(2)}) collective-permute-start(bf16[4,192,128]{2,1,0:T(8,128)(2,1)S(1)} %pad_maximum_fusion.5), channel_id=1, source_target_pairs={{0,4},{1,5},{2,6},{3,7},{4,0},{5,1},{6,2},{7,3},{8,12},{9,13},{10,... | collective-permute-start | bytes 589832 | tf_op jit(solution)/shard_map/ppermute | solution.py:98
  117.8 20.0 %collective-permute-start.27 = (bf16[2,4,10,16,512]{4,3,2,1,0:T(8,128)(2,1)}, bf16[2,4,10,16,512]{4,3,2,1,0:T(8,128)(2,1)}, u32[]{:S(2)}, u32[]{:S(2)}) collective-permute-start(bf16[2,4,10,16,512]{4,3,2,1,0:T(8,128)(2,1)} %add_convert_fusion), channel_id=1, source_target_pairs={{0,16},{1,17},{2,18},{3,19},{4,12},{5,13},{6,14},{7,15},{8,24},{9,... | collective-permute-start | bytes 3932168 | tf_op jit(solution)/shard_map/ppermute | solution.py:106
  127.7 35.7 %collective-permute-start.29 = (bf16[8,192,128]{2,1,0:T(8,128)(2,1)}, bf16[8,192,128]{2,1,0:T(8,128)(2,1)S(1)}, u32[]{:S(2)}, u32[]{:S(2)}) collective-permute-start(bf16[8,192,128]{2,1,0:T(8,128)(2,1)} %get-tuple-element.150), channel_id=1, source_target_pairs={{0,16},{1,17},{2,18},{3,19},{4,12},{5,13},{6,14},{7,15},{8,24},{9,... | collective-permute-start | bytes 1179656 | tf_op jit(solution)/shard_map/ppermute | solution.py:106
  131.9 15.9 %collective-permute-start.30 = (bf16[8,192,128]{2,1,0:T(8,128)(2,1)}, bf16[8,192,128]{2,1,0:T(8,128)(2,1)}, u32[]{:S(2)}, u32[]{:S(2)}) collective-permute-start(bf16[8,192,128]{2,1,0:T(8,128)(2,1)} %get-tuple-element.151), channel_id=1, source_target_pairs={{0,16},{1,17},{2,18},{3,19},{4,12},{5,13},{6,14},{7,15},{8,24},{9,... | collective-permute-start | bytes 1179656 | tf_op jit(solution)/shard_map/ppermute | solution.py:106
  140.2 20.7 %collective-permute-start.28 = (bf16[4,10,16,512]{3,2,1,0:T(8,128)(2,1)}, bf16[4,10,16,512]{3,2,1,0:T(8,128)(2,1)}, u32[]{:S(2)}, u32[]{:S(2)}) collective-permute-start(bf16[4,10,16,512]{3,2,1,0:T(8,128)(2,1)} %fusion.1), channel_id=1, source_target_pairs={{0,8},{1,9},{2,10},{3,11},{4,20},{5,21},{6,22},{7,23},{8,0},{9,1},... | collective-permute-start | bytes 1966088 | tf_op jit(solution)/shard_map/ppermute | solution.py:106
  149.6 13.8 %collective-permute-start.31 = (bf16[8,192,128]{2,1,0:T(8,128)(2,1)}, bf16[8,192,128]{2,1,0:T(8,128)(2,1)}, u32[]{:S(2)}, u32[]{:S(2)}) collective-permute-start(bf16[8,192,128]{2,1,0:T(8,128)(2,1)} %add_convert_fusion.2), channel_id=1, source_target_pairs={{0,8},{1,9},{2,10},{3,11},{4,20},{5,21},{6,22},{7,23},{8,0},{9,1},... | collective-permute-start | bytes 1179656 | tf_op jit(solution)/shard_map/ppermute | solution.py:106
  170.0 7.2 %collective-permute-start.33 = (bf16[4,64,512]{2,1,0:T(8,128)(2,1)}, bf16[4,64,512]{2,1,0:T(8,128)(2,1)S(1)}, u32[]{:S(2)}, u32[]{:S(2)}) collective-permute-start(bf16[4,64,512]{2,1,0:T(8,128)(2,1)} %get-tuple-element.154), channel_id=1, source_target_pairs={{0,8},{1,9},{2,10},{3,11},{4,20},{5,21},{6,22},{7,23},{8,0},{9,1},... | collective-permute-start | bytes 786440 | tf_op jit(solution)/shard_map/ppermute | solution.py:106
  170.0 9.0 %collective-permute-start.39 = (bf16[2,10,16,512]{3,2,1,0:T(8,128)(2,1)S(1)}, bf16[2,10,16,512]{3,2,1,0:T(8,128)(2,1)S(1)}, u32[]{:S(2)}, u32[]{:S(2)}) collective-permute-start(bf16[2,10,16,512]{3,2,1,0:T(8,128)(2,1)S(1)} %slice.91), channel_id=1, source_target_pairs={{0,1},{1,0},{2,3},{3,2},{4,5},{5,4},{6,7},{7,6},{8,9},{9,8},{10,11... | collective-permute-start | bytes 983048 | tf_op jit(solution)/shard_map/ppermute | solution.py:98
  170.7 13.9 %collective-permute-start.32 = (bf16[4,192,512]{2,1,0:T(8,128)(2,1)}, bf16[4,192,512]{2,1,0:T(8,128)(2,1)S(1)}, u32[]{:S(2)}, u32[]{:S(2)}) collective-permute-start(bf16[4,192,512]{2,1,0:T(8,128)(2,1)} %get-tuple-element.153), channel_id=1, source_target_pairs={{0,4},{1,5},{2,6},{3,7},{4,0},{5,1},{6,2},{7,3},{8,12},{9,13},{10,... | collective-permute-start | bytes 2359304 | tf_op jit(solution)/shard_map/ppermute | solution.py:98
  179.2 9.0 %collective-permute-start.40 = (bf16[10,16,512]{2,1,0:T(8,128)(2,1)S(1)}, bf16[10,16,512]{2,1,0:T(8,128)(2,1)S(1)}, u32[]{:S(2)}, u32[]{:S(2)}) collective-permute-start(bf16[10,16,512]{2,1,0:T(8,128)(2,1)S(1)} %slice_bitcast_fusion), channel_id=1, source_target_pairs={{0,2},{1,3},{2,0},{3,1},{4,6},{5,7},{6,4},{7,5},{8,10},{9,11},{10,... | collective-permute-start | bytes 491528 | tf_op jit(solution)/shard_map/ppermute | solution.py:98
  188.1 12.0 %collective-permute-start.35 = (bf16[256,512]{1,0:T(8,128)(2,1)}, bf16[256,512]{1,0:T(8,128)(2,1)S(1)}, u32[]{:S(2)}, u32[]{:S(2)}) collective-permute-start(bf16[256,512]{1,0:T(8,128)(2,1)} %get-tuple-element.156), channel_id=1, source_target_pairs={{0,1},{1,0},{2,3},{3,2},{4,5},{5,4},{6,7},{7,6},{8,9},{9,8},{10,11... | collective-permute-start | bytes 786440 | tf_op jit(solution)/shard_map/ppermute | solution.py:98
  188.9 11.3 %collective-permute-start.42 = (bf16[10,16,512]{2,1,0:T(8,128)(2,1)S(1)}, bf16[10,16,512]{2,1,0:T(8,128)(2,1)S(1)}, u32[]{:S(2)}, u32[]{:S(2)}) collective-permute-start(bf16[10,16,512]{2,1,0:T(8,128)(2,1)S(1)} %fusion.2), channel_id=1, source_target_pairs={{0,16},{1,17},{2,18},{3,19},{4,12},{5,13},{6,14},{7,15},{8,24},{9,... | collective-permute-start | bytes 491528 | tf_op jit(solution)/shard_map/ppermute | solution.py:106
  191.0 17.5 %collective-permute-start.36 = (bf16[256,512]{1,0:T(8,128)(2,1)}, bf16[256,512]{1,0:T(8,128)(2,1)S(1)}, u32[]{:S(2)}, u32[]{:S(2)}) collective-permute-start(bf16[256,512]{1,0:T(8,128)(2,1)} %get-tuple-element.157), channel_id=1, source_target_pairs={{0,2},{1,3},{2,0},{3,1},{4,6},{5,7},{6,4},{7,5},{8,10},{9,11},{10,... | collective-permute-start | bytes 786440 | tf_op jit(solution)/shard_map/ppermute | solution.py:98
  191.6 17.0 %collective-permute-start.37 = (bf16[256,512]{1,0:T(8,128)(2,1)}, bf16[256,512]{1,0:T(8,128)(2,1)S(1)}, u32[]{:S(2)}, u32[]{:S(2)}) collective-permute-start(bf16[256,512]{1,0:T(8,128)(2,1)} %get-tuple-element.158), channel_id=1, source_target_pairs={{0,3},{1,2},{2,1},{3,0},{4,7},{5,6},{6,5},{7,4},{8,11},{9,10},{10,... | collective-permute-start | bytes 786440 | tf_op jit(solution)/shard_map/ppermute | solution.py:98
  201.7 8.5 %collective-permute-start.44 = (bf16[4,10,16,512]{3,2,1,0:T(8,128)(2,1)S(1)}, bf16[4,10,16,512]{3,2,1,0:T(8,128)(2,1)S(1)}, u32[]{:S(2)}, u32[]{:S(2)}) collective-permute-start(bf16[4,10,16,512]{3,2,1,0:T(8,128)(2,1)S(1)} %pad_maximum_fusion.2.refs_5_), channel_id=1, source_target_pairs={{0,4},{1,5},{2,6},{3,7},{4,0},{5,1},{6,2},{7,3},{8,12},{9,13},{10,... | collective-permute-start | bytes 1966088 | tf_op jit(solution)/shard_map/ppermute | solution.py:98
  (54 other events, 244.6 us)

commit v6 on v5

--- a/solution.py
+++ b/solution.py
@@ -882,7 +882,7 @@
     if packed:
         piece = after(piece, loads[2])
         two = jnp.stack([piece, plan.swap(piece, (0, 2))])
-        two = after(two, kvs[1])
+        two = after(two, kvs[1], kvs[2])
         near = plan.swap(two, (0, 1))
         count = jnp.zeros((1,), F32)
     else:
@@ -998,11 +998,12 @@
             g_far = plan.turn(g_far, False)
         part = attend_back_part(plan, blk, 2, 4, True, False, info, lists, q, lse, kvs, extra)
         dkv2, dkv3, dq_part, g_ext, delta = part
-        far = [plan.turn(d, False) for d in (dkv3, dkv2)]
+        far = plan.turn(dkv3, False)
         dkv1, dq_part = attend_back_part(
             plan, blk, 1, 2, False, False, info, lists, q, lse, kvs, [g_ext, delta, dq_part]
         )
-        mid = plan.turn((dkv1.astype(F32) + far[0].astype(F32)).astype(BF16), True)
+        far_two = plan.turn(after(dkv2, dkv1), False)
+        mid = plan.turn((dkv1.astype(F32) + far.astype(F32)).astype(BF16), True)
         if packed:
             g_far = after(g_far, dkv1)
             g_mid = g_all[1].astype(F32) + g_core[1].astype(F32) + g_far[1].astype(F32)
@@ -1016,9 +1017,8 @@
             g_mid = after(g_mid, dkv0)
             g_near = g_all[0].astype(F32) + g_core[0].astype(F32) + g_far[0].astype(F32)
             g_near = (g_near + g_mid.astype(F32)).astype(BF16)
-            dq = after(dq, g_near)
             g_other = plan.swap(g_near[2:], (0, 1))
-        parts = [dkv0, far[1], mid]
+        parts = [dkv0, far_two, mid]
     else:
         part = attend_back_part(plan, blk, 0, nb, True, True, info, lists, q, lse, kvs, extra)
         dq = part[-1]

time: 217 us -> 214 us (0.986); the launches traced: 216 us -> 210 us
  Pallas kernels: 66.2 us -> 70.2 us
  waiting for transfers between devices: 65.7 us -> 61.9 us
  starting transfers between devices: 56.8 us -> 53.7 us
    ppermute x16, waiting for transfers between devices: 20.4 us -> 13.1 us  [turn(): return lax.ppermute(x, ('ctx', 'wt'), perm)]
    pallas_call x14, Pallas kernels: 66.2 us -> 70.2 us  [call(): pl.pallas_call(body, name=name, out_shape=list(outs), in_specs=in_specs,...]
    ppermute x29, waiting for transfers between devices: 45.3 us -> 48.9 us  [swap(): return lax.ppermute(x, ('ctx', 'wt'), perm)]
    ppermute x16, starting transfers between devices: 29.1 us -> 25.5 us  [turn(): return lax.ppermute(x, ('ctx', 'wt'), perm)]
    unnamed x82 -> x84, local copies, waits for them, and re-layouts: 5.87 us -> 4.38 us
  transfers between devices with their start and end apart: 45 -> 45, of which waited for: 23 -> 23; matrix products, arithmetic and copies ran while one was open for 8% -> 7% of each run, Pallas kernels for 17% -> 22%
where the time goes in v6:
time: 214 us; the launch traced here: 210 us
  Pallas kernels  70.2 us (33%)
  waiting for transfers between devices  61.9 us (29%)
  starting transfers between devices  53.7 us (25%)
  other arithmetic  12.8 us (6%)
  local copies, waits for them, and re-layouts  8.89 us (4%)
  between operations  2.14 us (1%)
    pallas_call x14, Pallas kernels, call(): pl.pallas_call(body, name=name, out_shape=list(outs), in_specs=in_specs,...  70.2 us
    ppermute x29, waiting for transfers between devices, swap(): return lax.ppermute(x, ('ctx', 'wt'), perm)  48.9 us
    ppermute x29, starting transfers between devices, swap(): return lax.ppermute(x, ('ctx', 'wt'), perm)  28.2 us
    ppermute x16, starting transfers between devices, turn(): return lax.ppermute(x, ('ctx', 'wt'), perm)  25.5 us
    ppermute x16, waiting for transfers between devices, turn(): return lax.ppermute(x, ('ctx', 'wt'), perm)  13.1 us
    unnamed x84, local copies, waits for them, and re-layouts  4.38 us
  transfers between devices with their start and end apart: 45, of which 23 were waited for; matrix products, arithmetic and copies ran while one was open for 7% of the time, Pallas kernels for 22%

profile of v6, /device:TPU:0, one launch (start us, length us, event | category | flops | bytes accessed | tf_op | source)
XLA Modules:
  0.0 209.7 jit_solution(4728468756225055959)
XLA Ops:
  2.6 2.3 %pack.1 = (bf16[256,512]{1,0:T(8,128)(2,1)}, bf16[256,512]{1,0:T(8,128)(2,1)}, bf16[256,512]{1,0:T(8,128)(2,1)}, bf16[256,512]{1,0:T(8,128)(2,1)}) custom-call(s32[2]{0:T(128)} %pad_add_fusion.info, bf16[192,512]{1,0:T(8,128)(2,1)} %x_ref.1, bf16[128,1536]{1,0:T(8,128)(2,1)} %w_ref.1, bf16[4,128]{1,0:T(4,128)(2,1)} %pad_maximum_fusion.6.vec_ref), custom_call_target="tpu_custom_call" | custom-call | bytes 1639432 | tf_op jit(solution)/shard_map/pack/pallas_call | solution.py:53
  4.9 4.0 %collective-permute-start.1 = (bf16[256,512]{1,0:T(8,128)(2,1)}, bf16[256,512]{1,0:T(8,128)(2,1)S(1)}, u32[]{:S(2)}, u32[]{:S(2)}) collective-permute-start(bf16[256,512]{1,0:T(8,128)(2,1)} %get-tuple-element.93), channel_id=1, source_target_pairs={{0,2},{1,3},{2,0},{3,1},{4,6},{5,7},{6,4},{7,5},{8,10},{9,11},{10,... | collective-permute-start | bytes 786440 | tf_op jit(solution)/shard_map/ppermute | solution.py:98
  14.7 2.3 %lists.1 = (s32[264]{0:T(512)}, s32[264]{0:T(512)}, s32[264]{0:T(512)}, s32[264]{0:T(512)}, s32[264]{0:T(512)}) custom-call(s32[2]{0:T(128)} %pad_add_fusion.info, s32[32]{0:T(128)} %deal.1, s32[4]{0:T(128)} %lengths.1, s32[8]{0:T(128)} %call_exported.0.codes), custom_call_target="tpu_custom_call" | custom-call | bytes 5464 | tf_op jit(solution)/shard_map/lists/pallas_call | solution.py:53
  17.1 10.9 %collective-permute-done.refs_1_.refs_9_ = bf16[256,512]{1,0:T(8,128)(2,1)S(1)} collective-permute-done((bf16[256,512]{1,0:T(8,128)(2,1)}, bf16[256,512]{1,0:T(8,128)(2,1)S(1)}, u32[]{:S(2)}, u32[]{:S(2)}) %collective-permute-start) | collective-permute-done | bytes 262176 | tf_op jit(solution)/shard_map/ppermute | solution.py:98
  31.4 4.8 %project.1 = (bf16[8,192,128]{2,1,0:T(8,128)(2,1)}, bf16[8,192,128]{2,1,0:T(8,128)(2,1)}, bf16[8,192,512]{2,1,0:T(8,128)(2,1)}, bf16[512,256]{1,0:T(8,128)(2,1)}, f32[8,512]{1,0:T(8,128)}) custom-call(s32[2]{0:T(128)} %pad_add_fusion.info, bf16[256,512]{1,0:T(8,128)(2,1)} %get-tuple-element.91.refs_0_.refs_8_, bf16[256,512]{1,0:T(8,128)(2,1)} %copy-done.5, ...), custom_call_target="tpu_custom_call" | custom-call | flops 402653184 | bytes 5783560 | tf_op jit(solution)/shard_map/project/pallas_call | solution.py:53
  39.3 6.5 %collective-permute-start.9 = (bf16[10,16,512]{2,1,0:T(8,128)(2,1)S(1)}, bf16[10,16,512]{2,1,0:T(8,128)(2,1)S(1)}, u32[]{:S(2)}, u32[]{:S(2)}) collective-permute-start(bf16[10,16,512]{2,1,0:T(8,128)(2,1)S(1)} %maximum_maximum_fusion), channel_id=1, source_target_pairs={{0,2},{1,3},{2,0},{3,1},{4,6},{5,7},{6,4},{7,5},{8,10},{9,11},{10,... | collective-permute-start | bytes 491528 | tf_op jit(solution)/shard_map/ppermute | solution.py:98
  45.8 7.4 %collective-permute-done.9 = bf16[10,16,512]{2,1,0:T(8,128)(2,1)S(1)} collective-permute-done((bf16[10,16,512]{2,1,0:T(8,128)(2,1)S(1)}, bf16[10,16,512]{2,1,0:T(8,128)(2,1)S(1)}, u32[]{:S(2)}, u32[]{:S(2)}) %collective-permute-start.9) | collective-permute-done | bytes 163872 | tf_op jit(solution)/shard_map/ppermute | solution.py:98
  54.4 5.4 %attend.3 = (f32[8,1,192]{2,1,0:T(1,128)}, f32[8,1,192]{2,1,0:T(1,128)}, f32[8,128,192]{2,1,0:T(8,128)}) custom-call(s32[2]{0:T(128)} %pad_add_fusion.info, s32[264]{0:T(512)} %get-tuple-element.96.pairs, bf16[8,192,128]{2,1,0:T(8,128)(2,1)} %get-tuple-element.100.q_ref, bf16[8,192,128]{2,1,0:T(8,128)(2,1)} %get-tuple-element.101.refs_0_), custom_call_target="tpu_custom_call" | custom-call | flops 2113929216 | bytes 1586216 | tf_op jit(solution)/shard_map/attend/pallas_call | solution.py:53
  59.8 2.9 %collective-permute-done.11 = bf16[2,10,16,512]{3,2,1,0:T(8,128)(2,1)S(1)} collective-permute-done((bf16[2,10,16,512]{3,2,1,0:T(8,128)(2,1)S(1)}, bf16[2,10,16,512]{3,2,1,0:T(8,128)(2,1)S(1)}, u32[]{:S(2)}, u32[]{:S(2)}) %collective-permute-start.11) | collective-permute-done | bytes 327712 | tf_op jit(solution)/shard_map/ppermute | solution.py:98
  64.0 5.9 %attend.4 = (f32[8,1,192]{2,1,0:T(1,128)}, f32[8,1,192]{2,1,0:T(1,128)}, f32[8,128,192]{2,1,0:T(8,128)}) custom-call(s32[2]{0:T(128)} %pad_add_fusion.info, s32[264]{0:T(512)} %get-tuple-element.106.pairs, bf16[8,192,128]{2,1,0:T(8,128)(2,1)} %get-tuple-element.100.q_ref, bf16[8,192,128]{2,1,0:T(8,128)(2,1)} %copy-done.32, bf16[8,192,128]{2,1,0:T(8,128)(2,1)} %copy-done.33, ...), custom_call_target="tpu_custom_call" | custom-call | flops 4227858432 | bytes 2778152 | tf_op jit(solution)/shard_map/attend/pallas_call | solution.py:53
  69.9 6.0 %attend.5 = (f32[8,1,192]{2,1,0:T(1,128)}, f32[8,1,192]{2,1,0:T(1,128)}, f32[8,128,192]{2,1,0:T(8,128)}, bf16[4,192,128]{2,1,0:T(8,128)(2,1)}, bf16[4,192,128]{2...) custom-call(s32[2]{0:T(128)} %pad_add_fusion.info, s32[264]{0:T(512)} %get-tuple-element.99.pairs, ...), custom_call_target="tpu_custom_call" | custom-call | flops 2113929216 | bytes 3570728 | tf_op jit(solution)/shard_map/attend/pallas_call | solution.py:53
  78.3 2.6 %collective-permute-start.18 = (bf16[4,10,16,512]{3,2,1,0:T(8,128)(2,1)S(1)}, bf16[4,10,16,512]{3,2,1,0:T(8,128)(2,1)S(1)}, u32[]{:S(2)}, u32[]{:S(2)}) collective-permute-start(bf16[4,10,16,512]{3,2,1,0:T(8,128)(2,1)S(1)} %collective-permute-done.16), channel_id=1, source_target_pairs={{0,16},{1,17},{2,18},{3,19},{4,12},{5,13},{6,14},{7,15},{8,24},{9,... | collective-permute-start | bytes 1966088 | tf_op jit(solution)/shard_map/ppermute | solution.py:106
  84.4 2.5 %collective-permute-start.13 = (bf16[192,128]{1,0:T(8,128)(2,1)S(1)}, bf16[192,128]{1,0:T(8,128)(2,1)S(1)}, u32[]{:S(2)}, u32[]{:S(2)}) collective-permute-start(bf16[192,128]{1,0:T(8,128)(2,1)S(1)} %get-tuple-element.173), channel_id=1, source_target_pairs={{0,1},{1,0},{2,3},{3,2},{4,5},{5,4},{6,7},{7,6},{8,9},{9,8},{10,11... | collective-permute-start | bytes 147464 | tf_op jit(solution)/shard_map/ppermute | solution.py:98
  92.3 8.3 %mlp.1 = (bf16[192,512]{1,0:T(8,128)(2,1)}, f32[8,128]{1,0:T(8,128)}, f32[192,512]{1,0:T(8,128)}, bf16[192,128]{1,0:T(8,128)(2,1)}, bf16[192,128]{1,0:T(8,128)(2...) custom-call(s32[2]{0:T(128)} %pad_add_fusion.info, ...), custom_call_target="tpu_custom_call" | custom-call | flops 1610612736 | bytes 8819468 | tf_op jit(solution)/shard_map/mlp/pallas_call | solution.py:53
  100.6 4.4 %mlp_grads.1 = (bf16[4,4,10,16,512]{4,3,2,1,0:T(8,128)(2,1)}, bf16[4,4,10,16,512]{4,3,2,1,0:T(8,128)(2,1)}) custom-call(s32[2]{0:T(128)} %pad_add_fusion.info, bf16[4,192,512]{2,1,0:T(8,128)(2,1)} %get-tuple-element.122.act_ref, bf16[4,192,512]{2,1,0:T(8,128)(2,1)} %get-tuple-element.123.gpre_ref, bf16[192,512]{1,0:T(8,128)(2,1)} %get-tuple-element.124.n2_ref, ...), custom_call_target="tpu_custom_call" | custom-call | flops 805306368 | bytes 7622664 | tf_op jit(solution)/shard_map/mlp_grads/pallas_call | solution.py:53
  109.6 2.8 %collective-permute-done.24.refs_5_ = bf16[192,128]{1,0:T(8,128)(2,1)S(1)} collective-permute-done((bf16[192,128]{1,0:T(8,128)(2,1)S(1)}, bf16[192,128]{1,0:T(8,128)(2,1)S(1)}, u32[]{:S(2)}, u32[]{:S(2)}) %collective-permute-start.24) | collective-permute-done | bytes 49184 | tf_op jit(solution)/shard_map/ppermute | solution.py:98
  114.2 3.0 %add_convert_fusion = bf16[2,4,10,16,512]{4,3,2,1,0:T(8,128)(2,1)} fusion(bf16[4,4,10,16,512]{4,3,2,1,0:T(8,128)(2,1)S(1)} %collective-permute-done.22, bf16[4,4,10,16,512]{4,3,2,1,0:T(8,128)(2,1)} %get-tuple-element.129), kind=kLoop, calls=%fused_computation | loop fusion | flops 2621440 | bytes 3932160 | tf_op jit(solution)/shard_map/convert_element_type | solution.py:996
  117.1 3.4 %collective-permute-start.27 = (bf16[2,4,10,16,512]{4,3,2,1,0:T(8,128)(2,1)}, bf16[2,4,10,16,512]{4,3,2,1,0:T(8,128)(2,1)}, u32[]{:S(2)}, u32[]{:S(2)}) collective-permute-start(bf16[2,4,10,16,512]{4,3,2,1,0:T(8,128)(2,1)} %add_convert_fusion), channel_id=1, source_target_pairs={{0,16},{1,17},{2,18},{3,19},{4,12},{5,13},{6,14},{7,15},{8,24},{9,... | collective-permute-start | bytes 3932168 | tf_op jit(solution)/shard_map/ppermute | solution.py:106
  121.3 6.4 %attend_back.3 = (bf16[8,192,128]{2,1,0:T(8,128)(2,1)}, bf16[8,192,128]{2,1,0:T(8,128)(2,1)}, f32[8,64,192]{2,1,0:T(8,128)}, bf16[8,192,128]{2,1,0:T(8,128)(2,1)}, f32[8,1,192]{2,1,0:T(1,128)}) custom-call(s32[2]{0:T(128)} %pad_add_fusion.info, s32[264]{0:T(512)} %get-tuple-element.120.pairs, bf16[8,192,128]{2,1,0:T(8,128)(2,1)} %get-tuple-element.100.q_ref, ...), custom_call_target="tpu_custom_call" | custom-call | flops 10569646080 | bytes 3945512 | tf_op jit(solution)/shard_map/attend_back/pallas_call | solution.py:53
  127.7 2.8 %collective-permute-start.29 = (bf16[8,192,128]{2,1,0:T(8,128)(2,1)}, bf16[8,192,128]{2,1,0:T(8,128)(2,1)}, u32[]{:S(2)}, u32[]{:S(2)}) collective-permute-start(bf16[8,192,128]{2,1,0:T(8,128)(2,1)} %get-tuple-element.150), channel_id=1, source_target_pairs={{0,16},{1,17},{2,18},{3,19},{4,12},{5,13},{6,14},{7,15},{8,24},{9,... | collective-permute-start | bytes 1179656 | tf_op jit(solution)/shard_map/ppermute | solution.py:106
  130.5 4.7 %attend_back.4 = (bf16[8,192,128]{2,1,0:T(8,128)(2,1)}, f32[8,64,192]{2,1,0:T(8,128)}) custom-call(s32[2]{0:T(128)} %pad_add_fusion.info, s32[264]{0:T(512)} %get-tuple-element.138.pairs, bf16[8,192,128]{2,1,0:T(8,128)(2,1)} %get-tuple-element.100.q_ref, f32[8,1,192]{2,1,0:T(1,128)} %get-tuple-element.119.lse_ref, bf16[8,192,128]{2,1,0:T(8,128)(2,1)} %copy-done.32, ...), custom_call_target="tpu_custom_call" | custom-call | flops 5284823040 | bytes 2372648 | tf_op jit(solution)/shard_map/attend_back/pallas_call | solution.py:53
  138.8 3.3 %collective-permute-start.38 = (bf16[4,10,16,512]{3,2,1,0:T(8,128)(2,1)}, bf16[4,10,16,512]{3,2,1,0:T(8,128)(2,1)}, u32[]{:S(2)}, u32[]{:S(2)}) collective-permute-start(bf16[4,10,16,512]{3,2,1,0:T(8,128)(2,1)} %fusion.1), channel_id=1, source_target_pairs={{0,8},{1,9},{2,10},{3,11},{4,20},{5,21},{6,22},{7,23},{8,0},{9,1},... | collective-permute-start | bytes 1966088 | tf_op jit(solution)/shard_map/ppermute | solution.py:106
  144.9 7.0 %attend_back.5 = (bf16[8,192,128]{2,1,0:T(8,128)(2,1)}, f32[8,64,192]{2,1,0:T(8,128)}, bf16[8,192,128]{2,1,0:T(8,128)(2,1)}) custom-call(s32[2]{0:T(128)} %pad_add_fusion.info, s32[264]{0:T(512)} %get-tuple-element.96.pairs, bf16[8,192,128]{2,1,0:T(8,128)(2,1)} %get-tuple-element.100.q_ref, f32[8,1,192]{2,1,0:T(1,128)} %get-tuple-element.119.lse_ref, ...), custom_call_target="tpu_custom_call" | custom-call | flops 5284823040 | bytes 2765864 | tf_op jit(solution)/shard_map/attend_back/pallas_call | solution.py:53
  152.0 4.3 %collective-permute-done.30.refs_10_ = bf16[8,192,128]{2,1,0:T(8,128)(2,1)} collective-permute-done((bf16[8,192,128]{2,1,0:T(8,128)(2,1)}, bf16[8,192,128]{2,1,0:T(8,128)(2,1)}, u32[]{:S(2)}, u32[]{:S(2)}) %collective-permute-start.30) | collective-permute-done | bytes 393248 | tf_op jit(solution)/shard_map/ppermute | solution.py:106
  156.3 5.7 %head_grads.1 = (bf16[4,192,512]{2,1,0:T(8,128)(2,1)}, bf16[4,192,512]{2,1,0:T(8,128)(2,1)}, bf16[4,64,512]{2,1,0:T(8,128)(2,1)}) custom-call(s32[2]{0:T(128)} %pad_add_fusion.info, bf16[8,192,128]{2,1,0:T(8,128)(2,1)} %get-tuple-element.144.dq_ref, bf16[512,256]{1,0:T(8,128)(2,1)} %get-tuple-element.145.wh_ref, ...), custom_call_target="tpu_custom_call" | custom-call | flops 805306368 | bytes 7340040 | tf_op jit(solution)/shard_map/head_grads/pallas_call | solution.py:53
  170.2 4.8 %collective-permute-done.39 = bf16[2,10,16,512]{3,2,1,0:T(8,128)(2,1)S(1)} collective-permute-done((bf16[2,10,16,512]{3,2,1,0:T(8,128)(2,1)S(1)}, bf16[2,10,16,512]{3,2,1,0:T(8,128)(2,1)S(1)}, u32[]{:S(2)}, u32[]{:S(2)}) %collective-permute-start.39) | collective-permute-done | bytes 327712 | tf_op jit(solution)/shard_map/ppermute | solution.py:98
  176.9 2.5 %merge.1 = (bf16[256,512]{1,0:T(8,128)(2,1)}, bf16[256,512]{1,0:T(8,128)(2,1)}, bf16[256,512]{1,0:T(8,128)(2,1)}, bf16[256,512]{1,0:T(8,128)(2,1)}) custom-call(bf16[4,192,512]{2,1,0:T(8,128)(2,1)} %get-tuple-element.151.own_ref, bf16[4,192,512]{2,1,0:T(8,128)(2,1)} %copy-done.13, bf16[4,64,512]{2,1,0:T(8,128)(2,1)} %copy-done.12, bf16[4,64,512]{2,1,0:T(8,128)(2,1)} %copy-done.23), custom_call_target="tpu_custom_call" | custom-call | bytes 3145728 | tf_op jit(solution)/shard_map/merge/pallas_call | solution.py:53
  184.8 2.4 %collective-permute-start.41 = (bf16[10,16,512]{2,1,0:T(8,128)(2,1)S(1)}, bf16[10,16,512]{2,1,0:T(8,128)(2,1)S(1)}, u32[]{:S(2)}, u32[]{:S(2)}) collective-permute-start(bf16[10,16,512]{2,1,0:T(8,128)(2,1)S(1)} %fusion.2), channel_id=1, source_target_pairs={{0,8},{1,9},{2,10},{3,11},{4,20},{5,21},{6,22},{7,23},{8,0},{9,1},... | collective-permute-start | bytes 491528 | tf_op jit(solution)/shard_map/ppermute | solution.py:106
  189.2 3.1 %collective-permute-done.41 = bf16[10,16,512]{2,1,0:T(8,128)(2,1)S(1)} collective-permute-done((bf16[10,16,512]{2,1,0:T(8,128)(2,1)S(1)}, bf16[10,16,512]{2,1,0:T(8,128)(2,1)S(1)}, u32[]{:S(2)}, u32[]{:S(2)}) %collective-permute-start.41) | collective-permute-done | bytes 163872 | tf_op jit(solution)/shard_map/ppermute | solution.py:106
  192.6 3.5 %collective-permute-done.34.refs_1_ = bf16[256,512]{1,0:T(8,128)(2,1)S(1)} collective-permute-done((bf16[256,512]{1,0:T(8,128)(2,1)}, bf16[256,512]{1,0:T(8,128)(2,1)S(1)}, u32[]{:S(2)}, u32[]{:S(2)}) %collective-permute-start.34) | collective-permute-done | bytes 262176 | tf_op jit(solution)/shard_map/ppermute | solution.py:98
  197.8 4.7 %collective-permute-done.35.refs_2_ = bf16[256,512]{1,0:T(8,128)(2,1)S(1)} collective-permute-done((bf16[256,512]{1,0:T(8,128)(2,1)}, bf16[256,512]{1,0:T(8,128)(2,1)S(1)}, u32[]{:S(2)}, u32[]{:S(2)}) %collective-permute-start.35) | collective-permute-done | bytes 262176 | tf_op jit(solution)/shard_map/ppermute | solution.py:98
  205.2 4.4 %last.1 = (f32[192,512]{1,0:T(8,128)}, f32[128,1536]{1,0:T(8,128)}, f32[1,128]{1,0:T(1,128)}, f32[1,128]{1,0:T(1,128)}, f32[128,2048]{1,0:T(8,128)}, /*index=5*/...) custom-call(s32[2]{0:T(128)} %pad_add_fusion.info, ...), custom_call_target="tpu_custom_call" | custom-call | bytes 7034892 | tf_op jit(solution)/shard_map/last/pallas_call | solution.py:53
  (188 shorter events, 62.5 us)
Async XLA Ops:
  4.9 23.2 %collective-permute-start.1 = (bf16[256,512]{1,0:T(8,128)(2,1)}, bf16[256,512]{1,0:T(8,128)(2,1)S(1)}, u32[]{:S(2)}, u32[]{:S(2)}) collective-permute-start(bf16[256,512]{1,0:T(8,128)(2,1)} %get-tuple-element.93), channel_id=1, source_target_pairs={{0,2},{1,3},{2,0},{3,1},{4,6},{5,7},{6,4},{7,5},{8,10},{9,11},{10,... | collective-permute-start | bytes 786440 | tf_op jit(solution)/shard_map/ppermute | solution.py:98
  8.9 19.2 %collective-permute-start.2 = (bf16[256,512]{1,0:T(8,128)(2,1)}, bf16[256,512]{1,0:T(8,128)(2,1)S(1)}, u32[]{:S(2)}, u32[]{:S(2)}) collective-permute-start(bf16[256,512]{1,0:T(8,128)(2,1)} %get-tuple-element.94), channel_id=1, source_target_pairs={{0,3},{1,2},{2,1},{3,0},{4,7},{5,6},{6,5},{7,4},{8,11},{9,10},{10,... | collective-permute-start | bytes 786440 | tf_op jit(solution)/shard_map/ppermute | solution.py:98
  10.3 17.8 %collective-permute-start = (bf16[256,512]{1,0:T(8,128)(2,1)}, bf16[256,512]{1,0:T(8,128)(2,1)S(1)}, u32[]{:S(2)}, u32[]{:S(2)}) collective-permute-start(bf16[256,512]{1,0:T(8,128)(2,1)} %get-tuple-element.92), channel_id=1, source_target_pairs={{0,1},{1,0},{2,3},{3,2},{4,5},{5,4},{6,7},{7,6},{8,9},{9,8},{10,11... | collective-permute-start | bytes 786440 | tf_op jit(solution)/shard_map/ppermute | solution.py:98
  10.5 18.2 %collective-permute-start.3 = (bf16[256,512]{1,0:T(8,128)(2,1)}, bf16[256,512]{1,0:T(8,128)(2,1)S(1)}, u32[]{:S(2)}, u32[]{:S(2)}) collective-permute-start(bf16[256,512]{1,0:T(8,128)(2,1)} %get-tuple-element.91.refs_0_.refs_8_), channel_id=1, source_target_pairs={{0,4},{1,5},{2,6},{3,7},{4,0},{5,1},{6,2},{7,3},{8,12},{9,13},{10,... | collective-permute-start | bytes 786440 | tf_op jit(solution)/shard_map/ppermute | solution.py:98
  36.2 17.0 %collective-permute-start.10 = (bf16[8,192,128]{2,1,0:T(8,128)(2,1)}, bf16[8,192,128]{2,1,0:T(8,128)(2,1)S(1)}, u32[]{:S(2)}, u32[]{:S(2)}) collective-permute-start(bf16[8,192,128]{2,1,0:T(8,128)(2,1)} %get-tuple-element.101.refs_0_), channel_id=1, source_target_pairs={{0,16},{1,17},{2,18},{3,19},{4,12},{5,13},{6,14},{7,15},{8,24},{9,... | collective-permute-start | bytes 1179656 | tf_op jit(solution)/shard_map/ppermute | solution.py:106
  37.8 15.4 %collective-permute-start.7 = (bf16[8,192,128]{2,1,0:T(8,128)(2,1)}, bf16[8,192,128]{2,1,0:T(8,128)(2,1)S(1)}, u32[]{:S(2)}, u32[]{:S(2)}) collective-permute-start(bf16[8,192,128]{2,1,0:T(8,128)(2,1)} %get-tuple-element.101.refs_0_), channel_id=1, source_target_pairs={{0,8},{1,9},{2,10},{3,11},{4,20},{5,21},{6,22},{7,23},{8,0},{9,1},... | collective-permute-start | bytes 1179656 | tf_op jit(solution)/shard_map/ppermute | solution.py:106
  39.3 13.9 %collective-permute-start.9 = (bf16[10,16,512]{2,1,0:T(8,128)(2,1)S(1)}, bf16[10,16,512]{2,1,0:T(8,128)(2,1)S(1)}, u32[]{:S(2)}, u32[]{:S(2)}) collective-permute-start(bf16[10,16,512]{2,1,0:T(8,128)(2,1)S(1)} %maximum_maximum_fusion), channel_id=1, source_target_pairs={{0,2},{1,3},{2,0},{3,1},{4,6},{5,7},{6,4},{7,5},{8,10},{9,11},{10,... | collective-permute-start | bytes 491528 | tf_op jit(solution)/shard_map/ppermute | solution.py:98
  53.3 9.4 %collective-permute-start.11 = (bf16[2,10,16,512]{3,2,1,0:T(8,128)(2,1)S(1)}, bf16[2,10,16,512]{3,2,1,0:T(8,128)(2,1)S(1)}, u32[]{:S(2)}, u32[]{:S(2)}) collective-permute-start(bf16[2,10,16,512]{3,2,1,0:T(8,128)(2,1)S(1)} %pad_maximum_fusion.3), channel_id=1, source_target_pairs={{0,1},{1,0},{2,3},{3,2},{4,5},{5,4},{6,7},{7,6},{8,9},{9,8},{10,11... | collective-permute-start | bytes 983048 | tf_op jit(solution)/shard_map/ppermute | solution.py:98
  53.4 9.4 %collective-permute-start.8 = (bf16[8,192,128]{2,1,0:T(8,128)(2,1)S(1)}, bf16[8,192,128]{2,1,0:T(8,128)(2,1)S(1)}, u32[]{:S(2)}, u32[]{:S(2)}) collective-permute-start(bf16[8,192,128]{2,1,0:T(8,128)(2,1)S(1)} %collective-permute-done.7.refs_0_), channel_id=1, source_target_pairs={{0,16},{1,17},{2,18},{3,19},{4,12},{5,13},{6,14},{7,15},{8,24},{9,... | collective-permute-start | bytes 1179656 | tf_op jit(solution)/shard_map/ppermute | solution.py:106
  62.8 18.1 %collective-permute-start.17 = (bf16[4,10,16,512]{3,2,1,0:T(8,128)(2,1)S(1)}, bf16[4,10,16,512]{3,2,1,0:T(8,128)(2,1)S(1)}, u32[]{:S(2)}, u32[]{:S(2)}) collective-permute-start(bf16[4,10,16,512]{3,2,1,0:T(8,128)(2,1)S(1)} %pad_maximum_fusion.1.refs_9_), channel_id=1, source_target_pairs={{0,16},{1,17},{2,18},{3,19},{4,12},{5,13},{6,14},{7,15},{8,24},{9,... | collective-permute-start | bytes 1966088 | tf_op jit(solution)/shard_map/ppermute | solution.py:106
  63.4 15.0 %collective-permute-start.16 = (bf16[4,10,16,512]{3,2,1,0:T(8,128)(2,1)S(1)}, bf16[4,10,16,512]{3,2,1,0:T(8,128)(2,1)S(1)}, u32[]{:S(2)}, u32[]{:S(2)}) collective-permute-start(bf16[4,10,16,512]{3,2,1,0:T(8,128)(2,1)S(1)} %pad_maximum_fusion.1.refs_9_), channel_id=1, source_target_pairs={{0,8},{1,9},{2,10},{3,11},{4,20},{5,21},{6,22},{7,23},{8,0},{9,1},... | collective-permute-start | bytes 1966088 | tf_op jit(solution)/shard_map/ppermute | solution.py:106
  78.3 11.6 %collective-permute-start.18 = (bf16[4,10,16,512]{3,2,1,0:T(8,128)(2,1)S(1)}, bf16[4,10,16,512]{3,2,1,0:T(8,128)(2,1)S(1)}, u32[]{:S(2)}, u32[]{:S(2)}) collective-permute-start(bf16[4,10,16,512]{3,2,1,0:T(8,128)(2,1)S(1)} %collective-permute-done.16), channel_id=1, source_target_pairs={{0,16},{1,17},{2,18},{3,19},{4,12},{5,13},{6,14},{7,15},{8,24},{9,... | collective-permute-start | bytes 1966088 | tf_op jit(solution)/shard_map/ppermute | solution.py:106
  81.0 11.2 %collective-permute-start.20 = (bf16[2,4,10,16,512]{4,3,2,1,0:T(8,128)(2,1)S(1)}, bf16[2,4,10,16,512]{4,3,2,1,0:T(8,128)(2,1)}, u32[]{:S(2)}, u32[]{:S(2)}) collective-permute-start(bf16[2,4,10,16,512]{4,3,2,1,0:T(8,128)(2,1)S(1)} %pad_maximum_fusion.refs_10_), channel_id=1, source_target_pairs={{0,4},{1,5},{2,6},{3,7},{4,0},{5,1},{6,2},{7,3},{8,12},{9,13},{10,... | collective-permute-start | bytes 3932168 | tf_op jit(solution)/shard_map/ppermute | solution.py:98
  105.0 9.1 %collective-permute-start.22 = (bf16[4,4,10,16,512]{4,3,2,1,0:T(8,128)(2,1)}, bf16[4,4,10,16,512]{4,3,2,1,0:T(8,128)(2,1)S(1)}, u32[]{:S(2)}, u32[]{:S(2)}) collective-permute-start(bf16[4,4,10,16,512]{4,3,2,1,0:T(8,128)(2,1)} %get-tuple-element.130), channel_id=1, source_target_pairs={{0,4},{1,5},{2,6},{3,7},{4,0},{5,1},{6,2},{7,3},{8,12},{9,13},{10,... | collective-permute-start | bytes 7864328 | tf_op jit(solution)/shard_map/ppermute | solution.py:98
  106.2 6.2 %collective-permute-start.24 = (bf16[192,128]{1,0:T(8,128)(2,1)S(1)}, bf16[192,128]{1,0:T(8,128)(2,1)S(1)}, u32[]{:S(2)}, u32[]{:S(2)}) collective-permute-start(bf16[192,128]{1,0:T(8,128)(2,1)S(1)} %copy-done.40), channel_id=1, source_target_pairs={{0,2},{1,3},{2,0},{3,1},{4,6},{5,7},{6,4},{7,5},{8,10},{9,11},{10,... | collective-permute-start | bytes 147464 | tf_op jit(solution)/shard_map/ppermute | solution.py:98
  114.1 6.5 %collective-permute-start.26 = (bf16[4,192,128]{2,1,0:T(8,128)(2,1)S(1)}, bf16[4,192,128]{2,1,0:T(8,128)(2,1)S(1)}, u32[]{:S(2)}, u32[]{:S(2)}) collective-permute-start(bf16[4,192,128]{2,1,0:T(8,128)(2,1)S(1)} %pad_maximum_fusion.5), channel_id=1, source_target_pairs={{0,4},{1,5},{2,6},{3,7},{4,0},{5,1},{6,2},{7,3},{8,12},{9,13},{10,... | collective-permute-start | bytes 589832 | tf_op jit(solution)/shard_map/ppermute | solution.py:98
  117.1 19.3 %collective-permute-start.27 = (bf16[2,4,10,16,512]{4,3,2,1,0:T(8,128)(2,1)}, bf16[2,4,10,16,512]{4,3,2,1,0:T(8,128)(2,1)}, u32[]{:S(2)}, u32[]{:S(2)}) collective-permute-start(bf16[2,4,10,16,512]{4,3,2,1,0:T(8,128)(2,1)} %add_convert_fusion), channel_id=1, source_target_pairs={{0,16},{1,17},{2,18},{3,19},{4,12},{5,13},{6,14},{7,15},{8,24},{9,... | collective-permute-start | bytes 3932168 | tf_op jit(solution)/shard_map/ppermute | solution.py:106
  127.7 14.3 %collective-permute-start.29 = (bf16[8,192,128]{2,1,0:T(8,128)(2,1)}, bf16[8,192,128]{2,1,0:T(8,128)(2,1)}, u32[]{:S(2)}, u32[]{:S(2)}) collective-permute-start(bf16[8,192,128]{2,1,0:T(8,128)(2,1)} %get-tuple-element.150), channel_id=1, source_target_pairs={{0,16},{1,17},{2,18},{3,19},{4,12},{5,13},{6,14},{7,15},{8,24},{9,... | collective-permute-start | bytes 1179656 | tf_op jit(solution)/shard_map/ppermute | solution.py:106
  135.3 16.7 %collective-permute-start.28 = (bf16[8,192,128]{2,1,0:T(8,128)(2,1)}, bf16[8,192,128]{2,1,0:T(8,128)(2,1)S(1)}, u32[]{:S(2)}, u32[]{:S(2)}) collective-permute-start(bf16[8,192,128]{2,1,0:T(8,128)(2,1)} %get-tuple-element.149), channel_id=1, source_target_pairs={{0,16},{1,17},{2,18},{3,19},{4,12},{5,13},{6,14},{7,15},{8,24},{9,... | collective-permute-start | bytes 1179656 | tf_op jit(solution)/shard_map/ppermute | solution.py:106
  138.8 25.1 %collective-permute-start.38 = (bf16[4,10,16,512]{3,2,1,0:T(8,128)(2,1)}, bf16[4,10,16,512]{3,2,1,0:T(8,128)(2,1)}, u32[]{:S(2)}, u32[]{:S(2)}) collective-permute-start(bf16[4,10,16,512]{3,2,1,0:T(8,128)(2,1)} %fusion.1), channel_id=1, source_target_pairs={{0,8},{1,9},{2,10},{3,11},{4,20},{5,21},{6,22},{7,23},{8,0},{9,1},... | collective-permute-start | bytes 1966088 | tf_op jit(solution)/shard_map/ppermute | solution.py:106
  143.9 12.4 %collective-permute-start.30 = (bf16[8,192,128]{2,1,0:T(8,128)(2,1)}, bf16[8,192,128]{2,1,0:T(8,128)(2,1)}, u32[]{:S(2)}, u32[]{:S(2)}) collective-permute-start(bf16[8,192,128]{2,1,0:T(8,128)(2,1)} %add_convert_fusion.2), channel_id=1, source_target_pairs={{0,8},{1,9},{2,10},{3,11},{4,20},{5,21},{6,22},{7,23},{8,0},{9,1},... | collective-permute-start | bytes 1179656 | tf_op jit(solution)/shard_map/ppermute | solution.py:106
  162.0 6.6 %collective-permute-start.32 = (bf16[4,64,512]{2,1,0:T(8,128)(2,1)}, bf16[4,64,512]{2,1,0:T(8,128)(2,1)S(1)}, u32[]{:S(2)}, u32[]{:S(2)}) collective-permute-start(bf16[4,64,512]{2,1,0:T(8,128)(2,1)} %get-tuple-element.153), channel_id=1, source_target_pairs={{0,8},{1,9},{2,10},{3,11},{4,20},{5,21},{6,22},{7,23},{8,0},{9,1},... | collective-permute-start | bytes 786440 | tf_op jit(solution)/shard_map/ppermute | solution.py:106
  165.6 9.4 %collective-permute-start.39 = (bf16[2,10,16,512]{3,2,1,0:T(8,128)(2,1)S(1)}, bf16[2,10,16,512]{3,2,1,0:T(8,128)(2,1)S(1)}, u32[]{:S(2)}, u32[]{:S(2)}) collective-permute-start(bf16[2,10,16,512]{3,2,1,0:T(8,128)(2,1)S(1)} %slice.91), channel_id=1, source_target_pairs={{0,1},{1,0},{2,3},{3,2},{4,5},{5,4},{6,7},{7,6},{8,9},{9,8},{10,11... | collective-permute-start | bytes 983048 | tf_op jit(solution)/shard_map/ppermute | solution.py:98
  166.4 9.6 %collective-permute-start.31 = (bf16[4,192,512]{2,1,0:T(8,128)(2,1)S(1)}, bf16[4,192,512]{2,1,0:T(8,128)(2,1)S(1)}, u32[]{:S(2)}, u32[]{:S(2)}) collective-permute-start(bf16[4,192,512]{2,1,0:T(8,128)(2,1)S(1)} %copy-done.30), channel_id=1, source_target_pairs={{0,4},{1,5},{2,6},{3,7},{4,0},{5,1},{6,2},{7,3},{8,12},{9,13},{10,... | collective-permute-start | bytes 2359304 | tf_op jit(solution)/shard_map/ppermute | solution.py:98
  168.8 7.2 %collective-permute-start.33 = (bf16[4,64,512]{2,1,0:T(8,128)(2,1)S(1)}, bf16[4,64,512]{2,1,0:T(8,128)(2,1)S(1)}, u32[]{:S(2)}, u32[]{:S(2)}) collective-permute-start(bf16[4,64,512]{2,1,0:T(8,128)(2,1)S(1)} %add_convert_fusion.4.dw_ref), channel_id=1, source_target_pairs={{0,16},{1,17},{2,18},{3,19},{4,12},{5,13},{6,14},{7,15},{8,24},{9,... | collective-permute-start | bytes 786440 | tf_op jit(solution)/shard_map/ppermute | solution.py:106
  175.1 9.7 %collective-permute-start.40 = (bf16[10,16,512]{2,1,0:T(8,128)(2,1)S(1)}, bf16[10,16,512]{2,1,0:T(8,128)(2,1)S(1)}, u32[]{:S(2)}, u32[]{:S(2)}) collective-permute-start(bf16[10,16,512]{2,1,0:T(8,128)(2,1)S(1)} %slice_bitcast_fusion), channel_id=1, source_target_pairs={{0,2},{1,3},{2,0},{3,1},{4,6},{5,7},{6,4},{7,5},{8,10},{9,11},{10,... | collective-permute-start | bytes 491528 | tf_op jit(solution)/shard_map/ppermute | solution.py:98
  179.4 16.6 %collective-permute-start.34 = (bf16[256,512]{1,0:T(8,128)(2,1)}, bf16[256,512]{1,0:T(8,128)(2,1)S(1)}, u32[]{:S(2)}, u32[]{:S(2)}) collective-permute-start(bf16[256,512]{1,0:T(8,128)(2,1)} %get-tuple-element.155), channel_id=1, source_target_pairs={{0,1},{1,0},{2,3},{3,2},{4,5},{5,4},{6,7},{7,6},{8,9},{9,8},{10,11... | collective-permute-start | bytes 786440 | tf_op jit(solution)/shard_map/ppermute | solution.py:98
  181.2 21.4 %collective-permute-start.35 = (bf16[256,512]{1,0:T(8,128)(2,1)}, bf16[256,512]{1,0:T(8,128)(2,1)S(1)}, u32[]{:S(2)}, u32[]{:S(2)}) collective-permute-start(bf16[256,512]{1,0:T(8,128)(2,1)} %get-tuple-element.156), channel_id=1, source_target_pairs={{0,2},{1,3},{2,0},{3,1},{4,6},{5,7},{6,4},{7,5},{8,10},{9,11},{10,... | collective-permute-start | bytes 786440 | tf_op jit(solution)/shard_map/ppermute | solution.py:98
  181.9 20.7 %collective-permute-start.36 = (bf16[256,512]{1,0:T(8,128)(2,1)}, bf16[256,512]{1,0:T(8,128)(2,1)S(1)}, u32[]{:S(2)}, u32[]{:S(2)}) collective-permute-start(bf16[256,512]{1,0:T(8,128)(2,1)} %get-tuple-element.157), channel_id=1, source_target_pairs={{0,3},{1,2},{2,1},{3,0},{4,7},{5,6},{6,5},{7,4},{8,11},{9,10},{10,... | collective-permute-start | bytes 786440 | tf_op jit(solution)/shard_map/ppermute | solution.py:98
  184.8 7.5 %collective-permute-start.41 = (bf16[10,16,512]{2,1,0:T(8,128)(2,1)S(1)}, bf16[10,16,512]{2,1,0:T(8,128)(2,1)S(1)}, u32[]{:S(2)}, u32[]{:S(2)}) collective-permute-start(bf16[10,16,512]{2,1,0:T(8,128)(2,1)S(1)} %fusion.2), channel_id=1, source_target_pairs={{0,8},{1,9},{2,10},{3,11},{4,20},{5,21},{6,22},{7,23},{8,0},{9,1},... | collective-permute-start | bytes 491528 | tf_op jit(solution)/shard_map/ppermute | solution.py:106
  188.1 8.0 %collective-permute-start.42 = (bf16[10,16,512]{2,1,0:T(8,128)(2,1)S(1)}, bf16[10,16,512]{2,1,0:T(8,128)(2,1)S(1)}, u32[]{:S(2)}, u32[]{:S(2)}) collective-permute-start(bf16[10,16,512]{2,1,0:T(8,128)(2,1)S(1)} %fusion.2), channel_id=1, source_target_pairs={{0,16},{1,17},{2,18},{3,19},{4,12},{5,13},{6,14},{7,15},{8,24},{9,... | collective-permute-start | bytes 491528 | tf_op jit(solution)/shard_map/ppermute | solution.py:106
  197.7 6.5 %collective-permute-start.44 = (bf16[4,10,16,512]{3,2,1,0:T(8,128)(2,1)S(1)}, bf16[4,10,16,512]{3,2,1,0:T(8,128)(2,1)S(1)}, u32[]{:S(2)}, u32[]{:S(2)}) collective-permute-start(bf16[4,10,16,512]{3,2,1,0:T(8,128)(2,1)S(1)} %pad_maximum_fusion.2.refs_5_), channel_id=1, source_target_pairs={{0,4},{1,5},{2,6},{3,7},{4,0},{5,1},{6,2},{7,3},{8,12},{9,13},{10,... | collective-permute-start | bytes 1966088 | tf_op jit(solution)/shard_map/ppermute | solution.py:98
  (55 other events, 250.6 us)

commit v7 on v6

--- a/solution.py
+++ b/solution.py
@@ -13,7 +13,7 @@
 WT_HEADS = 4
 CHUNK = 512
 TILE = 16
-WIDE = 4
+WIDE = 8
 WIDE_BACK = 4
 F32 = jnp.float32
 BF16 = jnp.bfloat16

time: 214 us -> 211 us (0.986)
  starting transfers between devices: 53.7 us -> 50 us
    ppermute x16, starting transfers between devices: 25.5 us -> 20.8 us  [turn(): return lax.ppermute(x, ('ctx', 'wt'), perm)]
  transfers between devices with their start and end apart: 45 -> 45, of which waited for: 23 -> 23; matrix products, arithmetic and copies ran while one was open for 7% -> 7% of each run, Pallas kernels for 22% -> 23%
where the time goes in v7:
time: 211 us; the launch traced here: 207 us
  Pallas kernels  71 us (34%)
  waiting for transfers between devices  61.8 us (29%)
  starting transfers between devices  50 us (24%)
  other arithmetic  12.8 us (6%)
  local copies, waits for them, and re-layouts  8.89 us (4%)
  between operations  2.13 us (1%)
    pallas_call x14, Pallas kernels, call(): pl.pallas_call(body, name=name, out_shape=list(outs), in_specs=in_specs,...  71 us
    ppermute x29, waiting for transfers between devices, swap(): return lax.ppermute(x, ('ctx', 'wt'), perm)  48.2 us
    ppermute x29, starting transfers between devices, swap(): return lax.ppermute(x, ('ctx', 'wt'), perm)  29.2 us
    ppermute x16, starting transfers between devices, turn(): return lax.ppermute(x, ('ctx', 'wt'), perm)  20.8 us
    ppermute x16, waiting for transfers between devices, turn(): return lax.ppermute(x, ('ctx', 'wt'), perm)  13.6 us
    unnamed x84, local copies, waits for them, and re-layouts  4.38 us
  transfers between devices with their start and end apart: 45, of which 23 were waited for; matrix products, arithmetic and copies ran while one was open for 7% of the time, Pallas kernels for 23%

profile of v7, /device:TPU:0, one launch (start us, length us, event | category | flops | bytes accessed | tf_op | source)
XLA Modules:
  0.0 206.7 jit_solution(5942738837584334559)
XLA Ops:
  2.6 2.3 %pack.1 = (bf16[256,512]{1,0:T(8,128)(2,1)}, bf16[256,512]{1,0:T(8,128)(2,1)}, bf16[256,512]{1,0:T(8,128)(2,1)}, bf16[256,512]{1,0:T(8,128)(2,1)}) custom-call(s32[2]{0:T(128)} %pad_add_fusion.info, bf16[192,512]{1,0:T(8,128)(2,1)} %x_ref.1, bf16[128,1536]{1,0:T(8,128)(2,1)} %w_ref.1, bf16[4,128]{1,0:T(4,128)(2,1)} %pad_maximum_fusion.6.vec_ref), custom_call_target="tpu_custom_call" | custom-call | bytes 1639432 | tf_op jit(solution)/shard_map/pack/pallas_call | solution.py:53
  4.9 4.0 %collective-permute-start.1 = (bf16[256,512]{1,0:T(8,128)(2,1)}, bf16[256,512]{1,0:T(8,128)(2,1)S(1)}, u32[]{:S(2)}, u32[]{:S(2)}) collective-permute-start(bf16[256,512]{1,0:T(8,128)(2,1)} %get-tuple-element.93), channel_id=1, source_target_pairs={{0,2},{1,3},{2,0},{3,1},{4,6},{5,7},{6,4},{7,5},{8,10},{9,11},{10,... | collective-permute-start | bytes 786440 | tf_op jit(solution)/shard_map/ppermute | solution.py:98
  14.7 2.5 %lists.1 = (s32[268]{0:T(512)}, s32[268]{0:T(512)}, s32[268]{0:T(512)}, s32[268]{0:T(512)}, s32[268]{0:T(512)}) custom-call(s32[2]{0:T(128)} %pad_add_fusion.info, s32[32]{0:T(128)} %deal.1, s32[4]{0:T(128)} %lengths.1, s32[8]{0:T(128)} %call_exported.0.codes), custom_call_target="tpu_custom_call" | custom-call | bytes 5544 | tf_op jit(solution)/shard_map/lists/pallas_call | solution.py:53
  17.2 10.8 %collective-permute-done.refs_1_.refs_9_ = bf16[256,512]{1,0:T(8,128)(2,1)S(1)} collective-permute-done((bf16[256,512]{1,0:T(8,128)(2,1)}, bf16[256,512]{1,0:T(8,128)(2,1)S(1)}, u32[]{:S(2)}, u32[]{:S(2)}) %collective-permute-start) | collective-permute-done | bytes 262176 | tf_op jit(solution)/shard_map/ppermute | solution.py:98
  31.4 4.9 %project.1 = (bf16[8,192,128]{2,1,0:T(8,128)(2,1)}, bf16[8,192,128]{2,1,0:T(8,128)(2,1)}, bf16[8,192,512]{2,1,0:T(8,128)(2,1)}, bf16[512,256]{1,0:T(8,128)(2,1)}, f32[8,512]{1,0:T(8,128)}) custom-call(s32[2]{0:T(128)} %pad_add_fusion.info, bf16[256,512]{1,0:T(8,128)(2,1)} %get-tuple-element.91.refs_0_.refs_8_, bf16[256,512]{1,0:T(8,128)(2,1)} %copy-done.5, ...), custom_call_target="tpu_custom_call" | custom-call | flops 402653184 | bytes 5783560 | tf_op jit(solution)/shard_map/project/pallas_call | solution.py:53
  39.4 6.5 %collective-permute-start.9 = (bf16[10,16,512]{2,1,0:T(8,128)(2,1)S(1)}, bf16[10,16,512]{2,1,0:T(8,128)(2,1)S(1)}, u32[]{:S(2)}, u32[]{:S(2)}) collective-permute-start(bf16[10,16,512]{2,1,0:T(8,128)(2,1)S(1)} %maximum_maximum_fusion), channel_id=1, source_target_pairs={{0,2},{1,3},{2,0},{3,1},{4,6},{5,7},{6,4},{7,5},{8,10},{9,11},{10,... | collective-permute-start | bytes 491528 | tf_op jit(solution)/shard_map/ppermute | solution.py:98
  45.9 7.4 %collective-permute-done.9 = bf16[10,16,512]{2,1,0:T(8,128)(2,1)S(1)} collective-permute-done((bf16[10,16,512]{2,1,0:T(8,128)(2,1)S(1)}, bf16[10,16,512]{2,1,0:T(8,128)(2,1)S(1)}, u32[]{:S(2)}, u32[]{:S(2)}) %collective-permute-start.9) | collective-permute-done | bytes 163872 | tf_op jit(solution)/shard_map/ppermute | solution.py:98
  54.5 4.7 %attend.3 = (f32[8,1,192]{2,1,0:T(1,128)}, f32[8,1,192]{2,1,0:T(1,128)}, f32[8,128,192]{2,1,0:T(8,128)}) custom-call(s32[2]{0:T(128)} %pad_add_fusion.info, s32[268]{0:T(512)} %get-tuple-element.96.pairs, bf16[8,192,128]{2,1,0:T(8,128)(2,1)} %get-tuple-element.100.q_ref, bf16[8,192,128]{2,1,0:T(8,128)(2,1)} %get-tuple-element.101.refs_0_), custom_call_target="tpu_custom_call" | custom-call | flops 2113929216 | bytes 1586232 | tf_op jit(solution)/shard_map/attend/pallas_call | solution.py:53
  59.2 3.5 %collective-permute-done.11 = bf16[2,10,16,512]{3,2,1,0:T(8,128)(2,1)S(1)} collective-permute-done((bf16[2,10,16,512]{3,2,1,0:T(8,128)(2,1)S(1)}, bf16[2,10,16,512]{3,2,1,0:T(8,128)(2,1)S(1)}, u32[]{:S(2)}, u32[]{:S(2)}) %collective-permute-start.11) | collective-permute-done | bytes 327712 | tf_op jit(solution)/shard_map/ppermute | solution.py:98
  64.0 5.2 %attend.4 = (f32[8,1,192]{2,1,0:T(1,128)}, f32[8,1,192]{2,1,0:T(1,128)}, f32[8,128,192]{2,1,0:T(8,128)}) custom-call(s32[2]{0:T(128)} %pad_add_fusion.info, s32[268]{0:T(512)} %get-tuple-element.106.pairs, bf16[8,192,128]{2,1,0:T(8,128)(2,1)} %get-tuple-element.100.q_ref, bf16[8,192,128]{2,1,0:T(8,128)(2,1)} %copy-done.32, bf16[8,192,128]{2,1,0:T(8,128)(2,1)} %copy-done.33, ...), custom_call_target="tpu_custom_call" | custom-call | flops 4227858432 | bytes 2778168 | tf_op jit(solution)/shard_map/attend/pallas_call | solution.py:53
  69.2 6.6 %attend.5 = (f32[8,1,192]{2,1,0:T(1,128)}, f32[8,1,192]{2,1,0:T(1,128)}, f32[8,128,192]{2,1,0:T(8,128)}, bf16[4,192,128]{2,1,0:T(8,128)(2,1)}, bf16[4,192,128]{2...) custom-call(s32[2]{0:T(128)} %pad_add_fusion.info, s32[268]{0:T(512)} %get-tuple-element.99.pairs, ...), custom_call_target="tpu_custom_call" | custom-call | flops 2113929216 | bytes 3570744 | tf_op jit(solution)/shard_map/attend/pallas_call | solution.py:53
  81.6 2.1 collective-permute-start.15
  83.6 2.3 %collective-permute-start.13 = (bf16[192,128]{1,0:T(8,128)(2,1)S(1)}, bf16[192,128]{1,0:T(8,128)(2,1)S(1)}, u32[]{:S(2)}, u32[]{:S(2)}) collective-permute-start(bf16[192,128]{1,0:T(8,128)(2,1)S(1)} %get-tuple-element.173), channel_id=1, source_target_pairs={{0,1},{1,0},{2,3},{3,2},{4,5},{5,4},{6,7},{7,6},{8,9},{9,8},{10,11... | collective-permute-start | bytes 147464 | tf_op jit(solution)/shard_map/ppermute | solution.py:98
  91.9 8.3 %mlp.1 = (bf16[192,512]{1,0:T(8,128)(2,1)}, f32[8,128]{1,0:T(8,128)}, f32[192,512]{1,0:T(8,128)}, bf16[192,128]{1,0:T(8,128)(2,1)}, bf16[192,128]{1,0:T(8,128)(2...) custom-call(s32[2]{0:T(128)} %pad_add_fusion.info, ...), custom_call_target="tpu_custom_call" | custom-call | flops 1610612736 | bytes 8819468 | tf_op jit(solution)/shard_map/mlp/pallas_call | solution.py:53
  100.2 4.4 %mlp_grads.1 = (bf16[4,4,10,16,512]{4,3,2,1,0:T(8,128)(2,1)}, bf16[4,4,10,16,512]{4,3,2,1,0:T(8,128)(2,1)}) custom-call(s32[2]{0:T(128)} %pad_add_fusion.info, bf16[4,192,512]{2,1,0:T(8,128)(2,1)} %get-tuple-element.122.act_ref, bf16[4,192,512]{2,1,0:T(8,128)(2,1)} %get-tuple-element.123.gpre_ref, bf16[192,512]{1,0:T(8,128)(2,1)} %get-tuple-element.124.n2_ref, ...), custom_call_target="tpu_custom_call" | custom-call | flops 805306368 | bytes 7622664 | tf_op jit(solution)/shard_map/mlp_grads/pallas_call | solution.py:53
  105.3 2.3 %collective-permute-start.24 = (bf16[192,128]{1,0:T(8,128)(2,1)S(1)}, bf16[192,128]{1,0:T(8,128)(2,1)S(1)}, u32[]{:S(2)}, u32[]{:S(2)}) collective-permute-start(bf16[192,128]{1,0:T(8,128)(2,1)S(1)} %copy-done.40), channel_id=1, source_target_pairs={{0,2},{1,3},{2,0},{3,1},{4,6},{5,7},{6,4},{7,5},{8,10},{9,11},{10,... | collective-permute-start | bytes 147464 | tf_op jit(solution)/shard_map/ppermute | solution.py:98
  109.2 2.4 %collective-permute-done.24.refs_5_ = bf16[192,128]{1,0:T(8,128)(2,1)S(1)} collective-permute-done((bf16[192,128]{1,0:T(8,128)(2,1)S(1)}, bf16[192,128]{1,0:T(8,128)(2,1)S(1)}, u32[]{:S(2)}, u32[]{:S(2)}) %collective-permute-start.24) | collective-permute-done | bytes 49184 | tf_op jit(solution)/shard_map/ppermute | solution.py:98
  113.6 3.0 %add_convert_fusion = bf16[2,4,10,16,512]{4,3,2,1,0:T(8,128)(2,1)} fusion(bf16[4,4,10,16,512]{4,3,2,1,0:T(8,128)(2,1)S(1)} %collective-permute-done.22, bf16[4,4,10,16,512]{4,3,2,1,0:T(8,128)(2,1)} %get-tuple-element.129), kind=kLoop, calls=%fused_computation | loop fusion | flops 2621440 | bytes 3932160 | tf_op jit(solution)/shard_map/convert_element_type | solution.py:996
  118.2 8.5 %attend_back.3 = (bf16[8,192,128]{2,1,0:T(8,128)(2,1)}, bf16[8,192,128]{2,1,0:T(8,128)(2,1)}, f32[8,64,192]{2,1,0:T(8,128)}, bf16[8,192,128]{2,1,0:T(8,128)(2,1)}, f32[8,1,192]{2,1,0:T(1,128)}) custom-call(s32[2]{0:T(128)} %pad_add_fusion.info, s32[268]{0:T(512)} %get-tuple-element.120.pairs, bf16[8,192,128]{2,1,0:T(8,128)(2,1)} %get-tuple-element.100.q_ref, ...), custom_call_target="tpu_custom_call" | custom-call | flops 10569646080 | bytes 3945528 | tf_op jit(solution)/shard_map/attend_back/pallas_call | solution.py:53
  127.3 4.1 %attend_back.4 = (bf16[8,192,128]{2,1,0:T(8,128)(2,1)}, f32[8,64,192]{2,1,0:T(8,128)}) custom-call(s32[2]{0:T(128)} %pad_add_fusion.info, s32[268]{0:T(512)} %get-tuple-element.138.pairs, bf16[8,192,128]{2,1,0:T(8,128)(2,1)} %get-tuple-element.100.q_ref, f32[8,1,192]{2,1,0:T(1,128)} %get-tuple-element.119.lse_ref, bf16[8,192,128]{2,1,0:T(8,128)(2,1)} %copy-done.32, ...), custom_call_target="tpu_custom_call" | custom-call | flops 5284823040 | bytes 2372664 | tf_op jit(solution)/shard_map/attend_back/pallas_call | solution.py:53
  131.3 2.2 %collective-permute-start.28 = (bf16[8,192,128]{2,1,0:T(8,128)(2,1)}, bf16[8,192,128]{2,1,0:T(8,128)(2,1)S(1)}, u32[]{:S(2)}, u32[]{:S(2)}) collective-permute-start(bf16[8,192,128]{2,1,0:T(8,128)(2,1)} %get-tuple-element.149), channel_id=1, source_target_pairs={{0,16},{1,17},{2,18},{3,19},{4,12},{5,13},{6,14},{7,15},{8,24},{9,... | collective-permute-start | bytes 1179656 | tf_op jit(solution)/shard_map/ppermute | solution.py:106
  134.6 2.3 %fusion.1 = bf16[4,10,16,512]{3,2,1,0:T(8,128)(2,1)} fusion(bf16[4,4,10,16,512]{4,3,2,1,0:T(8,128)(2,1)S(1)} %collective-permute-done.22, bf16[2,4,10,16,512]{4,3,2,1,0:T(8,128)(2,1)} %collective-permute-done.27, bf16[4,4,10,16,512]{4,3,2,1,0:T(8,128)(2,1)S(1)} %copy-done.1), kind=kLoop, calls=%fused_computation.6 | loop fusion | flops 1966080 | bytes 2621440 | tf_op jit(solution)/shard_map/convert_element_type | solution.py:1010
  141.8 7.0 %attend_back.5 = (bf16[8,192,128]{2,1,0:T(8,128)(2,1)}, f32[8,64,192]{2,1,0:T(8,128)}, bf16[8,192,128]{2,1,0:T(8,128)(2,1)}) custom-call(s32[2]{0:T(128)} %pad_add_fusion.info, s32[268]{0:T(512)} %get-tuple-element.96.pairs, bf16[8,192,128]{2,1,0:T(8,128)(2,1)} %get-tuple-element.100.q_ref, f32[8,1,192]{2,1,0:T(1,128)} %get-tuple-element.119.lse_ref, ...), custom_call_target="tpu_custom_call" | custom-call | flops 5284823040 | bytes 2765880 | tf_op jit(solution)/shard_map/attend_back/pallas_call | solution.py:53
  148.9 4.9 %collective-permute-done.30.refs_10_ = bf16[8,192,128]{2,1,0:T(8,128)(2,1)} collective-permute-done((bf16[8,192,128]{2,1,0:T(8,128)(2,1)}, bf16[8,192,128]{2,1,0:T(8,128)(2,1)}, u32[]{:S(2)}, u32[]{:S(2)}) %collective-permute-start.30) | collective-permute-done | bytes 393248 | tf_op jit(solution)/shard_map/ppermute | solution.py:106
  153.8 5.7 %head_grads.1 = (bf16[4,192,512]{2,1,0:T(8,128)(2,1)}, bf16[4,192,512]{2,1,0:T(8,128)(2,1)}, bf16[4,64,512]{2,1,0:T(8,128)(2,1)}) custom-call(s32[2]{0:T(128)} %pad_add_fusion.info, bf16[8,192,128]{2,1,0:T(8,128)(2,1)} %get-tuple-element.144.dq_ref, bf16[512,256]{1,0:T(8,128)(2,1)} %get-tuple-element.145.wh_ref, ...), custom_call_target="tpu_custom_call" | custom-call | flops 805306368 | bytes 7340040 | tf_op jit(solution)/shard_map/head_grads/pallas_call | solution.py:53
  163.4 2.8 %collective-permute-done.32 = bf16[4,64,512]{2,1,0:T(8,128)(2,1)S(1)} collective-permute-done((bf16[4,64,512]{2,1,0:T(8,128)(2,1)}, bf16[4,64,512]{2,1,0:T(8,128)(2,1)S(1)}, u32[]{:S(2)}, u32[]{:S(2)}) %collective-permute-start.32) | collective-permute-done | bytes 262176 | tf_op jit(solution)/shard_map/ppermute | solution.py:106
  167.1 4.8 %collective-permute-done.39 = bf16[2,10,16,512]{3,2,1,0:T(8,128)(2,1)S(1)} collective-permute-done((bf16[2,10,16,512]{3,2,1,0:T(8,128)(2,1)S(1)}, bf16[2,10,16,512]{3,2,1,0:T(8,128)(2,1)S(1)}, u32[]{:S(2)}, u32[]{:S(2)}) %collective-permute-start.39) | collective-permute-done | bytes 327712 | tf_op jit(solution)/shard_map/ppermute | solution.py:98
  174.8 2.5 %merge.1 = (bf16[256,512]{1,0:T(8,128)(2,1)}, bf16[256,512]{1,0:T(8,128)(2,1)}, bf16[256,512]{1,0:T(8,128)(2,1)}, bf16[256,512]{1,0:T(8,128)(2,1)}) custom-call(bf16[4,192,512]{2,1,0:T(8,128)(2,1)} %get-tuple-element.151.own_ref, bf16[4,192,512]{2,1,0:T(8,128)(2,1)} %copy-done.13, bf16[4,64,512]{2,1,0:T(8,128)(2,1)} %copy-done.12, bf16[4,64,512]{2,1,0:T(8,128)(2,1)} %copy-done.23), custom_call_target="tpu_custom_call" | custom-call | bytes 3145728 | tf_op jit(solution)/shard_map/merge/pallas_call | solution.py:53
  178.8 2.9 %collective-permute-start.36 = (bf16[256,512]{1,0:T(8,128)(2,1)}, bf16[256,512]{1,0:T(8,128)(2,1)S(1)}, u32[]{:S(2)}, u32[]{:S(2)}) collective-permute-start(bf16[256,512]{1,0:T(8,128)(2,1)} %get-tuple-element.157), channel_id=1, source_target_pairs={{0,3},{1,2},{2,1},{3,0},{4,7},{5,6},{6,5},{7,4},{8,11},{9,10},{10,... | collective-permute-start | bytes 786440 | tf_op jit(solution)/shard_map/ppermute | solution.py:98
  188.2 2.2 %collective-permute-start.43 = (bf16[10,16,512]{2,1,0:T(8,128)(2,1)S(1)}, bf16[10,16,512]{2,1,0:T(8,128)(2,1)S(1)}, u32[]{:S(2)}, u32[]{:S(2)}) collective-permute-start(bf16[10,16,512]{2,1,0:T(8,128)(2,1)S(1)} %collective-permute-done.41), channel_id=1, source_target_pairs={{0,16},{1,17},{2,18},{3,19},{4,12},{5,13},{6,14},{7,15},{8,24},{9,... | collective-permute-start | bytes 491528 | tf_op jit(solution)/shard_map/ppermute | solution.py:106
  193.9 5.6 %collective-permute-done.35.refs_2_ = bf16[256,512]{1,0:T(8,128)(2,1)S(1)} collective-permute-done((bf16[256,512]{1,0:T(8,128)(2,1)}, bf16[256,512]{1,0:T(8,128)(2,1)S(1)}, u32[]{:S(2)}, u32[]{:S(2)}) %collective-permute-start.35) | collective-permute-done | bytes 262176 | tf_op jit(solution)/shard_map/ppermute | solution.py:98
  202.1 4.4 %last.1 = (f32[192,512]{1,0:T(8,128)}, f32[128,1536]{1,0:T(8,128)}, f32[1,128]{1,0:T(1,128)}, f32[1,128]{1,0:T(1,128)}, f32[128,2048]{1,0:T(8,128)}, /*index=5*/...) custom-call(s32[2]{0:T(128)} %pad_add_fusion.info, ...), custom_call_target="tpu_custom_call" | custom-call | bytes 7034892 | tf_op jit(solution)/shard_map/last/pallas_call | solution.py:53
  (188 shorter events, 61.5 us)
Async XLA Ops:
  4.9 23.2 %collective-permute-start.1 = (bf16[256,512]{1,0:T(8,128)(2,1)}, bf16[256,512]{1,0:T(8,128)(2,1)S(1)}, u32[]{:S(2)}, u32[]{:S(2)}) collective-permute-start(bf16[256,512]{1,0:T(8,128)(2,1)} %get-tuple-element.93), channel_id=1, source_target_pairs={{0,2},{1,3},{2,0},{3,1},{4,6},{5,7},{6,4},{7,5},{8,10},{9,11},{10,... | collective-permute-start | bytes 786440 | tf_op jit(solution)/shard_map/ppermute | solution.py:98
  8.9 19.2 %collective-permute-start.2 = (bf16[256,512]{1,0:T(8,128)(2,1)}, bf16[256,512]{1,0:T(8,128)(2,1)S(1)}, u32[]{:S(2)}, u32[]{:S(2)}) collective-permute-start(bf16[256,512]{1,0:T(8,128)(2,1)} %get-tuple-element.94), channel_id=1, source_target_pairs={{0,3},{1,2},{2,1},{3,0},{4,7},{5,6},{6,5},{7,4},{8,11},{9,10},{10,... | collective-permute-start | bytes 786440 | tf_op jit(solution)/shard_map/ppermute | solution.py:98
  10.3 17.8 %collective-permute-start = (bf16[256,512]{1,0:T(8,128)(2,1)}, bf16[256,512]{1,0:T(8,128)(2,1)S(1)}, u32[]{:S(2)}, u32[]{:S(2)}) collective-permute-start(bf16[256,512]{1,0:T(8,128)(2,1)} %get-tuple-element.92), channel_id=1, source_target_pairs={{0,1},{1,0},{2,3},{3,2},{4,5},{5,4},{6,7},{7,6},{8,9},{9,8},{10,11... | collective-permute-start | bytes 786440 | tf_op jit(solution)/shard_map/ppermute | solution.py:98
  10.5 18.2 %collective-permute-start.3 = (bf16[256,512]{1,0:T(8,128)(2,1)}, bf16[256,512]{1,0:T(8,128)(2,1)S(1)}, u32[]{:S(2)}, u32[]{:S(2)}) collective-permute-start(bf16[256,512]{1,0:T(8,128)(2,1)} %get-tuple-element.91.refs_0_.refs_8_), channel_id=1, source_target_pairs={{0,4},{1,5},{2,6},{3,7},{4,0},{5,1},{6,2},{7,3},{8,12},{9,13},{10,... | collective-permute-start | bytes 786440 | tf_op jit(solution)/shard_map/ppermute | solution.py:98
  36.3 17.0 %collective-permute-start.10 = (bf16[8,192,128]{2,1,0:T(8,128)(2,1)}, bf16[8,192,128]{2,1,0:T(8,128)(2,1)S(1)}, u32[]{:S(2)}, u32[]{:S(2)}) collective-permute-start(bf16[8,192,128]{2,1,0:T(8,128)(2,1)} %get-tuple-element.101.refs_0_), channel_id=1, source_target_pairs={{0,16},{1,17},{2,18},{3,19},{4,12},{5,13},{6,14},{7,15},{8,24},{9,... | collective-permute-start | bytes 1179656 | tf_op jit(solution)/shard_map/ppermute | solution.py:106
  37.9 15.4 %collective-permute-start.7 = (bf16[8,192,128]{2,1,0:T(8,128)(2,1)}, bf16[8,192,128]{2,1,0:T(8,128)(2,1)S(1)}, u32[]{:S(2)}, u32[]{:S(2)}) collective-permute-start(bf16[8,192,128]{2,1,0:T(8,128)(2,1)} %get-tuple-element.101.refs_0_), channel_id=1, source_target_pairs={{0,8},{1,9},{2,10},{3,11},{4,20},{5,21},{6,22},{7,23},{8,0},{9,1},... | collective-permute-start | bytes 1179656 | tf_op jit(solution)/shard_map/ppermute | solution.py:106
  39.4 13.9 %collective-permute-start.9 = (bf16[10,16,512]{2,1,0:T(8,128)(2,1)S(1)}, bf16[10,16,512]{2,1,0:T(8,128)(2,1)S(1)}, u32[]{:S(2)}, u32[]{:S(2)}) collective-permute-start(bf16[10,16,512]{2,1,0:T(8,128)(2,1)S(1)} %maximum_maximum_fusion), channel_id=1, source_target_pairs={{0,2},{1,3},{2,0},{3,1},{4,6},{5,7},{6,4},{7,5},{8,10},{9,11},{10,... | collective-permute-start | bytes 491528 | tf_op jit(solution)/shard_map/ppermute | solution.py:98
  53.3 9.4 %collective-permute-start.11 = (bf16[2,10,16,512]{3,2,1,0:T(8,128)(2,1)S(1)}, bf16[2,10,16,512]{3,2,1,0:T(8,128)(2,1)S(1)}, u32[]{:S(2)}, u32[]{:S(2)}) collective-permute-start(bf16[2,10,16,512]{3,2,1,0:T(8,128)(2,1)S(1)} %pad_maximum_fusion.3), channel_id=1, source_target_pairs={{0,1},{1,0},{2,3},{3,2},{4,5},{5,4},{6,7},{7,6},{8,9},{9,8},{10,11... | collective-permute-start | bytes 983048 | tf_op jit(solution)/shard_map/ppermute | solution.py:98
  53.4 9.4 %collective-permute-start.8 = (bf16[8,192,128]{2,1,0:T(8,128)(2,1)S(1)}, bf16[8,192,128]{2,1,0:T(8,128)(2,1)S(1)}, u32[]{:S(2)}, u32[]{:S(2)}) collective-permute-start(bf16[8,192,128]{2,1,0:T(8,128)(2,1)S(1)} %collective-permute-done.7.refs_0_), channel_id=1, source_target_pairs={{0,16},{1,17},{2,18},{3,19},{4,12},{5,13},{6,14},{7,15},{8,24},{9,... | collective-permute-start | bytes 1179656 | tf_op jit(solution)/shard_map/ppermute | solution.py:106
  62.8 17.1 %collective-permute-start.17 = (bf16[4,10,16,512]{3,2,1,0:T(8,128)(2,1)S(1)}, bf16[4,10,16,512]{3,2,1,0:T(8,128)(2,1)S(1)}, u32[]{:S(2)}, u32[]{:S(2)}) collective-permute-start(bf16[4,10,16,512]{3,2,1,0:T(8,128)(2,1)S(1)} %pad_maximum_fusion.1.refs_9_), channel_id=1, source_target_pairs={{0,16},{1,17},{2,18},{3,19},{4,12},{5,13},{6,14},{7,15},{8,24},{9,... | collective-permute-start | bytes 1966088 | tf_op jit(solution)/shard_map/ppermute | solution.py:106
  63.4 15.0 %collective-permute-start.16 = (bf16[4,10,16,512]{3,2,1,0:T(8,128)(2,1)S(1)}, bf16[4,10,16,512]{3,2,1,0:T(8,128)(2,1)S(1)}, u32[]{:S(2)}, u32[]{:S(2)}) collective-permute-start(bf16[4,10,16,512]{3,2,1,0:T(8,128)(2,1)S(1)} %pad_maximum_fusion.1.refs_9_), channel_id=1, source_target_pairs={{0,8},{1,9},{2,10},{3,11},{4,20},{5,21},{6,22},{7,23},{8,0},{9,1},... | collective-permute-start | bytes 1966088 | tf_op jit(solution)/shard_map/ppermute | solution.py:106
  78.4 11.2 %collective-permute-start.18 = (bf16[4,10,16,512]{3,2,1,0:T(8,128)(2,1)S(1)}, bf16[4,10,16,512]{3,2,1,0:T(8,128)(2,1)S(1)}, u32[]{:S(2)}, u32[]{:S(2)}) collective-permute-start(bf16[4,10,16,512]{3,2,1,0:T(8,128)(2,1)S(1)} %collective-permute-done.16), channel_id=1, source_target_pairs={{0,16},{1,17},{2,18},{3,19},{4,12},{5,13},{6,14},{7,15},{8,24},{9,... | collective-permute-start | bytes 1966088 | tf_op jit(solution)/shard_map/ppermute | solution.py:106
  80.1 11.8 %collective-permute-start.20 = (bf16[2,4,10,16,512]{4,3,2,1,0:T(8,128)(2,1)S(1)}, bf16[2,4,10,16,512]{4,3,2,1,0:T(8,128)(2,1)}, u32[]{:S(2)}, u32[]{:S(2)}) collective-permute-start(bf16[2,4,10,16,512]{4,3,2,1,0:T(8,128)(2,1)S(1)} %pad_maximum_fusion.refs_10_), channel_id=1, source_target_pairs={{0,4},{1,5},{2,6},{3,7},{4,0},{5,1},{6,2},{7,3},{8,12},{9,13},{10,... | collective-permute-start | bytes 3932168 | tf_op jit(solution)/shard_map/ppermute | solution.py:98
  81.6 6.2 %collective-permute-start.15 = (bf16[192,128]{1,0:T(8,128)(2,1)S(1)}, bf16[192,128]{1,0:T(8,128)(2,1)S(1)}, u32[]{:S(2)}, u32[]{:S(2)}) collective-permute-start(bf16[192,128]{1,0:T(8,128)(2,1)S(1)} %get-tuple-element.171), channel_id=1, source_target_pairs={{0,3},{1,2},{2,1},{3,0},{4,7},{5,6},{6,5},{7,4},{8,11},{9,10},{10,... | collective-permute-start | bytes 147464 | tf_op jit(solution)/shard_map/ppermute | solution.py:98
  104.6 9.0 %collective-permute-start.22 = (bf16[4,4,10,16,512]{4,3,2,1,0:T(8,128)(2,1)}, bf16[4,4,10,16,512]{4,3,2,1,0:T(8,128)(2,1)S(1)}, u32[]{:S(2)}, u32[]{:S(2)}) collective-permute-start(bf16[4,4,10,16,512]{4,3,2,1,0:T(8,128)(2,1)} %get-tuple-element.130), channel_id=1, source_target_pairs={{0,4},{1,5},{2,6},{3,7},{4,0},{5,1},{6,2},{7,3},{8,12},{9,13},{10,... | collective-permute-start | bytes 7864328 | tf_op jit(solution)/shard_map/ppermute | solution.py:98
  105.3 6.3 %collective-permute-start.24 = (bf16[192,128]{1,0:T(8,128)(2,1)S(1)}, bf16[192,128]{1,0:T(8,128)(2,1)S(1)}, u32[]{:S(2)}, u32[]{:S(2)}) collective-permute-start(bf16[192,128]{1,0:T(8,128)(2,1)S(1)} %copy-done.40), channel_id=1, source_target_pairs={{0,2},{1,3},{2,0},{3,1},{4,6},{5,7},{6,4},{7,5},{8,10},{9,11},{10,... | collective-permute-start | bytes 147464 | tf_op jit(solution)/shard_map/ppermute | solution.py:98
  116.6 18.0 %collective-permute-start.27 = (bf16[2,4,10,16,512]{4,3,2,1,0:T(8,128)(2,1)}, bf16[2,4,10,16,512]{4,3,2,1,0:T(8,128)(2,1)}, u32[]{:S(2)}, u32[]{:S(2)}) collective-permute-start(bf16[2,4,10,16,512]{4,3,2,1,0:T(8,128)(2,1)} %add_convert_fusion), channel_id=1, source_target_pairs={{0,16},{1,17},{2,18},{3,19},{4,12},{5,13},{6,14},{7,15},{8,24},{9,... | collective-permute-start | bytes 3932168 | tf_op jit(solution)/shard_map/ppermute | solution.py:106
  126.6 12.2 %collective-permute-start.29 = (bf16[8,192,128]{2,1,0:T(8,128)(2,1)}, bf16[8,192,128]{2,1,0:T(8,128)(2,1)}, u32[]{:S(2)}, u32[]{:S(2)}) collective-permute-start(bf16[8,192,128]{2,1,0:T(8,128)(2,1)} %get-tuple-element.150), channel_id=1, source_target_pairs={{0,16},{1,17},{2,18},{3,19},{4,12},{5,13},{6,14},{7,15},{8,24},{9,... | collective-permute-start | bytes 1179656 | tf_op jit(solution)/shard_map/ppermute | solution.py:106
  131.3 17.5 %collective-permute-start.28 = (bf16[8,192,128]{2,1,0:T(8,128)(2,1)}, bf16[8,192,128]{2,1,0:T(8,128)(2,1)S(1)}, u32[]{:S(2)}, u32[]{:S(2)}) collective-permute-start(bf16[8,192,128]{2,1,0:T(8,128)(2,1)} %get-tuple-element.149), channel_id=1, source_target_pairs={{0,16},{1,17},{2,18},{3,19},{4,12},{5,13},{6,14},{7,15},{8,24},{9,... | collective-permute-start | bytes 1179656 | tf_op jit(solution)/shard_map/ppermute | solution.py:106
  136.9 23.8 %collective-permute-start.38 = (bf16[4,10,16,512]{3,2,1,0:T(8,128)(2,1)}, bf16[4,10,16,512]{3,2,1,0:T(8,128)(2,1)}, u32[]{:S(2)}, u32[]{:S(2)}) collective-permute-start(bf16[4,10,16,512]{3,2,1,0:T(8,128)(2,1)} %fusion.1), channel_id=1, source_target_pairs={{0,8},{1,9},{2,10},{3,11},{4,20},{5,21},{6,22},{7,23},{8,0},{9,1},... | collective-permute-start | bytes 1966088 | tf_op jit(solution)/shard_map/ppermute | solution.py:106
  140.7 13.1 %collective-permute-start.30 = (bf16[8,192,128]{2,1,0:T(8,128)(2,1)}, bf16[8,192,128]{2,1,0:T(8,128)(2,1)}, u32[]{:S(2)}, u32[]{:S(2)}) collective-permute-start(bf16[8,192,128]{2,1,0:T(8,128)(2,1)} %add_convert_fusion.2), channel_id=1, source_target_pairs={{0,8},{1,9},{2,10},{3,11},{4,20},{5,21},{6,22},{7,23},{8,0},{9,1},... | collective-permute-start | bytes 1179656 | tf_op jit(solution)/shard_map/ppermute | solution.py:106
  159.5 6.6 %collective-permute-start.32 = (bf16[4,64,512]{2,1,0:T(8,128)(2,1)}, bf16[4,64,512]{2,1,0:T(8,128)(2,1)S(1)}, u32[]{:S(2)}, u32[]{:S(2)}) collective-permute-start(bf16[4,64,512]{2,1,0:T(8,128)(2,1)} %get-tuple-element.153), channel_id=1, source_target_pairs={{0,8},{1,9},{2,10},{3,11},{4,20},{5,21},{6,22},{7,23},{8,0},{9,1},... | collective-permute-start | bytes 786440 | tf_op jit(solution)/shard_map/ppermute | solution.py:106
  162.5 9.4 %collective-permute-start.39 = (bf16[2,10,16,512]{3,2,1,0:T(8,128)(2,1)S(1)}, bf16[2,10,16,512]{3,2,1,0:T(8,128)(2,1)S(1)}, u32[]{:S(2)}, u32[]{:S(2)}) collective-permute-start(bf16[2,10,16,512]{3,2,1,0:T(8,128)(2,1)S(1)} %slice.91), channel_id=1, source_target_pairs={{0,1},{1,0},{2,3},{3,2},{4,5},{5,4},{6,7},{7,6},{8,9},{9,8},{10,11... | collective-permute-start | bytes 983048 | tf_op jit(solution)/shard_map/ppermute | solution.py:98
  163.4 10.4 %collective-permute-start.31 = (bf16[4,192,512]{2,1,0:T(8,128)(2,1)S(1)}, bf16[4,192,512]{2,1,0:T(8,128)(2,1)S(1)}, u32[]{:S(2)}, u32[]{:S(2)}) collective-permute-start(bf16[4,192,512]{2,1,0:T(8,128)(2,1)S(1)} %copy-done.30), channel_id=1, source_target_pairs={{0,4},{1,5},{2,6},{3,7},{4,0},{5,1},{6,2},{7,3},{8,12},{9,13},{10,... | collective-permute-start | bytes 2359304 | tf_op jit(solution)/shard_map/ppermute | solution.py:98
  166.3 7.6 %collective-permute-start.33 = (bf16[4,64,512]{2,1,0:T(8,128)(2,1)S(1)}, bf16[4,64,512]{2,1,0:T(8,128)(2,1)S(1)}, u32[]{:S(2)}, u32[]{:S(2)}) collective-permute-start(bf16[4,64,512]{2,1,0:T(8,128)(2,1)S(1)} %add_convert_fusion.4.dw_ref), channel_id=1, source_target_pairs={{0,16},{1,17},{2,18},{3,19},{4,12},{5,13},{6,14},{7,15},{8,24},{9,... | collective-permute-start | bytes 786440 | tf_op jit(solution)/shard_map/ppermute | solution.py:106
  172.0 9.7 %collective-permute-start.40 = (bf16[10,16,512]{2,1,0:T(8,128)(2,1)S(1)}, bf16[10,16,512]{2,1,0:T(8,128)(2,1)S(1)}, u32[]{:S(2)}, u32[]{:S(2)}) collective-permute-start(bf16[10,16,512]{2,1,0:T(8,128)(2,1)S(1)} %slice_bitcast_fusion), channel_id=1, source_target_pairs={{0,2},{1,3},{2,0},{3,1},{4,6},{5,7},{6,4},{7,5},{8,10},{9,11},{10,... | collective-permute-start | bytes 491528 | tf_op jit(solution)/shard_map/ppermute | solution.py:98
  177.3 15.1 %collective-permute-start.34 = (bf16[256,512]{1,0:T(8,128)(2,1)}, bf16[256,512]{1,0:T(8,128)(2,1)S(1)}, u32[]{:S(2)}, u32[]{:S(2)}) collective-permute-start(bf16[256,512]{1,0:T(8,128)(2,1)} %get-tuple-element.155), channel_id=1, source_target_pairs={{0,1},{1,0},{2,3},{3,2},{4,5},{5,4},{6,7},{7,6},{8,9},{9,8},{10,11... | collective-permute-start | bytes 786440 | tf_op jit(solution)/shard_map/ppermute | solution.py:98
  178.1 21.4 %collective-permute-start.35 = (bf16[256,512]{1,0:T(8,128)(2,1)}, bf16[256,512]{1,0:T(8,128)(2,1)S(1)}, u32[]{:S(2)}, u32[]{:S(2)}) collective-permute-start(bf16[256,512]{1,0:T(8,128)(2,1)} %get-tuple-element.156), channel_id=1, source_target_pairs={{0,2},{1,3},{2,0},{3,1},{4,6},{5,7},{6,4},{7,5},{8,10},{9,11},{10,... | collective-permute-start | bytes 786440 | tf_op jit(solution)/shard_map/ppermute | solution.py:98
  178.8 20.7 %collective-permute-start.36 = (bf16[256,512]{1,0:T(8,128)(2,1)}, bf16[256,512]{1,0:T(8,128)(2,1)S(1)}, u32[]{:S(2)}, u32[]{:S(2)}) collective-permute-start(bf16[256,512]{1,0:T(8,128)(2,1)} %get-tuple-element.157), channel_id=1, source_target_pairs={{0,3},{1,2},{2,1},{3,0},{4,7},{5,6},{6,5},{7,4},{8,11},{9,10},{10,... | collective-permute-start | bytes 786440 | tf_op jit(solution)/shard_map/ppermute | solution.py:98
  181.8 6.4 %collective-permute-start.41 = (bf16[10,16,512]{2,1,0:T(8,128)(2,1)S(1)}, bf16[10,16,512]{2,1,0:T(8,128)(2,1)S(1)}, u32[]{:S(2)}, u32[]{:S(2)}) collective-permute-start(bf16[10,16,512]{2,1,0:T(8,128)(2,1)S(1)} %fusion.2), channel_id=1, source_target_pairs={{0,8},{1,9},{2,10},{3,11},{4,20},{5,21},{6,22},{7,23},{8,0},{9,1},... | collective-permute-start | bytes 491528 | tf_op jit(solution)/shard_map/ppermute | solution.py:106
  184.3 8.2 %collective-permute-start.42 = (bf16[10,16,512]{2,1,0:T(8,128)(2,1)S(1)}, bf16[10,16,512]{2,1,0:T(8,128)(2,1)S(1)}, u32[]{:S(2)}, u32[]{:S(2)}) collective-permute-start(bf16[10,16,512]{2,1,0:T(8,128)(2,1)S(1)} %fusion.2), channel_id=1, source_target_pairs={{0,16},{1,17},{2,18},{3,19},{4,12},{5,13},{6,14},{7,15},{8,24},{9,... | collective-permute-start | bytes 491528 | tf_op jit(solution)/shard_map/ppermute | solution.py:106
  193.8 7.3 %collective-permute-start.44 = (bf16[4,10,16,512]{3,2,1,0:T(8,128)(2,1)S(1)}, bf16[4,10,16,512]{3,2,1,0:T(8,128)(2,1)S(1)}, u32[]{:S(2)}, u32[]{:S(2)}) collective-permute-start(bf16[4,10,16,512]{3,2,1,0:T(8,128)(2,1)S(1)} %pad_maximum_fusion.2.refs_5_), channel_id=1, source_target_pairs={{0,4},{1,5},{2,6},{3,7},{4,0},{5,1},{6,2},{7,3},{8,12},{9,13},{10,... | collective-permute-start | bytes 1966088 | tf_op jit(solution)/shard_map/ppermute | solution.py:98
  (55 other events, 251.6 us)

commit v8 on v7

--- a/solution.py
+++ b/solution.py
@@ -118,11 +118,13 @@
 def pack_body(plan, shard, blk):
     nw, half = plan.n_wt, shard // 2
 
-    def body(info, words_ref, w_ref, vec_ref, *outs):
+    def body(info, words_ref, w_ref, *refs):
+        vecs, outs = refs[:4], refs[4:]
         odd = (info[0] % 2) == 1
         rows = lax.broadcasted_iota(jnp.int32, (4, 4 * HEAD), 0)
         pick = jnp.where(lane_iota((4, 4 * HEAD)) == rows + 3 * HEAD, 1.0, 0.0).astype(BF16)
-        vec = mm(vec_ref[...], pick, TN)
+        stacked = jnp.concatenate([v[...].astype(F32) for v in vecs], axis=0).astype(BF16)
+        vec = mm(stacked, pick, TN)
         lane = lane_iota((shard, 4 * HEAD))
         for m in range(nw):
             pair = plan.head(info[0], info[1] ^ m) // 2
@@ -823,12 +825,12 @@
     codes = jnp.array([mc * n_wt + mw for mc, mw in plan.slots], jnp.int32)
     core = (1, 0)
 
-    vecs_here = jnp.stack([gain_attn, shift_attn, gain_mlp, shift_mlp])
+    vecs_here = [v.reshape(1, shard) for v in (gain_attn, shift_attn, gain_mlp, shift_mlp)]
     load = call(
         pack_body(plan, shard, blk),
         "pack",
-        [info, words, w_qkv, vecs_here],
-        [SMEM] + [VMEM] * 3,
+        [info, words, w_qkv, *vecs_here],
+        [SMEM] + [VMEM] * 6,
         [sds((blk + shard // 2, width), BF16)] * n_wt,
     )
     loads = [load[0]] + [plan.swap(load[m], (0, m)) for m in range(1, n_wt)]

time: 211 us -> 211 us (level)
  starting transfers between devices: 50 us -> 55.9 us
  Pallas kernels: 71 us -> 65.6 us
    ppermute x16, starting transfers between devices: 20.8 us -> 27.7 us  [turn(): return lax.ppermute(x, ('ctx', 'wt'), perm)]
    pallas_call x14, Pallas kernels: 71 us -> 65.6 us  [call(): pl.pallas_call(body, name=name, out_shape=list(outs), in_specs=in_specs,...]
  transfers between devices with their start and end apart: 45 -> 45, of which waited for: 23 -> 23; matrix products, arithmetic and copies ran while one was open for 7% -> 7% of each run, Pallas kernels for 23% -> 20%
where the time goes in v8:
time: 211 us; the launch traced here: 207 us
  Pallas kernels  65.6 us (31%)
  waiting for transfers between devices  62.8 us (30%)
  starting transfers between devices  55.9 us (26%)
  other arithmetic  11.6 us (5%)
  local copies, waits for them, and re-layouts  8.89 us (4%)
  between operations  2.13 us (1%)
    pallas_call x14, Pallas kernels, call(): pl.pallas_call(body, name=name, out_shape=list(outs), in_specs=in_specs,...  65.6 us
    ppermute x29, waiting for transfers between devices, swap(): return lax.ppermute(x, ('ctx', 'wt'), perm)  49 us
    ppermute x29, starting transfers between devices, swap(): return lax.ppermute(x, ('ctx', 'wt'), perm)  28.2 us
    ppermute x16, starting transfers between devices, turn(): return lax.ppermute(x, ('ctx', 'wt'), perm)  27.7 us
    ppermute x16, waiting for transfers between devices, turn(): return lax.ppermute(x, ('ctx', 'wt'), perm)  13.9 us
    unnamed x84, local copies, waits for them, and re-layouts  4.38 us
  transfers between devices with their start and end apart: 45, of which 23 were waited for; matrix products, arithmetic and copies ran while one was open for 7% of the time, Pallas kernels for 20%

profile of v8, /device:TPU:0, one launch (start us, length us, event | category | flops | bytes accessed | tf_op | source)
XLA Modules:
  0.0 206.9 jit_solution(2263800224971870436)
XLA Ops:
  1.3 2.3 %pack.1 = (bf16[256,512]{1,0:T(8,128)(2,1)}, bf16[256,512]{1,0:T(8,128)(2,1)}, bf16[256,512]{1,0:T(8,128)(2,1)}, bf16[256,512]{1,0:T(8,128)(2,1)}) custom-call(s32[2]{0:T(128)} %pad_add_fusion.info, bf16[192,512]{1,0:T(8,128)(2,1)} %x_ref.1, bf16[128,1536]{1,0:T(8,128)(2,1)} %w_ref.1, bf16[1,128]{1,0:T(2,128)(2,1)} %bitcast.80, bf16[1,128]{1,0:T(2,128)(2,1)} %bitcast.81, ...), custom_call_target="tpu_custom_call" | custom-call | bytes 1639432 | tf_op jit(solution)/shard_map/pack/pallas_call | solution.py:53
  3.6 4.0 %collective-permute-start.1 = (bf16[256,512]{1,0:T(8,128)(2,1)}, bf16[256,512]{1,0:T(8,128)(2,1)S(1)}, u32[]{:S(2)}, u32[]{:S(2)}) collective-permute-start(bf16[256,512]{1,0:T(8,128)(2,1)} %get-tuple-element.93), channel_id=1, source_target_pairs={{0,2},{1,3},{2,0},{3,1},{4,6},{5,7},{6,4},{7,5},{8,10},{9,11},{10,... | collective-permute-start | bytes 786440 | tf_op jit(solution)/shard_map/ppermute | solution.py:98
  15.6 11.1 %collective-permute-done.refs_1_.refs_9_ = bf16[256,512]{1,0:T(8,128)(2,1)S(1)} collective-permute-done((bf16[256,512]{1,0:T(8,128)(2,1)}, bf16[256,512]{1,0:T(8,128)(2,1)S(1)}, u32[]{:S(2)}, u32[]{:S(2)}) %collective-permute-start) | collective-permute-done | bytes 262176 | tf_op jit(solution)/shard_map/ppermute | solution.py:98
  30.2 4.9 %project.1 = (bf16[8,192,128]{2,1,0:T(8,128)(2,1)}, bf16[8,192,128]{2,1,0:T(8,128)(2,1)}, bf16[8,192,512]{2,1,0:T(8,128)(2,1)}, bf16[512,256]{1,0:T(8,128)(2,1)}, f32[8,512]{1,0:T(8,128)}) custom-call(s32[2]{0:T(128)} %pad_add_fusion.info, bf16[256,512]{1,0:T(8,128)(2,1)} %get-tuple-element.91.refs_0_.refs_8_, bf16[256,512]{1,0:T(8,128)(2,1)} %copy-done.5, ...), custom_call_target="tpu_custom_call" | custom-call | flops 402653184 | bytes 5783560 | tf_op jit(solution)/shard_map/project/pallas_call | solution.py:53
  38.1 6.5 %collective-permute-start.9 = (bf16[10,16,512]{2,1,0:T(8,128)(2,1)S(1)}, bf16[10,16,512]{2,1,0:T(8,128)(2,1)S(1)}, u32[]{:S(2)}, u32[]{:S(2)}) collective-permute-start(bf16[10,16,512]{2,1,0:T(8,128)(2,1)S(1)} %maximum_maximum_fusion), channel_id=1, source_target_pairs={{0,2},{1,3},{2,0},{3,1},{4,6},{5,7},{6,4},{7,5},{8,10},{9,11},{10,... | collective-permute-start | bytes 491528 | tf_op jit(solution)/shard_map/ppermute | solution.py:98
  44.6 7.4 %collective-permute-done.9 = bf16[10,16,512]{2,1,0:T(8,128)(2,1)S(1)} collective-permute-done((bf16[10,16,512]{2,1,0:T(8,128)(2,1)S(1)}, bf16[10,16,512]{2,1,0:T(8,128)(2,1)S(1)}, u32[]{:S(2)}, u32[]{:S(2)}) %collective-permute-start.9) | collective-permute-done | bytes 163872 | tf_op jit(solution)/shard_map/ppermute | solution.py:98
  53.2 4.7 %attend.3 = (f32[8,1,192]{2,1,0:T(1,128)}, f32[8,1,192]{2,1,0:T(1,128)}, f32[8,128,192]{2,1,0:T(8,128)}) custom-call(s32[2]{0:T(128)} %pad_add_fusion.info, s32[268]{0:T(512)} %get-tuple-element.96.pairs, bf16[8,192,128]{2,1,0:T(8,128)(2,1)} %get-tuple-element.100.q_ref, bf16[8,192,128]{2,1,0:T(8,128)(2,1)} %get-tuple-element.101.refs_0_), custom_call_target="tpu_custom_call" | custom-call | flops 2113929216 | bytes 1586232 | tf_op jit(solution)/shard_map/attend/pallas_call | solution.py:53
  58.0 3.5 %collective-permute-done.11 = bf16[2,10,16,512]{3,2,1,0:T(8,128)(2,1)S(1)} collective-permute-done((bf16[2,10,16,512]{3,2,1,0:T(8,128)(2,1)S(1)}, bf16[2,10,16,512]{3,2,1,0:T(8,128)(2,1)S(1)}, u32[]{:S(2)}, u32[]{:S(2)}) %collective-permute-start.11) | collective-permute-done | bytes 327712 | tf_op jit(solution)/shard_map/ppermute | solution.py:98
  62.7 4.4 %attend.4 = (f32[8,1,192]{2,1,0:T(1,128)}, f32[8,1,192]{2,1,0:T(1,128)}, f32[8,128,192]{2,1,0:T(8,128)}) custom-call(s32[2]{0:T(128)} %pad_add_fusion.info, s32[268]{0:T(512)} %get-tuple-element.106.pairs, bf16[8,192,128]{2,1,0:T(8,128)(2,1)} %get-tuple-element.100.q_ref, bf16[8,192,128]{2,1,0:T(8,128)(2,1)} %copy-done.32, bf16[8,192,128]{2,1,0:T(8,128)(2,1)} %copy-done.33, ...), custom_call_target="tpu_custom_call" | custom-call | flops 4227858432 | bytes 2778168 | tf_op jit(solution)/shard_map/attend/pallas_call | solution.py:53
  67.1 5.7 %attend.5 = (f32[8,1,192]{2,1,0:T(1,128)}, f32[8,1,192]{2,1,0:T(1,128)}, f32[8,128,192]{2,1,0:T(8,128)}, bf16[4,192,128]{2,1,0:T(8,128)(2,1)}, bf16[4,192,128]{2...) custom-call(s32[2]{0:T(128)} %pad_add_fusion.info, s32[268]{0:T(512)} %get-tuple-element.99.pairs, ...), custom_call_target="tpu_custom_call" | custom-call | flops 2113929216 | bytes 3570744 | tf_op jit(solution)/shard_map/attend/pallas_call | solution.py:53
  74.5 2.6 %collective-permute-done.16 = bf16[4,10,16,512]{3,2,1,0:T(8,128)(2,1)S(1)} collective-permute-done((bf16[4,10,16,512]{3,2,1,0:T(8,128)(2,1)S(1)}, bf16[4,10,16,512]{3,2,1,0:T(8,128)(2,1)S(1)}, u32[]{:S(2)}, u32[]{:S(2)}) %collective-permute-start.16) | collective-permute-done | bytes 655392 | tf_op jit(solution)/shard_map/ppermute | solution.py:106
  77.2 2.4 %collective-permute-start.18 = (bf16[4,10,16,512]{3,2,1,0:T(8,128)(2,1)S(1)}, bf16[4,10,16,512]{3,2,1,0:T(8,128)(2,1)S(1)}, u32[]{:S(2)}, u32[]{:S(2)}) collective-permute-start(bf16[4,10,16,512]{3,2,1,0:T(8,128)(2,1)S(1)} %collective-permute-done.16), channel_id=1, source_target_pairs={{0,16},{1,17},{2,18},{3,19},{4,12},{5,13},{6,14},{7,15},{8,24},{9,... | collective-permute-start | bytes 1966088 | tf_op jit(solution)/shard_map/ppermute | solution.py:106
  83.0 2.6 %collective-permute-start.13 = (bf16[192,128]{1,0:T(8,128)(2,1)S(1)}, bf16[192,128]{1,0:T(8,128)(2,1)S(1)}, u32[]{:S(2)}, u32[]{:S(2)}) collective-permute-start(bf16[192,128]{1,0:T(8,128)(2,1)S(1)} %get-tuple-element.173), channel_id=1, source_target_pairs={{0,1},{1,0},{2,3},{3,2},{4,5},{5,4},{6,7},{7,6},{8,9},{9,8},{10,11... | collective-permute-start | bytes 147464 | tf_op jit(solution)/shard_map/ppermute | solution.py:98
  91.0 8.3 %mlp.1 = (bf16[192,512]{1,0:T(8,128)(2,1)}, f32[8,128]{1,0:T(8,128)}, f32[192,512]{1,0:T(8,128)}, bf16[192,128]{1,0:T(8,128)(2,1)}, bf16[192,128]{1,0:T(8,128)(2...) custom-call(s32[2]{0:T(128)} %pad_add_fusion.info, ...), custom_call_target="tpu_custom_call" | custom-call | flops 1610612736 | bytes 8819468 | tf_op jit(solution)/shard_map/mlp/pallas_call | solution.py:53
  99.3 4.4 %mlp_grads.1 = (bf16[4,4,10,16,512]{4,3,2,1,0:T(8,128)(2,1)}, bf16[4,4,10,16,512]{4,3,2,1,0:T(8,128)(2,1)}) custom-call(s32[2]{0:T(128)} %pad_add_fusion.info, bf16[4,192,512]{2,1,0:T(8,128)(2,1)} %get-tuple-element.122.act_ref, bf16[4,192,512]{2,1,0:T(8,128)(2,1)} %get-tuple-element.123.gpre_ref, bf16[192,512]{1,0:T(8,128)(2,1)} %get-tuple-element.124.n2_ref, ...), custom_call_target="tpu_custom_call" | custom-call | flops 805306368 | bytes 7622664 | tf_op jit(solution)/shard_map/mlp_grads/pallas_call | solution.py:53
  108.3 3.4 %collective-permute-done.24.refs_5_ = bf16[192,128]{1,0:T(8,128)(2,1)S(1)} collective-permute-done((bf16[192,128]{1,0:T(8,128)(2,1)S(1)}, bf16[192,128]{1,0:T(8,128)(2,1)S(1)}, u32[]{:S(2)}, u32[]{:S(2)}) %collective-permute-start.24) | collective-permute-done | bytes 49184 | tf_op jit(solution)/shard_map/ppermute | solution.py:98
  112.8 3.0 %add_convert_fusion = bf16[2,4,10,16,512]{4,3,2,1,0:T(8,128)(2,1)} fusion(bf16[4,4,10,16,512]{4,3,2,1,0:T(8,128)(2,1)S(1)} %collective-permute-done.22, bf16[4,4,10,16,512]{4,3,2,1,0:T(8,128)(2,1)} %get-tuple-element.129), kind=kLoop, calls=%fused_computation | loop fusion | flops 2621440 | bytes 3932160 | tf_op jit(solution)/shard_map/convert_element_type | solution.py:998
  118.4 5.1 %attend_back.3 = (bf16[8,192,128]{2,1,0:T(8,128)(2,1)}, bf16[8,192,128]{2,1,0:T(8,128)(2,1)}, f32[8,64,192]{2,1,0:T(8,128)}, bf16[8,192,128]{2,1,0:T(8,128)(2,1)}, f32[8,1,192]{2,1,0:T(1,128)}) custom-call(s32[2]{0:T(128)} %pad_add_fusion.info, s32[268]{0:T(512)} %get-tuple-element.120.pairs, bf16[8,192,128]{2,1,0:T(8,128)(2,1)} %get-tuple-element.100.q_ref, ...), custom_call_target="tpu_custom_call" | custom-call | flops 10569646080 | bytes 3945528 | tf_op jit(solution)/shard_map/attend_back/pallas_call | solution.py:53
  123.5 5.0 %collective-permute-start.29 = (bf16[8,192,128]{2,1,0:T(8,128)(2,1)}, bf16[8,192,128]{2,1,0:T(8,128)(2,1)}, u32[]{:S(2)}, u32[]{:S(2)}) collective-permute-start(bf16[8,192,128]{2,1,0:T(8,128)(2,1)} %get-tuple-element.150), channel_id=1, source_target_pairs={{0,16},{1,17},{2,18},{3,19},{4,12},{5,13},{6,14},{7,15},{8,24},{9,... | collective-permute-start | bytes 1179656 | tf_op jit(solution)/shard_map/ppermute | solution.py:106
  128.5 4.1 %attend_back.4 = (bf16[8,192,128]{2,1,0:T(8,128)(2,1)}, f32[8,64,192]{2,1,0:T(8,128)}) custom-call(s32[2]{0:T(128)} %pad_add_fusion.info, s32[268]{0:T(512)} %get-tuple-element.138.pairs, bf16[8,192,128]{2,1,0:T(8,128)(2,1)} %get-tuple-element.100.q_ref, f32[8,1,192]{2,1,0:T(1,128)} %get-tuple-element.119.lse_ref, bf16[8,192,128]{2,1,0:T(8,128)(2,1)} %copy-done.32, ...), custom_call_target="tpu_custom_call" | custom-call | flops 5284823040 | bytes 2372664 | tf_op jit(solution)/shard_map/attend_back/pallas_call | solution.py:53
  133.8 2.3 %fusion.1 = bf16[4,10,16,512]{3,2,1,0:T(8,128)(2,1)} fusion(bf16[4,4,10,16,512]{4,3,2,1,0:T(8,128)(2,1)S(1)} %collective-permute-done.22, bf16[2,4,10,16,512]{4,3,2,1,0:T(8,128)(2,1)} %collective-permute-done.27, bf16[4,4,10,16,512]{4,3,2,1,0:T(8,128)(2,1)S(1)} %copy-done.1), kind=kLoop, calls=%fused_computation.6 | loop fusion | flops 1966080 | bytes 2621440 | tf_op jit(solution)/shard_map/convert_element_type | solution.py:1012
  136.1 3.8 %collective-permute-start.38 = (bf16[4,10,16,512]{3,2,1,0:T(8,128)(2,1)}, bf16[4,10,16,512]{3,2,1,0:T(8,128)(2,1)}, u32[]{:S(2)}, u32[]{:S(2)}) collective-permute-start(bf16[4,10,16,512]{3,2,1,0:T(8,128)(2,1)} %fusion.1), channel_id=1, source_target_pairs={{0,8},{1,9},{2,10},{3,11},{4,20},{5,21},{6,22},{7,23},{8,0},{9,1},... | collective-permute-start | bytes 1966088 | tf_op jit(solution)/shard_map/ppermute | solution.py:106
  142.1 7.0 %attend_back.5 = (bf16[8,192,128]{2,1,0:T(8,128)(2,1)}, f32[8,64,192]{2,1,0:T(8,128)}, bf16[8,192,128]{2,1,0:T(8,128)(2,1)}) custom-call(s32[2]{0:T(128)} %pad_add_fusion.info, s32[268]{0:T(512)} %get-tuple-element.96.pairs, bf16[8,192,128]{2,1,0:T(8,128)(2,1)} %get-tuple-element.100.q_ref, f32[8,1,192]{2,1,0:T(1,128)} %get-tuple-element.119.lse_ref, ...), custom_call_target="tpu_custom_call" | custom-call | flops 5284823040 | bytes 2765880 | tf_op jit(solution)/shard_map/attend_back/pallas_call | solution.py:53
  149.2 4.3 %collective-permute-done.30.refs_10_ = bf16[8,192,128]{2,1,0:T(8,128)(2,1)} collective-permute-done((bf16[8,192,128]{2,1,0:T(8,128)(2,1)}, bf16[8,192,128]{2,1,0:T(8,128)(2,1)}, u32[]{:S(2)}, u32[]{:S(2)}) %collective-permute-start.30) | collective-permute-done | bytes 393248 | tf_op jit(solution)/shard_map/ppermute | solution.py:106
  153.5 5.7 %head_grads.1 = (bf16[4,192,512]{2,1,0:T(8,128)(2,1)}, bf16[4,192,512]{2,1,0:T(8,128)(2,1)}, bf16[4,64,512]{2,1,0:T(8,128)(2,1)}) custom-call(s32[2]{0:T(128)} %pad_add_fusion.info, bf16[8,192,128]{2,1,0:T(8,128)(2,1)} %get-tuple-element.144.dq_ref, bf16[512,256]{1,0:T(8,128)(2,1)} %get-tuple-element.145.wh_ref, ...), custom_call_target="tpu_custom_call" | custom-call | flops 805306368 | bytes 7340040 | tf_op jit(solution)/shard_map/head_grads/pallas_call | solution.py:53
  163.6 2.3 %collective-permute-done.32 = bf16[4,64,512]{2,1,0:T(8,128)(2,1)S(1)} collective-permute-done((bf16[4,64,512]{2,1,0:T(8,128)(2,1)}, bf16[4,64,512]{2,1,0:T(8,128)(2,1)S(1)}, u32[]{:S(2)}, u32[]{:S(2)}) %collective-permute-start.32) | collective-permute-done | bytes 262176 | tf_op jit(solution)/shard_map/ppermute | solution.py:106
  167.4 4.8 %collective-permute-done.39 = bf16[2,10,16,512]{3,2,1,0:T(8,128)(2,1)S(1)} collective-permute-done((bf16[2,10,16,512]{3,2,1,0:T(8,128)(2,1)S(1)}, bf16[2,10,16,512]{3,2,1,0:T(8,128)(2,1)S(1)}, u32[]{:S(2)}, u32[]{:S(2)}) %collective-permute-start.39) | collective-permute-done | bytes 327712 | tf_op jit(solution)/shard_map/ppermute | solution.py:98
  174.1 2.5 %merge.1 = (bf16[256,512]{1,0:T(8,128)(2,1)}, bf16[256,512]{1,0:T(8,128)(2,1)}, bf16[256,512]{1,0:T(8,128)(2,1)}, bf16[256,512]{1,0:T(8,128)(2,1)}) custom-call(bf16[4,192,512]{2,1,0:T(8,128)(2,1)} %get-tuple-element.151.own_ref, bf16[4,192,512]{2,1,0:T(8,128)(2,1)} %copy-done.13, bf16[4,64,512]{2,1,0:T(8,128)(2,1)} %copy-done.12, bf16[4,64,512]{2,1,0:T(8,128)(2,1)} %copy-done.23), custom_call_target="tpu_custom_call" | custom-call | bytes 3145728 | tf_op jit(solution)/shard_map/merge/pallas_call | solution.py:53
  182.0 3.0 %collective-permute-start.41 = (bf16[10,16,512]{2,1,0:T(8,128)(2,1)S(1)}, bf16[10,16,512]{2,1,0:T(8,128)(2,1)S(1)}, u32[]{:S(2)}, u32[]{:S(2)}) collective-permute-start(bf16[10,16,512]{2,1,0:T(8,128)(2,1)S(1)} %fusion.2), channel_id=1, source_target_pairs={{0,8},{1,9},{2,10},{3,11},{4,20},{5,21},{6,22},{7,23},{8,0},{9,1},... | collective-permute-start | bytes 491528 | tf_op jit(solution)/shard_map/ppermute | solution.py:106
  190.8 2.4 %collective-permute-done.34.refs_1_ = bf16[256,512]{1,0:T(8,128)(2,1)S(1)} collective-permute-done((bf16[256,512]{1,0:T(8,128)(2,1)}, bf16[256,512]{1,0:T(8,128)(2,1)S(1)}, u32[]{:S(2)}, u32[]{:S(2)}) %collective-permute-start.34) | collective-permute-done | bytes 262176 | tf_op jit(solution)/shard_map/ppermute | solution.py:98
  194.7 5.0 %collective-permute-done.35.refs_2_ = bf16[256,512]{1,0:T(8,128)(2,1)S(1)} collective-permute-done((bf16[256,512]{1,0:T(8,128)(2,1)}, bf16[256,512]{1,0:T(8,128)(2,1)S(1)}, u32[]{:S(2)}, u32[]{:S(2)}) %collective-permute-start.35) | collective-permute-done | bytes 262176 | tf_op jit(solution)/shard_map/ppermute | solution.py:98
  202.3 4.4 %last.1 = (f32[192,512]{1,0:T(8,128)}, f32[128,1536]{1,0:T(8,128)}, f32[1,128]{1,0:T(1,128)}, f32[1,128]{1,0:T(1,128)}, f32[128,2048]{1,0:T(8,128)}, /*index=5*/...) custom-call(s32[2]{0:T(128)} %pad_add_fusion.info, ...), custom_call_target="tpu_custom_call" | custom-call | bytes 7034892 | tf_op jit(solution)/shard_map/last/pallas_call | solution.py:53
  (187 shorter events, 61.9 us)
Async XLA Ops:
  3.6 23.2 %collective-permute-start.1 = (bf16[256,512]{1,0:T(8,128)(2,1)}, bf16[256,512]{1,0:T(8,128)(2,1)S(1)}, u32[]{:S(2)}, u32[]{:S(2)}) collective-permute-start(bf16[256,512]{1,0:T(8,128)(2,1)} %get-tuple-element.93), channel_id=1, source_target_pairs={{0,2},{1,3},{2,0},{3,1},{4,6},{5,7},{6,4},{7,5},{8,10},{9,11},{10,... | collective-permute-start | bytes 786440 | tf_op jit(solution)/shard_map/ppermute | solution.py:98
  7.7 19.2 %collective-permute-start.2 = (bf16[256,512]{1,0:T(8,128)(2,1)}, bf16[256,512]{1,0:T(8,128)(2,1)S(1)}, u32[]{:S(2)}, u32[]{:S(2)}) collective-permute-start(bf16[256,512]{1,0:T(8,128)(2,1)} %get-tuple-element.94), channel_id=1, source_target_pairs={{0,3},{1,2},{2,1},{3,0},{4,7},{5,6},{6,5},{7,4},{8,11},{9,10},{10,... | collective-permute-start | bytes 786440 | tf_op jit(solution)/shard_map/ppermute | solution.py:98
  9.0 17.8 %collective-permute-start = (bf16[256,512]{1,0:T(8,128)(2,1)}, bf16[256,512]{1,0:T(8,128)(2,1)S(1)}, u32[]{:S(2)}, u32[]{:S(2)}) collective-permute-start(bf16[256,512]{1,0:T(8,128)(2,1)} %get-tuple-element.92), channel_id=1, source_target_pairs={{0,1},{1,0},{2,3},{3,2},{4,5},{5,4},{6,7},{7,6},{8,9},{9,8},{10,11... | collective-permute-start | bytes 786440 | tf_op jit(solution)/shard_map/ppermute | solution.py:98
  9.2 18.2 %collective-permute-start.3 = (bf16[256,512]{1,0:T(8,128)(2,1)}, bf16[256,512]{1,0:T(8,128)(2,1)S(1)}, u32[]{:S(2)}, u32[]{:S(2)}) collective-permute-start(bf16[256,512]{1,0:T(8,128)(2,1)} %get-tuple-element.91.refs_0_.refs_8_), channel_id=1, source_target_pairs={{0,4},{1,5},{2,6},{3,7},{4,0},{5,1},{6,2},{7,3},{8,12},{9,13},{10,... | collective-permute-start | bytes 786440 | tf_op jit(solution)/shard_map/ppermute | solution.py:98
  35.1 17.0 %collective-permute-start.10 = (bf16[8,192,128]{2,1,0:T(8,128)(2,1)}, bf16[8,192,128]{2,1,0:T(8,128)(2,1)S(1)}, u32[]{:S(2)}, u32[]{:S(2)}) collective-permute-start(bf16[8,192,128]{2,1,0:T(8,128)(2,1)} %get-tuple-element.101.refs_0_), channel_id=1, source_target_pairs={{0,16},{1,17},{2,18},{3,19},{4,12},{5,13},{6,14},{7,15},{8,24},{9,... | collective-permute-start | bytes 1179656 | tf_op jit(solution)/shard_map/ppermute | solution.py:106
  36.6 15.4 %collective-permute-start.7 = (bf16[8,192,128]{2,1,0:T(8,128)(2,1)}, bf16[8,192,128]{2,1,0:T(8,128)(2,1)S(1)}, u32[]{:S(2)}, u32[]{:S(2)}) collective-permute-start(bf16[8,192,128]{2,1,0:T(8,128)(2,1)} %get-tuple-element.101.refs_0_), channel_id=1, source_target_pairs={{0,8},{1,9},{2,10},{3,11},{4,20},{5,21},{6,22},{7,23},{8,0},{9,1},... | collective-permute-start | bytes 1179656 | tf_op jit(solution)/shard_map/ppermute | solution.py:106
  38.1 13.9 %collective-permute-start.9 = (bf16[10,16,512]{2,1,0:T(8,128)(2,1)S(1)}, bf16[10,16,512]{2,1,0:T(8,128)(2,1)S(1)}, u32[]{:S(2)}, u32[]{:S(2)}) collective-permute-start(bf16[10,16,512]{2,1,0:T(8,128)(2,1)S(1)} %maximum_maximum_fusion), channel_id=1, source_target_pairs={{0,2},{1,3},{2,0},{3,1},{4,6},{5,7},{6,4},{7,5},{8,10},{9,11},{10,... | collective-permute-start | bytes 491528 | tf_op jit(solution)/shard_map/ppermute | solution.py:98
  52.1 9.4 %collective-permute-start.11 = (bf16[2,10,16,512]{3,2,1,0:T(8,128)(2,1)S(1)}, bf16[2,10,16,512]{3,2,1,0:T(8,128)(2,1)S(1)}, u32[]{:S(2)}, u32[]{:S(2)}) collective-permute-start(bf16[2,10,16,512]{3,2,1,0:T(8,128)(2,1)S(1)} %pad_maximum_fusion.3), channel_id=1, source_target_pairs={{0,1},{1,0},{2,3},{3,2},{4,5},{5,4},{6,7},{7,6},{8,9},{9,8},{10,11... | collective-permute-start | bytes 983048 | tf_op jit(solution)/shard_map/ppermute | solution.py:98
  52.2 9.4 %collective-permute-start.8 = (bf16[8,192,128]{2,1,0:T(8,128)(2,1)S(1)}, bf16[8,192,128]{2,1,0:T(8,128)(2,1)S(1)}, u32[]{:S(2)}, u32[]{:S(2)}) collective-permute-start(bf16[8,192,128]{2,1,0:T(8,128)(2,1)S(1)} %collective-permute-done.7.refs_0_), channel_id=1, source_target_pairs={{0,16},{1,17},{2,18},{3,19},{4,12},{5,13},{6,14},{7,15},{8,24},{9,... | collective-permute-start | bytes 1179656 | tf_op jit(solution)/shard_map/ppermute | solution.py:106
  61.6 18.0 %collective-permute-start.17 = (bf16[4,10,16,512]{3,2,1,0:T(8,128)(2,1)S(1)}, bf16[4,10,16,512]{3,2,1,0:T(8,128)(2,1)S(1)}, u32[]{:S(2)}, u32[]{:S(2)}) collective-permute-start(bf16[4,10,16,512]{3,2,1,0:T(8,128)(2,1)S(1)} %pad_maximum_fusion.1.refs_9_), channel_id=1, source_target_pairs={{0,16},{1,17},{2,18},{3,19},{4,12},{5,13},{6,14},{7,15},{8,24},{9,... | collective-permute-start | bytes 1966088 | tf_op jit(solution)/shard_map/ppermute | solution.py:106
  62.2 15.0 %collective-permute-start.16 = (bf16[4,10,16,512]{3,2,1,0:T(8,128)(2,1)S(1)}, bf16[4,10,16,512]{3,2,1,0:T(8,128)(2,1)S(1)}, u32[]{:S(2)}, u32[]{:S(2)}) collective-permute-start(bf16[4,10,16,512]{3,2,1,0:T(8,128)(2,1)S(1)} %pad_maximum_fusion.1.refs_9_), channel_id=1, source_target_pairs={{0,8},{1,9},{2,10},{3,11},{4,20},{5,21},{6,22},{7,23},{8,0},{9,1},... | collective-permute-start | bytes 1966088 | tf_op jit(solution)/shard_map/ppermute | solution.py:106
  77.2 11.5 %collective-permute-start.18 = (bf16[4,10,16,512]{3,2,1,0:T(8,128)(2,1)S(1)}, bf16[4,10,16,512]{3,2,1,0:T(8,128)(2,1)S(1)}, u32[]{:S(2)}, u32[]{:S(2)}) collective-permute-start(bf16[4,10,16,512]{3,2,1,0:T(8,128)(2,1)S(1)} %collective-permute-done.16), channel_id=1, source_target_pairs={{0,16},{1,17},{2,18},{3,19},{4,12},{5,13},{6,14},{7,15},{8,24},{9,... | collective-permute-start | bytes 1966088 | tf_op jit(solution)/shard_map/ppermute | solution.py:106
  79.7 11.2 %collective-permute-start.20 = (bf16[2,4,10,16,512]{4,3,2,1,0:T(8,128)(2,1)S(1)}, bf16[2,4,10,16,512]{4,3,2,1,0:T(8,128)(2,1)}, u32[]{:S(2)}, u32[]{:S(2)}) collective-permute-start(bf16[2,4,10,16,512]{4,3,2,1,0:T(8,128)(2,1)S(1)} %pad_maximum_fusion.refs_10_), channel_id=1, source_target_pairs={{0,4},{1,5},{2,6},{3,7},{4,0},{5,1},{6,2},{7,3},{8,12},{9,13},{10,... | collective-permute-start | bytes 3932168 | tf_op jit(solution)/shard_map/ppermute | solution.py:98
  81.2 6.0 %collective-permute-start.15 = (bf16[192,128]{1,0:T(8,128)(2,1)S(1)}, bf16[192,128]{1,0:T(8,128)(2,1)S(1)}, u32[]{:S(2)}, u32[]{:S(2)}) collective-permute-start(bf16[192,128]{1,0:T(8,128)(2,1)S(1)} %get-tuple-element.171), channel_id=1, source_target_pairs={{0,3},{1,2},{2,1},{3,0},{4,7},{5,6},{6,5},{7,4},{8,11},{9,10},{10,... | collective-permute-start | bytes 147464 | tf_op jit(solution)/shard_map/ppermute | solution.py:98
  103.7 9.1 %collective-permute-start.22 = (bf16[4,4,10,16,512]{4,3,2,1,0:T(8,128)(2,1)}, bf16[4,4,10,16,512]{4,3,2,1,0:T(8,128)(2,1)S(1)}, u32[]{:S(2)}, u32[]{:S(2)}) collective-permute-start(bf16[4,4,10,16,512]{4,3,2,1,0:T(8,128)(2,1)} %get-tuple-element.130), channel_id=1, source_target_pairs={{0,4},{1,5},{2,6},{3,7},{4,0},{5,1},{6,2},{7,3},{8,12},{9,13},{10,... | collective-permute-start | bytes 7864328 | tf_op jit(solution)/shard_map/ppermute | solution.py:98
  104.9 6.7 %collective-permute-start.24 = (bf16[192,128]{1,0:T(8,128)(2,1)S(1)}, bf16[192,128]{1,0:T(8,128)(2,1)S(1)}, u32[]{:S(2)}, u32[]{:S(2)}) collective-permute-start(bf16[192,128]{1,0:T(8,128)(2,1)S(1)} %copy-done.40), channel_id=1, source_target_pairs={{0,2},{1,3},{2,0},{3,1},{4,6},{5,7},{6,4},{7,5},{8,10},{9,11},{10,... | collective-permute-start | bytes 147464 | tf_op jit(solution)/shard_map/ppermute | solution.py:98
  115.8 18.0 %collective-permute-start.27 = (bf16[2,4,10,16,512]{4,3,2,1,0:T(8,128)(2,1)}, bf16[2,4,10,16,512]{4,3,2,1,0:T(8,128)(2,1)}, u32[]{:S(2)}, u32[]{:S(2)}) collective-permute-start(bf16[2,4,10,16,512]{4,3,2,1,0:T(8,128)(2,1)} %add_convert_fusion), channel_id=1, source_target_pairs={{0,16},{1,17},{2,18},{3,19},{4,12},{5,13},{6,14},{7,15},{8,24},{9,... | collective-permute-start | bytes 3932168 | tf_op jit(solution)/shard_map/ppermute | solution.py:106
  123.5 16.4 %collective-permute-start.29 = (bf16[8,192,128]{2,1,0:T(8,128)(2,1)}, bf16[8,192,128]{2,1,0:T(8,128)(2,1)}, u32[]{:S(2)}, u32[]{:S(2)}) collective-permute-start(bf16[8,192,128]{2,1,0:T(8,128)(2,1)} %get-tuple-element.150), channel_id=1, source_target_pairs={{0,16},{1,17},{2,18},{3,19},{4,12},{5,13},{6,14},{7,15},{8,24},{9,... | collective-permute-start | bytes 1179656 | tf_op jit(solution)/shard_map/ppermute | solution.py:106
  132.5 16.6 %collective-permute-start.28 = (bf16[8,192,128]{2,1,0:T(8,128)(2,1)}, bf16[8,192,128]{2,1,0:T(8,128)(2,1)S(1)}, u32[]{:S(2)}, u32[]{:S(2)}) collective-permute-start(bf16[8,192,128]{2,1,0:T(8,128)(2,1)} %get-tuple-element.149), channel_id=1, source_target_pairs={{0,16},{1,17},{2,18},{3,19},{4,12},{5,13},{6,14},{7,15},{8,24},{9,... | collective-permute-start | bytes 1179656 | tf_op jit(solution)/shard_map/ppermute | solution.py:106
  136.1 24.9 %collective-permute-start.38 = (bf16[4,10,16,512]{3,2,1,0:T(8,128)(2,1)}, bf16[4,10,16,512]{3,2,1,0:T(8,128)(2,1)}, u32[]{:S(2)}, u32[]{:S(2)}) collective-permute-start(bf16[4,10,16,512]{3,2,1,0:T(8,128)(2,1)} %fusion.1), channel_id=1, source_target_pairs={{0,8},{1,9},{2,10},{3,11},{4,20},{5,21},{6,22},{7,23},{8,0},{9,1},... | collective-permute-start | bytes 1966088 | tf_op jit(solution)/shard_map/ppermute | solution.py:106
  141.7 11.7 %collective-permute-start.30 = (bf16[8,192,128]{2,1,0:T(8,128)(2,1)}, bf16[8,192,128]{2,1,0:T(8,128)(2,1)}, u32[]{:S(2)}, u32[]{:S(2)}) collective-permute-start(bf16[8,192,128]{2,1,0:T(8,128)(2,1)} %add_convert_fusion.2), channel_id=1, source_target_pairs={{0,8},{1,9},{2,10},{3,11},{4,20},{5,21},{6,22},{7,23},{8,0},{9,1},... | collective-permute-start | bytes 1179656 | tf_op jit(solution)/shard_map/ppermute | solution.py:106
  159.2 6.6 %collective-permute-start.32 = (bf16[4,64,512]{2,1,0:T(8,128)(2,1)}, bf16[4,64,512]{2,1,0:T(8,128)(2,1)S(1)}, u32[]{:S(2)}, u32[]{:S(2)}) collective-permute-start(bf16[4,64,512]{2,1,0:T(8,128)(2,1)} %get-tuple-element.153), channel_id=1, source_target_pairs={{0,8},{1,9},{2,10},{3,11},{4,20},{5,21},{6,22},{7,23},{8,0},{9,1},... | collective-permute-start | bytes 786440 | tf_op jit(solution)/shard_map/ppermute | solution.py:106
  162.8 9.3 %collective-permute-start.39 = (bf16[2,10,16,512]{3,2,1,0:T(8,128)(2,1)S(1)}, bf16[2,10,16,512]{3,2,1,0:T(8,128)(2,1)S(1)}, u32[]{:S(2)}, u32[]{:S(2)}) collective-permute-start(bf16[2,10,16,512]{3,2,1,0:T(8,128)(2,1)S(1)} %slice.91), channel_id=1, source_target_pairs={{0,1},{1,0},{2,3},{3,2},{4,5},{5,4},{6,7},{7,6},{8,9},{9,8},{10,11... | collective-permute-start | bytes 983048 | tf_op jit(solution)/shard_map/ppermute | solution.py:98
  163.6 9.6 %collective-permute-start.31 = (bf16[4,192,512]{2,1,0:T(8,128)(2,1)S(1)}, bf16[4,192,512]{2,1,0:T(8,128)(2,1)S(1)}, u32[]{:S(2)}, u32[]{:S(2)}) collective-permute-start(bf16[4,192,512]{2,1,0:T(8,128)(2,1)S(1)} %copy-done.30), channel_id=1, source_target_pairs={{0,4},{1,5},{2,6},{3,7},{4,0},{5,1},{6,2},{7,3},{8,12},{9,13},{10,... | collective-permute-start | bytes 2359304 | tf_op jit(solution)/shard_map/ppermute | solution.py:98
  165.9 7.2 %collective-permute-start.33 = (bf16[4,64,512]{2,1,0:T(8,128)(2,1)S(1)}, bf16[4,64,512]{2,1,0:T(8,128)(2,1)S(1)}, u32[]{:S(2)}, u32[]{:S(2)}) collective-permute-start(bf16[4,64,512]{2,1,0:T(8,128)(2,1)S(1)} %add_convert_fusion.4.dw_ref), channel_id=1, source_target_pairs={{0,16},{1,17},{2,18},{3,19},{4,12},{5,13},{6,14},{7,15},{8,24},{9,... | collective-permute-start | bytes 786440 | tf_op jit(solution)/shard_map/ppermute | solution.py:106
  172.3 9.7 %collective-permute-start.40 = (bf16[10,16,512]{2,1,0:T(8,128)(2,1)S(1)}, bf16[10,16,512]{2,1,0:T(8,128)(2,1)S(1)}, u32[]{:S(2)}, u32[]{:S(2)}) collective-permute-start(bf16[10,16,512]{2,1,0:T(8,128)(2,1)S(1)} %slice_bitcast_fusion), channel_id=1, source_target_pairs={{0,2},{1,3},{2,0},{3,1},{4,6},{5,7},{6,4},{7,5},{8,10},{9,11},{10,... | collective-permute-start | bytes 491528 | tf_op jit(solution)/shard_map/ppermute | solution.py:98
  176.6 16.6 %collective-permute-start.34 = (bf16[256,512]{1,0:T(8,128)(2,1)}, bf16[256,512]{1,0:T(8,128)(2,1)S(1)}, u32[]{:S(2)}, u32[]{:S(2)}) collective-permute-start(bf16[256,512]{1,0:T(8,128)(2,1)} %get-tuple-element.155), channel_id=1, source_target_pairs={{0,1},{1,0},{2,3},{3,2},{4,5},{5,4},{6,7},{7,6},{8,9},{9,8},{10,11... | collective-permute-start | bytes 786440 | tf_op jit(solution)/shard_map/ppermute | solution.py:98
  178.3 21.3 %collective-permute-start.35 = (bf16[256,512]{1,0:T(8,128)(2,1)}, bf16[256,512]{1,0:T(8,128)(2,1)S(1)}, u32[]{:S(2)}, u32[]{:S(2)}) collective-permute-start(bf16[256,512]{1,0:T(8,128)(2,1)} %get-tuple-element.156), channel_id=1, source_target_pairs={{0,2},{1,3},{2,0},{3,1},{4,6},{5,7},{6,4},{7,5},{8,10},{9,11},{10,... | collective-permute-start | bytes 786440 | tf_op jit(solution)/shard_map/ppermute | solution.py:98
  179.0 20.6 %collective-permute-start.36 = (bf16[256,512]{1,0:T(8,128)(2,1)}, bf16[256,512]{1,0:T(8,128)(2,1)S(1)}, u32[]{:S(2)}, u32[]{:S(2)}) collective-permute-start(bf16[256,512]{1,0:T(8,128)(2,1)} %get-tuple-element.157), channel_id=1, source_target_pairs={{0,3},{1,2},{2,1},{3,0},{4,7},{5,6},{6,5},{7,4},{8,11},{9,10},{10,... | collective-permute-start | bytes 786440 | tf_op jit(solution)/shard_map/ppermute | solution.py:98
  182.0 7.2 %collective-permute-start.41 = (bf16[10,16,512]{2,1,0:T(8,128)(2,1)S(1)}, bf16[10,16,512]{2,1,0:T(8,128)(2,1)S(1)}, u32[]{:S(2)}, u32[]{:S(2)}) collective-permute-start(bf16[10,16,512]{2,1,0:T(8,128)(2,1)S(1)} %fusion.2), channel_id=1, source_target_pairs={{0,8},{1,9},{2,10},{3,11},{4,20},{5,21},{6,22},{7,23},{8,0},{9,1},... | collective-permute-start | bytes 491528 | tf_op jit(solution)/shard_map/ppermute | solution.py:106
  185.8 7.4 %collective-permute-start.42 = (bf16[10,16,512]{2,1,0:T(8,128)(2,1)S(1)}, bf16[10,16,512]{2,1,0:T(8,128)(2,1)S(1)}, u32[]{:S(2)}, u32[]{:S(2)}) collective-permute-start(bf16[10,16,512]{2,1,0:T(8,128)(2,1)S(1)} %fusion.2), channel_id=1, source_target_pairs={{0,16},{1,17},{2,18},{3,19},{4,12},{5,13},{6,14},{7,15},{8,24},{9,... | collective-permute-start | bytes 491528 | tf_op jit(solution)/shard_map/ppermute | solution.py:106
  194.6 6.8 %collective-permute-start.44 = (bf16[4,10,16,512]{3,2,1,0:T(8,128)(2,1)S(1)}, bf16[4,10,16,512]{3,2,1,0:T(8,128)(2,1)S(1)}, u32[]{:S(2)}, u32[]{:S(2)}) collective-permute-start(bf16[4,10,16,512]{3,2,1,0:T(8,128)(2,1)S(1)} %pad_maximum_fusion.2.refs_5_), channel_id=1, source_target_pairs={{0,4},{1,5},{2,6},{3,7},{4,0},{5,1},{6,2},{7,3},{8,12},{9,13},{10,... | collective-permute-start | bytes 1966088 | tf_op jit(solution)/shard_map/ppermute | solution.py:98
  (55 other events, 244.8 us)

commit v9 on v8

--- a/solution.py
+++ b/solution.py
@@ -14,7 +14,7 @@
 CHUNK = 512
 TILE = 16
 WIDE = 8
-WIDE_BACK = 4
+WIDE_BACK = 8
 F32 = jnp.float32
 BF16 = jnp.bfloat16
 NEG = -1e30

time: 211 us -> 210 us (level)
  Pallas kernels: 65.6 us -> 72 us
  starting transfers between devices: 55.9 us -> 51.2 us
    ppermute x16, starting transfers between devices: 27.7 us -> 20 us  [turn(): return lax.ppermute(x, ('ctx', 'wt'), perm)]
    pallas_call x14, Pallas kernels: 65.6 us -> 72 us  [call(): pl.pallas_call(body, name=name, out_shape=list(outs), in_specs=in_specs,...]
    ppermute x29, starting transfers between devices: 28.2 us -> 31.2 us  [swap(): return lax.ppermute(x, ('ctx', 'wt'), perm)]
  transfers between devices with their start and end apart: 45 -> 45, of which waited for: 23 -> 22; matrix products, arithmetic and copies ran while one was open for 7% -> 7% of each run, Pallas kernels for 20% -> 23%
where the time goes in v9:
time: 210 us; the launch traced here: 206 us
  Pallas kernels  72 us (34%)
  waiting for transfers between devices  60.8 us (29%)
  starting transfers between devices  51.2 us (24%)
  other arithmetic  11.6 us (6%)
  local copies, waits for them, and re-layouts  8.18 us (4%)
  between operations  2.16 us (1%)
    pallas_call x14, Pallas kernels, call(): pl.pallas_call(body, name=name, out_shape=list(outs), in_specs=in_specs,...  72 us
    ppermute x29, waiting for transfers between devices, swap(): return lax.ppermute(x, ('ctx', 'wt'), perm)  48 us
    ppermute x29, starting transfers between devices, swap(): return lax.ppermute(x, ('ctx', 'wt'), perm)  31.2 us
    ppermute x16, starting transfers between devices, turn(): return lax.ppermute(x, ('ctx', 'wt'), perm)  20 us
    ppermute x16, waiting for transfers between devices, turn(): return lax.ppermute(x, ('ctx', 'wt'), perm)  12.8 us
  transfers between devices with their start and end apart: 45, of which 22 were waited for; matrix products, arithmetic and copies ran while one was open for 7% of the time, Pallas kernels for 23%

profile of v9, /device:TPU:0, one launch (start us, length us, event | category | flops | bytes accessed | tf_op | source)
XLA Modules:
  0.0 205.9 jit_solution(581344895856533765)
XLA Ops:
  1.3 2.3 %pack.1 = (bf16[256,512]{1,0:T(8,128)(2,1)}, bf16[256,512]{1,0:T(8,128)(2,1)}, bf16[256,512]{1,0:T(8,128)(2,1)}, bf16[256,512]{1,0:T(8,128)(2,1)}) custom-call(s32[2]{0:T(128)} %pad_add_fusion.info, bf16[192,512]{1,0:T(8,128)(2,1)} %x_ref.1, bf16[128,1536]{1,0:T(8,128)(2,1)} %w_ref.1, bf16[1,128]{1,0:T(2,128)(2,1)} %bitcast.80, bf16[1,128]{1,0:T(2,128)(2,1)} %bitcast.81, ...), custom_call_target="tpu_custom_call" | custom-call | bytes 1639432 | tf_op jit(solution)/shard_map/pack/pallas_call | solution.py:53
  3.6 4.0 %collective-permute-start.1 = (bf16[256,512]{1,0:T(8,128)(2,1)}, bf16[256,512]{1,0:T(8,128)(2,1)S(1)}, u32[]{:S(2)}, u32[]{:S(2)}) collective-permute-start(bf16[256,512]{1,0:T(8,128)(2,1)} %get-tuple-element.93), channel_id=1, source_target_pairs={{0,2},{1,3},{2,0},{3,1},{4,6},{5,7},{6,4},{7,5},{8,10},{9,11},{10,... | collective-permute-start | bytes 786440 | tf_op jit(solution)/shard_map/ppermute | solution.py:98
  13.4 2.6 %lists.1 = (s32[272]{0:T(512)}, s32[272]{0:T(512)}, s32[272]{0:T(512)}, s32[272]{0:T(512)}, s32[272]{0:T(512)}) custom-call(s32[2]{0:T(128)} %pad_add_fusion.info, s32[32]{0:T(128)} %deal.1, s32[4]{0:T(128)} %lengths.1, s32[8]{0:T(128)} %call_exported.0.codes), custom_call_target="tpu_custom_call" | custom-call | bytes 5624 | tf_op jit(solution)/shard_map/lists/pallas_call | solution.py:53
  16.1 10.7 %collective-permute-done.refs_1_.refs_9_ = bf16[256,512]{1,0:T(8,128)(2,1)S(1)} collective-permute-done((bf16[256,512]{1,0:T(8,128)(2,1)}, bf16[256,512]{1,0:T(8,128)(2,1)S(1)}, u32[]{:S(2)}, u32[]{:S(2)}) %collective-permute-start) | collective-permute-done | bytes 262176 | tf_op jit(solution)/shard_map/ppermute | solution.py:98
  30.2 4.9 %project.1 = (bf16[8,192,128]{2,1,0:T(8,128)(2,1)}, bf16[8,192,128]{2,1,0:T(8,128)(2,1)}, bf16[8,192,512]{2,1,0:T(8,128)(2,1)}, bf16[512,256]{1,0:T(8,128)(2,1)}, f32[8,512]{1,0:T(8,128)}) custom-call(s32[2]{0:T(128)} %pad_add_fusion.info, bf16[256,512]{1,0:T(8,128)(2,1)} %get-tuple-element.91.refs_0_.refs_8_, bf16[256,512]{1,0:T(8,128)(2,1)} %copy-done.5, ...), custom_call_target="tpu_custom_call" | custom-call | flops 402653184 | bytes 5783560 | tf_op jit(solution)/shard_map/project/pallas_call | solution.py:53
  38.1 6.5 %collective-permute-start.9 = (bf16[10,16,512]{2,1,0:T(8,128)(2,1)S(1)}, bf16[10,16,512]{2,1,0:T(8,128)(2,1)S(1)}, u32[]{:S(2)}, u32[]{:S(2)}) collective-permute-start(bf16[10,16,512]{2,1,0:T(8,128)(2,1)S(1)} %maximum_maximum_fusion), channel_id=1, source_target_pairs={{0,2},{1,3},{2,0},{3,1},{4,6},{5,7},{6,4},{7,5},{8,10},{9,11},{10,... | collective-permute-start | bytes 491528 | tf_op jit(solution)/shard_map/ppermute | solution.py:98
  44.6 7.4 %collective-permute-done.9 = bf16[10,16,512]{2,1,0:T(8,128)(2,1)S(1)} collective-permute-done((bf16[10,16,512]{2,1,0:T(8,128)(2,1)S(1)}, bf16[10,16,512]{2,1,0:T(8,128)(2,1)S(1)}, u32[]{:S(2)}, u32[]{:S(2)}) %collective-permute-start.9) | collective-permute-done | bytes 163872 | tf_op jit(solution)/shard_map/ppermute | solution.py:98
  53.2 4.7 %attend.3 = (f32[8,1,192]{2,1,0:T(1,128)}, f32[8,1,192]{2,1,0:T(1,128)}, f32[8,128,192]{2,1,0:T(8,128)}) custom-call(s32[2]{0:T(128)} %pad_add_fusion.info, s32[272]{0:T(512)} %get-tuple-element.96.pairs, bf16[8,192,128]{2,1,0:T(8,128)(2,1)} %get-tuple-element.100.q_ref, bf16[8,192,128]{2,1,0:T(8,128)(2,1)} %get-tuple-element.101.refs_0_), custom_call_target="tpu_custom_call" | custom-call | flops 2113929216 | bytes 1586248 | tf_op jit(solution)/shard_map/attend/pallas_call | solution.py:53
  58.0 3.5 %collective-permute-done.11 = bf16[2,10,16,512]{3,2,1,0:T(8,128)(2,1)S(1)} collective-permute-done((bf16[2,10,16,512]{3,2,1,0:T(8,128)(2,1)S(1)}, bf16[2,10,16,512]{3,2,1,0:T(8,128)(2,1)S(1)}, u32[]{:S(2)}, u32[]{:S(2)}) %collective-permute-start.11) | collective-permute-done | bytes 327712 | tf_op jit(solution)/shard_map/ppermute | solution.py:98
  62.7 6.1 %attend.4 = (f32[8,1,192]{2,1,0:T(1,128)}, f32[8,1,192]{2,1,0:T(1,128)}, f32[8,128,192]{2,1,0:T(8,128)}) custom-call(s32[2]{0:T(128)} %pad_add_fusion.info, s32[272]{0:T(512)} %get-tuple-element.106.pairs, bf16[8,192,128]{2,1,0:T(8,128)(2,1)} %get-tuple-element.100.q_ref, bf16[8,192,128]{2,1,0:T(8,128)(2,1)} %copy-done.32, bf16[8,192,128]{2,1,0:T(8,128)(2,1)} %copy-done.33, ...), custom_call_target="tpu_custom_call" | custom-call | flops 4227858432 | bytes 2778184 | tf_op jit(solution)/shard_map/attend/pallas_call | solution.py:53
  68.8 6.6 %attend.5 = (f32[8,1,192]{2,1,0:T(1,128)}, f32[8,1,192]{2,1,0:T(1,128)}, f32[8,128,192]{2,1,0:T(8,128)}, bf16[4,192,128]{2,1,0:T(8,128)(2,1)}, bf16[4,192,128]{2...) custom-call(s32[2]{0:T(128)} %pad_add_fusion.info, s32[272]{0:T(512)} %get-tuple-element.99.pairs, ...), custom_call_target="tpu_custom_call" | custom-call | flops 2113929216 | bytes 3570760 | tf_op jit(solution)/shard_map/attend/pallas_call | solution.py:53
  77.8 2.7 %collective-permute-start.20 = (bf16[2,4,10,16,512]{4,3,2,1,0:T(8,128)(2,1)S(1)}, bf16[2,4,10,16,512]{4,3,2,1,0:T(8,128)(2,1)}, u32[]{:S(2)}, u32[]{:S(2)}) collective-permute-start(bf16[2,4,10,16,512]{4,3,2,1,0:T(8,128)(2,1)S(1)} %pad_maximum_fusion.refs_10_), channel_id=1, source_target_pairs={{0,4},{1,5},{2,6},{3,7},{4,0},{5,1},{6,2},{7,3},{8,12},{9,13},{10,... | collective-permute-start | bytes 3932168 | tf_op jit(solution)/shard_map/ppermute | solution.py:98
  81.2 2.4 %collective-permute-start.15 = (bf16[192,128]{1,0:T(8,128)(2,1)S(1)}, bf16[192,128]{1,0:T(8,128)(2,1)S(1)}, u32[]{:S(2)}, u32[]{:S(2)}) collective-permute-start(bf16[192,128]{1,0:T(8,128)(2,1)S(1)} %get-tuple-element.171), channel_id=1, source_target_pairs={{0,3},{1,2},{2,1},{3,0},{4,7},{5,6},{6,5},{7,4},{8,11},{9,10},{10,... | collective-permute-start | bytes 147464 | tf_op jit(solution)/shard_map/ppermute | solution.py:98
  92.0 8.3 %mlp.1 = (bf16[192,512]{1,0:T(8,128)(2,1)}, f32[8,128]{1,0:T(8,128)}, f32[192,512]{1,0:T(8,128)}, bf16[192,128]{1,0:T(8,128)(2,1)}, bf16[192,128]{1,0:T(8,128)(2...) custom-call(s32[2]{0:T(128)} %pad_add_fusion.info, ...), custom_call_target="tpu_custom_call" | custom-call | flops 1610612736 | bytes 8819468 | tf_op jit(solution)/shard_map/mlp/pallas_call | solution.py:53
  100.3 4.4 %mlp_grads.1 = (bf16[4,4,10,16,512]{4,3,2,1,0:T(8,128)(2,1)}, bf16[4,4,10,16,512]{4,3,2,1,0:T(8,128)(2,1)}) custom-call(s32[2]{0:T(128)} %pad_add_fusion.info, bf16[4,192,512]{2,1,0:T(8,128)(2,1)} %get-tuple-element.122.act_ref, bf16[4,192,512]{2,1,0:T(8,128)(2,1)} %get-tuple-element.123.gpre_ref, bf16[192,512]{1,0:T(8,128)(2,1)} %get-tuple-element.124.n2_ref, ...), custom_call_target="tpu_custom_call" | custom-call | flops 805306368 | bytes 7622664 | tf_op jit(solution)/shard_map/mlp_grads/pallas_call | solution.py:53
  105.4 2.7 %collective-permute-start.24 = (bf16[192,128]{1,0:T(8,128)(2,1)S(1)}, bf16[192,128]{1,0:T(8,128)(2,1)S(1)}, u32[]{:S(2)}, u32[]{:S(2)}) collective-permute-start(bf16[192,128]{1,0:T(8,128)(2,1)S(1)} %copy-done.40), channel_id=1, source_target_pairs={{0,2},{1,3},{2,0},{3,1},{4,6},{5,7},{6,4},{7,5},{8,10},{9,11},{10,... | collective-permute-start | bytes 147464 | tf_op jit(solution)/shard_map/ppermute | solution.py:98
  111.5 2.5 %collective-permute-done.25.refs_6_ = bf16[192,128]{1,0:T(8,128)(2,1)S(1)} collective-permute-done((bf16[192,128]{1,0:T(8,128)(2,1)S(1)}, bf16[192,128]{1,0:T(8,128)(2,1)S(1)}, u32[]{:S(2)}, u32[]{:S(2)}) %collective-permute-start.25) | collective-permute-done | bytes 49184 | tf_op jit(solution)/shard_map/ppermute | solution.py:98
  114.1 3.0 %add_convert_fusion = bf16[2,4,10,16,512]{4,3,2,1,0:T(8,128)(2,1)} fusion(bf16[4,4,10,16,512]{4,3,2,1,0:T(8,128)(2,1)S(1)} %collective-permute-done.22, bf16[4,4,10,16,512]{4,3,2,1,0:T(8,128)(2,1)} %get-tuple-element.129), kind=kLoop, calls=%fused_computation | loop fusion | flops 2621440 | bytes 3932160 | tf_op jit(solution)/shard_map/convert_element_type | solution.py:998
  117.9 8.4 %attend_back.3 = (bf16[8,192,128]{2,1,0:T(8,128)(2,1)}, bf16[8,192,128]{2,1,0:T(8,128)(2,1)}, f32[8,64,192]{2,1,0:T(8,128)}, bf16[8,192,128]{2,1,0:T(8,128)(2,1)}, f32[8,1,192]{2,1,0:T(1,128)}) custom-call(s32[2]{0:T(128)} %pad_add_fusion.info, s32[272]{0:T(512)} %get-tuple-element.120.pairs, bf16[8,192,128]{2,1,0:T(8,128)(2,1)} %get-tuple-element.100.q_ref, ...), custom_call_target="tpu_custom_call" | custom-call | flops 10569646080 | bytes 3945544 | tf_op jit(solution)/shard_map/attend_back/pallas_call | solution.py:53
  126.4 4.6 %attend_back.4 = (bf16[8,192,128]{2,1,0:T(8,128)(2,1)}, f32[8,64,192]{2,1,0:T(8,128)}) custom-call(s32[2]{0:T(128)} %pad_add_fusion.info, s32[272]{0:T(512)} %get-tuple-element.138.pairs, bf16[8,192,128]{2,1,0:T(8,128)(2,1)} %get-tuple-element.100.q_ref, f32[8,1,192]{2,1,0:T(1,128)} %get-tuple-element.119.lse_ref, bf16[8,192,128]{2,1,0:T(8,128)(2,1)} %copy-done.32, ...), custom_call_target="tpu_custom_call" | custom-call | flops 5284823040 | bytes 2372680 | tf_op jit(solution)/shard_map/attend_back/pallas_call | solution.py:53
  135.1 2.3 %fusion.1 = bf16[4,10,16,512]{3,2,1,0:T(8,128)(2,1)} fusion(bf16[4,4,10,16,512]{4,3,2,1,0:T(8,128)(2,1)S(1)} %collective-permute-done.22, bf16[2,4,10,16,512]{4,3,2,1,0:T(8,128)(2,1)} %collective-permute-done.27, bf16[4,4,10,16,512]{4,3,2,1,0:T(8,128)(2,1)S(1)} %copy-done.1), kind=kLoop, calls=%fused_computation.6 | loop fusion | flops 1966080 | bytes 2621440 | tf_op jit(solution)/shard_map/convert_element_type | solution.py:1012
  137.4 2.5 %collective-permute-start.38 = (bf16[4,10,16,512]{3,2,1,0:T(8,128)(2,1)}, bf16[4,10,16,512]{3,2,1,0:T(8,128)(2,1)}, u32[]{:S(2)}, u32[]{:S(2)}) collective-permute-start(bf16[4,10,16,512]{3,2,1,0:T(8,128)(2,1)} %fusion.1), channel_id=1, source_target_pairs={{0,8},{1,9},{2,10},{3,11},{4,20},{5,21},{6,22},{7,23},{8,0},{9,1},... | collective-permute-start | bytes 1966088 | tf_op jit(solution)/shard_map/ppermute | solution.py:106
  142.3 6.6 %attend_back.5 = (bf16[8,192,128]{2,1,0:T(8,128)(2,1)}, f32[8,64,192]{2,1,0:T(8,128)}, bf16[8,192,128]{2,1,0:T(8,128)(2,1)}) custom-call(s32[2]{0:T(128)} %pad_add_fusion.info, s32[272]{0:T(512)} %get-tuple-element.96.pairs, bf16[8,192,128]{2,1,0:T(8,128)(2,1)} %get-tuple-element.100.q_ref, f32[8,1,192]{2,1,0:T(1,128)} %get-tuple-element.119.lse_ref, ...), custom_call_target="tpu_custom_call" | custom-call | flops 5284823040 | bytes 2765896 | tf_op jit(solution)/shard_map/attend_back/pallas_call | solution.py:53
  149.0 5.3 %collective-permute-done.30.refs_10_ = bf16[8,192,128]{2,1,0:T(8,128)(2,1)} collective-permute-done((bf16[8,192,128]{2,1,0:T(8,128)(2,1)}, bf16[8,192,128]{2,1,0:T(8,128)(2,1)}, u32[]{:S(2)}, u32[]{:S(2)}) %collective-permute-start.30) | collective-permute-done | bytes 393248 | tf_op jit(solution)/shard_map/ppermute | solution.py:106
  154.3 5.7 %head_grads.1 = (bf16[4,192,512]{2,1,0:T(8,128)(2,1)}, bf16[4,192,512]{2,1,0:T(8,128)(2,1)}, bf16[4,64,512]{2,1,0:T(8,128)(2,1)}) custom-call(s32[2]{0:T(128)} %pad_add_fusion.info, bf16[8,192,128]{2,1,0:T(8,128)(2,1)} %get-tuple-element.144.dq_ref, bf16[512,256]{1,0:T(8,128)(2,1)} %get-tuple-element.145.wh_ref, ...), custom_call_target="tpu_custom_call" | custom-call | flops 805306368 | bytes 7340040 | tf_op jit(solution)/shard_map/head_grads/pallas_call | solution.py:53
  163.9 2.8 %collective-permute-done.32 = bf16[4,64,512]{2,1,0:T(8,128)(2,1)S(1)} collective-permute-done((bf16[4,64,512]{2,1,0:T(8,128)(2,1)}, bf16[4,64,512]{2,1,0:T(8,128)(2,1)S(1)}, u32[]{:S(2)}, u32[]{:S(2)}) %collective-permute-start.32) | collective-permute-done | bytes 262176 | tf_op jit(solution)/shard_map/ppermute | solution.py:106
  167.2 4.7 %collective-permute-done.39 = bf16[2,10,16,512]{3,2,1,0:T(8,128)(2,1)S(1)} collective-permute-done((bf16[2,10,16,512]{3,2,1,0:T(8,128)(2,1)S(1)}, bf16[2,10,16,512]{3,2,1,0:T(8,128)(2,1)S(1)}, u32[]{:S(2)}, u32[]{:S(2)}) %collective-permute-start.39) | collective-permute-done | bytes 327712 | tf_op jit(solution)/shard_map/ppermute | solution.py:98
  174.2 2.5 %merge.1 = (bf16[256,512]{1,0:T(8,128)(2,1)}, bf16[256,512]{1,0:T(8,128)(2,1)}, bf16[256,512]{1,0:T(8,128)(2,1)}, bf16[256,512]{1,0:T(8,128)(2,1)}) custom-call(bf16[4,192,512]{2,1,0:T(8,128)(2,1)} %get-tuple-element.151.own_ref, bf16[4,192,512]{2,1,0:T(8,128)(2,1)} %copy-done.13, bf16[4,64,512]{2,1,0:T(8,128)(2,1)} %copy-done.12, bf16[4,64,512]{2,1,0:T(8,128)(2,1)} %copy-done.23), custom_call_target="tpu_custom_call" | custom-call | bytes 3145728 | tf_op jit(solution)/shard_map/merge/pallas_call | solution.py:53
  181.5 2.5 %collective-permute-start.41 = (bf16[10,16,512]{2,1,0:T(8,128)(2,1)S(1)}, bf16[10,16,512]{2,1,0:T(8,128)(2,1)S(1)}, u32[]{:S(2)}, u32[]{:S(2)}) collective-permute-start(bf16[10,16,512]{2,1,0:T(8,128)(2,1)S(1)} %fusion.2), channel_id=1, source_target_pairs={{0,8},{1,9},{2,10},{3,11},{4,20},{5,21},{6,22},{7,23},{8,0},{9,1},... | collective-permute-start | bytes 491528 | tf_op jit(solution)/shard_map/ppermute | solution.py:106
  187.5 3.2 %collective-permute-start.43 = (bf16[10,16,512]{2,1,0:T(8,128)(2,1)S(1)}, bf16[10,16,512]{2,1,0:T(8,128)(2,1)S(1)}, u32[]{:S(2)}, u32[]{:S(2)}) collective-permute-start(bf16[10,16,512]{2,1,0:T(8,128)(2,1)S(1)} %collective-permute-done.41), channel_id=1, source_target_pairs={{0,16},{1,17},{2,18},{3,19},{4,12},{5,13},{6,14},{7,15},{8,24},{9,... | collective-permute-start | bytes 491528 | tf_op jit(solution)/shard_map/ppermute | solution.py:106
  194.2 4.6 %collective-permute-done.35.refs_2_ = bf16[256,512]{1,0:T(8,128)(2,1)S(1)} collective-permute-done((bf16[256,512]{1,0:T(8,128)(2,1)}, bf16[256,512]{1,0:T(8,128)(2,1)S(1)}, u32[]{:S(2)}, u32[]{:S(2)}) %collective-permute-start.35) | collective-permute-done | bytes 262176 | tf_op jit(solution)/shard_map/ppermute | solution.py:98
  201.4 4.4 %last.1 = (f32[192,512]{1,0:T(8,128)}, f32[128,1536]{1,0:T(8,128)}, f32[1,128]{1,0:T(1,128)}, f32[1,128]{1,0:T(1,128)}, f32[128,2048]{1,0:T(8,128)}, /*index=5*/...) custom-call(s32[2]{0:T(128)} %pad_add_fusion.info, ...), custom_call_target="tpu_custom_call" | custom-call | bytes 7034892 | tf_op jit(solution)/shard_map/last/pallas_call | solution.py:53
  (187 shorter events, 58.6 us)
Async XLA Ops:
  3.6 23.2 %collective-permute-start.1 = (bf16[256,512]{1,0:T(8,128)(2,1)}, bf16[256,512]{1,0:T(8,128)(2,1)S(1)}, u32[]{:S(2)}, u32[]{:S(2)}) collective-permute-start(bf16[256,512]{1,0:T(8,128)(2,1)} %get-tuple-element.93), channel_id=1, source_target_pairs={{0,2},{1,3},{2,0},{3,1},{4,6},{5,7},{6,4},{7,5},{8,10},{9,11},{10,... | collective-permute-start | bytes 786440 | tf_op jit(solution)/shard_map/ppermute | solution.py:98
  7.7 19.2 %collective-permute-start.2 = (bf16[256,512]{1,0:T(8,128)(2,1)}, bf16[256,512]{1,0:T(8,128)(2,1)S(1)}, u32[]{:S(2)}, u32[]{:S(2)}) collective-permute-start(bf16[256,512]{1,0:T(8,128)(2,1)} %get-tuple-element.94), channel_id=1, source_target_pairs={{0,3},{1,2},{2,1},{3,0},{4,7},{5,6},{6,5},{7,4},{8,11},{9,10},{10,... | collective-permute-start | bytes 786440 | tf_op jit(solution)/shard_map/ppermute | solution.py:98
  9.0 17.8 %collective-permute-start = (bf16[256,512]{1,0:T(8,128)(2,1)}, bf16[256,512]{1,0:T(8,128)(2,1)S(1)}, u32[]{:S(2)}, u32[]{:S(2)}) collective-permute-start(bf16[256,512]{1,0:T(8,128)(2,1)} %get-tuple-element.92), channel_id=1, source_target_pairs={{0,1},{1,0},{2,3},{3,2},{4,5},{5,4},{6,7},{7,6},{8,9},{9,8},{10,11... | collective-permute-start | bytes 786440 | tf_op jit(solution)/shard_map/ppermute | solution.py:98
  9.2 18.2 %collective-permute-start.3 = (bf16[256,512]{1,0:T(8,128)(2,1)}, bf16[256,512]{1,0:T(8,128)(2,1)S(1)}, u32[]{:S(2)}, u32[]{:S(2)}) collective-permute-start(bf16[256,512]{1,0:T(8,128)(2,1)} %get-tuple-element.91.refs_0_.refs_8_), channel_id=1, source_target_pairs={{0,4},{1,5},{2,6},{3,7},{4,0},{5,1},{6,2},{7,3},{8,12},{9,13},{10,... | collective-permute-start | bytes 786440 | tf_op jit(solution)/shard_map/ppermute | solution.py:98
  35.1 17.0 %collective-permute-start.10 = (bf16[8,192,128]{2,1,0:T(8,128)(2,1)}, bf16[8,192,128]{2,1,0:T(8,128)(2,1)S(1)}, u32[]{:S(2)}, u32[]{:S(2)}) collective-permute-start(bf16[8,192,128]{2,1,0:T(8,128)(2,1)} %get-tuple-element.101.refs_0_), channel_id=1, source_target_pairs={{0,16},{1,17},{2,18},{3,19},{4,12},{5,13},{6,14},{7,15},{8,24},{9,... | collective-permute-start | bytes 1179656 | tf_op jit(solution)/shard_map/ppermute | solution.py:106
  36.6 15.4 %collective-permute-start.7 = (bf16[8,192,128]{2,1,0:T(8,128)(2,1)}, bf16[8,192,128]{2,1,0:T(8,128)(2,1)S(1)}, u32[]{:S(2)}, u32[]{:S(2)}) collective-permute-start(bf16[8,192,128]{2,1,0:T(8,128)(2,1)} %get-tuple-element.101.refs_0_), channel_id=1, source_target_pairs={{0,8},{1,9},{2,10},{3,11},{4,20},{5,21},{6,22},{7,23},{8,0},{9,1},... | collective-permute-start | bytes 1179656 | tf_op jit(solution)/shard_map/ppermute | solution.py:106
  38.1 13.9 %collective-permute-start.9 = (bf16[10,16,512]{2,1,0:T(8,128)(2,1)S(1)}, bf16[10,16,512]{2,1,0:T(8,128)(2,1)S(1)}, u32[]{:S(2)}, u32[]{:S(2)}) collective-permute-start(bf16[10,16,512]{2,1,0:T(8,128)(2,1)S(1)} %maximum_maximum_fusion), channel_id=1, source_target_pairs={{0,2},{1,3},{2,0},{3,1},{4,6},{5,7},{6,4},{7,5},{8,10},{9,11},{10,... | collective-permute-start | bytes 491528 | tf_op jit(solution)/shard_map/ppermute | solution.py:98
  52.1 9.4 %collective-permute-start.11 = (bf16[2,10,16,512]{3,2,1,0:T(8,128)(2,1)S(1)}, bf16[2,10,16,512]{3,2,1,0:T(8,128)(2,1)S(1)}, u32[]{:S(2)}, u32[]{:S(2)}) collective-permute-start(bf16[2,10,16,512]{3,2,1,0:T(8,128)(2,1)S(1)} %pad_maximum_fusion.3), channel_id=1, source_target_pairs={{0,1},{1,0},{2,3},{3,2},{4,5},{5,4},{6,7},{7,6},{8,9},{9,8},{10,11... | collective-permute-start | bytes 983048 | tf_op jit(solution)/shard_map/ppermute | solution.py:98
  52.2 9.4 %collective-permute-start.8 = (bf16[8,192,128]{2,1,0:T(8,128)(2,1)S(1)}, bf16[8,192,128]{2,1,0:T(8,128)(2,1)S(1)}, u32[]{:S(2)}, u32[]{:S(2)}) collective-permute-start(bf16[8,192,128]{2,1,0:T(8,128)(2,1)S(1)} %collective-permute-done.7.refs_0_), channel_id=1, source_target_pairs={{0,16},{1,17},{2,18},{3,19},{4,12},{5,13},{6,14},{7,15},{8,24},{9,... | collective-permute-start | bytes 1179656 | tf_op jit(solution)/shard_map/ppermute | solution.py:106
  61.6 16.0 %collective-permute-start.17 = (bf16[4,10,16,512]{3,2,1,0:T(8,128)(2,1)S(1)}, bf16[4,10,16,512]{3,2,1,0:T(8,128)(2,1)S(1)}, u32[]{:S(2)}, u32[]{:S(2)}) collective-permute-start(bf16[4,10,16,512]{3,2,1,0:T(8,128)(2,1)S(1)} %pad_maximum_fusion.1.refs_9_), channel_id=1, source_target_pairs={{0,16},{1,17},{2,18},{3,19},{4,12},{5,13},{6,14},{7,15},{8,24},{9,... | collective-permute-start | bytes 1966088 | tf_op jit(solution)/shard_map/ppermute | solution.py:106
  62.2 15.0 %collective-permute-start.16 = (bf16[4,10,16,512]{3,2,1,0:T(8,128)(2,1)S(1)}, bf16[4,10,16,512]{3,2,1,0:T(8,128)(2,1)S(1)}, u32[]{:S(2)}, u32[]{:S(2)}) collective-permute-start(bf16[4,10,16,512]{3,2,1,0:T(8,128)(2,1)S(1)} %pad_maximum_fusion.1.refs_9_), channel_id=1, source_target_pairs={{0,8},{1,9},{2,10},{3,11},{4,20},{5,21},{6,22},{7,23},{8,0},{9,1},... | collective-permute-start | bytes 1966088 | tf_op jit(solution)/shard_map/ppermute | solution.py:106
  77.2 12.5 %collective-permute-start.18 = (bf16[4,10,16,512]{3,2,1,0:T(8,128)(2,1)S(1)}, bf16[4,10,16,512]{3,2,1,0:T(8,128)(2,1)S(1)}, u32[]{:S(2)}, u32[]{:S(2)}) collective-permute-start(bf16[4,10,16,512]{3,2,1,0:T(8,128)(2,1)S(1)} %collective-permute-done.16), channel_id=1, source_target_pairs={{0,16},{1,17},{2,18},{3,19},{4,12},{5,13},{6,14},{7,15},{8,24},{9,... | collective-permute-start | bytes 1966088 | tf_op jit(solution)/shard_map/ppermute | solution.py:106
  77.8 14.2 %collective-permute-start.20 = (bf16[2,4,10,16,512]{4,3,2,1,0:T(8,128)(2,1)S(1)}, bf16[2,4,10,16,512]{4,3,2,1,0:T(8,128)(2,1)}, u32[]{:S(2)}, u32[]{:S(2)}) collective-permute-start(bf16[2,4,10,16,512]{4,3,2,1,0:T(8,128)(2,1)S(1)} %pad_maximum_fusion.refs_10_), channel_id=1, source_target_pairs={{0,4},{1,5},{2,6},{3,7},{4,0},{5,1},{6,2},{7,3},{8,12},{9,13},{10,... | collective-permute-start | bytes 3932168 | tf_op jit(solution)/shard_map/ppermute | solution.py:98
  81.2 6.3 %collective-permute-start.15 = (bf16[192,128]{1,0:T(8,128)(2,1)S(1)}, bf16[192,128]{1,0:T(8,128)(2,1)S(1)}, u32[]{:S(2)}, u32[]{:S(2)}) collective-permute-start(bf16[192,128]{1,0:T(8,128)(2,1)S(1)} %get-tuple-element.171), channel_id=1, source_target_pairs={{0,3},{1,2},{2,1},{3,0},{4,7},{5,6},{6,5},{7,4},{8,11},{9,10},{10,... | collective-permute-start | bytes 147464 | tf_op jit(solution)/shard_map/ppermute | solution.py:98
  104.7 9.4 %collective-permute-start.22 = (bf16[4,4,10,16,512]{4,3,2,1,0:T(8,128)(2,1)}, bf16[4,4,10,16,512]{4,3,2,1,0:T(8,128)(2,1)S(1)}, u32[]{:S(2)}, u32[]{:S(2)}) collective-permute-start(bf16[4,4,10,16,512]{4,3,2,1,0:T(8,128)(2,1)} %get-tuple-element.130), channel_id=1, source_target_pairs={{0,4},{1,5},{2,6},{3,7},{4,0},{5,1},{6,2},{7,3},{8,12},{9,13},{10,... | collective-permute-start | bytes 7864328 | tf_op jit(solution)/shard_map/ppermute | solution.py:98
  105.4 6.1 %collective-permute-start.24 = (bf16[192,128]{1,0:T(8,128)(2,1)S(1)}, bf16[192,128]{1,0:T(8,128)(2,1)S(1)}, u32[]{:S(2)}, u32[]{:S(2)}) collective-permute-start(bf16[192,128]{1,0:T(8,128)(2,1)S(1)} %copy-done.40), channel_id=1, source_target_pairs={{0,2},{1,3},{2,0},{3,1},{4,6},{5,7},{6,4},{7,5},{8,10},{9,11},{10,... | collective-permute-start | bytes 147464 | tf_op jit(solution)/shard_map/ppermute | solution.py:98
  117.1 18.0 %collective-permute-start.27 = (bf16[2,4,10,16,512]{4,3,2,1,0:T(8,128)(2,1)}, bf16[2,4,10,16,512]{4,3,2,1,0:T(8,128)(2,1)}, u32[]{:S(2)}, u32[]{:S(2)}) collective-permute-start(bf16[2,4,10,16,512]{4,3,2,1,0:T(8,128)(2,1)} %add_convert_fusion), channel_id=1, source_target_pairs={{0,16},{1,17},{2,18},{3,19},{4,12},{5,13},{6,14},{7,15},{8,24},{9,... | collective-permute-start | bytes 3932168 | tf_op jit(solution)/shard_map/ppermute | solution.py:106
  126.3 13.5 %collective-permute-start.29 = (bf16[8,192,128]{2,1,0:T(8,128)(2,1)}, bf16[8,192,128]{2,1,0:T(8,128)(2,1)}, u32[]{:S(2)}, u32[]{:S(2)}) collective-permute-start(bf16[8,192,128]{2,1,0:T(8,128)(2,1)} %get-tuple-element.150), channel_id=1, source_target_pairs={{0,16},{1,17},{2,18},{3,19},{4,12},{5,13},{6,14},{7,15},{8,24},{9,... | collective-permute-start | bytes 1179656 | tf_op jit(solution)/shard_map/ppermute | solution.py:106
  131.0 18.0 %collective-permute-start.28 = (bf16[8,192,128]{2,1,0:T(8,128)(2,1)}, bf16[8,192,128]{2,1,0:T(8,128)(2,1)S(1)}, u32[]{:S(2)}, u32[]{:S(2)}) collective-permute-start(bf16[8,192,128]{2,1,0:T(8,128)(2,1)} %get-tuple-element.149), channel_id=1, source_target_pairs={{0,16},{1,17},{2,18},{3,19},{4,12},{5,13},{6,14},{7,15},{8,24},{9,... | collective-permute-start | bytes 1179656 | tf_op jit(solution)/shard_map/ppermute | solution.py:106
  137.4 23.9 %collective-permute-start.38 = (bf16[4,10,16,512]{3,2,1,0:T(8,128)(2,1)}, bf16[4,10,16,512]{3,2,1,0:T(8,128)(2,1)}, u32[]{:S(2)}, u32[]{:S(2)}) collective-permute-start(bf16[4,10,16,512]{3,2,1,0:T(8,128)(2,1)} %fusion.1), channel_id=1, source_target_pairs={{0,8},{1,9},{2,10},{3,11},{4,20},{5,21},{6,22},{7,23},{8,0},{9,1},... | collective-permute-start | bytes 1966088 | tf_op jit(solution)/shard_map/ppermute | solution.py:106
  141.7 12.6 %collective-permute-start.30 = (bf16[8,192,128]{2,1,0:T(8,128)(2,1)}, bf16[8,192,128]{2,1,0:T(8,128)(2,1)}, u32[]{:S(2)}, u32[]{:S(2)}) collective-permute-start(bf16[8,192,128]{2,1,0:T(8,128)(2,1)} %add_convert_fusion.2), channel_id=1, source_target_pairs={{0,8},{1,9},{2,10},{3,11},{4,20},{5,21},{6,22},{7,23},{8,0},{9,1},... | collective-permute-start | bytes 1179656 | tf_op jit(solution)/shard_map/ppermute | solution.py:106
  160.0 6.6 %collective-permute-start.32 = (bf16[4,64,512]{2,1,0:T(8,128)(2,1)}, bf16[4,64,512]{2,1,0:T(8,128)(2,1)S(1)}, u32[]{:S(2)}, u32[]{:S(2)}) collective-permute-start(bf16[4,64,512]{2,1,0:T(8,128)(2,1)} %get-tuple-element.153), channel_id=1, source_target_pairs={{0,8},{1,9},{2,10},{3,11},{4,20},{5,21},{6,22},{7,23},{8,0},{9,1},... | collective-permute-start | bytes 786440 | tf_op jit(solution)/shard_map/ppermute | solution.py:106
  163.0 8.9 %collective-permute-start.39 = (bf16[2,10,16,512]{3,2,1,0:T(8,128)(2,1)S(1)}, bf16[2,10,16,512]{3,2,1,0:T(8,128)(2,1)S(1)}, u32[]{:S(2)}, u32[]{:S(2)}) collective-permute-start(bf16[2,10,16,512]{3,2,1,0:T(8,128)(2,1)S(1)} %slice.91), channel_id=1, source_target_pairs={{0,1},{1,0},{2,3},{3,2},{4,5},{5,4},{6,7},{7,6},{8,9},{9,8},{10,11... | collective-permute-start | bytes 983048 | tf_op jit(solution)/shard_map/ppermute | solution.py:98
  163.9 9.3 %collective-permute-start.31 = (bf16[4,192,512]{2,1,0:T(8,128)(2,1)S(1)}, bf16[4,192,512]{2,1,0:T(8,128)(2,1)S(1)}, u32[]{:S(2)}, u32[]{:S(2)}) collective-permute-start(bf16[4,192,512]{2,1,0:T(8,128)(2,1)S(1)} %copy-done.30), channel_id=1, source_target_pairs={{0,4},{1,5},{2,6},{3,7},{4,0},{5,1},{6,2},{7,3},{8,12},{9,13},{10,... | collective-permute-start | bytes 2359304 | tf_op jit(solution)/shard_map/ppermute | solution.py:98
  166.7 6.5 %collective-permute-start.33 = (bf16[4,64,512]{2,1,0:T(8,128)(2,1)S(1)}, bf16[4,64,512]{2,1,0:T(8,128)(2,1)S(1)}, u32[]{:S(2)}, u32[]{:S(2)}) collective-permute-start(bf16[4,64,512]{2,1,0:T(8,128)(2,1)S(1)} %add_convert_fusion.4.dw_ref), channel_id=1, source_target_pairs={{0,16},{1,17},{2,18},{3,19},{4,12},{5,13},{6,14},{7,15},{8,24},{9,... | collective-permute-start | bytes 786440 | tf_op jit(solution)/shard_map/ppermute | solution.py:106
  172.1 9.3 %collective-permute-start.40 = (bf16[10,16,512]{2,1,0:T(8,128)(2,1)S(1)}, bf16[10,16,512]{2,1,0:T(8,128)(2,1)S(1)}, u32[]{:S(2)}, u32[]{:S(2)}) collective-permute-start(bf16[10,16,512]{2,1,0:T(8,128)(2,1)S(1)} %slice_bitcast_fusion), channel_id=1, source_target_pairs={{0,2},{1,3},{2,0},{3,1},{4,6},{5,7},{6,4},{7,5},{8,10},{9,11},{10,... | collective-permute-start | bytes 491528 | tf_op jit(solution)/shard_map/ppermute | solution.py:98
  176.7 15.7 %collective-permute-start.34 = (bf16[256,512]{1,0:T(8,128)(2,1)}, bf16[256,512]{1,0:T(8,128)(2,1)S(1)}, u32[]{:S(2)}, u32[]{:S(2)}) collective-permute-start(bf16[256,512]{1,0:T(8,128)(2,1)} %get-tuple-element.155), channel_id=1, source_target_pairs={{0,1},{1,0},{2,3},{3,2},{4,5},{5,4},{6,7},{7,6},{8,9},{9,8},{10,11... | collective-permute-start | bytes 786440 | tf_op jit(solution)/shard_map/ppermute | solution.py:98
  177.6 21.1 %collective-permute-start.35 = (bf16[256,512]{1,0:T(8,128)(2,1)}, bf16[256,512]{1,0:T(8,128)(2,1)S(1)}, u32[]{:S(2)}, u32[]{:S(2)}) collective-permute-start(bf16[256,512]{1,0:T(8,128)(2,1)} %get-tuple-element.156), channel_id=1, source_target_pairs={{0,2},{1,3},{2,0},{3,1},{4,6},{5,7},{6,4},{7,5},{8,10},{9,11},{10,... | collective-permute-start | bytes 786440 | tf_op jit(solution)/shard_map/ppermute | solution.py:98
  178.8 19.9 %collective-permute-start.36 = (bf16[256,512]{1,0:T(8,128)(2,1)}, bf16[256,512]{1,0:T(8,128)(2,1)S(1)}, u32[]{:S(2)}, u32[]{:S(2)}) collective-permute-start(bf16[256,512]{1,0:T(8,128)(2,1)} %get-tuple-element.157), channel_id=1, source_target_pairs={{0,3},{1,2},{2,1},{3,0},{4,7},{5,6},{6,5},{7,4},{8,11},{9,10},{10,... | collective-permute-start | bytes 786440 | tf_op jit(solution)/shard_map/ppermute | solution.py:98
  184.8 7.7 %collective-permute-start.42 = (bf16[10,16,512]{2,1,0:T(8,128)(2,1)S(1)}, bf16[10,16,512]{2,1,0:T(8,128)(2,1)S(1)}, u32[]{:S(2)}, u32[]{:S(2)}) collective-permute-start(bf16[10,16,512]{2,1,0:T(8,128)(2,1)S(1)} %fusion.2), channel_id=1, source_target_pairs={{0,16},{1,17},{2,18},{3,19},{4,12},{5,13},{6,14},{7,15},{8,24},{9,... | collective-permute-start | bytes 491528 | tf_op jit(solution)/shard_map/ppermute | solution.py:106
  187.5 6.5 %collective-permute-start.43 = (bf16[10,16,512]{2,1,0:T(8,128)(2,1)S(1)}, bf16[10,16,512]{2,1,0:T(8,128)(2,1)S(1)}, u32[]{:S(2)}, u32[]{:S(2)}) collective-permute-start(bf16[10,16,512]{2,1,0:T(8,128)(2,1)S(1)} %collective-permute-done.41), channel_id=1, source_target_pairs={{0,16},{1,17},{2,18},{3,19},{4,12},{5,13},{6,14},{7,15},{8,24},{9,... | collective-permute-start | bytes 491528 | tf_op jit(solution)/shard_map/ppermute | solution.py:106
  194.1 6.4 %collective-permute-start.44 = (bf16[4,10,16,512]{3,2,1,0:T(8,128)(2,1)S(1)}, bf16[4,10,16,512]{3,2,1,0:T(8,128)(2,1)S(1)}, u32[]{:S(2)}, u32[]{:S(2)}) collective-permute-start(bf16[4,10,16,512]{3,2,1,0:T(8,128)(2,1)S(1)} %pad_maximum_fusion.2.refs_5_), channel_id=1, source_target_pairs={{0,4},{1,5},{2,6},{3,7},{4,0},{5,1},{6,2},{7,3},{8,12},{9,13},{10,... | collective-permute-start | bytes 1966088 | tf_op jit(solution)/shard_map/ppermute | solution.py:98
  (55 other events, 261.4 us)
